TPU v7x, 32 devices: a whole 2x2x4 slice. The times are simulated.
32 devices in a mesh: grp: 2 (over x), chan: 4 (over y, core), ctx: 4 (over z).
Axes of the slice: x: 2, y: 2, z: 4, core: 2. Of those that a mesh axis runs over, the one named last changes fastest.
Arguments:
- features: bfloat16 [4096, 4096], P(('grp', 'ctx'), 'chan'), parts along dimension 0, may hold values from -6 to 6
- filter_taps: bfloat16 [2048, 4096], P(None, 'chan'), may hold values from -0.125 to 0.125
- skip_gain: float32 [4096], P('chan'), may hold values from -4 to 4
- in_weight: bfloat16 [4096, 3, 4096], P(None, None, 'chan'), may hold values from -0.09375 to 0.09375
- out_weight: bfloat16 [4096, 4096], P(None, 'chan'), may hold values from -0.125 to 0.125
Outputs:
- layer_out: bfloat16 [4096, 4096], P(('grp', 'ctx'), 'chan'), parts along dimension 0
There are 2 independent parts, one for each index of `grp`. A program takes and returns all parts, laid end to end along the dimension named above; an argument that names none is the same for every part. Nothing has to cross between parts.
All inputs are finite; a program needn't handle non-finite values.
Results may differ from a plain program's by a relative error of at most 0.013.
Values may be sent and summed in bfloat16 or wider, within the bound.
No kernel may reach another device: no remote copies, remote signals or barrier semaphores. Data moves between devices by JAX's collectives and lax.ppermute only.
A program may use at most 320 MiB of HBM per device.

v0:
```python
import math

import jax
import jax.numpy as jnp
from jax import lax
from jax.sharding import PartitionSpec as P

P_SIZE = 128


def dft_tables(block_len):
    period = 2 * block_len
    freq_col = jnp.arange(period, dtype=jnp.int32)[:, None]
    place_row = jnp.arange(period, dtype=jnp.int32)[None, :]
    angles = (freq_col * place_row % period).astype(jnp.float32) * (2.0 * math.pi / period)
    forward = jnp.concatenate([jnp.cos(angles), -jnp.sin(angles)], axis=0).astype(jnp.bfloat16)
    out_place = jnp.arange(block_len, dtype=jnp.int32)[:, None] + block_len
    angle_out = (out_place * place_row % period).astype(jnp.float32) * (2.0 * math.pi / period)
    inverse = (jnp.concatenate([jnp.cos(angle_out), -jnp.sin(angle_out)], axis=1) / period).astype(
        jnp.bfloat16
    )
    return (forward, inverse)


def input_spectra(token_rows, forward):
    channels = token_rows.shape[1]
    grouped = token_rows.reshape(token_rows.shape[0] // P_SIZE, P_SIZE, channels)
    spectra = jnp.einsum(
        "fp,bpc->bfc", forward[:, :P_SIZE], grouped, preferred_element_type=jnp.float32
    )
    return spectra.astype(jnp.bfloat16)


def segment_spectra(padded, forward):
    channels = padded.shape[1]
    count = padded.shape[0] // P_SIZE - 1
    tap_blocks = padded.reshape(count + 1, P_SIZE, channels)
    segments = jnp.concatenate([tap_blocks[:-1], tap_blocks[1:]], axis=1)
    spectra = jnp.einsum("fn,knc->kfc", forward, segments, preferred_element_type=jnp.float32)
    return spectra.astype(jnp.bfloat16)


def shards(features, filter_taps, skip_gain, in_weight, out_weight):
    forward, inverse = dft_tables(P_SIZE)
    channels = in_weight.shape[2]
    tok_rows = features.shape[0]
    per_dev = tok_rows // P_SIZE
    period = 2 * P_SIZE
    total_blocks = per_dev * lax.axis_size("ctx")
    first_mine = lax.axis_index("ctx") * per_dev
    last_mine = first_mine + per_dev - 1
    padded_all = jnp.concatenate([jnp.zeros((P_SIZE, channels), jnp.bfloat16), filter_taps], axis=0)
    lag_spectra = segment_spectra(padded_all, forward)
    flipped = jnp.concatenate([lag_spectra[::-1], jnp.zeros_like(lag_spectra)], axis=0)
    flat_in = in_weight.reshape(in_weight.shape[0], 3 * channels)
    weight_slice = flat_in
    projected = jnp.dot(
        lax.all_gather(features, "chan", axis=1, tiled=True),
        weight_slice,
        preferred_element_type=jnp.float32,
    )
    query_rows = projected[:, :channels].astype(jnp.bfloat16)
    mixed_in = (projected[:, channels : 2 * channels] * projected[:, 2 * channels :]).astype(
        jnp.bfloat16
    )

    def add_spectra(running, source):
        source_re = source[:, :period].astype(jnp.float32)
        source_im = source[:, period:].astype(jnp.float32)
        outputs = []
        for out_block in range(per_dev):
            start_lag = total_blocks - 1 - (first_mine + out_block)
            window = lax.dynamic_slice_in_dim(flipped, start_lag, source.shape[0], 0).astype(
                jnp.float32
            )
            lag_re = window[:, :period]
            lag_im = window[:, period:]
            out_re = jnp.sum(lag_re * source_re - lag_im * source_im, axis=0)
            out_im = jnp.sum(lag_re * source_im + lag_im * source_re, axis=0)
            outputs.append(jnp.concatenate([out_re, out_im], axis=0))
        return running + jnp.stack(outputs)

    zero_spectra = jnp.zeros((per_dev, 2 * period, channels), jnp.float32)
    portion = lax.all_gather(mixed_in, "ctx", axis=0, tiled=True)
    first_in = jnp.int32(0) // P_SIZE

    def accumulate(current):
        return add_spectra(current, input_spectra(portion, forward))

    summed = lax.cond(first_in <= last_mine, accumulate, lambda current: current, zero_spectra)
    block_spectra = summed.astype(jnp.bfloat16)
    conv_out = jnp.einsum(
        "tf,bfc->btc", inverse, block_spectra, preferred_element_type=jnp.float32
    ).reshape(tok_rows, channels)
    gated_rows = (
        query_rows.astype(jnp.float32)
        * (conv_out + skip_gain[None, :] * mixed_in.astype(jnp.float32))
    ).astype(jnp.bfloat16)
    weight_slice = out_weight
    layer_out = jnp.dot(
        lax.all_gather(gated_rows, "chan", axis=1, tiled=True),
        weight_slice,
        preferred_element_type=jnp.float32,
    )
    return layer_out.astype(jnp.bfloat16)


def solution(mesh):
    return jax.shard_map(
        shards,
        mesh=mesh,
        in_specs=(
            P(("grp", "ctx"), "chan"),
            P(None, "chan"),
            P("chan"),
            P(None, None, "chan"),
            P(None, "chan"),
        ),
        out_specs=P(("grp", "ctx"), "chan"),
        check_vma=False,
    )
```

profile of v0, /device:TPU:0, one launch (start us, length us, event | category | flops | bytes accessed | tf_op | source)
XLA Modules:
  0.0 333.9 jit_solution(129528146827862470)
XLA Ops:
  6.5 0.7 all-gather.4.cloned.1.call-update
  7.3 31.7 %copy.13 = bf16[4096,3,1024]{0,2,1:T(8,128)(2,1)} copy(bf16[4096,3,1024]{2,0,1:T(8,128)(2,1)} %param.10) | data formatting | bytes 50331648 | tf_op args[3]
  39.0 7.1 %all-gather.4.cloned.1.call-done = bf16[512,4096]{1,0:T(8,128)(2,1)} async-done(((bf16[512,1024]{1,0:T(8,128)(2,1)}), bf16[512,4096]{1,0:T(8,128)(2,1)}) %all-gather.4.cloned.1.call-update) | async-done | bytes 4194320 | tf_op jit(solution)/shard_map/all_gather | solution.py:58
  46.1 17.9 %fusion.50 = f32[512,3072]{1,0:T(8,128)S(1)} fusion(bf16[512,4096]{1,0:T(8,128)(2,1)} %all-gather.4.cloned.1.call-done, bf16[4096,3072]{0,1:T(8,128)(2,1)} %bitcast.39), kind=kOutput, calls=%fused_computation.93 | convolution fusion | flops 12884901888 | bytes 35651584 | tf_op jit(solution)/shard_map/dot_general | solution.py:57
  64.0 2.6 copy-done
  66.6 1.3 fusion.25
  67.9 4.5 %pad_slice_fusion = bf16[2048,1024]{1,0:T(8,128)(2,1)} fusion(bf16[2048,1024]{1,0:T(8,128)(2,1)} %param.8), kind=kLoop, calls=%fused_computation.52 | loop fusion | bytes 8388608 | tf_op jit(solution)/shard_map/slice | solution.py:38
  72.4 6.5 %copy.14 = bf16[16,128,1024]{1,2,0:T(8,128)(2,1)} copy(bf16[16,128,1024]{2,1,0:T(8,128)(2,1)} %bitcast.41) | data formatting | bytes 8388608 | tf_op jit(solution)/shard_map/slice | solution.py:38
  78.9 6.4 %copy.15 = bf16[16,128,1024]{1,2,0:T(8,128)(2,1)} copy(bf16[16,128,1024]{2,1,0:T(8,128)(2,1)} %bitcast.40) | data formatting | bytes 8388608 | tf_op jit(solution)/shard_map/slice | solution.py:38
  85.3 1.1 negate_convert_fusion
  86.4 10.4 %convert_bitcast_fusion.1 = bf16[16,512,1024]{1,2,0:T(8,128)(2,1)} fusion(bf16[16,128,1024]{1,2,0:T(8,128)(2,1)} %copy.15, bf16[16,128,1024]{1,2,0:T(8,128)(2,1)} %copy.14, bf16[256,256]{1,0:T(8,128)(2,1)S(1)} %get-tuple-element.49, bf16[256,256]{1,0:T(8,128)(2,1)S(1)} %get-tuple-element.50), kind=kOutput, calls=%fused_computation.48 | convolution fusion | flops 4320657408 | bytes 25427968 | tf_op jit(solution)/shard_map/fn,knc->kfc/dot_general | solution.py:39
  96.8 13.8 %rev.3 = bf16[16,512,1024]{1,2,0:T(8,128)(2,1)} reverse(bf16[16,512,1024]{1,2,0:T(8,128)(2,1)} %convert_bitcast_fusion.1), dimensions={0} | reverse | bytes 33554432 | tf_op jit(solution)/shard_map/rev | solution.py:54
  110.6 1.2 fusion.46
  111.8 36.9 %all-gather.6.cloned.1.call-done = bf16[2048,1024]{1,0:T(8,128)(2,1)} async-done(((bf16[512,1024]{1,0:T(8,128)(2,1)}), bf16[2048,1024]{1,0:T(8,128)(2,1)}) %all-gather.6.cloned.1.call-update) | async-done | bytes 4194320 | tf_op jit(solution)/shard_map/all_gather | solution.py:84
  148.8 110.0 %conditional.1 = (bf16[4,512,1024]{1,2,0:T(8,128)(2,1)}) conditional(s32[]{:T(128)} %convert_element_type.68, () %tuple.13, (bf16[16,512,1024]{1,2,0:T(8,128)(2,1)}, s32[]{:T(128)}, bf16[2048,1024]{1,0:T(8,128)(2,1)}, bf16[512,256]{1,0:T(8,128)(2,1)S(1)}) %tuple.14), branch_computations={%region_0.1_spmd, %region_1.10_spmd} | conditional | flops 2344615936 | bytes 344064256 | solution.py:90
  148.8 45.6 %fusion.18 = (f32[16,512,1024]{1,2,0:T(8,128)}, f32[16,512,1024]{1,2,0:T(8,128)}, f32[16,512,1024]{1,2,0:T(8,128)}, f32[16,512,1024]{1,2,0:T(8,128)}) fusion(s32[]{:T(128)S(6)} %select_n.25, bf16[16,512,1024]{1,2,0:T(8,128)(2,1)} %get-tuple-element.19, s32[]{:T(128)S(6)} %select_n.24, s32[]{:T(128)S(6)} %select_n.26, s32[]{:T(128)S(6)} %select_n.23), kind=kLoop, calls=%fused_computation.38 | loop fusion | flops 33554432 | bytes 150994960 | tf_op jit(solution)/shard_map/cond/branch_1_fun/convert_element_type | solution.py:73
  194.3 10.4 %convert_bitcast_fusion = bf16[16,512,1024]{1,2,0:T(8,128)(2,1)} fusion(bf16[16,128,1024]{2,1,0:T(8,128)(2,1)} %bitcast.42, bf16[512,256]{1,0:T(8,128)(2,1)S(1)} %get-tuple-element.22), kind=kOutput, calls=%fused_computation.40 | convolution fusion | flops 2155872256 | bytes 21102592 | tf_op jit(solution)/shard_map/cond/branch_1_fun/fp,bpc->bfc/dot_general | solution.py:28
  204.8 49.9 %fusion.5 = (bf16[256,1024]{0,1:T(8,128)(2,1)S(1)}, bf16[256,1024]{0,1:T(8,128)(2,1)S(1)}, bf16[256,1024]{0,1:T(8,128)(2,1)S(1)}, bf16[256,1024]{0,1:T(8,128)(2,...) fusion(f32[16,512,1024]{1,2,0:T(8,128)} %get-tuple-element.40, ...), kind=kLoop, calls=%fused_computation.25 | loop fusion | flops 140509184 | bytes 155189248 | tf_op jit(solution)/shard_map/cond/branch_1_fun/reduce_sum | solution.py:78
  254.7 1.4 maximum_bitcast_fusion
  256.3 2.5 pad_maximum_fusion
  258.7 3.7 %fusion.40 = f32[4,1024,128]{1,2,0:T(8,128)S(1)} fusion(bf16[4,512,1024]{1,2,0:T(8,128)(2,1)} %get-tuple-element.51, f32[128,256]{1,0:T(8,128)} %get-tuple-element.48, f32[128,256]{1,0:T(8,128)S(1)} %get-tuple-element.47), kind=kOutput, calls=%fused_computation.82 | convolution fusion | flops 537067520 | bytes 6553600 | tf_op jit(solution)/shard_map/tf,bfc->btc/dot_general | solution.py:92
  262.4 4.7 %fusion.27 = bf16[512,1024]{1,0:T(8,128)(2,1)} fusion(f32[4,1024,128]{1,2,0:T(8,128)S(1)} %fusion.40, f32[512,3072]{1,0:T(8,128)} %copy-done, f32[1024]{0:T(1024)S(1)} %copy-done.1), kind=kLoop, calls=%fused_computation.58 | loop fusion | flops 4194304 | bytes 8392704 | tf_op jit(solution)/shard_map/convert_element_type | solution.py:98
  267.1 50.1 %all-gather.8.cloned.1.call-done = bf16[512,4096]{1,0:T(8,128)(2,1)} async-done(((bf16[512,1024]{1,0:T(8,128)(2,1)}), bf16[512,4096]{1,0:T(8,128)(2,1)}) %all-gather.8.cloned.1.call-update) | async-done | bytes 4194320 | tf_op jit(solution)/shard_map/all_gather | solution.py:101
  317.2 10.1 %convolution_convert_fusion = bf16[512,1024]{1,0:T(8,128)(2,1)} fusion(bf16[512,4096]{1,0:T(8,128)(2,1)} %all-gather.8.cloned.1.call-done, bf16[4096,1024]{1,0:T(8,128)(2,1)} %param.11), kind=kOutput, calls=%fused_computation.59 | convolution fusion | flops 4295491584 | bytes 13631488 | tf_op jit(solution)/shard_map/dot_general | solution.py:100
  (11 shorter events, 0.3 us)
Async XLA Ops:
  6.5 39.6 %all-gather.4.cloned.1.call-start = ((), (), s32[]{:S(2)}) async-start(), calls=%async_computation | async-start | bytes 5242880 | tf_op jit(solution)/shard_map/all_gather | solution.py:58
  7.3 141.5 %all-gather.6.cloned.1.call-start = ((), (), s32[]{:S(2)}) async-start(), calls=%async_computation.1 | async-start | bytes 5242880 | tf_op jit(solution)/shard_map/all_gather | solution.py:84
  64.0 2.6 copy-start
  67.9 249.4 %all-gather.8.cloned.1.call-start = ((), (), s32[]{:S(2)}) async-start(), calls=%async_computation.2 | async-start | bytes 5242880 | tf_op jit(solution)/shard_map/all_gather | solution.py:101
  258.7 3.7 %copy-start.1 = (f32[1024]{0:T(1024)S(1)}, f32[1024]{0:T(1024)}, u32[]{:S(2)}) copy-start(f32[1024]{0:T(1024)} %param.9) | copy-start | bytes 12292
Sparse Core Ops, SparseCore 0:
  8.9 37.1 all-gather.3
  68.0 80.7 all-gather.5
  267.3 49.9 all-gather.7
where the time goes:
time: 335 us; the launch traced here: 334 us
  other arithmetic  108 us (32%)
  waiting for transfers between devices  94.9 us (28%)
  local copies, waits for them, and re-layouts  65.4 us (20%)
  matrix products  52.5 us (16%)
  between operations  13.2 us (4%)
    all_gather x1, waiting for transfers between devices, shards(): lax.all_gather(gated_rows, 'chan', axis=1, tiled=True)  50.1 us
    reduce_sum x1, other arithmetic, add_spectra(): out_re = jnp.sum(lag_re * source_re - lag_im * source_im, axis=0)  49.9 us
    convert_element_type x1, other arithmetic, add_spectra(): lax.dynamic_slice_in_dim(flipped, start_lag, source.shape[0], 0)  45.6 us
    all_gather x1, waiting for transfers between devices, shards(): portion = lax.all_gather(mixed_in, 'ctx', axis=0, tiled=True)  36.9 us
    unnamed x5, local copies, waits for them, and re-layouts  34.3 us
    dot_general x1, matrix products, shards(): jnp.dot(lax.all_gather(features, 'chan', axis=1, tiled=True), weight_slic...  17.9 us
    slice x3, local copies, waits for them, and re-layouts, segment_spectra(): segments = jnp.concatenate([tap_blocks[:-1], tap_blocks[1:]], axis=1)  17.3 us
    rev x1, local copies, waits for them, and re-layouts, shards(): lag_spectra[::-1]  13.8 us
  transfers between devices with their start and end apart: 3, of which 3 were waited for; matrix products, arithmetic and copies ran while one was open for 23% of the time, Pallas kernels for 0%

commit v1 on v0

v1 whole, which is shorter than its diff:
```python
import functools
import math

import jax
import jax.numpy as jnp
import ml_dtypes
import numpy as np
from jax import lax
from jax.experimental import pallas as pl
from jax.experimental.pallas import tpu as pltpu
from jax.sharding import PartitionSpec as P


BF16 = jnp.bfloat16
F32 = jnp.float32
LANES = 128
MIB = 1 << 20
CHUNKS = 2
BLOCK = 256
VMEM = pl.BlockSpec(memory_space=pltpu.VMEM)


def real_dft_tables(block):
    period = 2 * block
    freq = np.arange(block)[:, None]
    place = np.arange(block)[None, :]
    angle = (freq * place % period) * (2.0 * math.pi / period)
    lower = -np.sin(angle)
    lower[0] = 1.0 - 2.0 * (np.arange(block) % 2)
    forward = np.concatenate([np.cos(angle), lower], axis=0)
    out_place = np.arange(block)[:, None] + block
    freq_row = np.arange(block)[None, :]
    angle_out = (out_place * freq_row % period) * (2.0 * math.pi / period)
    weight = np.where(freq_row == 0, 1.0, 2.0)
    lower_out = -np.sin(angle_out) * weight
    lower_out[:, 0] = 1.0 - 2.0 * (np.arange(block) % 2)
    inverse = np.concatenate([np.cos(angle_out) * weight, lower_out], axis=1) / period
    return forward.astype(ml_dtypes.bfloat16), inverse.astype(ml_dtypes.bfloat16)


def call(kernel, out, operands, limit, flops, moved, scratch=()):
    return pl.pallas_call(
        kernel,
        out_shape=out,
        in_specs=[VMEM] * len(operands),
        out_specs=jax.tree.map(lambda _: VMEM, out),
        scratch_shapes=scratch,
        compiler_params=pltpu.CompilerParams(vmem_limit_bytes=limit * MIB),
        cost_estimate=pl.CostEstimate(flops=flops, bytes_accessed=moved, transcendentals=0),
    )(*operands)


def chan_sources():
    n_chan, chan = lax.axis_size("chan"), lax.axis_index("chan")
    sources = [chan, chan ^ 1]
    for hop in range(1, n_chan // 2):
        far = (chan - 2 * hop + n_chan) % n_chan
        sources += [far, far ^ 1]
    return sources


def rows_at(first, count):
    return pl.ds(pl.multiple_of(first * count, count), count)


def prologue_kernel(
    width, fwd_ref, skip_ref, taps_ref, w_ref, kv_ref, query_ref, out_ref, skip_out, taps_in, prev_ref, sems
):
    block = fwd_ref.shape[1]
    cols = rows_at(lax.axis_index("ctx"), width)
    copies = [
        pltpu.make_async_copy(taps_ref.at[:, cols], taps_in, sems.at[0]),
        pltpu.make_async_copy(w_ref.at[1:3], kv_ref, sems.at[1]),
        pltpu.make_async_copy(w_ref.at[0], query_ref, sems.at[2]),
    ]
    for copy in copies:
        copy.start()
    prev_ref[...] = jnp.zeros_like(prev_ref)
    skip_out[...] = skip_ref[...]
    copies[0].wait()

    @pl.loop(0, out_ref.shape[0])
    def _(k):
        now = jnp.dot(fwd_ref[...], taps_in[rows_at(k, block), :], preferred_element_type=F32)
        parity = lax.broadcasted_iota(jnp.int32, now.shape, 0) % 2
        out_ref[k] = prev_ref[...] + jnp.where(parity == 0, now, -now)
        prev_ref[...] = now

    for copy in copies[1:]:
        copy.wait()


def prologue(forward, skip, taps, w, width):
    rows, block = forward.shape
    count = taps.shape[0] // block
    out = [
        jax.ShapeDtypeStruct((2, *w.shape[1:]), BF16),
        jax.ShapeDtypeStruct(w.shape[1:], BF16),
        jax.ShapeDtypeStruct((count, rows, width), F32),
        jax.ShapeDtypeStruct(skip.shape, F32),
    ]
    hbm = pl.BlockSpec(memory_space=pl.ANY)
    return pl.pallas_call(
        functools.partial(prologue_kernel, width),
        out_shape=out,
        in_specs=[VMEM, VMEM, hbm, hbm],
        out_specs=[VMEM] * 4,
        scratch_shapes=[
            pltpu.VMEM((taps.shape[0], width), BF16),
            pltpu.VMEM((rows, width), F32),
            pltpu.SemaphoreType.DMA((3,)),
        ],
        compiler_params=pltpu.CompilerParams(vmem_limit_bytes=6 * MIB),
        cost_estimate=pl.CostEstimate(
            flops=2 * count * rows * block * width,
            bytes_accessed=2 * w.size + count * width * (rows * 4 + block * 2),
            transcendentals=0,
        ),
        name="prologue",
    )(forward, skip, taps, w)


def kv_kernel(n_pieces, n_out, starts, w_ref, *refs):
    pieces, outs = refs[:n_pieces], refs[n_pieces:]
    tokens, width = outs[0].shape
    depth = pieces[0].shape[1]
    me = lax.axis_index("ctx")
    sources = chan_sources()
    for k in range(n_out):
        cols = rows_at((me + k) % n_out, width)
        key = value = None
        for j, piece in enumerate(pieces):
            x = piece[starts[j] : starts[j] + tokens, :]
            rows = rows_at(sources[j], depth)
            a = jnp.dot(x, w_ref[0, rows, cols], preferred_element_type=F32)
            b = jnp.dot(x, w_ref[1, rows, cols], preferred_element_type=F32)
            key = a if key is None else key + a
            value = b if value is None else value + b
        outs[k][...] = (key * value).astype(BF16)


def mixed_inputs(pieces, starts, tokens, w, n_ctx):
    total, width = w.shape[1], w.shape[2] // n_ctx
    return call(
        functools.partial(kv_kernel, len(pieces), n_ctx, starts),
        [jax.ShapeDtypeStruct((tokens, width), BF16)] * n_ctx,
        [w, *pieces],
        6,
        4 * tokens * total * width * n_ctx,
        4 * total * width * n_ctx + 2 * tokens * total,
    )


def query_kernel(n_pieces, n_ctx, starts, w_ref, *refs):
    pieces, out_ref = refs[:n_pieces], refs[-1]
    depth = pieces[0].shape[1]
    tokens = out_ref.shape[0]
    width = out_ref.shape[1] // n_ctx
    me = lax.axis_index("ctx")
    sources = chan_sources()
    for k in range(n_ctx):
        cols = rows_at((me + k) % n_ctx, width)
        acc = None
        for j, piece in enumerate(pieces):
            x = piece[starts[j] : starts[j] + tokens, :]
            a = jnp.dot(x, w_ref[rows_at(sources[j], depth), cols], preferred_element_type=F32)
            acc = a if acc is None else acc + a
        out_ref[:, k * width : (k + 1) * width] = acc.astype(BF16)


def queries(pieces, starts, tokens, w, n_ctx):
    total, channels = w.shape
    return call(
        functools.partial(query_kernel, len(pieces), n_ctx, starts),
        jax.ShapeDtypeStruct((tokens, channels), BF16),
        [w, *pieces],
        6,
        2 * tokens * total * channels,
        2 * total * channels + 2 * tokens * total,
    )


def block_products(g_ref, x_ref, y_ref, wanted, width, block):
    def tile(i, first):
        upper = pl.ds(i * 8, 8) if first else rows_at(i, 8)
        lower = pl.ds(block + i * 8, 8) if first else rows_at(block // 8 + i, 8)
        for lane in range(width // LANES):
            cols = pl.ds(lane * LANES, LANES)
            last = max(wanted) + 1
            g_re = [g_ref[b, upper, cols] for b in range(last)]
            g_im = [g_ref[b, lower, cols] for b in range(last)]
            x_re = [x_ref[b, upper, cols] for b in range(last)]
            x_im = [x_ref[b, lower, cols] for b in range(last)]
            g_di = g_re
            if first:
                edge = lax.broadcasted_iota(jnp.int32, (8, LANES), 0) == 0
                g_di = [jnp.where(edge, im, re) for re, im in zip(g_re, g_im)]
                g_im = [jnp.where(edge, 0.0, im) for im in g_im]
            for b in wanted:
                re = g_re[b] * x_re[0] - g_im[b] * x_im[0]
                im = g_di[b] * x_im[0] + g_im[b] * x_re[0]
                for a in range(1, b + 1):
                    re = re + (g_re[b - a] * x_re[a] - g_im[b - a] * x_im[a])
                    im = im + (g_di[b - a] * x_im[a] + g_im[b - a] * x_re[a])
                y_ref[b, upper, cols] = re
                y_ref[b, lower, cols] = im

    tile(0, True)
    pl.loop(1, block // 8)(lambda i: tile(i, False))


def conv_kernel(n_ctx, chunks, fwd_ref, inv_ref, g_ref, *refs):
    n_in = n_ctx * chunks
    ins, outs = refs[:n_in], refs[n_in : 2 * n_in]
    x_ref, y_ref = refs[2 * n_in :]
    me = lax.axis_index("ctx")
    blocks, rows, width = g_ref.shape
    block = rows // 2
    tokens = ins[0].shape[0]
    parts = block // tokens
    per_dev = blocks // n_ctx
    for k in range(n_ctx):
        source = (me - k + n_ctx) % n_ctx
        for b in range(per_dev):
            total = None
            for p in range(parts):
                piece = ins[(b * parts + p) * n_ctx + k][...]
                a = jnp.dot(fwd_ref[:, p * tokens : (p + 1) * tokens], piece, preferred_element_type=F32)
                total = a if total is None else total + a
            x_ref[source * per_dev + b] = total

    block_products(g_ref, x_ref, y_ref, range(blocks), width, block)

    for c in range(chunks):
        for k in range(n_ctx):
            target = (me + k) % n_ctx
            spectrum = y_ref[target * per_dev + c // parts].astype(BF16)
            rows_out = slice(c % parts * tokens, (c % parts + 1) * tokens)
            outs[c * n_ctx + k][...] = jnp.dot(
                inv_ref[rows_out, :], spectrum, preferred_element_type=F32
            ).astype(BF16)


def convolve(forward, inverse, spectra, mixed, n_ctx):
    chunks = len(mixed)
    blocks, rows, width = spectra.shape
    n_in = n_ctx * chunks
    outs = call(
        functools.partial(conv_kernel, n_ctx, chunks),
        [jax.ShapeDtypeStruct(mixed[0][0].shape, BF16)] * n_in,
        [forward, inverse, spectra, *[m for group in mixed for m in group]],
        14,
        2 * blocks * rows * rows * width,
        blocks * rows * width * 8,
        [pltpu.VMEM((blocks, rows, width), F32)] * 2,
    )
    return [outs[c * n_ctx : (c + 1) * n_ctx] for c in range(chunks)]


def gate_kernel(n_ctx, skip_ref, q_ref, *refs):
    mixed, conv, out_ref = refs[:n_ctx], refs[n_ctx : 2 * n_ctx], refs[-1]
    _, width = mixed[0].shape
    me = lax.axis_index("ctx")
    for m in range(n_ctx):
        cols = slice(m * width, (m + 1) * width)
        skip = skip_ref[pl.ds((me + m) % n_ctx, 1), :]
        query = q_ref[:, cols].astype(F32)
        total = conv[(-m) % n_ctx][...].astype(F32) + skip * mixed[m][...].astype(F32)
        out_ref[:, cols] = (query * total).astype(BF16)


def gate(skip, query, mixed, conv, n_ctx):
    shape = (mixed[0].shape[0], query.shape[1])
    return call(
        functools.partial(gate_kernel, n_ctx),
        jax.ShapeDtypeStruct(shape, BF16),
        [skip, query, *mixed, *conv],
        4,
        3 * shape[0] * shape[1],
        8 * shape[0] * shape[1],
    )


def out_kernel(n_pieces, n_ctx, columns, w_ref, *refs):
    pieces, out_ref = refs[:n_pieces], refs[-1]
    width = pieces[0].shape[1] // n_ctx
    cols = rows_at(pl.program_id(0), columns)
    me = lax.axis_index("ctx")
    acc = None
    for j, source in enumerate(chan_sources()):
        for m in range(n_ctx):
            w = w_ref[rows_at(source * n_ctx + (me + m) % n_ctx, width), cols]
            a = jnp.dot(pieces[j][:, m * width : (m + 1) * width], w, preferred_element_type=F32)
            acc = a if acc is None else acc + a
    out_ref[...] = acc.astype(BF16)


def project_out(pieces, w, chunk, rows, before, n_ctx, columns=256):
    tokens = pieces[0].shape[0]
    total, out_width = w.shape
    operands = [w, *pieces]
    specs = [VMEM] * len(operands)
    aliases = {}
    if before is not None:
        specs.append(pl.BlockSpec(memory_space=pl.ANY))
        aliases = {len(operands): 0}
        operands.append(before)
    return pl.pallas_call(
        functools.partial(out_kernel, len(pieces), n_ctx, columns),
        out_shape=jax.ShapeDtypeStruct((rows, out_width), BF16),
        grid=(out_width // columns,),
        in_specs=specs,
        out_specs=pl.BlockSpec((tokens, columns), lambda i: (chunk, i)),
        input_output_aliases=aliases,
        compiler_params=pltpu.CompilerParams(vmem_limit_bytes=6 * MIB),
        cost_estimate=pl.CostEstimate(
            flops=2 * tokens * total * out_width,
            bytes_accessed=2 * total * out_width + 2 * tokens * (total + out_width),
            transcendentals=0,
        ),
        name="out_projection",
    )(*operands)


def shift(x, axis, by):
    n = lax.axis_size(axis)
    return lax.ppermute(x, axis, [(i, (i + by) % n) for i in range(n)])


def swap_cores(x):
    n = lax.axis_size("chan")
    return lax.ppermute(x, "chan", [(i, i ^ 1) for i in range(n)])


def gather_far(x):
    pieces = []
    for hop in range(1, lax.axis_size("chan") // 2):
        far = shift(x, "chan", 2 * hop)
        pieces += [far, swap_cores(far)]
    return pieces


def exchange(parts):
    out = [parts[0]]
    for k in range(1, len(parts)):
        out.append(shift(parts[k], "ctx", k))
    return out


def layer(features, filter_taps, skip_gain, in_weight, out_weight):
    return layer_body(features, filter_taps, skip_gain, in_weight, out_weight)


def layer_body(features, filter_taps, skip_gain, in_weight, out_weight):
    n_ctx = lax.axis_size("ctx")
    rows, channels = features.shape[0], in_weight.shape[2]
    width = channels // n_ctx
    tokens = rows // CHUNKS
    forward, inverse = (jnp.asarray(t) for t in real_dft_tables(BLOCK))
    skip = skip_gain.reshape(n_ctx, width)

    far = [gather_far(features[:tokens])]
    near = swap_cores(features)
    later, skip = lax.optimization_barrier((features, skip))
    for c in range(1, CHUNKS):
        far.append(gather_far(later[c * tokens : (c + 1) * tokens]))
    w_kv, w_q, spectra, skip = prologue(forward, skip, filter_taps, in_weight.transpose(1, 0, 2), width)

    mixed, arrived, query = [], [], []
    for c in range(CHUNKS):
        pieces = [features, near, *far[c]]
        starts = [c * tokens] * 2 + [0] * len(far[c])
        mixed.append(mixed_inputs(pieces, starts, tokens, w_kv, n_ctx))
        arrived.append(exchange(mixed[c]))
        query.append(queries(pieces, starts, tokens, w_q, n_ctx))
    conv = convolve(forward, inverse, spectra, arrived, n_ctx)

    out = None
    for c in range(CHUNKS):
        back = exchange(conv[c])
        gated = gate(skip, query[c], mixed[c], back, n_ctx)
        beside = swap_cores(gated)
        pieces = [gated, beside, *gather_far(gated)]
        out = project_out(pieces, out_weight, c, rows, out, n_ctx)
    return out


P_SIZE = 128


def dft_tables(block_len):
    period = 2 * block_len
    freq_col = jnp.arange(period, dtype=jnp.int32)[:, None]
    place_row = jnp.arange(period, dtype=jnp.int32)[None, :]
    angles = (freq_col * place_row % period).astype(F32) * (2.0 * math.pi / period)
    forward = jnp.concatenate([jnp.cos(angles), -jnp.sin(angles)], axis=0).astype(BF16)
    out_place = jnp.arange(block_len, dtype=jnp.int32)[:, None] + block_len
    angle_out = (out_place * place_row % period).astype(F32) * (2.0 * math.pi / period)
    inverse = (jnp.concatenate([jnp.cos(angle_out), -jnp.sin(angle_out)], axis=1) / period).astype(BF16)
    return (forward, inverse)


def plain_layer(features, filter_taps, skip_gain, in_weight, out_weight):
    forward, inverse = dft_tables(P_SIZE)
    channels = in_weight.shape[2]
    tok_rows = features.shape[0]
    per_dev = tok_rows // P_SIZE
    period = 2 * P_SIZE
    total_blocks = per_dev * lax.axis_size("ctx")
    first_mine = lax.axis_index("ctx") * per_dev
    padded = jnp.concatenate([jnp.zeros((P_SIZE, channels), BF16), filter_taps], axis=0)
    tap_blocks = padded.reshape(total_blocks + 1, P_SIZE, channels)
    segments = jnp.concatenate([tap_blocks[:-1], tap_blocks[1:]], axis=1)
    lag = jnp.einsum("fn,knc->kfc", forward, segments, preferred_element_type=F32).astype(BF16)
    flipped = jnp.concatenate([lag[::-1], jnp.zeros_like(lag)], axis=0)
    gathered = lax.all_gather(features, "chan", axis=1, tiled=True)
    w = in_weight.transpose(1, 0, 2)
    q, k, v = (jnp.dot(gathered, w[s], preferred_element_type=F32) for s in range(3))
    query = q.astype(BF16)
    mixed = (k * v).astype(BF16)
    everyone = lax.all_gather(mixed, "ctx", axis=0, tiled=True).reshape(total_blocks, P_SIZE, channels)
    source = jnp.einsum("fp,bpc->bfc", forward[:, :P_SIZE], everyone, preferred_element_type=F32)
    source = source.astype(BF16).astype(F32)
    source_re, source_im = source[:, :period], source[:, period:]
    outputs = []
    for out_block in range(per_dev):
        start = total_blocks - 1 - (first_mine + out_block)
        window = lax.dynamic_slice_in_dim(flipped, start, total_blocks, 0).astype(F32)
        lag_re, lag_im = window[:, :period], window[:, period:]
        out_re = jnp.sum(lag_re * source_re - lag_im * source_im, axis=0)
        out_im = jnp.sum(lag_re * source_im + lag_im * source_re, axis=0)
        outputs.append(jnp.concatenate([out_re, out_im], axis=0))
    spectra = jnp.stack(outputs).astype(BF16)
    conv = jnp.einsum("tf,bfc->btc", inverse, spectra, preferred_element_type=F32)
    conv = conv.reshape(tok_rows, channels)
    gated = (query.astype(F32) * (conv + skip_gain[None, :] * mixed.astype(F32))).astype(BF16)
    everything = lax.all_gather(gated, "chan", axis=1, tiled=True)
    return jnp.dot(everything, out_weight, preferred_element_type=F32).astype(BF16)


def shards(features, filter_taps, skip_gain, in_weight, out_weight):
    slices = in_weight.shape[2] % (lax.axis_size("ctx") * LANES) == 0
    paired = lax.axis_size("chan") % 2 == 0
    blocks = features.shape[0] % BLOCK == 0 and BLOCK % (features.shape[0] // CHUNKS) == 0
    chosen = layer if slices and paired and blocks else plain_layer
    return chosen(features, filter_taps, skip_gain, in_weight, out_weight)


def solution(mesh):
    return jax.shard_map(
        shards,
        mesh=mesh,
        in_specs=(
            P(("grp", "ctx"), "chan"),
            P(None, "chan"),
            P("chan"),
            P(None, None, "chan"),
            P(None, "chan"),
        ),
        out_specs=P(("grp", "ctx"), "chan"),
        check_vma=False,
    )
```

time: 335 us -> 127 us (0.38)
  the two profiles are of different devices: /device:TPU:0 before, /device:TPU:9 now
where the time goes in v1:
time: 127 us; the launch traced here: 126 us
  waiting for transfers between devices  61 us (48%)
  Pallas kernels  34.6 us (27%)
  starting transfers between devices  24.6 us (19%)
  local copies, waits for them, and re-layouts  6.01 us (5%)
    ppermute x16, waiting for transfers between devices, shift(): return lax.ppermute(x, axis, [(i, (i + by) % n) for i in range(n)])  60.9 us
    pallas_call x7, Pallas kernels, call(): pl.pallas_call(kernel, out_shape=out, in_specs=[VMEM] * len(operands), ou...  18.6 us
    ppermute x16, starting transfers between devices, shift(): return lax.ppermute(x, axis, [(i, (i + by) % n) for i in range(n)])  17 us
    pallas_call x1, Pallas kernels, prologue(): pl.pallas_call(functools.partial(prologue_kernel, width), out_shape=out,...  8.39 us
    pallas_call x2, Pallas kernels, project_out(): pl.pallas_call(functools.partial(out_kernel, len(pieces), n_ctx, columns)...  7.57 us
    ppermute x7, starting transfers between devices, swap_cores(): return lax.ppermute(x, 'chan', [(i, i ^ 1) for i in range(n)])  7.56 us
    unnamed x14, local copies, waits for them, and re-layouts  3.16 us
  transfers between devices with their start and end apart: 23, of which 12 were waited for; matrix products, arithmetic and copies ran while one was open for 2% of the time, Pallas kernels for 21%

profile of v1, /device:TPU:9, one launch (start us, length us, event | category | flops | bytes accessed | tf_op | source)
XLA Modules:
  0.0 126.3 jit_solution(7063752639771827263)
XLA Ops:
  5.1 10.2 %collective-permute-done.3.refs_2_ = bf16[256,1024]{1,0:T(8,128)(2,1)S(1)} collective-permute-done((bf16[256,1024]{1,0:T(8,128)(2,1)S(1)}, bf16[256,1024]{1,0:T(8,128)(2,1)S(1)}, u32[]{:S(2)}, u32[]{:S(2)}) %collective-permute-start.3) | collective-permute-done | bytes 524320 | tf_op jit(solution)/shard_map/ppermute | solution.py:327
  16.6 9.9 %collective-permute-done.1.refs_2_ = bf16[256,1024]{1,0:T(8,128)(2,1)S(1)} collective-permute-done((bf16[256,1024]{1,0:T(8,128)(2,1)S(1)}, bf16[256,1024]{1,0:T(8,128)(2,1)S(1)}, u32[]{:S(2)}, u32[]{:S(2)}) %collective-permute-start.1) | collective-permute-done | bytes 524320 | tf_op jit(solution)/shard_map/ppermute | solution.py:327
  27.4 2.2 %copy-done.1 = bf16[2048,1024]{1,0:T(8,128)(2,1)S(1)} copy-done((bf16[2048,1024]{1,0:T(8,128)(2,1)S(1)}, bf16[2048,1024]{1,0:T(8,128)(2,1)}, u32[]{:S(2)}) %copy-start.1) | copy-done | bytes 4194328
  30.5 8.4 %prologue.1 = (bf16[2,4096,1024]{2,1,0:T(8,128)(2,1)S(1)}, bf16[4096,1024]{1,0:T(8,128)(2,1)S(1)}, f32[8,512,256]{2,1,0:T(8,128)S(1)}, f32[4,256]{1,0:T(4,128)S(1)}) custom-call(bf16[512,256]{1,0:T(8,128)(2,1)S(1)} %copy-done.2, f32[4,256]{1,0:T(4,128)S(1)} %reshape.3.skip_ref, bf16[2048,1024]{1,0:T(8,128)(2,1)S(1)} %copy-done.1, bf16[3,4096,1024]{2,1,0:T(8,128)(2,1)} %bitcast.3), custom_call_target="tpu_custom_call" | custom-call | flops 536870912 | bytes 30408704 | tf_op jit(solution)/shard_map/prologue/pallas_call | solution.py:103
  39.0 4.6 %shard_map.75 = (bf16[256,256]{1,0:T(8,128)(2,1)S(1)}, bf16[256,256]{1,0:T(8,128)(2,1)S(1)}, bf16[256,256]{1,0:T(8,128)(2,1)S(1)}, bf16[256,256]{1,0:T(8,128)(2,1)S(1)}) custom-call(bf16[2,4096,1024]{2,1,0:T(8,128)(2,1)S(1)} %get-tuple-element.31.w_ref, bf16[512,1024]{1,0:T(8,128)(2,1)S(1)} %copy-done, bf16[512,1024]{1,0:T(8,128)(2,1)S(1)} %collective-permute-done.refs_1_, ...), custom_call_target="tpu_custom_call" | custom-call | flops 4294967296 | bytes 18874368 | tf_op jit(solution)/shard_map/pallas_call | solution.py:42
  47.4 4.6 %shard_map.74 = (bf16[256,256]{1,0:T(8,128)(2,1)S(1)}, bf16[256,256]{1,0:T(8,128)(2,1)S(1)}, bf16[256,256]{1,0:T(8,128)(2,1)S(1)}, bf16[256,256]{1,0:T(8,128)(2,1)S(1)}) custom-call(bf16[2,4096,1024]{2,1,0:T(8,128)(2,1)S(1)} %get-tuple-element.31.w_ref, bf16[512,1024]{1,0:T(8,128)(2,1)S(1)} %copy-done, bf16[512,1024]{1,0:T(8,128)(2,1)S(1)} %collective-permute-done.refs_1_, ...), custom_call_target="tpu_custom_call" | custom-call | flops 4294967296 | bytes 18874368 | tf_op jit(solution)/shard_map/pallas_call | solution.py:42
  52.2 3.1 %collective-permute-start.9 = (bf16[256,256]{1,0:T(8,128)(2,1)S(1)}, bf16[256,256]{1,0:T(8,128)(2,1)S(1)}, u32[]{:S(2)}, u32[]{:S(2)}) collective-permute-start(bf16[256,256]{1,0:T(8,128)(2,1)S(1)} %get-tuple-element.34.refs_2_), channel_id=1, source_target_pairs={{0,2},{1,3},{2,0},{3,1},{4,6},{5,7},{6,4},{7,5},{8,10},{9,11},{10,... | collective-permute-start | bytes 393224 | tf_op jit(solution)/shard_map/ppermute | solution.py:327
  55.3 1.4 %collective-permute-done.6.refs_2_ = bf16[256,256]{1,0:T(8,128)(2,1)S(1)} collective-permute-done((bf16[256,256]{1,0:T(8,128)(2,1)S(1)}, bf16[256,256]{1,0:T(8,128)(2,1)S(1)}, u32[]{:S(2)}, u32[]{:S(2)}) %collective-permute-start.6) | collective-permute-done | bytes 131104 | tf_op jit(solution)/shard_map/ppermute | solution.py:327
  56.7 7.3 %collective-permute-done.7.refs_3_ = bf16[256,256]{1,0:T(8,128)(2,1)S(1)} collective-permute-done((bf16[256,256]{1,0:T(8,128)(2,1)S(1)}, bf16[256,256]{1,0:T(8,128)(2,1)S(1)}, u32[]{:S(2)}, u32[]{:S(2)}) %collective-permute-start.7) | collective-permute-done | bytes 131104 | tf_op jit(solution)/shard_map/ppermute | solution.py:327
  64.7 2.8 %collective-permute-done.9.refs_6_ = bf16[256,256]{1,0:T(8,128)(2,1)S(1)} collective-permute-done((bf16[256,256]{1,0:T(8,128)(2,1)S(1)}, bf16[256,256]{1,0:T(8,128)(2,1)S(1)}, u32[]{:S(2)}, u32[]{:S(2)}) %collective-permute-start.9) | collective-permute-done | bytes 131104 | tf_op jit(solution)/shard_map/ppermute | solution.py:327
  67.5 2.1 %collective-permute-done.10.refs_7_ = bf16[256,256]{1,0:T(8,128)(2,1)S(1)} collective-permute-done((bf16[256,256]{1,0:T(8,128)(2,1)S(1)}, bf16[256,256]{1,0:T(8,128)(2,1)S(1)}, u32[]{:S(2)}, u32[]{:S(2)}) %collective-permute-start.10) | collective-permute-done | bytes 131104 | tf_op jit(solution)/shard_map/ppermute | solution.py:327
  69.6 4.1 %shard_map.76 = (bf16[256,256]{1,0:T(8,128)(2,1)S(1)}, bf16[256,256]{1,0:T(8,128)(2,1)S(1)}, bf16[256,256]{1,0:T(8,128)(2,1)S(1)}, bf16[256,256]{1,0:T(8,128)(2,...) custom-call(bf16[512,256]{1,0:T(8,128)(2,1)S(1)} %copy-done.3, ...), custom_call_target="tpu_custom_call" | custom-call | flops 1073741824 | bytes 8388608 | tf_op jit(solution)/shard_map/pallas_call | solution.py:42
  76.2 2.4 %shard_map.78.q_ref = bf16[256,1024]{1,0:T(8,128)(2,1)S(1)} custom-call(bf16[4096,1024]{1,0:T(8,128)(2,1)S(1)} %get-tuple-element.29.w_ref, bf16[512,1024]{1,0:T(8,128)(2,1)S(1)} %copy-done, bf16[512,1024]{1,0:T(8,128)(2,1)S(1)} %collective-permute-done.refs_1_, bf16[256,1024]{1,0:T(8,128)(2,1)S(1)} %collective-permute-done.3.refs_2_, ...), custom_call_target="tpu_custom_call" | custom-call | flops 2147483648 | bytes 10485760 | tf_op jit(solution)/shard_map/pallas_call | solution.py:42
  78.9 3.1 %collective-permute-start.12 = (bf16[256,256]{1,0:T(8,128)(2,1)S(1)}, bf16[256,256]{1,0:T(8,128)(2,1)S(1)}, u32[]{:S(2)}, u32[]{:S(2)}) collective-permute-start(bf16[256,256]{1,0:T(8,128)(2,1)S(1)} %get-tuple-element.43), channel_id=1, source_target_pairs={{0,2},{1,3},{2,0},{3,1},{4,6},{5,7},{6,4},{7,5},{8,10},{9,11},{10,... | collective-permute-start | bytes 393224 | tf_op jit(solution)/shard_map/ppermute | solution.py:327
  82.0 2.5 %collective-permute-done.18.refs_6_ = bf16[256,256]{1,0:T(8,128)(2,1)S(1)} collective-permute-done((bf16[256,256]{1,0:T(8,128)(2,1)S(1)}, bf16[256,256]{1,0:T(8,128)(2,1)S(1)}, u32[]{:S(2)}, u32[]{:S(2)}) %collective-permute-start.18) | collective-permute-done | bytes 131104 | tf_op jit(solution)/shard_map/ppermute | solution.py:327
  84.5 8.3 %collective-permute-done.19.refs_7_ = bf16[256,256]{1,0:T(8,128)(2,1)S(1)} collective-permute-done((bf16[256,256]{1,0:T(8,128)(2,1)S(1)}, bf16[256,256]{1,0:T(8,128)(2,1)S(1)}, u32[]{:S(2)}, u32[]{:S(2)}) %collective-permute-start.19) | collective-permute-done | bytes 131104 | tf_op jit(solution)/shard_map/ppermute | solution.py:327
  94.4 2.4 %shard_map.73.q_ref = bf16[256,1024]{1,0:T(8,128)(2,1)S(1)} custom-call(bf16[4096,1024]{1,0:T(8,128)(2,1)S(1)} %get-tuple-element.29.w_ref, bf16[512,1024]{1,0:T(8,128)(2,1)S(1)} %copy-done, bf16[512,1024]{1,0:T(8,128)(2,1)S(1)} %collective-permute-done.refs_1_, bf16[256,1024]{1,0:T(8,128)(2,1)S(1)} %collective-permute-done.1.refs_2_, ...), custom_call_target="tpu_custom_call" | custom-call | flops 2147483648 | bytes 10485760 | tf_op jit(solution)/shard_map/pallas_call | solution.py:42
  96.8 1.6 %collective-permute-done.13.refs_7_ = bf16[256,256]{1,0:T(8,128)(2,1)S(1)} collective-permute-done((bf16[256,256]{1,0:T(8,128)(2,1)S(1)}, bf16[256,256]{1,0:T(8,128)(2,1)S(1)}, u32[]{:S(2)}, u32[]{:S(2)}) %collective-permute-start.13) | collective-permute-done | bytes 131104 | tf_op jit(solution)/shard_map/ppermute | solution.py:327
  100.7 5.3 %collective-permute-done.21.refs_2_ = bf16[256,1024]{1,0:T(8,128)(2,1)S(1)} collective-permute-done((bf16[256,1024]{1,0:T(8,128)(2,1)S(1)}, bf16[256,1024]{1,0:T(8,128)(2,1)S(1)}, u32[]{:S(2)}, u32[]{:S(2)}) %collective-permute-start.21) | collective-permute-done | bytes 524320 | tf_op jit(solution)/shard_map/ppermute | solution.py:327
  106.0 2.5 %collective-permute-start.22 = (bf16[256,1024]{1,0:T(8,128)(2,1)S(1)}, bf16[256,1024]{1,0:T(8,128)(2,1)S(1)}, u32[]{:S(2)}, u32[]{:S(2)}) collective-permute-start(bf16[256,1024]{1,0:T(8,128)(2,1)S(1)} %collective-permute-done.21.refs_2_), channel_id=1, source_target_pairs={{0,4},{4,0},{8,12},{12,8},{1,5},{5,1},{9,13},{13,9},{2,6},{6,2},{1... | collective-permute-start | bytes 1572872 | tf_op jit(solution)/shard_map/ppermute | solution.py:332
  108.5 8.7 %collective-permute-done.15.refs_2_ = bf16[256,1024]{1,0:T(8,128)(2,1)S(1)} collective-permute-done((bf16[256,1024]{1,0:T(8,128)(2,1)S(1)}, bf16[256,1024]{1,0:T(8,128)(2,1)S(1)}, u32[]{:S(2)}, u32[]{:S(2)}) %collective-permute-start.15) | collective-permute-done | bytes 524320 | tf_op jit(solution)/shard_map/ppermute | solution.py:327
  117.3 1.4 %collective-permute-start.16 = (bf16[256,1024]{1,0:T(8,128)(2,1)S(1)}, bf16[256,1024]{1,0:T(8,128)(2,1)S(1)}, u32[]{:S(2)}, u32[]{:S(2)}) collective-permute-start(bf16[256,1024]{1,0:T(8,128)(2,1)S(1)} %collective-permute-done.15.refs_2_), channel_id=1, source_target_pairs={{0,4},{4,0},{8,12},{12,8},{1,5},{5,1},{9,13},{13,9},{2,6},{6,2},{1... | collective-permute-start | bytes 1572872 | tf_op jit(solution)/shard_map/ppermute | solution.py:332
  118.7 3.8 %out_projection.2.refs_4_ = bf16[512,1024]{1,0:T(8,128)(2,1)} custom-call(bf16[4096,1024]{1,0:T(8,128)(2,1)S(1)} %bitcast.2, bf16[256,1024]{1,0:T(8,128)(2,1)S(1)} %shard_map.79.refs_0_, bf16[256,1024]{1,0:T(8,128)(2,1)S(1)} %collective-permute-done.20.refs_1_, bf16[256,1024]{1,0:T(8,128)(2,1)S(1)} %collective-permute-done.21.refs_2_, ...), custom_call_target="tpu_custom_call" | custom-call | flops 2147483648 | bytes 11010048 | tf_op jit(solution)/shard_map/out_projection/pallas_call | solution.py:308
  122.5 3.8 %out_projection.3 = bf16[512,1024]{1,0:T(8,128)(2,1)} custom-call(bf16[4096,1024]{1,0:T(8,128)(2,1)S(1)} %bitcast.2, bf16[256,1024]{1,0:T(8,128)(2,1)S(1)} %shard_map.77.refs_0_, bf16[256,1024]{1,0:T(8,128)(2,1)S(1)} %collective-permute-done.14.refs_1_, bf16[256,1024]{1,0:T(8,128)(2,1)S(1)} %collective-permute-done.15.refs_2_, ...), custom_call_target="tpu_custom_call", output_to_operand_aliasing={{}: (5, {})} | custom-call | flops 2147483648 | bytes 11010048 | tf_op jit(solution)/shard_map/out_projection/pallas_call | solution.py:308
  (50 shorter events, 19.6 us)
Async XLA Ops:
  0.0 38.9 %collective-permute-start = (bf16[512,1024]{1,0:T(8,128)(2,1)}, bf16[512,1024]{1,0:T(8,128)(2,1)S(1)}, u32[]{:S(2)}, u32[]{:S(2)}) collective-permute-start(bf16[512,1024]{1,0:T(8,128)(2,1)} %refs_0_.7), channel_id=1, source_target_pairs={{0,4},{4,0},{8,12},{12,8},{1,5},{5,1},{9,13},{13,9},{2,6},{6,2},{1... | collective-permute-start | bytes 3145736 | tf_op jit(solution)/shard_map/ppermute | solution.py:332
  1.8 13.5 %collective-permute-start.3 = (bf16[256,1024]{1,0:T(8,128)(2,1)S(1)}, bf16[256,1024]{1,0:T(8,128)(2,1)S(1)}, u32[]{:S(2)}, u32[]{:S(2)}) collective-permute-start(bf16[256,1024]{1,0:T(8,128)(2,1)S(1)} %slice.7), channel_id=1, source_target_pairs={{0,8},{4,12},{8,0},{12,4},{1,9},{5,13},{9,1},{13,5},{2,10},{6,14},... | collective-permute-start | bytes 1572872 | tf_op jit(solution)/shard_map/ppermute | solution.py:327
  4.8 21.7 %collective-permute-start.1 = (bf16[256,1024]{1,0:T(8,128)(2,1)S(1)}, bf16[256,1024]{1,0:T(8,128)(2,1)S(1)}, u32[]{:S(2)}, u32[]{:S(2)}) collective-permute-start(bf16[256,1024]{1,0:T(8,128)(2,1)S(1)} %slice.6), channel_id=1, source_target_pairs={{0,8},{4,12},{8,0},{12,4},{1,9},{5,13},{9,1},{13,5},{2,10},{6,14},... | collective-permute-start | bytes 1572872 | tf_op jit(solution)/shard_map/ppermute | solution.py:327
  15.3 23.6 %collective-permute-start.4 = (bf16[256,1024]{1,0:T(8,128)(2,1)S(1)}, bf16[256,1024]{1,0:T(8,128)(2,1)S(1)}, u32[]{:S(2)}, u32[]{:S(2)}) collective-permute-start(bf16[256,1024]{1,0:T(8,128)(2,1)S(1)} %collective-permute-done.3.refs_2_), channel_id=1, source_target_pairs={{0,4},{4,0},{8,12},{12,8},{1,5},{5,1},{9,13},{13,9},{2,6},{6,2},{1... | collective-permute-start | bytes 1572872 | tf_op jit(solution)/shard_map/ppermute | solution.py:332
  26.5 20.9 %collective-permute-start.2 = (bf16[256,1024]{1,0:T(8,128)(2,1)S(1)}, bf16[256,1024]{1,0:T(8,128)(2,1)S(1)}, u32[]{:S(2)}, u32[]{:S(2)}) collective-permute-start(bf16[256,1024]{1,0:T(8,128)(2,1)S(1)} %collective-permute-done.1.refs_2_), channel_id=1, source_target_pairs={{0,4},{4,0},{8,12},{12,8},{1,5},{5,1},{9,13},{13,9},{2,6},{6,2},{1... | collective-permute-start | bytes 1572872 | tf_op jit(solution)/shard_map/ppermute | solution.py:332
  43.6 11.7 %collective-permute-start.5 = (bf16[256,256]{1,0:T(8,128)(2,1)S(1)}, bf16[256,256]{1,0:T(8,128)(2,1)S(1)}, u32[]{:S(2)}, u32[]{:S(2)}) collective-permute-start(bf16[256,256]{1,0:T(8,128)(2,1)S(1)} %get-tuple-element.38.refs_1_), channel_id=1, source_target_pairs={{0,1},{1,2},{2,3},{3,0},{4,5},{5,6},{6,7},{7,4},{8,9},{9,10},{10,1... | collective-permute-start | bytes 393224 | tf_op jit(solution)/shard_map/ppermute | solution.py:327
  45.0 11.8 %collective-permute-start.6 = (bf16[256,256]{1,0:T(8,128)(2,1)S(1)}, bf16[256,256]{1,0:T(8,128)(2,1)S(1)}, u32[]{:S(2)}, u32[]{:S(2)}) collective-permute-start(bf16[256,256]{1,0:T(8,128)(2,1)S(1)} %get-tuple-element.39.refs_2_), channel_id=1, source_target_pairs={{0,2},{1,3},{2,0},{3,1},{4,6},{5,7},{6,4},{7,5},{8,10},{9,11},{10,... | collective-permute-start | bytes 393224 | tf_op jit(solution)/shard_map/ppermute | solution.py:327
  46.0 17.9 %collective-permute-start.7 = (bf16[256,256]{1,0:T(8,128)(2,1)S(1)}, bf16[256,256]{1,0:T(8,128)(2,1)S(1)}, u32[]{:S(2)}, u32[]{:S(2)}) collective-permute-start(bf16[256,256]{1,0:T(8,128)(2,1)S(1)} %get-tuple-element.40.refs_3_), channel_id=1, source_target_pairs={{0,3},{1,0},{2,1},{3,2},{4,7},{5,4},{6,5},{7,6},{8,11},{9,8},{10,9... | collective-permute-start | bytes 393224 | tf_op jit(solution)/shard_map/ppermute | solution.py:327
  52.1 12.6 %collective-permute-start.8 = (bf16[256,256]{1,0:T(8,128)(2,1)S(1)}, bf16[256,256]{1,0:T(8,128)(2,1)S(1)}, u32[]{:S(2)}, u32[]{:S(2)}) collective-permute-start(bf16[256,256]{1,0:T(8,128)(2,1)S(1)} %get-tuple-element.33.refs_1_), channel_id=1, source_target_pairs={{0,1},{1,2},{2,3},{3,0},{4,5},{5,6},{6,7},{7,4},{8,9},{9,10},{10,1... | collective-permute-start | bytes 393224 | tf_op jit(solution)/shard_map/ppermute | solution.py:327
  52.2 15.3 %collective-permute-start.9 = (bf16[256,256]{1,0:T(8,128)(2,1)S(1)}, bf16[256,256]{1,0:T(8,128)(2,1)S(1)}, u32[]{:S(2)}, u32[]{:S(2)}) collective-permute-start(bf16[256,256]{1,0:T(8,128)(2,1)S(1)} %get-tuple-element.34.refs_2_), channel_id=1, source_target_pairs={{0,2},{1,3},{2,0},{3,1},{4,6},{5,7},{6,4},{7,5},{8,10},{9,11},{10,... | collective-permute-start | bytes 393224 | tf_op jit(solution)/shard_map/ppermute | solution.py:327
  55.3 14.3 %collective-permute-start.10 = (bf16[256,256]{1,0:T(8,128)(2,1)S(1)}, bf16[256,256]{1,0:T(8,128)(2,1)S(1)}, u32[]{:S(2)}, u32[]{:S(2)}) collective-permute-start(bf16[256,256]{1,0:T(8,128)(2,1)S(1)} %get-tuple-element.35.refs_3_), channel_id=1, source_target_pairs={{0,3},{1,0},{2,1},{3,2},{4,7},{5,4},{6,5},{7,6},{8,11},{9,8},{10,9... | collective-permute-start | bytes 393224 | tf_op jit(solution)/shard_map/ppermute | solution.py:327
  73.7 8.2 %collective-permute-start.17 = (bf16[256,256]{1,0:T(8,128)(2,1)S(1)}, bf16[256,256]{1,0:T(8,128)(2,1)S(1)}, u32[]{:S(2)}, u32[]{:S(2)}) collective-permute-start(bf16[256,256]{1,0:T(8,128)(2,1)S(1)} %get-tuple-element.46), channel_id=1, source_target_pairs={{0,1},{1,2},{2,3},{3,0},{4,5},{5,6},{6,7},{7,4},{8,9},{9,10},{10,1... | collective-permute-start | bytes 393224 | tf_op jit(solution)/shard_map/ppermute | solution.py:327
  73.8 10.7 %collective-permute-start.18 = (bf16[256,256]{1,0:T(8,128)(2,1)S(1)}, bf16[256,256]{1,0:T(8,128)(2,1)S(1)}, u32[]{:S(2)}, u32[]{:S(2)}) collective-permute-start(bf16[256,256]{1,0:T(8,128)(2,1)S(1)} %get-tuple-element.47), channel_id=1, source_target_pairs={{0,2},{1,3},{2,0},{3,1},{4,6},{5,7},{6,4},{7,5},{8,10},{9,11},{10,... | collective-permute-start | bytes 393224 | tf_op jit(solution)/shard_map/ppermute | solution.py:327
  74.9 18.0 %collective-permute-start.19 = (bf16[256,256]{1,0:T(8,128)(2,1)S(1)}, bf16[256,256]{1,0:T(8,128)(2,1)S(1)}, u32[]{:S(2)}, u32[]{:S(2)}) collective-permute-start(bf16[256,256]{1,0:T(8,128)(2,1)S(1)} %get-tuple-element.48), channel_id=1, source_target_pairs={{0,3},{1,0},{2,1},{3,2},{4,7},{5,4},{6,5},{7,6},{8,11},{9,8},{10,9... | collective-permute-start | bytes 393224 | tf_op jit(solution)/shard_map/ppermute | solution.py:327
  78.7 40.1 %slice-start = ((s8[8388608]{0:T(1024)(128)(4,1)}), s8[4194304]{0:T(1024)(128)(4,1)S(1)}, s32[]{:S(2)}) async-start(s8[8388608]{0:T(1024)(128)(4,1)} %bitcast.1), calls=%async_computation | async-start | bytes 8388608
  78.7 18.1 %collective-permute-start.11 = (bf16[256,256]{1,0:T(8,128)(2,1)S(1)}, bf16[256,256]{1,0:T(8,128)(2,1)S(1)}, u32[]{:S(2)}, u32[]{:S(2)}) collective-permute-start(bf16[256,256]{1,0:T(8,128)(2,1)S(1)} %get-tuple-element.42), channel_id=1, source_target_pairs={{0,1},{1,2},{2,3},{3,0},{4,5},{5,6},{6,7},{7,4},{8,9},{9,10},{10,1... | collective-permute-start | bytes 393224 | tf_op jit(solution)/shard_map/ppermute | solution.py:327
  78.9 17.9 %collective-permute-start.12 = (bf16[256,256]{1,0:T(8,128)(2,1)S(1)}, bf16[256,256]{1,0:T(8,128)(2,1)S(1)}, u32[]{:S(2)}, u32[]{:S(2)}) collective-permute-start(bf16[256,256]{1,0:T(8,128)(2,1)S(1)} %get-tuple-element.43), channel_id=1, source_target_pairs={{0,2},{1,3},{2,0},{3,1},{4,6},{5,7},{6,4},{7,5},{8,10},{9,11},{10,... | collective-permute-start | bytes 393224 | tf_op jit(solution)/shard_map/ppermute | solution.py:327
  82.0 16.5 %collective-permute-start.13 = (bf16[256,256]{1,0:T(8,128)(2,1)S(1)}, bf16[256,256]{1,0:T(8,128)(2,1)S(1)}, u32[]{:S(2)}, u32[]{:S(2)}) collective-permute-start(bf16[256,256]{1,0:T(8,128)(2,1)S(1)} %get-tuple-element.44), channel_id=1, source_target_pairs={{0,3},{1,0},{2,1},{3,2},{4,7},{5,4},{6,5},{7,6},{8,11},{9,8},{10,9... | collective-permute-start | bytes 393224 | tf_op jit(solution)/shard_map/ppermute | solution.py:327
  93.1 13.0 %collective-permute-start.21 = (bf16[256,1024]{1,0:T(8,128)(2,1)S(1)}, bf16[256,1024]{1,0:T(8,128)(2,1)S(1)}, u32[]{:S(2)}, u32[]{:S(2)}) collective-permute-start(bf16[256,1024]{1,0:T(8,128)(2,1)S(1)} %shard_map.79.refs_0_), channel_id=1, source_target_pairs={{0,8},{4,12},{8,0},{12,4},{1,9},{5,13},{9,1},{13,5},{2,10},{6,14},... | collective-permute-start | bytes 1572872 | tf_op jit(solution)/shard_map/ppermute | solution.py:327
  98.7 18.6 %collective-permute-start.15 = (bf16[256,1024]{1,0:T(8,128)(2,1)S(1)}, bf16[256,1024]{1,0:T(8,128)(2,1)S(1)}, u32[]{:S(2)}, u32[]{:S(2)}) collective-permute-start(bf16[256,1024]{1,0:T(8,128)(2,1)S(1)} %shard_map.77.refs_0_), channel_id=1, source_target_pairs={{0,8},{4,12},{8,0},{12,4},{1,9},{5,13},{9,1},{13,5},{2,10},{6,14},... | collective-permute-start | bytes 1572872 | tf_op jit(solution)/shard_map/ppermute | solution.py:327
  100.0 18.7 %collective-permute-start.20 = (bf16[256,1024]{1,0:T(8,128)(2,1)S(1)}, bf16[256,1024]{1,0:T(8,128)(2,1)S(1)}, u32[]{:S(2)}, u32[]{:S(2)}) collective-permute-start(bf16[256,1024]{1,0:T(8,128)(2,1)S(1)} %shard_map.79.refs_0_), channel_id=1, source_target_pairs={{0,4},{4,0},{8,12},{12,8},{1,5},{5,1},{9,13},{13,9},{2,6},{6,2},{1... | collective-permute-start | bytes 1572872 | tf_op jit(solution)/shard_map/ppermute | solution.py:332
  106.0 12.7 %collective-permute-start.22 = (bf16[256,1024]{1,0:T(8,128)(2,1)S(1)}, bf16[256,1024]{1,0:T(8,128)(2,1)S(1)}, u32[]{:S(2)}, u32[]{:S(2)}) collective-permute-start(bf16[256,1024]{1,0:T(8,128)(2,1)S(1)} %collective-permute-done.21.refs_2_), channel_id=1, source_target_pairs={{0,4},{4,0},{8,12},{12,8},{1,5},{5,1},{9,13},{13,9},{2,6},{6,2},{1... | collective-permute-start | bytes 1572872 | tf_op jit(solution)/shard_map/ppermute | solution.py:332
  108.5 14.0 %collective-permute-start.14 = (bf16[256,1024]{1,0:T(8,128)(2,1)S(1)}, bf16[256,1024]{1,0:T(8,128)(2,1)S(1)}, u32[]{:S(2)}, u32[]{:S(2)}) collective-permute-start(bf16[256,1024]{1,0:T(8,128)(2,1)S(1)} %shard_map.77.refs_0_), channel_id=1, source_target_pairs={{0,4},{4,0},{8,12},{12,8},{1,5},{5,1},{9,13},{13,9},{2,6},{6,2},{1... | collective-permute-start | bytes 1572872 | tf_op jit(solution)/shard_map/ppermute | solution.py:332
  117.3 5.3 %collective-permute-start.16 = (bf16[256,1024]{1,0:T(8,128)(2,1)S(1)}, bf16[256,1024]{1,0:T(8,128)(2,1)S(1)}, u32[]{:S(2)}, u32[]{:S(2)}) collective-permute-start(bf16[256,1024]{1,0:T(8,128)(2,1)S(1)} %collective-permute-done.15.refs_2_), channel_id=1, source_target_pairs={{0,4},{4,0},{8,12},{12,8},{1,5},{5,1},{9,13},{13,9},{2,6},{6,2},{1... | collective-permute-start | bytes 1572872 | tf_op jit(solution)/shard_map/ppermute | solution.py:332
  (6 other events, 84.4 us)

commit v2 on v1

--- a/solution.py
+++ b/solution.py
@@ -16,8 +16,8 @@
 LANES = 128
 MIB = 1 << 20
 CHUNKS = 2
-BLOCK = 256
 VMEM = pl.BlockSpec(memory_space=pltpu.VMEM)
+HBM = pl.BlockSpec(memory_space=pltpu.HBM)
 
 
 def real_dft_tables(block):
@@ -59,25 +59,46 @@
     return sources
 
 
+def paired(n):
+    return n & (n - 1) == 0
+
+
+def target(me, k, n):
+    return me ^ k if paired(n) else (me + k) % n
+
+
+def origin(me, k, n):
+    return me ^ k if paired(n) else (me - k + n) % n
+
+
+def mirror(k, n):
+    return k if paired(n) else -k % n
+
+
 def rows_at(first, count):
     return pl.ds(pl.multiple_of(first * count, count), count)
 
 
 def prologue_kernel(
-    width, fwd_ref, skip_ref, taps_ref, w_ref, kv_ref, query_ref, out_ref, skip_out, taps_in, prev_ref, sems
+    width, skip_hbm, fwd_hbm, inv_hbm, taps_ref, w_ref, fwd_ref, inv_ref, kv_ref, query_ref, out_ref, skip_out, skip_ref, taps_in, prev_ref, sems
 ):
-    block = fwd_ref.shape[1]
+    block = inv_ref.shape[0]
     cols = rows_at(lax.axis_index("ctx"), width)
     copies = [
-        pltpu.make_async_copy(taps_ref.at[:, cols], taps_in, sems.at[0]),
-        pltpu.make_async_copy(w_ref.at[1:3], kv_ref, sems.at[1]),
-        pltpu.make_async_copy(w_ref.at[0], query_ref, sems.at[2]),
+        pltpu.make_async_copy(skip_hbm, skip_ref, sems.at[5]),
+        pltpu.make_async_copy(fwd_hbm, fwd_ref, sems.at[0]),
+        pltpu.make_async_copy(taps_ref.at[:, cols], taps_in, sems.at[1]),
+        pltpu.make_async_copy(inv_hbm, inv_ref, sems.at[2]),
+        pltpu.make_async_copy(w_ref.at[1:3], kv_ref, sems.at[3]),
+        pltpu.make_async_copy(w_ref.at[0], query_ref, sems.at[4]),
     ]
     for copy in copies:
         copy.start()
     prev_ref[...] = jnp.zeros_like(prev_ref)
-    skip_out[...] = skip_ref[...]
-    copies[0].wait()
+    for copy in copies[:3]:
+        copy.wait()
+    for k in range(skip_out.shape[0]):
+        skip_out[k, :] = skip_ref[k * width : (k + 1) * width]
 
     @pl.loop(0, out_ref.shape[0])
     def _(k):
@@ -86,29 +107,31 @@
         out_ref[k] = prev_ref[...] + jnp.where(parity == 0, now, -now)
         prev_ref[...] = now
 
-    for copy in copies[1:]:
+    for copy in copies[3:]:
         copy.wait()
 
 
-def prologue(forward, skip, taps, w, width):
-    rows, block = forward.shape
+def prologue(tables, skip, taps, w, n_ctx):
+    rows, block = tables[0].shape
+    width = w.shape[2] // n_ctx
     count = taps.shape[0] // block
     out = [
+        *(jax.ShapeDtypeStruct(t.shape, BF16) for t in tables),
         jax.ShapeDtypeStruct((2, *w.shape[1:]), BF16),
         jax.ShapeDtypeStruct(w.shape[1:], BF16),
         jax.ShapeDtypeStruct((count, rows, width), F32),
-        jax.ShapeDtypeStruct(skip.shape, F32),
+        jax.ShapeDtypeStruct((n_ctx, width), F32),
     ]
-    hbm = pl.BlockSpec(memory_space=pl.ANY)
     return pl.pallas_call(
         functools.partial(prologue_kernel, width),
         out_shape=out,
-        in_specs=[VMEM, VMEM, hbm, hbm],
-        out_specs=[VMEM] * 4,
+        in_specs=[HBM] * 5,
+        out_specs=[VMEM] * len(out),
         scratch_shapes=[
+            pltpu.VMEM(skip.shape, F32),
             pltpu.VMEM((taps.shape[0], width), BF16),
             pltpu.VMEM((rows, width), F32),
-            pltpu.SemaphoreType.DMA((3,)),
+            pltpu.SemaphoreType.DMA((6,)),
         ],
         compiler_params=pltpu.CompilerParams(vmem_limit_bytes=6 * MIB),
         cost_estimate=pl.CostEstimate(
@@ -117,7 +140,7 @@
             transcendentals=0,
         ),
         name="prologue",
-    )(forward, skip, taps, w)
+    )(*(pltpu.with_memory_space_constraint(x, pltpu.HBM) for x in (skip, *tables, taps, w)))
 
 
 def kv_kernel(n_pieces, n_out, starts, w_ref, *refs):
@@ -127,7 +150,7 @@
     me = lax.axis_index("ctx")
     sources = chan_sources()
     for k in range(n_out):
-        cols = rows_at((me + k) % n_out, width)
+        cols = rows_at(target(me, k, n_out), width)
         key = value = None
         for j, piece in enumerate(pieces):
             x = piece[starts[j] : starts[j] + tokens, :]
@@ -159,7 +182,7 @@
     me = lax.axis_index("ctx")
     sources = chan_sources()
     for k in range(n_ctx):
-        cols = rows_at((me + k) % n_ctx, width)
+        cols = rows_at(target(me, k, n_ctx), width)
         acc = None
         for j, piece in enumerate(pieces):
             x = piece[starts[j] : starts[j] + tokens, :]
@@ -180,81 +203,111 @@
     )
 
 
-def block_products(g_ref, x_ref, y_ref, wanted, width, block):
+def block_products(g_ref, x_ref, before_ref, after_ref, plan, width, block):
+    lags = sorted({lag for _, _, terms in plan for lag, _ in terms})
+    slots = sorted({slot for _, _, terms in plan for _, slot in terms})
+
     def tile(i, first):
         upper = pl.ds(i * 8, 8) if first else rows_at(i, 8)
         lower = pl.ds(block + i * 8, 8) if first else rows_at(block // 8 + i, 8)
         for lane in range(width // LANES):
             cols = pl.ds(lane * LANES, LANES)
-            last = max(wanted) + 1
-            g_re = [g_ref[b, upper, cols] for b in range(last)]
-            g_im = [g_ref[b, lower, cols] for b in range(last)]
-            x_re = [x_ref[b, upper, cols] for b in range(last)]
-            x_im = [x_ref[b, lower, cols] for b in range(last)]
+            g_re = {b: g_ref[b, upper, cols] for b in lags}
+            g_im = {b: g_ref[b, lower, cols] for b in lags}
+            x_re = {b: x_ref[b, upper, cols] for b in slots}
+            x_im = {b: x_ref[b, lower, cols] for b in slots}
             g_di = g_re
             if first:
                 edge = lax.broadcasted_iota(jnp.int32, (8, LANES), 0) == 0
-                g_di = [jnp.where(edge, im, re) for re, im in zip(g_re, g_im)]
-                g_im = [jnp.where(edge, 0.0, im) for im in g_im]
-            for b in wanted:
-                re = g_re[b] * x_re[0] - g_im[b] * x_im[0]
-                im = g_di[b] * x_im[0] + g_im[b] * x_re[0]
-                for a in range(1, b + 1):
-                    re = re + (g_re[b - a] * x_re[a] - g_im[b - a] * x_im[a])
-                    im = im + (g_di[b - a] * x_im[a] + g_im[b - a] * x_re[a])
-                y_ref[b, upper, cols] = re
-                y_ref[b, lower, cols] = im
+                g_di = {b: jnp.where(edge, g_im[b], g_re[b]) for b in lags}
+                g_im = {b: jnp.where(edge, 0.0, g_im[b]) for b in lags}
+            for start, end, terms in plan:
+                re = im = None
+                if start is not None:
+                    re, im = before_ref[start, upper, cols], before_ref[start, lower, cols]
+                for lag, slot in terms:
+                    up = g_re[lag] * x_re[slot] - g_im[lag] * x_im[slot]
+                    down = g_di[lag] * x_im[slot] + g_im[lag] * x_re[slot]
+                    re = up if re is None else re + up
+                    im = down if im is None else im + down
+                after_ref[end, upper, cols] = re
+                after_ref[end, lower, cols] = im
 
     tile(0, True)
     pl.loop(1, block // 8)(lambda i: tile(i, False))
 
 
-def conv_kernel(n_ctx, chunks, fwd_ref, inv_ref, g_ref, *refs):
-    n_in = n_ctx * chunks
-    ins, outs = refs[:n_in], refs[n_in : 2 * n_in]
-    x_ref, y_ref = refs[2 * n_in :]
+def forward_dft(n_ctx, fwd_ref, ins, x_ref):
     me = lax.axis_index("ctx")
+    for k in range(n_ctx):
+        x_ref[origin(me, k, n_ctx)] = jnp.dot(fwd_ref[...], ins[k][...], preferred_element_type=F32)
+
+
+def inverse_dft(n_ctx, inv_ref, y_ref, outs):
+    me = lax.axis_index("ctx")
+    for k in range(n_ctx):
+        spectrum = y_ref[target(me, k, n_ctx)].astype(BF16)
+        outs[k][...] = jnp.dot(inv_ref[...], spectrum, preferred_element_type=F32).astype(BF16)
+
+
+def early_kernel(n_ctx, fwd_ref, g_ref, *refs):
+    ins, sum_ref, x_ref = refs[:n_ctx], refs[n_ctx], refs[n_ctx + 1]
     blocks, rows, width = g_ref.shape
-    block = rows // 2
-    tokens = ins[0].shape[0]
-    parts = block // tokens
-    per_dev = blocks // n_ctx
-    for k in range(n_ctx):
-        source = (me - k + n_ctx) % n_ctx
-        for b in range(per_dev):
-            total = None
-            for p in range(parts):
-                piece = ins[(b * parts + p) * n_ctx + k][...]
-                a = jnp.dot(fwd_ref[:, p * tokens : (p + 1) * tokens], piece, preferred_element_type=F32)
-                total = a if total is None else total + a
-            x_ref[source * per_dev + b] = total
-
-    block_products(g_ref, x_ref, y_ref, range(blocks), width, block)
-
-    for c in range(chunks):
-        for k in range(n_ctx):
-            target = (me + k) % n_ctx
-            spectrum = y_ref[target * per_dev + c // parts].astype(BF16)
-            rows_out = slice(c % parts * tokens, (c % parts + 1) * tokens)
-            outs[c * n_ctx + k][...] = jnp.dot(
-                inv_ref[rows_out, :], spectrum, preferred_element_type=F32
-            ).astype(BF16)
-
-
-def convolve(forward, inverse, spectra, mixed, n_ctx):
-    chunks = len(mixed)
+    forward_dft(n_ctx, fwd_ref, ins, x_ref)
+    plan = [(None, b, [(b - a, a // 2) for a in range(0, b + 1, 2)]) for b in range(blocks)]
+    block_products(g_ref, x_ref, None, sum_ref, plan, width, rows // 2)
+
+
+def middle_kernel(n_ctx, fwd_ref, inv_ref, g_ref, sum_ref, *refs):
+    ins, x_ref, outs, y_ref = refs[:n_ctx], refs[n_ctx], refs[n_ctx + 1 : 2 * n_ctx + 1], refs[-1]
+    blocks, rows, width = g_ref.shape
+    forward_dft(n_ctx, fwd_ref, ins, x_ref)
+    plan = [(b, b // 2, [(b - a, a // 2) for a in range(1, b, 2)]) for b in range(0, blocks, 2)]
+    block_products(g_ref, x_ref, sum_ref, y_ref, plan, width, rows // 2)
+    inverse_dft(n_ctx, inv_ref, y_ref, outs)
+
+
+def late_kernel(n_ctx, inv_ref, g_ref, sum_ref, x_ref, *refs):
+    outs, y_ref = refs[:n_ctx], refs[-1]
+    blocks, rows, width = g_ref.shape
+    plan = [(b, b // 2, [(b - a, a // 2) for a in range(1, b + 1, 2)]) for b in range(1, blocks, 2)]
+    block_products(g_ref, x_ref, sum_ref, y_ref, plan, width, rows // 2)
+    inverse_dft(n_ctx, inv_ref, y_ref, outs)
+
+
+def convolve(forward, inverse, spectra, arrived, n_ctx):
     blocks, rows, width = spectra.shape
-    n_in = n_ctx * chunks
-    outs = call(
-        functools.partial(conv_kernel, n_ctx, chunks),
-        [jax.ShapeDtypeStruct(mixed[0][0].shape, BF16)] * n_in,
-        [forward, inverse, spectra, *[m for group in mixed for m in group]],
-        14,
-        2 * blocks * rows * rows * width,
-        blocks * rows * width * 8,
-        [pltpu.VMEM((blocks, rows, width), F32)] * 2,
-    )
-    return [outs[c * n_ctx : (c + 1) * n_ctx] for c in range(chunks)]
+    half = (n_ctx, rows, width)
+    piece = jax.ShapeDtypeStruct((rows // 2, width), BF16)
+    flops, moved = blocks * rows * rows * width // 2, blocks * rows * width * 8
+    sums = call(
+        functools.partial(early_kernel, n_ctx),
+        jax.ShapeDtypeStruct(spectra.shape, F32),
+        [forward, spectra, *arrived[0]],
+        6,
+        flops,
+        moved,
+        [pltpu.VMEM(half, F32)],
+    )
+    x, *even = call(
+        functools.partial(middle_kernel, n_ctx),
+        [jax.ShapeDtypeStruct(half, F32)] + [piece] * n_ctx,
+        [forward, inverse, spectra, sums, *arrived[1]],
+        6,
+        flops,
+        moved,
+        [pltpu.VMEM(half, F32)],
+    )
+    odd = call(
+        functools.partial(late_kernel, n_ctx),
+        [piece] * n_ctx,
+        [inverse, spectra, sums, x],
+        6,
+        flops,
+        moved,
+        [pltpu.VMEM(half, F32)],
+    )
+    return even, odd
 
 
 def gate_kernel(n_ctx, skip_ref, q_ref, *refs):
@@ -263,9 +316,9 @@
     me = lax.axis_index("ctx")
     for m in range(n_ctx):
         cols = slice(m * width, (m + 1) * width)
-        skip = skip_ref[pl.ds((me + m) % n_ctx, 1), :]
+        skip = skip_ref[pl.ds(target(me, m, n_ctx), 1), :]
         query = q_ref[:, cols].astype(F32)
-        total = conv[(-m) % n_ctx][...].astype(F32) + skip * mixed[m][...].astype(F32)
+        total = conv[mirror(m, n_ctx)][...].astype(F32) + skip * mixed[m][...].astype(F32)
         out_ref[:, cols] = (query * total).astype(BF16)
 
 
@@ -281,41 +334,48 @@
     )
 
 
-def out_kernel(n_pieces, n_ctx, columns, w_ref, *refs):
-    pieces, out_ref = refs[:n_pieces], refs[-1]
+def out_kernel(which, has_before, n_ctx, w_ref, *refs):
+    pieces, out_ref = refs[: len(which)], refs[-1]
+    columns = out_ref.shape[1]
     width = pieces[0].shape[1] // n_ctx
     cols = rows_at(pl.program_id(0), columns)
     me = lax.axis_index("ctx")
-    acc = None
-    for j, source in enumerate(chan_sources()):
+    sources = chan_sources()
+    acc = refs[len(which)][:, cols] if has_before else None
+    for piece, j in zip(pieces, which):
         for m in range(n_ctx):
-            w = w_ref[rows_at(source * n_ctx + (me + m) % n_ctx, width), cols]
-            a = jnp.dot(pieces[j][:, m * width : (m + 1) * width], w, preferred_element_type=F32)
+            w = w_ref[rows_at(sources[j] * n_ctx + target(me, m, n_ctx), width), cols]
+            a = jnp.dot(piece[:, m * width : (m + 1) * width], w, preferred_element_type=F32)
             acc = a if acc is None else acc + a
-    out_ref[...] = acc.astype(BF16)
-
-
-def project_out(pieces, w, chunk, rows, before, n_ctx, columns=256):
+    out_ref[...] = acc.astype(out_ref.dtype)
+
+
+def project_out(pieces, which, w, before, n_ctx, final=None, columns=256):
     tokens = pieces[0].shape[0]
-    total, out_width = w.shape
-    operands = [w, *pieces]
+    _, out_width = w.shape
+    operands = [w, *(pieces[j] for j in which)] + ([] if before is None else [before])
     specs = [VMEM] * len(operands)
     aliases = {}
-    if before is not None:
-        specs.append(pl.BlockSpec(memory_space=pl.ANY))
-        aliases = {len(operands): 0}
-        operands.append(before)
+    out_spec, shape = pl.BlockSpec((tokens, columns), lambda i: (0, i)), (tokens, out_width)
+    if final is not None:
+        chunk, rows, so_far = final
+        out_spec, shape = pl.BlockSpec((tokens, columns), lambda i: (chunk, i)), (rows, out_width)
+        if so_far is not None:
+            specs.append(pl.BlockSpec(memory_space=pl.ANY))
+            aliases = {len(operands): 0}
+            operands.append(so_far)
+    share = len(which) * pieces[0].shape[1]
     return pl.pallas_call(
-        functools.partial(out_kernel, len(pieces), n_ctx, columns),
-        out_shape=jax.ShapeDtypeStruct((rows, out_width), BF16),
+        functools.partial(out_kernel, tuple(which), before is not None, n_ctx),
+        out_shape=jax.ShapeDtypeStruct(shape, F32 if final is None else BF16),
         grid=(out_width // columns,),
         in_specs=specs,
-        out_specs=pl.BlockSpec((tokens, columns), lambda i: (chunk, i)),
+        out_specs=out_spec,
         input_output_aliases=aliases,
         compiler_params=pltpu.CompilerParams(vmem_limit_bytes=6 * MIB),
         cost_estimate=pl.CostEstimate(
-            flops=2 * tokens * total * out_width,
-            bytes_accessed=2 * total * out_width + 2 * tokens * (total + out_width),
+            flops=2 * tokens * share * out_width,
+            bytes_accessed=2 * share * out_width + 2 * tokens * (share + out_width),
             transcendentals=0,
         ),
         name="out_projection",
@@ -341,9 +401,9 @@
 
 
 def exchange(parts):
-    out = [parts[0]]
-    for k in range(1, len(parts)):
-        out.append(shift(parts[k], "ctx", k))
+    out, n = [parts[0]], len(parts)
+    for k in range(1, n):
+        out.append(lax.ppermute(parts[k], "ctx", [(i, target(i, k, n)) for i in range(n)]))
     return out
 
 
@@ -353,18 +413,17 @@
 
 def layer_body(features, filter_taps, skip_gain, in_weight, out_weight):
     n_ctx = lax.axis_size("ctx")
-    rows, channels = features.shape[0], in_weight.shape[2]
-    width = channels // n_ctx
+    rows = features.shape[0]
     tokens = rows // CHUNKS
-    forward, inverse = (jnp.asarray(t) for t in real_dft_tables(BLOCK))
-    skip = skip_gain.reshape(n_ctx, width)
+    tables = [jnp.asarray(t) for t in real_dft_tables(tokens)]
 
     far = [gather_far(features[:tokens])]
     near = swap_cores(features)
-    later, skip = lax.optimization_barrier((features, skip))
-    for c in range(1, CHUNKS):
-        far.append(gather_far(later[c * tokens : (c + 1) * tokens]))
-    w_kv, w_q, spectra, skip = prologue(forward, skip, filter_taps, in_weight.transpose(1, 0, 2), width)
+    later, skip = lax.optimization_barrier((features, skip_gain))
+    far.append(gather_far(later[tokens:]))
+    forward, inverse, w_kv, w_q, spectra, skip = prologue(
+        tables, skip, filter_taps, in_weight.transpose(1, 0, 2), n_ctx
+    )
 
     mixed, arrived, query = [], [], []
     for c in range(CHUNKS):
@@ -375,14 +434,17 @@
         query.append(queries(pieces, starts, tokens, w_q, n_ctx))
     conv = convolve(forward, inverse, spectra, arrived, n_ctx)
 
-    out = None
+    gathered = []
     for c in range(CHUNKS):
         back = exchange(conv[c])
         gated = gate(skip, query[c], mixed[c], back, n_ctx)
         beside = swap_cores(gated)
-        pieces = [gated, beside, *gather_far(gated)]
-        out = project_out(pieces, out_weight, c, rows, out, n_ctx)
-    return out
+        gathered.append([gated, beside, *gather_far(gated)])
+    every = range(len(gathered[0]))
+    out = project_out(gathered[0], every, out_weight, None, n_ctx, (0, rows, None))
+    part = project_out(gathered[1], every[:2], out_weight, None, n_ctx)
+    part = project_out(gathered[1], every[2:-1], out_weight, part, n_ctx)
+    return project_out(gathered[1], every[-1:], out_weight, part, n_ctx, (1, rows, out))
 
 
 P_SIZE = 128
@@ -440,9 +502,9 @@
 
 def shards(features, filter_taps, skip_gain, in_weight, out_weight):
     slices = in_weight.shape[2] % (lax.axis_size("ctx") * LANES) == 0
-    paired = lax.axis_size("chan") % 2 == 0
-    blocks = features.shape[0] % BLOCK == 0 and BLOCK % (features.shape[0] // CHUNKS) == 0
-    chosen = layer if slices and paired and blocks else plain_layer
+    cores = lax.axis_size("chan") % 2 == 0 and lax.axis_size("chan") > 2
+    blocks = features.shape[0] % (CHUNKS * LANES) == 0
+    chosen = layer if slices and cores and blocks else plain_layer
     return chosen(features, filter_taps, skip_gain, in_weight, out_weight)
 
 

time: 127 us -> 124 us (0.976)
  the two profiles are of different devices: /device:TPU:9 before, /device:TPU:19 now
where the time goes in v2:
time: 124 us
  waiting for transfers between devices  53.8 us (43%)
  Pallas kernels  38.1 us (31%)
  starting transfers between devices  29.2 us (24%)
  local copies, waits for them, and re-layouts  2.22 us (2%)
    ppermute x4, waiting for transfers between devices, shift(): return lax.ppermute(x, axis, [(i, (i + by) % n) for i in range(n)])  29 us
    ppermute x12, waiting for transfers between devices, exchange(): lax.ppermute(parts[k], 'ctx', [(i, target(i, k, n)) for i in range(n)])  24.8 us
    pallas_call x9, Pallas kernels, call(): pl.pallas_call(kernel, out_shape=out, in_specs=[VMEM] * len(operands), ou...  19.8 us
    ppermute x7, starting transfers between devices, swap_cores(): return lax.ppermute(x, 'chan', [(i, i ^ 1) for i in range(n)])  13.4 us
    ppermute x12, starting transfers between devices, exchange(): lax.ppermute(parts[k], 'ctx', [(i, target(i, k, n)) for i in range(n)])  11.7 us
    pallas_call x4, Pallas kernels, project_out(): pl.pallas_call(functools.partial(out_kernel, tuple(which), before is not...  9.41 us
    pallas_call x1, Pallas kernels, prologue(): pl.pallas_call(functools.partial(prologue_kernel, width), out_shape=out,...  8.81 us
    ppermute x4, starting transfers between devices, shift(): return lax.ppermute(x, axis, [(i, (i + by) % n) for i in range(n)])  4.2 us
  transfers between devices with their start and end apart: 23, of which 8 were waited for; matrix products, arithmetic and copies ran while one was open for 2% of the time, Pallas kernels for 28%

profile of v2, /device:TPU:19, one launch (start us, length us, event | category | flops | bytes accessed | tf_op | source)
XLA Modules:
  0.0 123.5 jit_solution(11676689044312537661)
XLA Ops:
  4.4 10.9 %collective-permute-done.3.refs_2_ = bf16[256,1024]{1,0:T(8,128)(2,1)S(1)} collective-permute-done((bf16[256,1024]{1,0:T(8,128)(2,1)S(1)}, bf16[256,1024]{1,0:T(8,128)(2,1)S(1)}, u32[]{:S(2)}, u32[]{:S(2)}) %collective-permute-start.3) | collective-permute-done | bytes 524320 | tf_op jit(solution)/shard_map/ppermute | solution.py:387
  16.6 9.9 %collective-permute-done.1.refs_2_ = bf16[256,1024]{1,0:T(8,128)(2,1)S(1)} collective-permute-done((bf16[256,1024]{1,0:T(8,128)(2,1)S(1)}, bf16[256,1024]{1,0:T(8,128)(2,1)S(1)}, u32[]{:S(2)}, u32[]{:S(2)}) %collective-permute-start.1) | collective-permute-done | bytes 524320 | tf_op jit(solution)/shard_map/ppermute | solution.py:387
  27.4 8.8 %prologue.1 = (bf16[512,256]{1,0:T(8,128)(2,1)S(1)}, bf16[256,512]{1,0:T(8,128)(2,1)S(1)}, bf16[2,4096,1024]{2,1,0:T(8,128)(2,1)S(1)}, bf16[4096,1024]{1,0:T(8,1...) custom-call(f32[1024]{0:T(1024)} %skip_hbm, bf16[512,256]{1,0:T(8,128)(2,1)} %constant.4.clone.fwd_hbm, ...), custom_call_target="tpu_custom_call" | custom-call | flops 536870912 | bytes 30408704 | tf_op jit(solution)/shard_map/prologue/pallas_call | solution.py:125
  36.3 4.6 %shard_map.75 = (bf16[256,256]{1,0:T(8,128)(2,1)S(1)}, bf16[256,256]{1,0:T(8,128)(2,1)S(1)}, bf16[256,256]{1,0:T(8,128)(2,1)S(1)}, bf16[256,256]{1,0:T(8,128)(2,1)S(1)}) custom-call(bf16[2,4096,1024]{2,1,0:T(8,128)(2,1)S(1)} %get-tuple-element.34.w_ref, bf16[512,1024]{1,0:T(8,128)(2,1)S(1)} %copy-done, bf16[512,1024]{1,0:T(8,128)(2,1)S(1)} %collective-permute-done.refs_1_, ...), custom_call_target="tpu_custom_call" | custom-call | flops 4294967296 | bytes 18874368 | tf_op jit(solution)/shard_map/pallas_call | solution.py:42
  43.6 4.6 %shard_map.74 = (bf16[256,256]{1,0:T(8,128)(2,1)S(1)}, bf16[256,256]{1,0:T(8,128)(2,1)S(1)}, bf16[256,256]{1,0:T(8,128)(2,1)S(1)}, bf16[256,256]{1,0:T(8,128)(2,1)S(1)}) custom-call(bf16[2,4096,1024]{2,1,0:T(8,128)(2,1)S(1)} %get-tuple-element.34.w_ref, bf16[512,1024]{1,0:T(8,128)(2,1)S(1)} %copy-done, bf16[512,1024]{1,0:T(8,128)(2,1)S(1)} %collective-permute-done.refs_1_, ...), custom_call_target="tpu_custom_call" | custom-call | flops 4294967296 | bytes 18874368 | tf_op jit(solution)/shard_map/pallas_call | solution.py:42
  48.3 2.3 %collective-permute-start.8 = (bf16[256,256]{1,0:T(8,128)(2,1)S(1)}, bf16[256,256]{1,0:T(8,128)(2,1)S(1)}, u32[]{:S(2)}, u32[]{:S(2)}) collective-permute-start(bf16[256,256]{1,0:T(8,128)(2,1)S(1)} %get-tuple-element.36.refs_1_), channel_id=1, source_target_pairs={{0,1},{1,0},{2,3},{3,2},{4,5},{5,4},{6,7},{7,6},{8,9},{9,8},{10,11... | collective-permute-start | bytes 393224 | tf_op jit(solution)/shard_map/ppermute | solution.py:406
  51.8 9.2 %collective-permute-done.7.refs_3_ = bf16[256,256]{1,0:T(8,128)(2,1)S(1)} collective-permute-done((bf16[256,256]{1,0:T(8,128)(2,1)S(1)}, bf16[256,256]{1,0:T(8,128)(2,1)S(1)}, u32[]{:S(2)}, u32[]{:S(2)}) %collective-permute-start.7) | collective-permute-done | bytes 131104 | tf_op jit(solution)/shard_map/ppermute | solution.py:406
  61.0 2.1 %shard_map.76.sum_ref = f32[8,512,256]{2,1,0:T(8,128)S(1)} custom-call(bf16[512,256]{1,0:T(8,128)(2,1)S(1)} %get-tuple-element.41.fwd_ref, f32[8,512,256]{2,1,0:T(8,128)S(1)} %get-tuple-element.40.g_ref, bf16[256,256]{1,0:T(8,128)(2,1)S(1)} %get-tuple-element.42.refs_0_, bf16[256,256]{1,0:T(8,128)(2,1)S(1)} %collective-permute-done.5.refs_1_, ...), custom_call_target="tpu_custom_call" | custom-call | flops 268435456 | bytes 8388608 | tf_op jit(solution)/shard_map/pallas_call | solution.py:42
  63.2 3.5 %collective-permute-done.10.refs_3_ = bf16[256,256]{1,0:T(8,128)(2,1)S(1)} collective-permute-done((bf16[256,256]{1,0:T(8,128)(2,1)S(1)}, bf16[256,256]{1,0:T(8,128)(2,1)S(1)}, u32[]{:S(2)}, u32[]{:S(2)}) %collective-permute-start.10) | collective-permute-done | bytes 131104 | tf_op jit(solution)/shard_map/ppermute | solution.py:406
  66.6 1.6 %shard_map.77 = (f32[4,512,256]{2,1,0:T(8,128)S(1)}, bf16[256,256]{1,0:T(8,128)(2,1)S(1)}, bf16[256,256]{1,0:T(8,128)(2,1)S(1)}, bf16[256,256]{1,0:T(8,128)(2,1)S(1)}, bf16[256,256]{1,0:T(8,128)(2,1)S(1)}) custom-call(bf16[512,256]{1,0:T(8,128)(2,1)S(1)} %get-tuple-element.41.fwd_ref, bf16[256,512]{1,0:T(8,128)(2,1)S(1)} %get-tuple-element.39.inv_ref, ...), custom_call_target="tpu_custom_call" | custom-call | flops 268435456 | bytes 8388608 | tf_op jit(solution)/shard_map/pallas_call | solution.py:42
  71.0 2.4 %shard_map.80.q_ref = bf16[256,1024]{1,0:T(8,128)(2,1)S(1)} custom-call(bf16[4096,1024]{1,0:T(8,128)(2,1)S(1)} %get-tuple-element.32.w_ref, bf16[512,1024]{1,0:T(8,128)(2,1)S(1)} %copy-done, bf16[512,1024]{1,0:T(8,128)(2,1)S(1)} %collective-permute-done.refs_1_, bf16[256,1024]{1,0:T(8,128)(2,1)S(1)} %collective-permute-done.3.refs_2_, ...), custom_call_target="tpu_custom_call" | custom-call | flops 2147483648 | bytes 10485760 | tf_op jit(solution)/shard_map/pallas_call | solution.py:42
  73.4 1.6 %shard_map.78 = (bf16[256,256]{1,0:T(8,128)(2,1)S(1)}, bf16[256,256]{1,0:T(8,128)(2,1)S(1)}, bf16[256,256]{1,0:T(8,128)(2,1)S(1)}, bf16[256,256]{1,0:T(8,128)(2,1)S(1)}) custom-call(bf16[256,512]{1,0:T(8,128)(2,1)S(1)} %get-tuple-element.39.inv_ref, f32[8,512,256]{2,1,0:T(8,128)S(1)} %get-tuple-element.40.g_ref, f32[8,512,256]{2,1,0:T(8,128)S(1)} %shard_map.76.sum_ref, ...), custom_call_target="tpu_custom_call" | custom-call | flops 268435456 | bytes 8388608 | tf_op jit(solution)/shard_map/pallas_call | solution.py:42
  77.7 10.4 %collective-permute-done.19.refs_7_ = bf16[256,256]{1,0:T(8,128)(2,1)S(1)} collective-permute-done((bf16[256,256]{1,0:T(8,128)(2,1)S(1)}, bf16[256,256]{1,0:T(8,128)(2,1)S(1)}, u32[]{:S(2)}, u32[]{:S(2)}) %collective-permute-start.19) | collective-permute-done | bytes 131104 | tf_op jit(solution)/shard_map/ppermute | solution.py:406
  89.7 2.4 %shard_map.73.q_ref = bf16[256,1024]{1,0:T(8,128)(2,1)S(1)} custom-call(bf16[4096,1024]{1,0:T(8,128)(2,1)S(1)} %get-tuple-element.32.w_ref, bf16[512,1024]{1,0:T(8,128)(2,1)S(1)} %copy-done, bf16[512,1024]{1,0:T(8,128)(2,1)S(1)} %collective-permute-done.refs_1_, bf16[256,1024]{1,0:T(8,128)(2,1)S(1)} %collective-permute-done.1.refs_2_, ...), custom_call_target="tpu_custom_call" | custom-call | flops 2147483648 | bytes 10485760 | tf_op jit(solution)/shard_map/pallas_call | solution.py:42
  92.2 1.6 %collective-permute-done.13.refs_7_ = bf16[256,256]{1,0:T(8,128)(2,1)S(1)} collective-permute-done((bf16[256,256]{1,0:T(8,128)(2,1)S(1)}, bf16[256,256]{1,0:T(8,128)(2,1)S(1)}, u32[]{:S(2)}, u32[]{:S(2)}) %collective-permute-start.13) | collective-permute-done | bytes 131104 | tf_op jit(solution)/shard_map/ppermute | solution.py:406
  95.3 1.6 %collective-permute-start.16 = (bf16[256,1024]{1,0:T(8,128)(2,1)S(1)}, bf16[256,1024]{1,0:T(8,128)(2,1)S(1)}, u32[]{:S(2)}, u32[]{:S(2)}) collective-permute-start(bf16[256,1024]{1,0:T(8,128)(2,1)S(1)} %shard_map.79.refs_0_), channel_id=1, source_target_pairs={{0,4},{4,0},{8,12},{12,8},{1,5},{5,1},{9,13},{13,9},{2,6},{6,2},{1... | collective-permute-start | bytes 1572872 | tf_op jit(solution)/shard_map/ppermute | solution.py:392
  96.9 2.8 %collective-permute-done.21.refs_2_ = bf16[256,1024]{1,0:T(8,128)(2,1)S(1)} collective-permute-done((bf16[256,1024]{1,0:T(8,128)(2,1)S(1)}, bf16[256,1024]{1,0:T(8,128)(2,1)S(1)}, u32[]{:S(2)}, u32[]{:S(2)}) %collective-permute-start.21) | collective-permute-done | bytes 524320 | tf_op jit(solution)/shard_map/ppermute | solution.py:387
  99.7 5.8 %collective-permute-start.22 = (bf16[256,1024]{1,0:T(8,128)(2,1)S(1)}, bf16[256,1024]{1,0:T(8,128)(2,1)S(1)}, u32[]{:S(2)}, u32[]{:S(2)}) collective-permute-start(bf16[256,1024]{1,0:T(8,128)(2,1)S(1)} %collective-permute-done.21.refs_2_), channel_id=1, source_target_pairs={{0,4},{4,0},{8,12},{12,8},{1,5},{5,1},{9,13},{13,9},{2,6},{6,2},{1... | collective-permute-start | bytes 1572872 | tf_op jit(solution)/shard_map/ppermute | solution.py:392
  105.5 5.4 %collective-permute-done.14.refs_0_ = bf16[256,1024]{1,0:T(8,128)(2,1)S(1)} collective-permute-done((bf16[256,1024]{1,0:T(8,128)(2,1)S(1)}, bf16[256,1024]{1,0:T(8,128)(2,1)S(1)}, u32[]{:S(2)}, u32[]{:S(2)}) %collective-permute-start.14) | collective-permute-done | bytes 524320 | tf_op jit(solution)/shard_map/ppermute | solution.py:387
  111.0 3.1 %collective-permute-start.15 = (bf16[256,1024]{1,0:T(8,128)(2,1)S(1)}, bf16[256,1024]{1,0:T(8,128)(2,1)S(1)}, u32[]{:S(2)}, u32[]{:S(2)}) collective-permute-start(bf16[256,1024]{1,0:T(8,128)(2,1)S(1)} %collective-permute-done.14.refs_0_), channel_id=1, source_target_pairs={{0,4},{4,0},{8,12},{12,8},{1,5},{5,1},{9,13},{13,9},{2,6},{6,2},{1... | collective-permute-start | bytes 1572872 | tf_op jit(solution)/shard_map/ppermute | solution.py:392
  114.1 2.0 %out_projection.4.refs_1_ = f32[256,1024]{1,0:T(8,128)S(1)} custom-call(bf16[4096,1024]{1,0:T(8,128)(2,1)S(1)} %bitcast.2, bf16[256,1024]{1,0:T(8,128)(2,1)S(1)} %shard_map.79.refs_0_, bf16[256,1024]{1,0:T(8,128)(2,1)S(1)} %collective-permute-done.16.refs_1_), custom_call_target="tpu_custom_call" | custom-call | flops 1073741824 | bytes 5767168 | tf_op jit(solution)/shard_map/out_projection/pallas_call | solution.py:368
  116.0 1.4 %out_projection.5.refs_1_ = f32[256,1024]{1,0:T(8,128)S(1)} custom-call(bf16[4096,1024]{1,0:T(8,128)(2,1)S(1)} %bitcast.2, bf16[256,1024]{1,0:T(8,128)(2,1)S(1)} %collective-permute-done.14.refs_0_, f32[256,1024]{1,0:T(8,128)S(1)} %out_projection.4.refs_1_), custom_call_target="tpu_custom_call" | custom-call | flops 536870912 | bytes 3145728 | tf_op jit(solution)/shard_map/out_projection/pallas_call | solution.py:368
  117.5 3.8 %out_projection.6.refs_2_ = bf16[512,1024]{1,0:T(8,128)(2,1)} custom-call(bf16[4096,1024]{1,0:T(8,128)(2,1)S(1)} %bitcast.2, bf16[256,1024]{1,0:T(8,128)(2,1)S(1)} %shard_map.81.refs_0_, bf16[256,1024]{1,0:T(8,128)(2,1)S(1)} %collective-permute-done.20.refs_1_, bf16[256,1024]{1,0:T(8,128)(2,1)S(1)} %collective-permute-done.21.refs_2_, ...), custom_call_target="tpu_custom_call" | custom-call | flops 2147483648 | bytes 11010048 | tf_op jit(solution)/shard_map/out_projection/pallas_call | solution.py:368
  121.2 2.3 %out_projection.7 = bf16[512,1024]{1,0:T(8,128)(2,1)} custom-call(bf16[4096,1024]{1,0:T(8,128)(2,1)S(1)} %bitcast.2, bf16[256,1024]{1,0:T(8,128)(2,1)S(1)} %collective-permute-done.15.refs_0_, f32[256,1024]{1,0:T(8,128)S(1)} %out_projection.5.refs_1_, bf16[512,1024]{1,0:T(8,128)(2,1)} %out_projection.6.refs_2_), custom_call_target="tpu_custom_call", output_to_operand_aliasing={{}: (3, {})} | custom-call | flops 536870912 | bytes 3145728 | tf_op jit(solution)/shard_map/out_projection/pallas_call | solution.py:368
  (45 shorter events, 19.2 us)
Async XLA Ops:
  0.0 36.2 %collective-permute-start = (bf16[512,1024]{1,0:T(8,128)(2,1)}, bf16[512,1024]{1,0:T(8,128)(2,1)S(1)}, u32[]{:S(2)}, u32[]{:S(2)}) collective-permute-start(bf16[512,1024]{1,0:T(8,128)(2,1)} %refs_0_.7), channel_id=1, source_target_pairs={{0,4},{4,0},{8,12},{12,8},{1,5},{5,1},{9,13},{13,9},{2,6},{6,2},{1... | collective-permute-start | bytes 3145736 | tf_op jit(solution)/shard_map/ppermute | solution.py:392
  1.8 13.5 %collective-permute-start.3 = (bf16[256,1024]{1,0:T(8,128)(2,1)S(1)}, bf16[256,1024]{1,0:T(8,128)(2,1)S(1)}, u32[]{:S(2)}, u32[]{:S(2)}) collective-permute-start(bf16[256,1024]{1,0:T(8,128)(2,1)S(1)} %slice.7), channel_id=1, source_target_pairs={{0,8},{4,12},{8,0},{12,4},{1,9},{5,13},{9,1},{13,5},{2,10},{6,14},... | collective-permute-start | bytes 1572872 | tf_op jit(solution)/shard_map/ppermute | solution.py:387
  4.1 22.4 %collective-permute-start.1 = (bf16[256,1024]{1,0:T(8,128)(2,1)S(1)}, bf16[256,1024]{1,0:T(8,128)(2,1)S(1)}, u32[]{:S(2)}, u32[]{:S(2)}) collective-permute-start(bf16[256,1024]{1,0:T(8,128)(2,1)S(1)} %slice.6), channel_id=1, source_target_pairs={{0,8},{4,12},{8,0},{12,4},{1,9},{5,13},{9,1},{13,5},{2,10},{6,14},... | collective-permute-start | bytes 1572872 | tf_op jit(solution)/shard_map/ppermute | solution.py:387
  15.3 20.9 %collective-permute-start.4 = (bf16[256,1024]{1,0:T(8,128)(2,1)S(1)}, bf16[256,1024]{1,0:T(8,128)(2,1)S(1)}, u32[]{:S(2)}, u32[]{:S(2)}) collective-permute-start(bf16[256,1024]{1,0:T(8,128)(2,1)S(1)} %collective-permute-done.3.refs_2_), channel_id=1, source_target_pairs={{0,4},{4,0},{8,12},{12,8},{1,5},{5,1},{9,13},{13,9},{2,6},{6,2},{1... | collective-permute-start | bytes 1572872 | tf_op jit(solution)/shard_map/ppermute | solution.py:392
  26.5 17.1 %collective-permute-start.2 = (bf16[256,1024]{1,0:T(8,128)(2,1)S(1)}, bf16[256,1024]{1,0:T(8,128)(2,1)S(1)}, u32[]{:S(2)}, u32[]{:S(2)}) collective-permute-start(bf16[256,1024]{1,0:T(8,128)(2,1)S(1)} %collective-permute-done.1.refs_2_), channel_id=1, source_target_pairs={{0,4},{4,0},{8,12},{12,8},{1,5},{5,1},{9,13},{13,9},{2,6},{6,2},{1... | collective-permute-start | bytes 1572872 | tf_op jit(solution)/shard_map/ppermute | solution.py:392
  40.9 9.6 %collective-permute-start.5 = (bf16[256,256]{1,0:T(8,128)(2,1)S(1)}, bf16[256,256]{1,0:T(8,128)(2,1)S(1)}, u32[]{:S(2)}, u32[]{:S(2)}) collective-permute-start(bf16[256,256]{1,0:T(8,128)(2,1)S(1)} %get-tuple-element.43.refs_1_), channel_id=1, source_target_pairs={{0,1},{1,0},{2,3},{3,2},{4,5},{5,4},{6,7},{7,6},{8,9},{9,8},{10,11... | collective-permute-start | bytes 393224 | tf_op jit(solution)/shard_map/ppermute | solution.py:406
  42.3 9.5 %collective-permute-start.6 = (bf16[256,256]{1,0:T(8,128)(2,1)S(1)}, bf16[256,256]{1,0:T(8,128)(2,1)S(1)}, u32[]{:S(2)}, u32[]{:S(2)}) collective-permute-start(bf16[256,256]{1,0:T(8,128)(2,1)S(1)} %get-tuple-element.44.refs_2_), channel_id=1, source_target_pairs={{0,2},{1,3},{2,0},{3,1},{4,6},{5,7},{6,4},{7,5},{8,10},{9,11},{10,... | collective-permute-start | bytes 393224 | tf_op jit(solution)/shard_map/ppermute | solution.py:406
  42.3 18.7 %collective-permute-start.7 = (bf16[256,256]{1,0:T(8,128)(2,1)S(1)}, bf16[256,256]{1,0:T(8,128)(2,1)S(1)}, u32[]{:S(2)}, u32[]{:S(2)}) collective-permute-start(bf16[256,256]{1,0:T(8,128)(2,1)S(1)} %get-tuple-element.45.refs_3_), channel_id=1, source_target_pairs={{0,3},{1,2},{2,1},{3,0},{4,7},{5,6},{6,5},{7,4},{8,11},{9,10},{10,... | collective-permute-start | bytes 393224 | tf_op jit(solution)/shard_map/ppermute | solution.py:406
  48.3 14.9 %collective-permute-start.8 = (bf16[256,256]{1,0:T(8,128)(2,1)S(1)}, bf16[256,256]{1,0:T(8,128)(2,1)S(1)}, u32[]{:S(2)}, u32[]{:S(2)}) collective-permute-start(bf16[256,256]{1,0:T(8,128)(2,1)S(1)} %get-tuple-element.36.refs_1_), channel_id=1, source_target_pairs={{0,1},{1,0},{2,3},{3,2},{4,5},{5,4},{6,7},{7,6},{8,9},{9,8},{10,11... | collective-permute-start | bytes 393224 | tf_op jit(solution)/shard_map/ppermute | solution.py:406
  50.5 12.6 %collective-permute-start.9 = (bf16[256,256]{1,0:T(8,128)(2,1)S(1)}, bf16[256,256]{1,0:T(8,128)(2,1)S(1)}, u32[]{:S(2)}, u32[]{:S(2)}) collective-permute-start(bf16[256,256]{1,0:T(8,128)(2,1)S(1)} %get-tuple-element.37.refs_2_), channel_id=1, source_target_pairs={{0,2},{1,3},{2,0},{3,1},{4,6},{5,7},{6,4},{7,5},{8,10},{9,11},{10,... | collective-permute-start | bytes 393224 | tf_op jit(solution)/shard_map/ppermute | solution.py:406
  50.5 16.1 %collective-permute-start.10 = (bf16[256,256]{1,0:T(8,128)(2,1)S(1)}, bf16[256,256]{1,0:T(8,128)(2,1)S(1)}, u32[]{:S(2)}, u32[]{:S(2)}) collective-permute-start(bf16[256,256]{1,0:T(8,128)(2,1)S(1)} %get-tuple-element.38.refs_3_), channel_id=1, source_target_pairs={{0,3},{1,2},{2,1},{3,0},{4,7},{5,6},{6,5},{7,4},{8,11},{9,10},{10,... | collective-permute-start | bytes 393224 | tf_op jit(solution)/shard_map/ppermute | solution.py:406
  68.3 8.2 %collective-permute-start.17 = (bf16[256,256]{1,0:T(8,128)(2,1)S(1)}, bf16[256,256]{1,0:T(8,128)(2,1)S(1)}, u32[]{:S(2)}, u32[]{:S(2)}) collective-permute-start(bf16[256,256]{1,0:T(8,128)(2,1)S(1)} %get-tuple-element.52), channel_id=1, source_target_pairs={{0,1},{1,0},{2,3},{3,2},{4,5},{5,4},{6,7},{7,6},{8,9},{9,8},{10,11... | collective-permute-start | bytes 393224 | tf_op jit(solution)/shard_map/ppermute | solution.py:406
  68.4 9.4 %collective-permute-start.18 = (bf16[256,256]{1,0:T(8,128)(2,1)S(1)}, bf16[256,256]{1,0:T(8,128)(2,1)S(1)}, u32[]{:S(2)}, u32[]{:S(2)}) collective-permute-start(bf16[256,256]{1,0:T(8,128)(2,1)S(1)} %get-tuple-element.53), channel_id=1, source_target_pairs={{0,2},{1,3},{2,0},{3,1},{4,6},{5,7},{6,4},{7,5},{8,10},{9,11},{10,... | collective-permute-start | bytes 393224 | tf_op jit(solution)/shard_map/ppermute | solution.py:406
  69.8 18.4 %collective-permute-start.19 = (bf16[256,256]{1,0:T(8,128)(2,1)S(1)}, bf16[256,256]{1,0:T(8,128)(2,1)S(1)}, u32[]{:S(2)}, u32[]{:S(2)}) collective-permute-start(bf16[256,256]{1,0:T(8,128)(2,1)S(1)} %get-tuple-element.54), channel_id=1, source_target_pairs={{0,3},{1,2},{2,1},{3,0},{4,7},{5,6},{6,5},{7,4},{8,11},{9,10},{10,... | collective-permute-start | bytes 393224 | tf_op jit(solution)/shard_map/ppermute | solution.py:406
  75.0 39.1 %slice-start = ((s8[8388608]{0:T(1024)(128)(4,1)}), s8[4194304]{0:T(1024)(128)(4,1)S(1)}, s32[]{:S(2)}) async-start(s8[8388608]{0:T(1024)(128)(4,1)} %bitcast.1), calls=%async_computation | async-start | bytes 8388608
  75.0 17.1 %collective-permute-start.11 = (bf16[256,256]{1,0:T(8,128)(2,1)S(1)}, bf16[256,256]{1,0:T(8,128)(2,1)S(1)}, u32[]{:S(2)}, u32[]{:S(2)}) collective-permute-start(bf16[256,256]{1,0:T(8,128)(2,1)S(1)} %get-tuple-element.48), channel_id=1, source_target_pairs={{0,1},{1,0},{2,3},{3,2},{4,5},{5,4},{6,7},{7,6},{8,9},{9,8},{10,11... | collective-permute-start | bytes 393224 | tf_op jit(solution)/shard_map/ppermute | solution.py:406
  76.1 16.1 %collective-permute-start.12 = (bf16[256,256]{1,0:T(8,128)(2,1)S(1)}, bf16[256,256]{1,0:T(8,128)(2,1)S(1)}, u32[]{:S(2)}, u32[]{:S(2)}) collective-permute-start(bf16[256,256]{1,0:T(8,128)(2,1)S(1)} %get-tuple-element.49), channel_id=1, source_target_pairs={{0,2},{1,3},{2,0},{3,1},{4,6},{5,7},{6,4},{7,5},{8,10},{9,11},{10,... | collective-permute-start | bytes 393224 | tf_op jit(solution)/shard_map/ppermute | solution.py:406
  76.5 17.3 %collective-permute-start.13 = (bf16[256,256]{1,0:T(8,128)(2,1)S(1)}, bf16[256,256]{1,0:T(8,128)(2,1)S(1)}, u32[]{:S(2)}, u32[]{:S(2)}) collective-permute-start(bf16[256,256]{1,0:T(8,128)(2,1)S(1)} %get-tuple-element.50), channel_id=1, source_target_pairs={{0,3},{1,2},{2,1},{3,0},{4,7},{5,6},{6,5},{7,4},{8,11},{9,10},{10,... | collective-permute-start | bytes 393224 | tf_op jit(solution)/shard_map/ppermute | solution.py:406
  88.4 11.3 %collective-permute-start.21 = (bf16[256,1024]{1,0:T(8,128)(2,1)S(1)}, bf16[256,1024]{1,0:T(8,128)(2,1)S(1)}, u32[]{:S(2)}, u32[]{:S(2)}) collective-permute-start(bf16[256,1024]{1,0:T(8,128)(2,1)S(1)} %shard_map.81.refs_0_), channel_id=1, source_target_pairs={{0,8},{4,12},{8,0},{12,4},{1,9},{5,13},{9,1},{13,5},{2,10},{6,14},... | collective-permute-start | bytes 1572872 | tf_op jit(solution)/shard_map/ppermute | solution.py:387
  94.0 16.9 %collective-permute-start.14 = (bf16[256,1024]{1,0:T(8,128)(2,1)S(1)}, bf16[256,1024]{1,0:T(8,128)(2,1)S(1)}, u32[]{:S(2)}, u32[]{:S(2)}) collective-permute-start(bf16[256,1024]{1,0:T(8,128)(2,1)S(1)} %shard_map.79.refs_0_), channel_id=1, source_target_pairs={{0,8},{4,12},{8,0},{12,4},{1,9},{5,13},{9,1},{13,5},{2,10},{6,14},... | collective-permute-start | bytes 1572872 | tf_op jit(solution)/shard_map/ppermute | solution.py:387
  95.3 18.7 %collective-permute-start.16 = (bf16[256,1024]{1,0:T(8,128)(2,1)S(1)}, bf16[256,1024]{1,0:T(8,128)(2,1)S(1)}, u32[]{:S(2)}, u32[]{:S(2)}) collective-permute-start(bf16[256,1024]{1,0:T(8,128)(2,1)S(1)} %shard_map.79.refs_0_), channel_id=1, source_target_pairs={{0,4},{4,0},{8,12},{12,8},{1,5},{5,1},{9,13},{13,9},{2,6},{6,2},{1... | collective-permute-start | bytes 1572872 | tf_op jit(solution)/shard_map/ppermute | solution.py:392
  96.9 20.5 %collective-permute-start.20 = (bf16[256,1024]{1,0:T(8,128)(2,1)S(1)}, bf16[256,1024]{1,0:T(8,128)(2,1)S(1)}, u32[]{:S(2)}, u32[]{:S(2)}) collective-permute-start(bf16[256,1024]{1,0:T(8,128)(2,1)S(1)} %shard_map.81.refs_0_), channel_id=1, source_target_pairs={{0,4},{4,0},{8,12},{12,8},{1,5},{5,1},{9,13},{13,9},{2,6},{6,2},{1... | collective-permute-start | bytes 1572872 | tf_op jit(solution)/shard_map/ppermute | solution.py:392
  99.7 17.7 %collective-permute-start.22 = (bf16[256,1024]{1,0:T(8,128)(2,1)S(1)}, bf16[256,1024]{1,0:T(8,128)(2,1)S(1)}, u32[]{:S(2)}, u32[]{:S(2)}) collective-permute-start(bf16[256,1024]{1,0:T(8,128)(2,1)S(1)} %collective-permute-done.21.refs_2_), channel_id=1, source_target_pairs={{0,4},{4,0},{8,12},{12,8},{1,5},{5,1},{9,13},{13,9},{2,6},{6,2},{1... | collective-permute-start | bytes 1572872 | tf_op jit(solution)/shard_map/ppermute | solution.py:392
  111.0 10.3 %collective-permute-start.15 = (bf16[256,1024]{1,0:T(8,128)(2,1)S(1)}, bf16[256,1024]{1,0:T(8,128)(2,1)S(1)}, u32[]{:S(2)}, u32[]{:S(2)}) collective-permute-start(bf16[256,1024]{1,0:T(8,128)(2,1)S(1)} %collective-permute-done.14.refs_0_), channel_id=1, source_target_pairs={{0,4},{4,0},{8,12},{12,8},{1,5},{5,1},{9,13},{13,9},{2,6},{6,2},{1... | collective-permute-start | bytes 1572872 | tf_op jit(solution)/shard_map/ppermute | solution.py:392
  (2 other events, 34.6 us)

commit v3 on v2

--- a/solution.py
+++ b/solution.py
@@ -143,34 +143,46 @@
     )(*(pltpu.with_memory_space_constraint(x, pltpu.HBM) for x in (skip, *tables, taps, w)))
 
 
-def kv_kernel(n_pieces, n_out, starts, w_ref, *refs):
-    pieces, outs = refs[:n_pieces], refs[n_pieces:]
-    tokens, width = outs[0].shape
+def kv_kernel(which, starts, n_ctx, has_before, last, w_ref, *refs):
+    pieces, refs = refs[: len(which)], refs[len(which) :]
+    before, outs = (refs[:2], refs[2:]) if has_before else ((), refs)
+    tokens = outs[0].shape[0]
+    width = w_ref.shape[2] // n_ctx
     depth = pieces[0].shape[1]
     me = lax.axis_index("ctx")
     sources = chan_sources()
-    for k in range(n_out):
-        cols = rows_at(target(me, k, n_out), width)
-        key = value = None
-        for j, piece in enumerate(pieces):
-            x = piece[starts[j] : starts[j] + tokens, :]
+    for k in range(n_ctx):
+        cols = rows_at(target(me, k, n_ctx), width)
+        mine = slice(k * width, (k + 1) * width)
+        key, value = (ref[:, mine] for ref in before) if has_before else (None, None)
+        for piece, j, start in zip(pieces, which, starts):
+            x = piece[start : start + tokens, :]
             rows = rows_at(sources[j], depth)
             a = jnp.dot(x, w_ref[0, rows, cols], preferred_element_type=F32)
             b = jnp.dot(x, w_ref[1, rows, cols], preferred_element_type=F32)
             key = a if key is None else key + a
             value = b if value is None else value + b
-        outs[k][...] = (key * value).astype(BF16)
-
-
-def mixed_inputs(pieces, starts, tokens, w, n_ctx):
-    total, width = w.shape[1], w.shape[2] // n_ctx
+        if last:
+            outs[k][...] = (key * value).astype(BF16)
+        else:
+            outs[0][:, mine] = key
+            outs[1][:, mine] = value
+
+
+def keys_values(pieces, which, starts, tokens, w, before, n_ctx, last):
+    channels = w.shape[2]
+    share = len(which) * pieces[0].shape[1]
+    if last:
+        out = [jax.ShapeDtypeStruct((tokens, channels // n_ctx), BF16)] * n_ctx
+    else:
+        out = [jax.ShapeDtypeStruct((tokens, channels), F32)] * 2
     return call(
-        functools.partial(kv_kernel, len(pieces), n_ctx, starts),
-        [jax.ShapeDtypeStruct((tokens, width), BF16)] * n_ctx,
-        [w, *pieces],
+        functools.partial(kv_kernel, tuple(which), tuple(starts), n_ctx, bool(before), last),
+        out,
+        [w, *(pieces[j] for j in which), *before],
         6,
-        4 * tokens * total * width * n_ctx,
-        4 * total * width * n_ctx + 2 * tokens * total,
+        4 * tokens * share * channels,
+        4 * share * channels + 2 * tokens * share,
     )
 
 
@@ -429,7 +441,11 @@
     for c in range(CHUNKS):
         pieces = [features, near, *far[c]]
         starts = [c * tokens] * 2 + [0] * len(far[c])
-        mixed.append(mixed_inputs(pieces, starts, tokens, w_kv, n_ctx))
+        total = ()
+        for part, which in ("a", (0, 1)), ("b", range(2, len(pieces) - 1)), ("c", (len(pieces) - 1,)):
+            chosen = [starts[j] for j in which]
+            total = keys_values(pieces, which, chosen, tokens, w_kv, total, n_ctx, part == "c")
+        mixed.append(total)
         arrived.append(exchange(mixed[c]))
         query.append(queries(pieces, starts, tokens, w_q, n_ctx))
     conv = convolve(forward, inverse, spectra, arrived, n_ctx)

time: 124 us -> 115 us (0.927)
  waiting for transfers between devices: 53.8 us -> 44.6 us
    ppermute x4, waiting for transfers between devices: 29 us -> 20.3 us  [shift(): return lax.ppermute(x, axis, [(i, (i + by) % n) for i in range(n)])]
    pallas_call x9 -> x13, Pallas kernels: 19.8 us -> 20.8 us  [call(): pl.pallas_call(kernel, out_shape=out, in_specs=[VMEM] * len(operands), ou...]
  transfers between devices with their start and end apart: 23 -> 23, of which waited for: 8 -> 8; matrix products, arithmetic and copies ran while one was open for 2% -> 2% of each run, Pallas kernels for 28% -> 30%
where the time goes in v3:
time: 115 us
  waiting for transfers between devices  44.6 us (39%)
  Pallas kernels  39 us (34%)
  starting transfers between devices  29.1 us (25%)
  local copies, waits for them, and re-layouts  2.17 us (2%)
    ppermute x12, waiting for transfers between devices, exchange(): lax.ppermute(parts[k], 'ctx', [(i, target(i, k, n)) for i in range(n)])  24.3 us
    pallas_call x13, Pallas kernels, call(): pl.pallas_call(kernel, out_shape=out, in_specs=[VMEM] * len(operands), ou...  20.8 us
    ppermute x4, waiting for transfers between devices, shift(): return lax.ppermute(x, axis, [(i, (i + by) % n) for i in range(n)])  20.3 us
    ppermute x7, starting transfers between devices, swap_cores(): return lax.ppermute(x, 'chan', [(i, i ^ 1) for i in range(n)])  13.3 us
    ppermute x12, starting transfers between devices, exchange(): lax.ppermute(parts[k], 'ctx', [(i, target(i, k, n)) for i in range(n)])  11.7 us
    pallas_call x4, Pallas kernels, project_out(): pl.pallas_call(functools.partial(out_kernel, tuple(which), before is not...  9.41 us
    pallas_call x1, Pallas kernels, prologue(): pl.pallas_call(functools.partial(prologue_kernel, width), out_shape=out,...  8.81 us
    ppermute x4, starting transfers between devices, shift(): return lax.ppermute(x, axis, [(i, (i + by) % n) for i in range(n)])  4.12 us
  transfers between devices with their start and end apart: 23, of which 8 were waited for; matrix products, arithmetic and copies ran while one was open for 2% of the time, Pallas kernels for 30%

profile of v3, /device:TPU:19, one launch (start us, length us, event | category | flops | bytes accessed | tf_op | source)
XLA Modules:
  0.0 115.1 jit_solution(1163627961988770417)
XLA Ops:
  4.4 10.9 %collective-permute-done.3.refs_0_.refs_2_ = bf16[256,1024]{1,0:T(8,128)(2,1)S(1)} collective-permute-done((bf16[256,1024]{1,0:T(8,128)(2,1)S(1)}, bf16[256,1024]{1,0:T(8,128)(2,1)S(1)}, u32[]{:S(2)}, u32[]{:S(2)}) %collective-permute-start.3) | collective-permute-done | bytes 524320 | tf_op jit(solution)/shard_map/ppermute | solution.py:399
  16.6 8.8 %prologue.1 = (bf16[512,256]{1,0:T(8,128)(2,1)S(1)}, bf16[256,512]{1,0:T(8,128)(2,1)S(1)}, bf16[2,4096,1024]{2,1,0:T(8,128)(2,1)S(1)}, bf16[4096,1024]{1,0:T(8,1...) custom-call(f32[1024]{0:T(1024)} %skip_hbm, bf16[512,256]{1,0:T(8,128)(2,1)} %constant.4.clone.fwd_hbm, ...), custom_call_target="tpu_custom_call" | custom-call | flops 536870912 | bytes 30408704 | tf_op jit(solution)/shard_map/prologue/pallas_call | solution.py:125
  27.4 2.4 %shard_map.77 = (f32[256,1024]{1,0:T(8,128)S(1)}, f32[256,1024]{1,0:T(8,128)S(1)}) custom-call(bf16[2,4096,1024]{2,1,0:T(8,128)(2,1)S(1)} %get-tuple-element.42.w_ref, bf16[512,1024]{1,0:T(8,128)(2,1)S(1)} %copy-done, bf16[512,1024]{1,0:T(8,128)(2,1)S(1)} %collective-permute-done.refs_1_), custom_call_target="tpu_custom_call" | custom-call | flops 2147483648 | bytes 9437184 | tf_op jit(solution)/shard_map/pallas_call | solution.py:42
  32.5 1.4 %collective-permute-start.5 = (bf16[256,256]{1,0:T(8,128)(2,1)S(1)}, bf16[256,256]{1,0:T(8,128)(2,1)S(1)}, u32[]{:S(2)}, u32[]{:S(2)}) collective-permute-start(bf16[256,256]{1,0:T(8,128)(2,1)S(1)} %get-tuple-element.59.refs_1_), channel_id=1, source_target_pairs={{0,1},{1,0},{2,3},{3,2},{4,5},{5,4},{6,7},{7,6},{8,9},{9,8},{10,11... | collective-permute-start | bytes 393224 | tf_op jit(solution)/shard_map/ppermute | solution.py:418
  35.2 2.4 %shard_map.74 = (f32[256,1024]{1,0:T(8,128)S(1)}, f32[256,1024]{1,0:T(8,128)S(1)}) custom-call(bf16[2,4096,1024]{2,1,0:T(8,128)(2,1)S(1)} %get-tuple-element.42.w_ref, bf16[512,1024]{1,0:T(8,128)(2,1)S(1)} %copy-done, bf16[512,1024]{1,0:T(8,128)(2,1)S(1)} %collective-permute-done.refs_1_), custom_call_target="tpu_custom_call" | custom-call | flops 2147483648 | bytes 9437184 | tf_op jit(solution)/shard_map/pallas_call | solution.py:42
  40.3 2.4 %collective-permute-start.8 = (bf16[256,256]{1,0:T(8,128)(2,1)S(1)}, bf16[256,256]{1,0:T(8,128)(2,1)S(1)}, u32[]{:S(2)}, u32[]{:S(2)}) collective-permute-start(bf16[256,256]{1,0:T(8,128)(2,1)S(1)} %get-tuple-element.48.refs_1_), channel_id=1, source_target_pairs={{0,1},{1,0},{2,3},{3,2},{4,5},{5,4},{6,7},{7,6},{8,9},{9,8},{10,11... | collective-permute-start | bytes 393224 | tf_op jit(solution)/shard_map/ppermute | solution.py:418
  44.0 8.7 %collective-permute-done.7.refs_3_ = bf16[256,256]{1,0:T(8,128)(2,1)S(1)} collective-permute-done((bf16[256,256]{1,0:T(8,128)(2,1)S(1)}, bf16[256,256]{1,0:T(8,128)(2,1)S(1)}, u32[]{:S(2)}, u32[]{:S(2)}) %collective-permute-start.7) | collective-permute-done | bytes 131104 | tf_op jit(solution)/shard_map/ppermute | solution.py:418
  52.6 2.1 %shard_map.80.sum_ref = f32[8,512,256]{2,1,0:T(8,128)S(1)} custom-call(bf16[512,256]{1,0:T(8,128)(2,1)S(1)} %get-tuple-element.53.fwd_ref, f32[8,512,256]{2,1,0:T(8,128)S(1)} %get-tuple-element.52.g_ref, bf16[256,256]{1,0:T(8,128)(2,1)S(1)} %get-tuple-element.58.refs_0_, bf16[256,256]{1,0:T(8,128)(2,1)S(1)} %collective-permute-done.5.refs_1_, ...), custom_call_target="tpu_custom_call" | custom-call | flops 268435456 | bytes 8388608 | tf_op jit(solution)/shard_map/pallas_call | solution.py:42
  54.8 3.5 %collective-permute-done.10.refs_3_ = bf16[256,256]{1,0:T(8,128)(2,1)S(1)} collective-permute-done((bf16[256,256]{1,0:T(8,128)(2,1)S(1)}, bf16[256,256]{1,0:T(8,128)(2,1)S(1)}, u32[]{:S(2)}, u32[]{:S(2)}) %collective-permute-start.10) | collective-permute-done | bytes 131104 | tf_op jit(solution)/shard_map/ppermute | solution.py:418
  58.2 1.6 %shard_map.81 = (f32[4,512,256]{2,1,0:T(8,128)S(1)}, bf16[256,256]{1,0:T(8,128)(2,1)S(1)}, bf16[256,256]{1,0:T(8,128)(2,1)S(1)}, bf16[256,256]{1,0:T(8,128)(2,1)S(1)}, bf16[256,256]{1,0:T(8,128)(2,1)S(1)}) custom-call(bf16[512,256]{1,0:T(8,128)(2,1)S(1)} %get-tuple-element.53.fwd_ref, bf16[256,512]{1,0:T(8,128)(2,1)S(1)} %get-tuple-element.51.inv_ref, ...), custom_call_target="tpu_custom_call" | custom-call | flops 268435456 | bytes 8388608 | tf_op jit(solution)/shard_map/pallas_call | solution.py:42
  62.6 2.4 %shard_map.84.q_ref = bf16[256,1024]{1,0:T(8,128)(2,1)S(1)} custom-call(bf16[4096,1024]{1,0:T(8,128)(2,1)S(1)} %get-tuple-element.40.w_ref, bf16[512,1024]{1,0:T(8,128)(2,1)S(1)} %copy-done, bf16[512,1024]{1,0:T(8,128)(2,1)S(1)} %collective-permute-done.refs_1_, bf16[256,1024]{1,0:T(8,128)(2,1)S(1)} %collective-permute-done.3.refs_0_.refs_2_, ...), custom_call_target="tpu_custom_call" | custom-call | flops 2147483648 | bytes 10485760 | tf_op jit(solution)/shard_map/pallas_call | solution.py:42
  65.0 1.6 %shard_map.82 = (bf16[256,256]{1,0:T(8,128)(2,1)S(1)}, bf16[256,256]{1,0:T(8,128)(2,1)S(1)}, bf16[256,256]{1,0:T(8,128)(2,1)S(1)}, bf16[256,256]{1,0:T(8,128)(2,1)S(1)}) custom-call(bf16[256,512]{1,0:T(8,128)(2,1)S(1)} %get-tuple-element.51.inv_ref, f32[8,512,256]{2,1,0:T(8,128)S(1)} %get-tuple-element.52.g_ref, f32[8,512,256]{2,1,0:T(8,128)S(1)} %shard_map.80.sum_ref, ...), custom_call_target="tpu_custom_call" | custom-call | flops 268435456 | bytes 8388608 | tf_op jit(solution)/shard_map/pallas_call | solution.py:42
  69.3 10.5 %collective-permute-done.19.refs_7_ = bf16[256,256]{1,0:T(8,128)(2,1)S(1)} collective-permute-done((bf16[256,256]{1,0:T(8,128)(2,1)S(1)}, bf16[256,256]{1,0:T(8,128)(2,1)S(1)}, u32[]{:S(2)}, u32[]{:S(2)}) %collective-permute-start.19) | collective-permute-done | bytes 131104 | tf_op jit(solution)/shard_map/ppermute | solution.py:418
  81.3 2.4 %shard_map.73.q_ref = bf16[256,1024]{1,0:T(8,128)(2,1)S(1)} custom-call(bf16[4096,1024]{1,0:T(8,128)(2,1)S(1)} %get-tuple-element.40.w_ref, bf16[512,1024]{1,0:T(8,128)(2,1)S(1)} %copy-done, bf16[512,1024]{1,0:T(8,128)(2,1)S(1)} %collective-permute-done.refs_1_, bf16[256,1024]{1,0:T(8,128)(2,1)S(1)} %collective-permute-done.1.refs_2_.refs_0_, ...), custom_call_target="tpu_custom_call" | custom-call | flops 2147483648 | bytes 10485760 | tf_op jit(solution)/shard_map/pallas_call | solution.py:42
  83.7 1.7 %collective-permute-done.13.refs_7_ = bf16[256,256]{1,0:T(8,128)(2,1)S(1)} collective-permute-done((bf16[256,256]{1,0:T(8,128)(2,1)S(1)}, bf16[256,256]{1,0:T(8,128)(2,1)S(1)}, u32[]{:S(2)}, u32[]{:S(2)}) %collective-permute-start.13) | collective-permute-done | bytes 131104 | tf_op jit(solution)/shard_map/ppermute | solution.py:418
  86.9 1.6 %collective-permute-start.16 = (bf16[256,1024]{1,0:T(8,128)(2,1)S(1)}, bf16[256,1024]{1,0:T(8,128)(2,1)S(1)}, u32[]{:S(2)}, u32[]{:S(2)}) collective-permute-start(bf16[256,1024]{1,0:T(8,128)(2,1)S(1)} %shard_map.83.refs_0_), channel_id=1, source_target_pairs={{0,4},{4,0},{8,12},{12,8},{1,5},{5,1},{9,13},{13,9},{2,6},{6,2},{1... | collective-permute-start | bytes 1572872 | tf_op jit(solution)/shard_map/ppermute | solution.py:404
  88.5 2.9 %collective-permute-done.21.refs_2_ = bf16[256,1024]{1,0:T(8,128)(2,1)S(1)} collective-permute-done((bf16[256,1024]{1,0:T(8,128)(2,1)S(1)}, bf16[256,1024]{1,0:T(8,128)(2,1)S(1)}, u32[]{:S(2)}, u32[]{:S(2)}) %collective-permute-start.21) | collective-permute-done | bytes 524320 | tf_op jit(solution)/shard_map/ppermute | solution.py:399
  91.4 5.7 %collective-permute-start.22 = (bf16[256,1024]{1,0:T(8,128)(2,1)S(1)}, bf16[256,1024]{1,0:T(8,128)(2,1)S(1)}, u32[]{:S(2)}, u32[]{:S(2)}) collective-permute-start(bf16[256,1024]{1,0:T(8,128)(2,1)S(1)} %collective-permute-done.21.refs_2_), channel_id=1, source_target_pairs={{0,4},{4,0},{8,12},{12,8},{1,5},{5,1},{9,13},{13,9},{2,6},{6,2},{1... | collective-permute-start | bytes 1572872 | tf_op jit(solution)/shard_map/ppermute | solution.py:404
  97.1 5.5 %collective-permute-done.14.refs_0_ = bf16[256,1024]{1,0:T(8,128)(2,1)S(1)} collective-permute-done((bf16[256,1024]{1,0:T(8,128)(2,1)S(1)}, bf16[256,1024]{1,0:T(8,128)(2,1)S(1)}, u32[]{:S(2)}, u32[]{:S(2)}) %collective-permute-start.14) | collective-permute-done | bytes 524320 | tf_op jit(solution)/shard_map/ppermute | solution.py:399
  102.6 3.1 %collective-permute-start.15 = (bf16[256,1024]{1,0:T(8,128)(2,1)S(1)}, bf16[256,1024]{1,0:T(8,128)(2,1)S(1)}, u32[]{:S(2)}, u32[]{:S(2)}) collective-permute-start(bf16[256,1024]{1,0:T(8,128)(2,1)S(1)} %collective-permute-done.14.refs_0_), channel_id=1, source_target_pairs={{0,4},{4,0},{8,12},{12,8},{1,5},{5,1},{9,13},{13,9},{2,6},{6,2},{1... | collective-permute-start | bytes 1572872 | tf_op jit(solution)/shard_map/ppermute | solution.py:404
  105.7 1.9 %out_projection.4.refs_1_ = f32[256,1024]{1,0:T(8,128)S(1)} custom-call(bf16[4096,1024]{1,0:T(8,128)(2,1)S(1)} %bitcast.2, bf16[256,1024]{1,0:T(8,128)(2,1)S(1)} %shard_map.83.refs_0_, bf16[256,1024]{1,0:T(8,128)(2,1)S(1)} %collective-permute-done.16.refs_1_), custom_call_target="tpu_custom_call" | custom-call | flops 1073741824 | bytes 5767168 | tf_op jit(solution)/shard_map/out_projection/pallas_call | solution.py:380
  107.6 1.4 %out_projection.5.refs_1_ = f32[256,1024]{1,0:T(8,128)S(1)} custom-call(bf16[4096,1024]{1,0:T(8,128)(2,1)S(1)} %bitcast.2, bf16[256,1024]{1,0:T(8,128)(2,1)S(1)} %collective-permute-done.14.refs_0_, f32[256,1024]{1,0:T(8,128)S(1)} %out_projection.4.refs_1_), custom_call_target="tpu_custom_call" | custom-call | flops 536870912 | bytes 3145728 | tf_op jit(solution)/shard_map/out_projection/pallas_call | solution.py:380
  109.1 3.8 %out_projection.6.refs_2_ = bf16[512,1024]{1,0:T(8,128)(2,1)} custom-call(bf16[4096,1024]{1,0:T(8,128)(2,1)S(1)} %bitcast.2, bf16[256,1024]{1,0:T(8,128)(2,1)S(1)} %shard_map.85.refs_0_, bf16[256,1024]{1,0:T(8,128)(2,1)S(1)} %collective-permute-done.20.refs_1_, bf16[256,1024]{1,0:T(8,128)(2,1)S(1)} %collective-permute-done.21.refs_2_, ...), custom_call_target="tpu_custom_call" | custom-call | flops 2147483648 | bytes 11010048 | tf_op jit(solution)/shard_map/out_projection/pallas_call | solution.py:380
  112.8 2.3 %out_projection.7 = bf16[512,1024]{1,0:T(8,128)(2,1)} custom-call(bf16[4096,1024]{1,0:T(8,128)(2,1)S(1)} %bitcast.2, bf16[256,1024]{1,0:T(8,128)(2,1)S(1)} %collective-permute-done.15.refs_0_, f32[256,1024]{1,0:T(8,128)S(1)} %out_projection.5.refs_1_, bf16[512,1024]{1,0:T(8,128)(2,1)} %out_projection.6.refs_2_), custom_call_target="tpu_custom_call", output_to_operand_aliasing={{}: (3, {})} | custom-call | flops 536870912 | bytes 3145728 | tf_op jit(solution)/shard_map/out_projection/pallas_call | solution.py:380
  (49 shorter events, 24.1 us)
Async XLA Ops:
  0.0 27.4 %collective-permute-start = (bf16[512,1024]{1,0:T(8,128)(2,1)}, bf16[512,1024]{1,0:T(8,128)(2,1)S(1)}, u32[]{:S(2)}, u32[]{:S(2)}) collective-permute-start(bf16[512,1024]{1,0:T(8,128)(2,1)} %refs_0_.7), channel_id=1, source_target_pairs={{0,4},{4,0},{8,12},{12,8},{1,5},{5,1},{9,13},{13,9},{2,6},{6,2},{1... | collective-permute-start | bytes 3145736 | tf_op jit(solution)/shard_map/ppermute | solution.py:404
  1.8 13.5 %collective-permute-start.3 = (bf16[256,1024]{1,0:T(8,128)(2,1)S(1)}, bf16[256,1024]{1,0:T(8,128)(2,1)S(1)}, u32[]{:S(2)}, u32[]{:S(2)}) collective-permute-start(bf16[256,1024]{1,0:T(8,128)(2,1)S(1)} %slice.7), channel_id=1, source_target_pairs={{0,8},{4,12},{8,0},{12,4},{1,9},{5,13},{9,1},{13,5},{2,10},{6,14},... | collective-permute-start | bytes 1572872 | tf_op jit(solution)/shard_map/ppermute | solution.py:399
  4.1 22.4 %collective-permute-start.1 = (bf16[256,1024]{1,0:T(8,128)(2,1)S(1)}, bf16[256,1024]{1,0:T(8,128)(2,1)S(1)}, u32[]{:S(2)}, u32[]{:S(2)}) collective-permute-start(bf16[256,1024]{1,0:T(8,128)(2,1)S(1)} %slice.6), channel_id=1, source_target_pairs={{0,8},{4,12},{8,0},{12,4},{1,9},{5,13},{9,1},{13,5},{2,10},{6,14},... | collective-permute-start | bytes 1572872 | tf_op jit(solution)/shard_map/ppermute | solution.py:399
  15.3 15.9 %collective-permute-start.4 = (bf16[256,1024]{1,0:T(8,128)(2,1)S(1)}, bf16[256,1024]{1,0:T(8,128)(2,1)S(1)}, u32[]{:S(2)}, u32[]{:S(2)}) collective-permute-start(bf16[256,1024]{1,0:T(8,128)(2,1)S(1)} %collective-permute-done.3.refs_0_.refs_2_), channel_id=1, source_target_pairs={{0,4},{4,0},{8,12},{12,8},{1,5},{5,1},{9,13},{13,9},{2,6},{6,2},{1... | collective-permute-start | bytes 1572872 | tf_op jit(solution)/shard_map/ppermute | solution.py:404
  26.5 12.5 %collective-permute-start.2 = (bf16[256,1024]{1,0:T(8,128)(2,1)S(1)}, bf16[256,1024]{1,0:T(8,128)(2,1)S(1)}, u32[]{:S(2)}, u32[]{:S(2)}) collective-permute-start(bf16[256,1024]{1,0:T(8,128)(2,1)S(1)} %collective-permute-done.1.refs_2_.refs_0_), channel_id=1, source_target_pairs={{0,4},{4,0},{8,12},{12,8},{1,5},{5,1},{9,13},{13,9},{2,6},{6,2},{1... | collective-permute-start | bytes 1572872 | tf_op jit(solution)/shard_map/ppermute | solution.py:404
  32.5 10.2 %collective-permute-start.5 = (bf16[256,256]{1,0:T(8,128)(2,1)S(1)}, bf16[256,256]{1,0:T(8,128)(2,1)S(1)}, u32[]{:S(2)}, u32[]{:S(2)}) collective-permute-start(bf16[256,256]{1,0:T(8,128)(2,1)S(1)} %get-tuple-element.59.refs_1_), channel_id=1, source_target_pairs={{0,1},{1,0},{2,3},{3,2},{4,5},{5,4},{6,7},{7,6},{8,9},{9,8},{10,11... | collective-permute-start | bytes 393224 | tf_op jit(solution)/shard_map/ppermute | solution.py:418
  33.9 10.0 %collective-permute-start.6 = (bf16[256,256]{1,0:T(8,128)(2,1)S(1)}, bf16[256,256]{1,0:T(8,128)(2,1)S(1)}, u32[]{:S(2)}, u32[]{:S(2)}) collective-permute-start(bf16[256,256]{1,0:T(8,128)(2,1)S(1)} %get-tuple-element.60.refs_2_), channel_id=1, source_target_pairs={{0,2},{1,3},{2,0},{3,1},{4,6},{5,7},{6,4},{7,5},{8,10},{9,11},{10,... | collective-permute-start | bytes 393224 | tf_op jit(solution)/shard_map/ppermute | solution.py:418
  34.0 18.7 %collective-permute-start.7 = (bf16[256,256]{1,0:T(8,128)(2,1)S(1)}, bf16[256,256]{1,0:T(8,128)(2,1)S(1)}, u32[]{:S(2)}, u32[]{:S(2)}) collective-permute-start(bf16[256,256]{1,0:T(8,128)(2,1)S(1)} %get-tuple-element.61.refs_3_), channel_id=1, source_target_pairs={{0,3},{1,2},{2,1},{3,0},{4,7},{5,6},{6,5},{7,4},{8,11},{9,10},{10,... | collective-permute-start | bytes 393224 | tf_op jit(solution)/shard_map/ppermute | solution.py:418
  40.3 14.4 %collective-permute-start.8 = (bf16[256,256]{1,0:T(8,128)(2,1)S(1)}, bf16[256,256]{1,0:T(8,128)(2,1)S(1)}, u32[]{:S(2)}, u32[]{:S(2)}) collective-permute-start(bf16[256,256]{1,0:T(8,128)(2,1)S(1)} %get-tuple-element.48.refs_1_), channel_id=1, source_target_pairs={{0,1},{1,0},{2,3},{3,2},{4,5},{5,4},{6,7},{7,6},{8,9},{9,8},{10,11... | collective-permute-start | bytes 393224 | tf_op jit(solution)/shard_map/ppermute | solution.py:418
  42.7 12.1 %collective-permute-start.9 = (bf16[256,256]{1,0:T(8,128)(2,1)S(1)}, bf16[256,256]{1,0:T(8,128)(2,1)S(1)}, u32[]{:S(2)}, u32[]{:S(2)}) collective-permute-start(bf16[256,256]{1,0:T(8,128)(2,1)S(1)} %get-tuple-element.49.refs_2_), channel_id=1, source_target_pairs={{0,2},{1,3},{2,0},{3,1},{4,6},{5,7},{6,4},{7,5},{8,10},{9,11},{10,... | collective-permute-start | bytes 393224 | tf_op jit(solution)/shard_map/ppermute | solution.py:418
  42.7 15.5 %collective-permute-start.10 = (bf16[256,256]{1,0:T(8,128)(2,1)S(1)}, bf16[256,256]{1,0:T(8,128)(2,1)S(1)}, u32[]{:S(2)}, u32[]{:S(2)}) collective-permute-start(bf16[256,256]{1,0:T(8,128)(2,1)S(1)} %get-tuple-element.50.refs_3_), channel_id=1, source_target_pairs={{0,3},{1,2},{2,1},{3,0},{4,7},{5,6},{6,5},{7,4},{8,11},{9,10},{10,... | collective-permute-start | bytes 393224 | tf_op jit(solution)/shard_map/ppermute | solution.py:418
  59.9 8.2 %collective-permute-start.17 = (bf16[256,256]{1,0:T(8,128)(2,1)S(1)}, bf16[256,256]{1,0:T(8,128)(2,1)S(1)}, u32[]{:S(2)}, u32[]{:S(2)}) collective-permute-start(bf16[256,256]{1,0:T(8,128)(2,1)S(1)} %get-tuple-element.68), channel_id=1, source_target_pairs={{0,1},{1,0},{2,3},{3,2},{4,5},{5,4},{6,7},{7,6},{8,9},{9,8},{10,11... | collective-permute-start | bytes 393224 | tf_op jit(solution)/shard_map/ppermute | solution.py:418
  60.0 9.4 %collective-permute-start.18 = (bf16[256,256]{1,0:T(8,128)(2,1)S(1)}, bf16[256,256]{1,0:T(8,128)(2,1)S(1)}, u32[]{:S(2)}, u32[]{:S(2)}) collective-permute-start(bf16[256,256]{1,0:T(8,128)(2,1)S(1)} %get-tuple-element.69), channel_id=1, source_target_pairs={{0,2},{1,3},{2,0},{3,1},{4,6},{5,7},{6,4},{7,5},{8,10},{9,11},{10,... | collective-permute-start | bytes 393224 | tf_op jit(solution)/shard_map/ppermute | solution.py:418
  61.3 18.5 %collective-permute-start.19 = (bf16[256,256]{1,0:T(8,128)(2,1)S(1)}, bf16[256,256]{1,0:T(8,128)(2,1)S(1)}, u32[]{:S(2)}, u32[]{:S(2)}) collective-permute-start(bf16[256,256]{1,0:T(8,128)(2,1)S(1)} %get-tuple-element.70), channel_id=1, source_target_pairs={{0,3},{1,2},{2,1},{3,0},{4,7},{5,6},{6,5},{7,4},{8,11},{9,10},{10,... | collective-permute-start | bytes 393224 | tf_op jit(solution)/shard_map/ppermute | solution.py:418
  66.6 39.1 %slice-start = ((s8[8388608]{0:T(1024)(128)(4,1)}), s8[4194304]{0:T(1024)(128)(4,1)S(1)}, s32[]{:S(2)}) async-start(s8[8388608]{0:T(1024)(128)(4,1)} %bitcast.1), calls=%async_computation | async-start | bytes 8388608
  66.6 17.1 %collective-permute-start.11 = (bf16[256,256]{1,0:T(8,128)(2,1)S(1)}, bf16[256,256]{1,0:T(8,128)(2,1)S(1)}, u32[]{:S(2)}, u32[]{:S(2)}) collective-permute-start(bf16[256,256]{1,0:T(8,128)(2,1)S(1)} %get-tuple-element.64), channel_id=1, source_target_pairs={{0,1},{1,0},{2,3},{3,2},{4,5},{5,4},{6,7},{7,6},{8,9},{9,8},{10,11... | collective-permute-start | bytes 393224 | tf_op jit(solution)/shard_map/ppermute | solution.py:418
  67.6 16.1 %collective-permute-start.12 = (bf16[256,256]{1,0:T(8,128)(2,1)S(1)}, bf16[256,256]{1,0:T(8,128)(2,1)S(1)}, u32[]{:S(2)}, u32[]{:S(2)}) collective-permute-start(bf16[256,256]{1,0:T(8,128)(2,1)S(1)} %get-tuple-element.65), channel_id=1, source_target_pairs={{0,2},{1,3},{2,0},{3,1},{4,6},{5,7},{6,4},{7,5},{8,10},{9,11},{10,... | collective-permute-start | bytes 393224 | tf_op jit(solution)/shard_map/ppermute | solution.py:418
  68.1 17.3 %collective-permute-start.13 = (bf16[256,256]{1,0:T(8,128)(2,1)S(1)}, bf16[256,256]{1,0:T(8,128)(2,1)S(1)}, u32[]{:S(2)}, u32[]{:S(2)}) collective-permute-start(bf16[256,256]{1,0:T(8,128)(2,1)S(1)} %get-tuple-element.66), channel_id=1, source_target_pairs={{0,3},{1,2},{2,1},{3,0},{4,7},{5,6},{6,5},{7,4},{8,11},{9,10},{10,... | collective-permute-start | bytes 393224 | tf_op jit(solution)/shard_map/ppermute | solution.py:418
  80.0 11.3 %collective-permute-start.21 = (bf16[256,1024]{1,0:T(8,128)(2,1)S(1)}, bf16[256,1024]{1,0:T(8,128)(2,1)S(1)}, u32[]{:S(2)}, u32[]{:S(2)}) collective-permute-start(bf16[256,1024]{1,0:T(8,128)(2,1)S(1)} %shard_map.85.refs_0_), channel_id=1, source_target_pairs={{0,8},{4,12},{8,0},{12,4},{1,9},{5,13},{9,1},{13,5},{2,10},{6,14},... | collective-permute-start | bytes 1572872 | tf_op jit(solution)/shard_map/ppermute | solution.py:399
  85.6 17.0 %collective-permute-start.14 = (bf16[256,1024]{1,0:T(8,128)(2,1)S(1)}, bf16[256,1024]{1,0:T(8,128)(2,1)S(1)}, u32[]{:S(2)}, u32[]{:S(2)}) collective-permute-start(bf16[256,1024]{1,0:T(8,128)(2,1)S(1)} %shard_map.83.refs_0_), channel_id=1, source_target_pairs={{0,8},{4,12},{8,0},{12,4},{1,9},{5,13},{9,1},{13,5},{2,10},{6,14},... | collective-permute-start | bytes 1572872 | tf_op jit(solution)/shard_map/ppermute | solution.py:399
  86.9 18.8 %collective-permute-start.16 = (bf16[256,1024]{1,0:T(8,128)(2,1)S(1)}, bf16[256,1024]{1,0:T(8,128)(2,1)S(1)}, u32[]{:S(2)}, u32[]{:S(2)}) collective-permute-start(bf16[256,1024]{1,0:T(8,128)(2,1)S(1)} %shard_map.83.refs_0_), channel_id=1, source_target_pairs={{0,4},{4,0},{8,12},{12,8},{1,5},{5,1},{9,13},{13,9},{2,6},{6,2},{1... | collective-permute-start | bytes 1572872 | tf_op jit(solution)/shard_map/ppermute | solution.py:404
  88.5 20.6 %collective-permute-start.20 = (bf16[256,1024]{1,0:T(8,128)(2,1)S(1)}, bf16[256,1024]{1,0:T(8,128)(2,1)S(1)}, u32[]{:S(2)}, u32[]{:S(2)}) collective-permute-start(bf16[256,1024]{1,0:T(8,128)(2,1)S(1)} %shard_map.85.refs_0_), channel_id=1, source_target_pairs={{0,4},{4,0},{8,12},{12,8},{1,5},{5,1},{9,13},{13,9},{2,6},{6,2},{1... | collective-permute-start | bytes 1572872 | tf_op jit(solution)/shard_map/ppermute | solution.py:404
  91.4 17.7 %collective-permute-start.22 = (bf16[256,1024]{1,0:T(8,128)(2,1)S(1)}, bf16[256,1024]{1,0:T(8,128)(2,1)S(1)}, u32[]{:S(2)}, u32[]{:S(2)}) collective-permute-start(bf16[256,1024]{1,0:T(8,128)(2,1)S(1)} %collective-permute-done.21.refs_2_), channel_id=1, source_target_pairs={{0,4},{4,0},{8,12},{12,8},{1,5},{5,1},{9,13},{13,9},{2,6},{6,2},{1... | collective-permute-start | bytes 1572872 | tf_op jit(solution)/shard_map/ppermute | solution.py:404
  102.6 10.2 %collective-permute-start.15 = (bf16[256,1024]{1,0:T(8,128)(2,1)S(1)}, bf16[256,1024]{1,0:T(8,128)(2,1)S(1)}, u32[]{:S(2)}, u32[]{:S(2)}) collective-permute-start(bf16[256,1024]{1,0:T(8,128)(2,1)S(1)} %collective-permute-done.14.refs_0_), channel_id=1, source_target_pairs={{0,4},{4,0},{8,12},{12,8},{1,5},{5,1},{9,13},{13,9},{2,6},{6,2},{1... | collective-permute-start | bytes 1572872 | tf_op jit(solution)/shard_map/ppermute | solution.py:404
  (2 other events, 36.4 us)

commit v4 on v3

--- a/solution.py
+++ b/solution.py
@@ -80,17 +80,16 @@
 
 
 def prologue_kernel(
-    width, skip_hbm, fwd_hbm, inv_hbm, taps_ref, w_ref, fwd_ref, inv_ref, kv_ref, query_ref, out_ref, skip_out, skip_ref, taps_in, prev_ref, sems
+    width, skip_hbm, fwd_hbm, inv_hbm, taps_ref, w_ref, fwd_ref, inv_ref, kv_ref, out_ref, skip_out, skip_ref, taps_in, prev_ref, sems
 ):
     block = inv_ref.shape[0]
     cols = rows_at(lax.axis_index("ctx"), width)
     copies = [
-        pltpu.make_async_copy(skip_hbm, skip_ref, sems.at[5]),
+        pltpu.make_async_copy(skip_hbm, skip_ref, sems.at[4]),
         pltpu.make_async_copy(fwd_hbm, fwd_ref, sems.at[0]),
         pltpu.make_async_copy(taps_ref.at[:, cols], taps_in, sems.at[1]),
         pltpu.make_async_copy(inv_hbm, inv_ref, sems.at[2]),
         pltpu.make_async_copy(w_ref.at[1:3], kv_ref, sems.at[3]),
-        pltpu.make_async_copy(w_ref.at[0], query_ref, sems.at[4]),
     ]
     for copy in copies:
         copy.start()
@@ -118,7 +117,6 @@
     out = [
         *(jax.ShapeDtypeStruct(t.shape, BF16) for t in tables),
         jax.ShapeDtypeStruct((2, *w.shape[1:]), BF16),
-        jax.ShapeDtypeStruct(w.shape[1:], BF16),
         jax.ShapeDtypeStruct((count, rows, width), F32),
         jax.ShapeDtypeStruct((n_ctx, width), F32),
     ]
@@ -131,7 +129,7 @@
             pltpu.VMEM(skip.shape, F32),
             pltpu.VMEM((taps.shape[0], width), BF16),
             pltpu.VMEM((rows, width), F32),
-            pltpu.SemaphoreType.DMA((6,)),
+            pltpu.SemaphoreType.DMA((5,)),
         ],
         compiler_params=pltpu.CompilerParams(vmem_limit_bytes=6 * MIB),
         cost_estimate=pl.CostEstimate(
@@ -186,33 +184,61 @@
     )
 
 
-def query_kernel(n_pieces, n_ctx, starts, w_ref, *refs):
-    pieces, out_ref = refs[:n_pieces], refs[-1]
+def query_kernel(starts, n_ctx, load, w_ref, *refs):
+    pieces, refs = refs[: len(starts)], refs[len(starts) :]
+    out_ref, acc_ref = refs[0], refs[-1]
+    tokens = out_ref.shape[0]
     depth = pieces[0].shape[1]
-    tokens = out_ref.shape[0]
     width = out_ref.shape[1] // n_ctx
     me = lax.axis_index("ctx")
-    sources = chan_sources()
-    for k in range(n_ctx):
-        cols = rows_at(target(me, k, n_ctx), width)
-        acc = None
-        for j, piece in enumerate(pieces):
+    rows = [rows_at(source, depth) for source in chan_sources()]
+    copies = []
+    if load:
+        kept_ref, sems = refs[1:3]
+        copies = [
+            pltpu.make_async_copy(w_ref.at[0, r], kept_ref.at[r], sems.at[j]) for j, r in enumerate(rows)
+        ]
+        w_ref = kept_ref
+    for copy in copies:
+        copy.start()
+    for j, piece in enumerate(pieces):
+        if load:
+            copies[j].wait()
+        for k in range(n_ctx):
+            mine = slice(k * width, (k + 1) * width)
             x = piece[starts[j] : starts[j] + tokens, :]
-            a = jnp.dot(x, w_ref[rows_at(sources[j], depth), cols], preferred_element_type=F32)
-            acc = a if acc is None else acc + a
-        out_ref[:, k * width : (k + 1) * width] = acc.astype(BF16)
-
-
-def queries(pieces, starts, tokens, w, n_ctx):
-    total, channels = w.shape
-    return call(
-        functools.partial(query_kernel, len(pieces), n_ctx, starts),
-        jax.ShapeDtypeStruct((tokens, channels), BF16),
-        [w, *pieces],
-        6,
-        2 * tokens * total * channels,
-        2 * total * channels + 2 * tokens * total,
-    )
+            cols = rows_at(target(me, k, n_ctx), width)
+            a = jnp.dot(x, w_ref[rows[j], cols], preferred_element_type=F32)
+            if j > 0:
+                a = acc_ref[:, mine] + a
+            if j < len(pieces) - 1:
+                acc_ref[:, mine] = a
+            else:
+                out_ref[:, mine] = a.astype(BF16)
+
+
+def queries(pieces, starts, tokens, w, n_ctx, load):
+    total, channels = w.shape[-2:]
+    out = [jax.ShapeDtypeStruct((tokens, channels), BF16)]
+    scratch = [pltpu.VMEM((tokens, channels), F32)]
+    if load:
+        w = pltpu.with_memory_space_constraint(w, pltpu.HBM)
+        out.append(jax.ShapeDtypeStruct((total, channels), BF16))
+        scratch.insert(0, pltpu.SemaphoreType.DMA((len(pieces),)))
+    return pl.pallas_call(
+        functools.partial(query_kernel, tuple(starts), n_ctx, load),
+        out_shape=out,
+        in_specs=[HBM if load else VMEM] + [VMEM] * len(pieces),
+        out_specs=[VMEM] * len(out),
+        scratch_shapes=scratch,
+        compiler_params=pltpu.CompilerParams(vmem_limit_bytes=6 * MIB),
+        cost_estimate=pl.CostEstimate(
+            flops=2 * tokens * total * channels,
+            bytes_accessed=2 * total * channels + 2 * tokens * total,
+            transcendentals=0,
+        ),
+        name="q_projection",
+    )(w, *pieces)
 
 
 def block_products(g_ref, x_ref, before_ref, after_ref, plan, width, block):
@@ -257,9 +283,12 @@
 
 def inverse_dft(n_ctx, inv_ref, y_ref, outs):
     me = lax.axis_index("ctx")
-    for k in range(n_ctx):
-        spectrum = y_ref[target(me, k, n_ctx)].astype(BF16)
-        outs[k][...] = jnp.dot(inv_ref[...], spectrum, preferred_element_type=F32).astype(BF16)
+    tokens = outs[0].shape[0]
+    for p in range(len(outs) // n_ctx):
+        for k in range(n_ctx):
+            spectrum = y_ref[target(me, k, n_ctx)].astype(BF16)
+            part = inv_ref[p * tokens : (p + 1) * tokens, :]
+            outs[p * n_ctx + k][...] = jnp.dot(part, spectrum, preferred_element_type=F32).astype(BF16)
 
 
 def early_kernel(n_ctx, fwd_ref, g_ref, *refs):
@@ -280,7 +309,7 @@
 
 
 def late_kernel(n_ctx, inv_ref, g_ref, sum_ref, x_ref, *refs):
-    outs, y_ref = refs[:n_ctx], refs[-1]
+    outs, y_ref = refs[:-1], refs[-1]
     blocks, rows, width = g_ref.shape
     plan = [(b, b // 2, [(b - a, a // 2) for a in range(1, b + 1, 2)]) for b in range(1, blocks, 2)]
     block_products(g_ref, x_ref, sum_ref, y_ref, plan, width, rows // 2)
@@ -312,32 +341,33 @@
     )
     odd = call(
         functools.partial(late_kernel, n_ctx),
-        [piece] * n_ctx,
+        [jax.ShapeDtypeStruct((rows // 4, width), BF16)] * (2 * n_ctx),
         [inverse, spectra, sums, x],
         6,
         flops,
         moved,
         [pltpu.VMEM(half, F32)],
     )
-    return even, odd
-
-
-def gate_kernel(n_ctx, skip_ref, q_ref, *refs):
+    return even, odd[:n_ctx], odd[n_ctx:]
+
+
+def gate_kernel(n_ctx, start, skip_ref, q_ref, *refs):
     mixed, conv, out_ref = refs[:n_ctx], refs[n_ctx : 2 * n_ctx], refs[-1]
-    _, width = mixed[0].shape
+    tokens, width = conv[0].shape
+    rows = slice(start, start + tokens)
     me = lax.axis_index("ctx")
     for m in range(n_ctx):
         cols = slice(m * width, (m + 1) * width)
         skip = skip_ref[pl.ds(target(me, m, n_ctx), 1), :]
-        query = q_ref[:, cols].astype(F32)
-        total = conv[mirror(m, n_ctx)][...].astype(F32) + skip * mixed[m][...].astype(F32)
+        query = q_ref[rows, cols].astype(F32)
+        total = conv[mirror(m, n_ctx)][...].astype(F32) + skip * mixed[m][rows, :].astype(F32)
         out_ref[:, cols] = (query * total).astype(BF16)
 
 
-def gate(skip, query, mixed, conv, n_ctx):
-    shape = (mixed[0].shape[0], query.shape[1])
+def gate(skip, query, mixed, conv, start, n_ctx):
+    shape = (conv[0].shape[0], query.shape[1])
     return call(
-        functools.partial(gate_kernel, n_ctx),
+        functools.partial(gate_kernel, n_ctx, start),
         jax.ShapeDtypeStruct(shape, BF16),
         [skip, query, *mixed, *conv],
         4,
@@ -428,16 +458,15 @@
     rows = features.shape[0]
     tokens = rows // CHUNKS
     tables = [jnp.asarray(t) for t in real_dft_tables(tokens)]
+    w = in_weight.transpose(1, 0, 2)
 
     far = [gather_far(features[:tokens])]
     near = swap_cores(features)
     later, skip = lax.optimization_barrier((features, skip_gain))
     far.append(gather_far(later[tokens:]))
-    forward, inverse, w_kv, w_q, spectra, skip = prologue(
-        tables, skip, filter_taps, in_weight.transpose(1, 0, 2), n_ctx
-    )
-
-    mixed, arrived, query = [], [], []
+    forward, inverse, w_kv, spectra, skip = prologue(tables, skip, filter_taps, w, n_ctx)
+
+    mixed, arrived, query, w_q = [], [], [], None
     for c in range(CHUNKS):
         pieces = [features, near, *far[c]]
         starts = [c * tokens] * 2 + [0] * len(far[c])
@@ -447,20 +476,23 @@
             total = keys_values(pieces, which, chosen, tokens, w_kv, total, n_ctx, part == "c")
         mixed.append(total)
         arrived.append(exchange(mixed[c]))
-        query.append(queries(pieces, starts, tokens, w_q, n_ctx))
+        made, *kept = queries(pieces, starts, tokens, w if c == 0 else w_q, n_ctx, c == 0)
+        query.append(made)
+        w_q = kept[0] if kept else w_q
     conv = convolve(forward, inverse, spectra, arrived, n_ctx)
 
     gathered = []
-    for c in range(CHUNKS):
-        back = exchange(conv[c])
-        gated = gate(skip, query[c], mixed[c], back, n_ctx)
+    for r, (c, start) in enumerate(((0, 0), (1, 0), (1, tokens // 2))):
+        back = exchange(conv[r])
+        gated = gate(skip, query[c], mixed[c], back, start, n_ctx)
         beside = swap_cores(gated)
         gathered.append([gated, beside, *gather_far(gated)])
     every = range(len(gathered[0]))
     out = project_out(gathered[0], every, out_weight, None, n_ctx, (0, rows, None))
-    part = project_out(gathered[1], every[:2], out_weight, None, n_ctx)
-    part = project_out(gathered[1], every[2:-1], out_weight, part, n_ctx)
-    return project_out(gathered[1], every[-1:], out_weight, part, n_ctx, (1, rows, out))
+    out = project_out(gathered[1], every, out_weight, None, n_ctx, (2, rows, out))
+    part = project_out(gathered[2], every[:2], out_weight, None, n_ctx)
+    part = project_out(gathered[2], every[2:-1], out_weight, part, n_ctx)
+    return project_out(gathered[2], every[-1:], out_weight, part, n_ctx, (3, rows, out))
 
 
 P_SIZE = 128

time: 115 us -> 120 us (1.043)
  the two profiles are of different devices: /device:TPU:19 before, /device:TPU:0 now
where the time goes in v4:
time: 120 us
  waiting for transfers between devices  46.5 us (39%)
  Pallas kernels  40.4 us (34%)
  starting transfers between devices  30.9 us (26%)
  local copies, waits for them, and re-layouts  2.17 us (2%)
    ppermute x5, waiting for transfers between devices, shift(): return lax.ppermute(x, axis, [(i, (i + by) % n) for i in range(n)])  27.3 us
    ppermute x15, starting transfers between devices, exchange(): lax.ppermute(parts[k], 'ctx', [(i, target(i, k, n)) for i in range(n)])  23.6 us
    ppermute x15, waiting for transfers between devices, exchange(): lax.ppermute(parts[k], 'ctx', [(i, target(i, k, n)) for i in range(n)])  19.1 us
    pallas_call x12, Pallas kernels, call(): pl.pallas_call(kernel, out_shape=out, in_specs=[VMEM] * len(operands), ou...  16 us
    pallas_call x5, Pallas kernels, project_out(): pl.pallas_call(functools.partial(out_kernel, tuple(which), before is not...  11.2 us
    pallas_call x2, Pallas kernels, queries(): pl.pallas_call(functools.partial(query_kernel, tuple(starts), n_ctx, load...  6.69 us
    pallas_call x1, Pallas kernels, prologue(): pl.pallas_call(functools.partial(prologue_kernel, width), out_shape=out,...  6.42 us
    ppermute x5, starting transfers between devices, shift(): return lax.ppermute(x, axis, [(i, (i + by) % n) for i in range(n)])  5.68 us
  transfers between devices with their start and end apart: 29, of which 10 were waited for; matrix products, arithmetic and copies ran while one was open for 2% of the time, Pallas kernels for 30%

profile of v4, /device:TPU:0, one launch (start us, length us, event | category | flops | bytes accessed | tf_op | source)
XLA Modules:
  0.0 120.1 jit_solution(16049783339553037740)
XLA Ops:
  1.6 2.6 %collective-permute-start.1 = (bf16[256,1024]{1,0:T(8,128)(2,1)S(1)}, bf16[256,1024]{1,0:T(8,128)(2,1)S(1)}, u32[]{:S(2)}, u32[]{:S(2)}) collective-permute-start(bf16[256,1024]{1,0:T(8,128)(2,1)S(1)} %slice.6), channel_id=1, source_target_pairs={{0,8},{4,12},{8,0},{12,4},{1,9},{5,13},{9,1},{13,5},{2,10},{6,14},... | collective-permute-start | bytes 1572872 | tf_op jit(solution)/shard_map/ppermute | solution.py:429
  5.3 11.6 %collective-permute-done.1.refs_2_.refs_0_ = bf16[256,1024]{1,0:T(8,128)(2,1)S(1)} collective-permute-done((bf16[256,1024]{1,0:T(8,128)(2,1)S(1)}, bf16[256,1024]{1,0:T(8,128)(2,1)S(1)}, u32[]{:S(2)}, u32[]{:S(2)}) %collective-permute-start.1) | collective-permute-done | bytes 524320 | tf_op jit(solution)/shard_map/ppermute | solution.py:429
  16.9 6.4 %prologue.1 = (bf16[512,256]{1,0:T(8,128)(2,1)S(1)}, bf16[256,512]{1,0:T(8,128)(2,1)S(1)}, bf16[2,4096,1024]{2,1,0:T(8,128)(2,1)S(1)}, f32[8,512,256]{2,1,0:T(8,128)S(1)}, f32[4,256]{1,0:T(4,128)S(1)}) custom-call(f32[1024]{0:T(1024)} %skip_hbm, bf16[512,256]{1,0:T(8,128)(2,1)} %constant.4.clone.fwd_hbm, bf16[256,512]{1,0:T(8,128)(2,1)} %constant.5.clone.inv_hbm, ...), custom_call_target="tpu_custom_call" | custom-call | flops 536870912 | bytes 30408704 | tf_op jit(solution)/shard_map/prologue/pallas_call | solution.py:123
  23.4 4.6 %collective-permute-done.3.refs_2_.refs_0_ = bf16[256,1024]{1,0:T(8,128)(2,1)S(1)} collective-permute-done((bf16[256,1024]{1,0:T(8,128)(2,1)S(1)}, bf16[256,1024]{1,0:T(8,128)(2,1)S(1)}, u32[]{:S(2)}, u32[]{:S(2)}) %collective-permute-start.3) | collective-permute-done | bytes 524320 | tf_op jit(solution)/shard_map/ppermute | solution.py:429
  28.0 2.4 %shard_map.76 = (f32[256,1024]{1,0:T(8,128)S(1)}, f32[256,1024]{1,0:T(8,128)S(1)}) custom-call(bf16[2,4096,1024]{2,1,0:T(8,128)(2,1)S(1)} %get-tuple-element.47.w_ref, bf16[512,1024]{1,0:T(8,128)(2,1)S(1)} %copy-done, bf16[512,1024]{1,0:T(8,128)(2,1)S(1)} %collective-permute-done.refs_1_), custom_call_target="tpu_custom_call" | custom-call | flops 2147483648 | bytes 9437184 | tf_op jit(solution)/shard_map/pallas_call | solution.py:42
  33.1 1.9 %collective-permute-start.5 = (bf16[256,256]{1,0:T(8,128)(2,1)S(1)}, bf16[256,256]{1,0:T(8,128)(2,1)S(1)}, u32[]{:S(2)}, u32[]{:S(2)}) collective-permute-start(bf16[256,256]{1,0:T(8,128)(2,1)S(1)} %get-tuple-element.64.refs_1_), channel_id=1, source_target_pairs={{0,1},{1,0},{2,3},{3,2},{4,5},{5,4},{6,7},{7,6},{8,9},{9,8},{10,11... | collective-permute-start | bytes 393224 | tf_op jit(solution)/shard_map/ppermute | solution.py:448
  35.0 2.6 %collective-permute-start.6 = (bf16[256,256]{1,0:T(8,128)(2,1)S(1)}, bf16[256,256]{1,0:T(8,128)(2,1)S(1)}, u32[]{:S(2)}, u32[]{:S(2)}) collective-permute-start(bf16[256,256]{1,0:T(8,128)(2,1)S(1)} %get-tuple-element.65.refs_2_), channel_id=1, source_target_pairs={{0,2},{1,3},{2,0},{3,1},{4,6},{5,7},{6,4},{7,5},{8,10},{9,11},{10,... | collective-permute-start | bytes 393224 | tf_op jit(solution)/shard_map/ppermute | solution.py:448
  37.6 2.4 %shard_map.73 = (f32[256,1024]{1,0:T(8,128)S(1)}, f32[256,1024]{1,0:T(8,128)S(1)}) custom-call(bf16[2,4096,1024]{2,1,0:T(8,128)(2,1)S(1)} %get-tuple-element.47.w_ref, bf16[512,1024]{1,0:T(8,128)(2,1)S(1)} %copy-done, bf16[512,1024]{1,0:T(8,128)(2,1)S(1)} %collective-permute-done.refs_1_), custom_call_target="tpu_custom_call" | custom-call | flops 2147483648 | bytes 9437184 | tf_op jit(solution)/shard_map/pallas_call | solution.py:42
  43.7 3.5 %collective-permute-start.9 = (bf16[256,256]{1,0:T(8,128)(2,1)S(1)}, bf16[256,256]{1,0:T(8,128)(2,1)S(1)}, u32[]{:S(2)}, u32[]{:S(2)}) collective-permute-start(bf16[256,256]{1,0:T(8,128)(2,1)S(1)} %get-tuple-element.54.refs_2_), channel_id=1, source_target_pairs={{0,2},{1,3},{2,0},{3,1},{4,6},{5,7},{6,4},{7,5},{8,10},{9,11},{10,... | collective-permute-start | bytes 393224 | tf_op jit(solution)/shard_map/ppermute | solution.py:448
  47.9 2.1 %shard_map.79.sum_ref = f32[8,512,256]{2,1,0:T(8,128)S(1)} custom-call(bf16[512,256]{1,0:T(8,128)(2,1)S(1)} %get-tuple-element.58.fwd_ref, f32[8,512,256]{2,1,0:T(8,128)S(1)} %get-tuple-element.57.g_ref, bf16[256,256]{1,0:T(8,128)(2,1)S(1)} %get-tuple-element.63.refs_0_, bf16[256,256]{1,0:T(8,128)(2,1)S(1)} %collective-permute-done.5.refs_1_, ...), custom_call_target="tpu_custom_call" | custom-call | flops 268435456 | bytes 8388608 | tf_op jit(solution)/shard_map/pallas_call | solution.py:42
  50.5 8.6 %collective-permute-done.9.refs_2_ = bf16[256,256]{1,0:T(8,128)(2,1)S(1)} collective-permute-done((bf16[256,256]{1,0:T(8,128)(2,1)S(1)}, bf16[256,256]{1,0:T(8,128)(2,1)S(1)}, u32[]{:S(2)}, u32[]{:S(2)}) %collective-permute-start.9) | collective-permute-done | bytes 131104 | tf_op jit(solution)/shard_map/ppermute | solution.py:448
  60.8 2.7 %collective-permute-start.23 = (bf16[256,256]{1,0:T(8,128)(2,1)S(1)}, bf16[256,256]{1,0:T(8,128)(2,1)S(1)}, u32[]{:S(2)}, u32[]{:S(2)}) collective-permute-start(bf16[256,256]{1,0:T(8,128)(2,1)S(1)} %get-tuple-element.78), channel_id=1, source_target_pairs={{0,1},{1,0},{2,3},{3,2},{4,5},{5,4},{6,7},{7,6},{8,9},{9,8},{10,11... | collective-permute-start | bytes 393224 | tf_op jit(solution)/shard_map/ppermute | solution.py:448
  66.0 4.3 %q_projection.2 = (bf16[256,1024]{1,0:T(8,128)(2,1)S(1)}, bf16[4096,1024]{1,0:T(8,128)(2,1)S(1)}) custom-call(bf16[3,4096,1024]{2,1,0:T(8,128)(2,1)} %bitcast.4, bf16[512,1024]{1,0:T(8,128)(2,1)S(1)} %copy-done, bf16[512,1024]{1,0:T(8,128)(2,1)S(1)} %collective-permute-done.refs_1_, bf16[256,1024]{1,0:T(8,128)(2,1)S(1)} %collective-permute-done.1.refs_2_.refs_0_, ...), custom_call_target="tpu_custom_call" | custom-call | flops 2147483648 | bytes 10485760 | tf_op jit(solution)/shard_map/q_projection/pallas_call | solution.py:228
  70.2 5.7 %collective-permute-done.24.refs_6_ = bf16[256,256]{1,0:T(8,128)(2,1)S(1)} collective-permute-done((bf16[256,256]{1,0:T(8,128)(2,1)S(1)}, bf16[256,256]{1,0:T(8,128)(2,1)S(1)}, u32[]{:S(2)}, u32[]{:S(2)}) %collective-permute-start.24) | collective-permute-done | bytes 131104 | tf_op jit(solution)/shard_map/ppermute | solution.py:448
  79.4 2.0 %collective-permute-start.17 = (bf16[128,256]{1,0:T(8,128)(2,1)S(1)}, bf16[128,256]{1,0:T(8,128)(2,1)S(1)}, u32[]{:S(2)}, u32[]{:S(2)}) collective-permute-start(bf16[128,256]{1,0:T(8,128)(2,1)S(1)} %get-tuple-element.73), channel_id=1, source_target_pairs={{0,1},{1,0},{2,3},{3,2},{4,5},{5,4},{6,7},{7,6},{8,9},{9,8},{10,11... | collective-permute-start | bytes 196616 | tf_op jit(solution)/shard_map/ppermute | solution.py:448
  84.9 2.3 %collective-permute-start.12 = (bf16[128,256]{1,0:T(8,128)(2,1)S(1)}, bf16[128,256]{1,0:T(8,128)(2,1)S(1)}, u32[]{:S(2)}, u32[]{:S(2)}) collective-permute-start(bf16[128,256]{1,0:T(8,128)(2,1)S(1)} %get-tuple-element.70), channel_id=1, source_target_pairs={{0,2},{1,3},{2,0},{3,1},{4,6},{5,7},{6,4},{7,5},{8,10},{9,11},{10,... | collective-permute-start | bytes 196616 | tf_op jit(solution)/shard_map/ppermute | solution.py:448
  87.2 2.8 %collective-permute-done.18.refs_6_ = bf16[128,256]{1,0:T(8,128)(2,1)S(1)} collective-permute-done((bf16[128,256]{1,0:T(8,128)(2,1)S(1)}, bf16[128,256]{1,0:T(8,128)(2,1)S(1)}, u32[]{:S(2)}, u32[]{:S(2)}) %collective-permute-start.18) | collective-permute-done | bytes 65568 | tf_op jit(solution)/shard_map/ppermute | solution.py:448
  90.0 1.7 %collective-permute-start.13 = (bf16[128,256]{1,0:T(8,128)(2,1)S(1)}, bf16[128,256]{1,0:T(8,128)(2,1)S(1)}, u32[]{:S(2)}, u32[]{:S(2)}) collective-permute-start(bf16[128,256]{1,0:T(8,128)(2,1)S(1)} %get-tuple-element.71), channel_id=1, source_target_pairs={{0,3},{1,2},{2,1},{3,0},{4,7},{5,6},{6,5},{7,4},{8,11},{9,10},{10,... | collective-permute-start | bytes 196616 | tf_op jit(solution)/shard_map/ppermute | solution.py:448
  92.3 2.4 %q_projection.3.q_ref = bf16[256,1024]{1,0:T(8,128)(2,1)S(1)} custom-call(bf16[4096,1024]{1,0:T(8,128)(2,1)S(1)} %get-tuple-element.45.w_ref, bf16[512,1024]{1,0:T(8,128)(2,1)S(1)} %copy-done, bf16[512,1024]{1,0:T(8,128)(2,1)S(1)} %collective-permute-done.refs_1_, bf16[256,1024]{1,0:T(8,128)(2,1)S(1)} %collective-permute-done.3.refs_2_.refs_0_, ...), custom_call_target="tpu_custom_call" | custom-call | flops 2147483648 | bytes 10485760 | tf_op jit(solution)/shard_map/q_projection/pallas_call | solution.py:228
  97.2 6.9 %collective-permute-done.21.refs_2_ = bf16[128,1024]{1,0:T(8,128)(2,1)S(1)} collective-permute-done((bf16[128,1024]{1,0:T(8,128)(2,1)S(1)}, bf16[128,1024]{1,0:T(8,128)(2,1)S(1)}, u32[]{:S(2)}, u32[]{:S(2)}) %collective-permute-start.21) | collective-permute-done | bytes 262176 | tf_op jit(solution)/shard_map/ppermute | solution.py:429
  104.6 4.2 %collective-permute-done.14.refs_0_ = bf16[128,1024]{1,0:T(8,128)(2,1)S(1)} collective-permute-done((bf16[128,1024]{1,0:T(8,128)(2,1)S(1)}, bf16[128,1024]{1,0:T(8,128)(2,1)S(1)}, u32[]{:S(2)}, u32[]{:S(2)}) %collective-permute-start.14) | collective-permute-done | bytes 262176 | tf_op jit(solution)/shard_map/ppermute | solution.py:429
  111.5 3.8 %out_projection.7.refs_4_ = bf16[512,1024]{1,0:T(8,128)(2,1)} custom-call(bf16[4096,1024]{1,0:T(8,128)(2,1)S(1)} %bitcast.2, bf16[256,1024]{1,0:T(8,128)(2,1)S(1)} %shard_map.84.refs_0_, bf16[256,1024]{1,0:T(8,128)(2,1)S(1)} %collective-permute-done.26.refs_1_, bf16[256,1024]{1,0:T(8,128)(2,1)S(1)} %collective-permute-done.27.refs_2_, ...), custom_call_target="tpu_custom_call" | custom-call | flops 2147483648 | bytes 11010048 | tf_op jit(solution)/shard_map/out_projection/pallas_call | solution.py:410
  115.3 2.8 %out_projection.8.refs_2_ = bf16[512,1024]{1,0:T(8,128)(2,1)} custom-call(bf16[4096,1024]{1,0:T(8,128)(2,1)S(1)} %bitcast.2, bf16[128,1024]{1,0:T(8,128)(2,1)S(1)} %shard_map.83.refs_0_, bf16[128,1024]{1,0:T(8,128)(2,1)S(1)} %collective-permute-done.20.refs_1_, ...), custom_call_target="tpu_custom_call", output_to_operand_aliasing={{}: (5, {})} | custom-call | flops 1073741824 | bytes 9699328 | tf_op jit(solution)/shard_map/out_projection/pallas_call | solution.py:410
  118.1 2.0 %out_projection.9 = bf16[512,1024]{1,0:T(8,128)(2,1)} custom-call(bf16[4096,1024]{1,0:T(8,128)(2,1)S(1)} %bitcast.2, bf16[128,1024]{1,0:T(8,128)(2,1)S(1)} %collective-permute-done.15.refs_0_, f32[128,1024]{1,0:T(8,128)S(1)} %out_projection.6.refs_1_, bf16[512,1024]{1,0:T(8,128)(2,1)} %out_projection.8.refs_2_), custom_call_target="tpu_custom_call", output_to_operand_aliasing={{}: (3, {})} | custom-call | flops 268435456 | bytes 2621440 | tf_op jit(solution)/shard_map/out_projection/pallas_call | solution.py:410
  (63 shorter events, 27.4 us)
Async XLA Ops:
  0.0 28.0 %collective-permute-start = (bf16[512,1024]{1,0:T(8,128)(2,1)}, bf16[512,1024]{1,0:T(8,128)(2,1)S(1)}, u32[]{:S(2)}, u32[]{:S(2)}) collective-permute-start(bf16[512,1024]{1,0:T(8,128)(2,1)} %refs_0_.7), channel_id=1, source_target_pairs={{0,4},{4,0},{8,12},{12,8},{1,5},{5,1},{9,13},{13,9},{2,6},{6,2},{1... | collective-permute-start | bytes 3145736 | tf_op jit(solution)/shard_map/ppermute | solution.py:434
  1.6 15.3 %collective-permute-start.1 = (bf16[256,1024]{1,0:T(8,128)(2,1)S(1)}, bf16[256,1024]{1,0:T(8,128)(2,1)S(1)}, u32[]{:S(2)}, u32[]{:S(2)}) collective-permute-start(bf16[256,1024]{1,0:T(8,128)(2,1)S(1)} %slice.6), channel_id=1, source_target_pairs={{0,8},{4,12},{8,0},{12,4},{1,9},{5,13},{9,1},{13,5},{2,10},{6,14},... | collective-permute-start | bytes 1572872 | tf_op jit(solution)/shard_map/ppermute | solution.py:429
  5.2 22.8 %collective-permute-start.3 = (bf16[256,1024]{1,0:T(8,128)(2,1)S(1)}, bf16[256,1024]{1,0:T(8,128)(2,1)S(1)}, u32[]{:S(2)}, u32[]{:S(2)}) collective-permute-start(bf16[256,1024]{1,0:T(8,128)(2,1)S(1)} %slice.7), channel_id=1, source_target_pairs={{0,8},{4,12},{8,0},{12,4},{1,9},{5,13},{9,1},{13,5},{2,10},{6,14},... | collective-permute-start | bytes 1572872 | tf_op jit(solution)/shard_map/ppermute | solution.py:429
  16.9 14.9 %collective-permute-start.2 = (bf16[256,1024]{1,0:T(8,128)(2,1)S(1)}, bf16[256,1024]{1,0:T(8,128)(2,1)S(1)}, u32[]{:S(2)}, u32[]{:S(2)}) collective-permute-start(bf16[256,1024]{1,0:T(8,128)(2,1)S(1)} %collective-permute-done.1.refs_2_.refs_0_), channel_id=1, source_target_pairs={{0,4},{4,0},{8,12},{12,8},{1,5},{5,1},{9,13},{13,9},{2,6},{6,2},{1... | collective-permute-start | bytes 1572872 | tf_op jit(solution)/shard_map/ppermute | solution.py:434
  28.0 13.4 %collective-permute-start.4 = (bf16[256,1024]{1,0:T(8,128)(2,1)S(1)}, bf16[256,1024]{1,0:T(8,128)(2,1)S(1)}, u32[]{:S(2)}, u32[]{:S(2)}) collective-permute-start(bf16[256,1024]{1,0:T(8,128)(2,1)S(1)} %collective-permute-done.3.refs_2_.refs_0_), channel_id=1, source_target_pairs={{0,4},{4,0},{8,12},{12,8},{1,5},{5,1},{9,13},{13,9},{2,6},{6,2},{1... | collective-permute-start | bytes 1572872 | tf_op jit(solution)/shard_map/ppermute | solution.py:434
  33.1 14.1 %collective-permute-start.5 = (bf16[256,256]{1,0:T(8,128)(2,1)S(1)}, bf16[256,256]{1,0:T(8,128)(2,1)S(1)}, u32[]{:S(2)}, u32[]{:S(2)}) collective-permute-start(bf16[256,256]{1,0:T(8,128)(2,1)S(1)} %get-tuple-element.64.refs_1_), channel_id=1, source_target_pairs={{0,1},{1,0},{2,3},{3,2},{4,5},{5,4},{6,7},{7,6},{8,9},{9,8},{10,11... | collective-permute-start | bytes 393224 | tf_op jit(solution)/shard_map/ppermute | solution.py:448
  35.0 12.9 %collective-permute-start.6 = (bf16[256,256]{1,0:T(8,128)(2,1)S(1)}, bf16[256,256]{1,0:T(8,128)(2,1)S(1)}, u32[]{:S(2)}, u32[]{:S(2)}) collective-permute-start(bf16[256,256]{1,0:T(8,128)(2,1)S(1)} %get-tuple-element.65.refs_2_), channel_id=1, source_target_pairs={{0,2},{1,3},{2,0},{3,1},{4,6},{5,7},{6,4},{7,5},{8,10},{9,11},{10,... | collective-permute-start | bytes 393224 | tf_op jit(solution)/shard_map/ppermute | solution.py:448
  37.6 10.4 %collective-permute-start.7 = (bf16[256,256]{1,0:T(8,128)(2,1)S(1)}, bf16[256,256]{1,0:T(8,128)(2,1)S(1)}, u32[]{:S(2)}, u32[]{:S(2)}) collective-permute-start(bf16[256,256]{1,0:T(8,128)(2,1)S(1)} %get-tuple-element.66.refs_3_), channel_id=1, source_target_pairs={{0,3},{1,2},{2,1},{3,0},{4,7},{5,6},{6,5},{7,4},{8,11},{9,10},{10,... | collective-permute-start | bytes 393224 | tf_op jit(solution)/shard_map/ppermute | solution.py:448
  43.7 15.5 %collective-permute-start.9 = (bf16[256,256]{1,0:T(8,128)(2,1)S(1)}, bf16[256,256]{1,0:T(8,128)(2,1)S(1)}, u32[]{:S(2)}, u32[]{:S(2)}) collective-permute-start(bf16[256,256]{1,0:T(8,128)(2,1)S(1)} %get-tuple-element.54.refs_2_), channel_id=1, source_target_pairs={{0,2},{1,3},{2,0},{3,1},{4,6},{5,7},{6,4},{7,5},{8,10},{9,11},{10,... | collective-permute-start | bytes 393224 | tf_op jit(solution)/shard_map/ppermute | solution.py:448
  47.2 12.0 %collective-permute-start.10 = (bf16[256,256]{1,0:T(8,128)(2,1)S(1)}, bf16[256,256]{1,0:T(8,128)(2,1)S(1)}, u32[]{:S(2)}, u32[]{:S(2)}) collective-permute-start(bf16[256,256]{1,0:T(8,128)(2,1)S(1)} %get-tuple-element.55.refs_3_), channel_id=1, source_target_pairs={{0,3},{1,2},{2,1},{3,0},{4,7},{5,6},{6,5},{7,4},{8,11},{9,10},{10,... | collective-permute-start | bytes 393224 | tf_op jit(solution)/shard_map/ppermute | solution.py:448
  60.8 9.4 %collective-permute-start.23 = (bf16[256,256]{1,0:T(8,128)(2,1)S(1)}, bf16[256,256]{1,0:T(8,128)(2,1)S(1)}, u32[]{:S(2)}, u32[]{:S(2)}) collective-permute-start(bf16[256,256]{1,0:T(8,128)(2,1)S(1)} %get-tuple-element.78), channel_id=1, source_target_pairs={{0,1},{1,0},{2,3},{3,2},{4,5},{5,4},{6,7},{7,6},{8,9},{9,8},{10,11... | collective-permute-start | bytes 393224 | tf_op jit(solution)/shard_map/ppermute | solution.py:448
  63.5 12.4 %collective-permute-start.24 = (bf16[256,256]{1,0:T(8,128)(2,1)S(1)}, bf16[256,256]{1,0:T(8,128)(2,1)S(1)}, u32[]{:S(2)}, u32[]{:S(2)}) collective-permute-start(bf16[256,256]{1,0:T(8,128)(2,1)S(1)} %get-tuple-element.79), channel_id=1, source_target_pairs={{0,2},{1,3},{2,0},{3,1},{4,6},{5,7},{6,4},{7,5},{8,10},{9,11},{10,... | collective-permute-start | bytes 393224 | tf_op jit(solution)/shard_map/ppermute | solution.py:448
  64.6 11.4 %collective-permute-start.25 = (bf16[256,256]{1,0:T(8,128)(2,1)S(1)}, bf16[256,256]{1,0:T(8,128)(2,1)S(1)}, u32[]{:S(2)}, u32[]{:S(2)}) collective-permute-start(bf16[256,256]{1,0:T(8,128)(2,1)S(1)} %get-tuple-element.80), channel_id=1, source_target_pairs={{0,3},{1,2},{2,1},{3,0},{4,7},{5,6},{6,5},{7,4},{8,11},{9,10},{10,... | collective-permute-start | bytes 393224 | tf_op jit(solution)/shard_map/ppermute | solution.py:448
  76.2 15.6 %collective-permute-start.27 = (bf16[256,1024]{1,0:T(8,128)(2,1)S(1)}, bf16[256,1024]{1,0:T(8,128)(2,1)S(1)}, u32[]{:S(2)}, u32[]{:S(2)}) collective-permute-start(bf16[256,1024]{1,0:T(8,128)(2,1)S(1)} %shard_map.84.refs_0_), channel_id=1, source_target_pairs={{0,8},{4,12},{8,0},{12,4},{1,9},{5,13},{9,1},{13,5},{2,10},{6,14},... | collective-permute-start | bytes 1572872 | tf_op jit(solution)/shard_map/ppermute | solution.py:429
  82.4 9.4 %collective-permute-start.19 = (bf16[128,256]{1,0:T(8,128)(2,1)S(1)}, bf16[128,256]{1,0:T(8,128)(2,1)S(1)}, u32[]{:S(2)}, u32[]{:S(2)}) collective-permute-start(bf16[128,256]{1,0:T(8,128)(2,1)S(1)} %get-tuple-element.75), channel_id=1, source_target_pairs={{0,3},{1,2},{2,1},{3,0},{4,7},{5,6},{6,5},{7,4},{8,11},{9,10},{10,... | collective-permute-start | bytes 196616 | tf_op jit(solution)/shard_map/ppermute | solution.py:448
  83.8 11.0 %collective-permute-start.11 = (bf16[128,256]{1,0:T(8,128)(2,1)S(1)}, bf16[128,256]{1,0:T(8,128)(2,1)S(1)}, u32[]{:S(2)}, u32[]{:S(2)}) collective-permute-start(bf16[128,256]{1,0:T(8,128)(2,1)S(1)} %get-tuple-element.69), channel_id=1, source_target_pairs={{0,1},{1,0},{2,3},{3,2},{4,5},{5,4},{6,7},{7,6},{8,9},{9,8},{10,11... | collective-permute-start | bytes 196616 | tf_op jit(solution)/shard_map/ppermute | solution.py:448
  84.9 10.5 %collective-permute-start.12 = (bf16[128,256]{1,0:T(8,128)(2,1)S(1)}, bf16[128,256]{1,0:T(8,128)(2,1)S(1)}, u32[]{:S(2)}, u32[]{:S(2)}) collective-permute-start(bf16[128,256]{1,0:T(8,128)(2,1)S(1)} %get-tuple-element.70), channel_id=1, source_target_pairs={{0,2},{1,3},{2,0},{3,1},{4,6},{5,7},{6,4},{7,5},{8,10},{9,11},{10,... | collective-permute-start | bytes 196616 | tf_op jit(solution)/shard_map/ppermute | solution.py:448
  91.8 19.7 %collective-permute-start.26 = (bf16[256,1024]{1,0:T(8,128)(2,1)S(1)}, bf16[256,1024]{1,0:T(8,128)(2,1)S(1)}, u32[]{:S(2)}, u32[]{:S(2)}) collective-permute-start(bf16[256,1024]{1,0:T(8,128)(2,1)S(1)} %shard_map.84.refs_0_), channel_id=1, source_target_pairs={{0,4},{4,0},{8,12},{12,8},{1,5},{5,1},{9,13},{13,9},{2,6},{6,2},{1... | collective-permute-start | bytes 1572872 | tf_op jit(solution)/shard_map/ppermute | solution.py:434
  91.8 19.7 %collective-permute-start.28 = (bf16[256,1024]{1,0:T(8,128)(2,1)S(1)}, bf16[256,1024]{1,0:T(8,128)(2,1)S(1)}, u32[]{:S(2)}, u32[]{:S(2)}) collective-permute-start(bf16[256,1024]{1,0:T(8,128)(2,1)S(1)} %collective-permute-done.27.refs_2_), channel_id=1, source_target_pairs={{0,4},{4,0},{8,12},{12,8},{1,5},{5,1},{9,13},{13,9},{2,6},{6,2},{1... | collective-permute-start | bytes 1572872 | tf_op jit(solution)/shard_map/ppermute | solution.py:434
  94.8 9.2 %collective-permute-start.21 = (bf16[128,1024]{1,0:T(8,128)(2,1)S(1)}, bf16[128,1024]{1,0:T(8,128)(2,1)S(1)}, u32[]{:S(2)}, u32[]{:S(2)}) collective-permute-start(bf16[128,1024]{1,0:T(8,128)(2,1)S(1)} %shard_map.83.refs_0_), channel_id=1, source_target_pairs={{0,8},{4,12},{8,0},{12,4},{1,9},{5,13},{9,1},{13,5},{2,10},{6,14},... | collective-permute-start | bytes 786440 | tf_op jit(solution)/shard_map/ppermute | solution.py:429
  96.3 12.5 %collective-permute-start.14 = (bf16[128,1024]{1,0:T(8,128)(2,1)S(1)}, bf16[128,1024]{1,0:T(8,128)(2,1)S(1)}, u32[]{:S(2)}, u32[]{:S(2)}) collective-permute-start(bf16[128,1024]{1,0:T(8,128)(2,1)S(1)} %shard_map.82.refs_0_), channel_id=1, source_target_pairs={{0,8},{4,12},{8,0},{12,4},{1,9},{5,13},{9,1},{13,5},{2,10},{6,14},... | collective-permute-start | bytes 786440 | tf_op jit(solution)/shard_map/ppermute | solution.py:429
  104.1 11.2 %collective-permute-start.20 = (bf16[128,1024]{1,0:T(8,128)(2,1)S(1)}, bf16[128,1024]{1,0:T(8,128)(2,1)S(1)}, u32[]{:S(2)}, u32[]{:S(2)}) collective-permute-start(bf16[128,1024]{1,0:T(8,128)(2,1)S(1)} %shard_map.83.refs_0_), channel_id=1, source_target_pairs={{0,4},{4,0},{8,12},{12,8},{1,5},{5,1},{9,13},{13,9},{2,6},{6,2},{1... | collective-permute-start | bytes 786440 | tf_op jit(solution)/shard_map/ppermute | solution.py:434
  104.1 11.2 %collective-permute-start.22 = (bf16[128,1024]{1,0:T(8,128)(2,1)S(1)}, bf16[128,1024]{1,0:T(8,128)(2,1)S(1)}, u32[]{:S(2)}, u32[]{:S(2)}) collective-permute-start(bf16[128,1024]{1,0:T(8,128)(2,1)S(1)} %collective-permute-done.21.refs_2_), channel_id=1, source_target_pairs={{0,4},{4,0},{8,12},{12,8},{1,5},{5,1},{9,13},{13,9},{2,6},{6,2},{1... | collective-permute-start | bytes 786440 | tf_op jit(solution)/shard_map/ppermute | solution.py:434
  108.8 9.3 %collective-permute-start.15 = (bf16[128,1024]{1,0:T(8,128)(2,1)S(1)}, bf16[128,1024]{1,0:T(8,128)(2,1)S(1)}, u32[]{:S(2)}, u32[]{:S(2)}) collective-permute-start(bf16[128,1024]{1,0:T(8,128)(2,1)S(1)} %collective-permute-done.14.refs_0_), channel_id=1, source_target_pairs={{0,4},{4,0},{8,12},{12,8},{1,5},{5,1},{9,13},{13,9},{2,6},{6,2},{1... | collective-permute-start | bytes 786440 | tf_op jit(solution)/shard_map/ppermute | solution.py:434
  (8 other events, 93.0 us)

commit v5 on v4

--- a/solution.py
+++ b/solution.py
@@ -376,26 +376,29 @@
     )
 
 
-def out_kernel(which, has_before, n_ctx, w_ref, *refs):
-    pieces, out_ref = refs[: len(which)], refs[-1]
+def out_kernel(which, parts, has_before, n_ctx, w_ref, *refs):
+    pieces, out_ref = refs[: len(which) * parts], refs[-1]
     columns = out_ref.shape[1]
     width = pieces[0].shape[1] // n_ctx
     cols = rows_at(pl.program_id(0), columns)
     me = lax.axis_index("ctx")
     sources = chan_sources()
-    acc = refs[len(which)][:, cols] if has_before else None
-    for piece, j in zip(pieces, which):
+    acc = refs[len(pieces)][:, cols] if has_before else None
+    for i, j in enumerate(which):
         for m in range(n_ctx):
             w = w_ref[rows_at(sources[j] * n_ctx + target(me, m, n_ctx), width), cols]
-            a = jnp.dot(piece[:, m * width : (m + 1) * width], w, preferred_element_type=F32)
+            mine = slice(m * width, (m + 1) * width)
+            x = jnp.concatenate([p[:, mine] for p in pieces[i * parts : (i + 1) * parts]], axis=0)
+            a = jnp.dot(x, w, preferred_element_type=F32)
             acc = a if acc is None else acc + a
     out_ref[...] = acc.astype(out_ref.dtype)
 
 
-def project_out(pieces, which, w, before, n_ctx, final=None, columns=256):
-    tokens = pieces[0].shape[0]
+def project_out(gathered, which, w, before, n_ctx, final=None, columns=256):
+    parts = len(gathered)
+    tokens = sum(pieces[0].shape[0] for pieces in gathered)
     _, out_width = w.shape
-    operands = [w, *(pieces[j] for j in which)] + ([] if before is None else [before])
+    operands = [w, *(pieces[j] for j in which for pieces in gathered)] + ([] if before is None else [before])
     specs = [VMEM] * len(operands)
     aliases = {}
     out_spec, shape = pl.BlockSpec((tokens, columns), lambda i: (0, i)), (tokens, out_width)
@@ -406,9 +409,9 @@
             specs.append(pl.BlockSpec(memory_space=pl.ANY))
             aliases = {len(operands): 0}
             operands.append(so_far)
-    share = len(which) * pieces[0].shape[1]
+    share = len(which) * gathered[0][0].shape[1]
     return pl.pallas_call(
-        functools.partial(out_kernel, tuple(which), before is not None, n_ctx),
+        functools.partial(out_kernel, tuple(which), parts, before is not None, n_ctx),
         out_shape=jax.ShapeDtypeStruct(shape, F32 if final is None else BF16),
         grid=(out_width // columns,),
         in_specs=specs,
@@ -488,11 +491,10 @@
         beside = swap_cores(gated)
         gathered.append([gated, beside, *gather_far(gated)])
     every = range(len(gathered[0]))
-    out = project_out(gathered[0], every, out_weight, None, n_ctx, (0, rows, None))
-    out = project_out(gathered[1], every, out_weight, None, n_ctx, (2, rows, out))
-    part = project_out(gathered[2], every[:2], out_weight, None, n_ctx)
-    part = project_out(gathered[2], every[2:-1], out_weight, part, n_ctx)
-    return project_out(gathered[2], every[-1:], out_weight, part, n_ctx, (3, rows, out))
+    out = project_out(gathered[:1], every, out_weight, None, n_ctx, (0, rows, None))
+    part = project_out(gathered[1:], every[:2], out_weight, None, n_ctx)
+    part = project_out(gathered[1:], every[2:-1], out_weight, part, n_ctx)
+    return project_out(gathered[1:], every[-1:], out_weight, part, n_ctx, (1, rows, out))
 
 
 P_SIZE = 128

time: 120 us -> 120 us (level)
  waiting for transfers between devices: 46.5 us -> 48.9 us
  Pallas kernels: 40.4 us -> 38.6 us
    ppermute x15, waiting for transfers between devices: 19.1 us -> 22.6 us  [exchange(): lax.ppermute(parts[k], 'ctx', [(i, target(i, k, n)) for i in range(n)])]
    pallas_call x5 -> x4, Pallas kernels: 11.2 us -> 9.46 us  [project_out(): pl.pallas_call(functools.partial(out_kernel, tuple(which), parts, before...]
  transfers between devices with their start and end apart: 29 -> 29, of which waited for: 10 -> 13; matrix products, arithmetic and copies ran while one was open for 2% -> 2% of each run, Pallas kernels for 30% -> 29%
where the time goes in v5:
time: 120 us
  waiting for transfers between devices  48.9 us (41%)
  Pallas kernels  38.6 us (32%)
  starting transfers between devices  30.1 us (25%)
  local copies, waits for them, and re-layouts  2.17 us (2%)
    ppermute x5, waiting for transfers between devices, shift(): return lax.ppermute(x, axis, [(i, (i + by) % n) for i in range(n)])  26.2 us
    ppermute x15, starting transfers between devices, exchange(): lax.ppermute(parts[k], 'ctx', [(i, target(i, k, n)) for i in range(n)])  23.7 us
    ppermute x15, waiting for transfers between devices, exchange(): lax.ppermute(parts[k], 'ctx', [(i, target(i, k, n)) for i in range(n)])  22.6 us
    pallas_call x12, Pallas kernels, call(): pl.pallas_call(kernel, out_shape=out, in_specs=[VMEM] * len(operands), ou...  16 us
    pallas_call x4, Pallas kernels, project_out(): pl.pallas_call(functools.partial(out_kernel, tuple(which), parts, before...  9.46 us
    pallas_call x2, Pallas kernels, queries(): pl.pallas_call(functools.partial(query_kernel, tuple(starts), n_ctx, load...  6.69 us
    pallas_call x1, Pallas kernels, prologue(): pl.pallas_call(functools.partial(prologue_kernel, width), out_shape=out,...  6.42 us
    ppermute x5, starting transfers between devices, shift(): return lax.ppermute(x, axis, [(i, (i + by) % n) for i in range(n)])  5.29 us
  transfers between devices with their start and end apart: 29, of which 13 were waited for; matrix products, arithmetic and copies ran while one was open for 2% of the time, Pallas kernels for 29%

profile of v5, /device:TPU:0, one launch (start us, length us, event | category | flops | bytes accessed | tf_op | source)
XLA Modules:
  0.0 119.9 jit_solution(5039698922669422196)
XLA Ops:
  1.6 2.6 %collective-permute-start.1 = (bf16[256,1024]{1,0:T(8,128)(2,1)S(1)}, bf16[256,1024]{1,0:T(8,128)(2,1)S(1)}, u32[]{:S(2)}, u32[]{:S(2)}) collective-permute-start(bf16[256,1024]{1,0:T(8,128)(2,1)S(1)} %slice.6), channel_id=1, source_target_pairs={{0,8},{4,12},{8,0},{12,4},{1,9},{5,13},{9,1},{13,5},{2,10},{6,14},... | collective-permute-start | bytes 1572872 | tf_op jit(solution)/shard_map/ppermute | solution.py:432
  5.3 11.6 %collective-permute-done.1.refs_2_.refs_0_ = bf16[256,1024]{1,0:T(8,128)(2,1)S(1)} collective-permute-done((bf16[256,1024]{1,0:T(8,128)(2,1)S(1)}, bf16[256,1024]{1,0:T(8,128)(2,1)S(1)}, u32[]{:S(2)}, u32[]{:S(2)}) %collective-permute-start.1) | collective-permute-done | bytes 524320 | tf_op jit(solution)/shard_map/ppermute | solution.py:432
  16.9 6.4 %prologue.1 = (bf16[512,256]{1,0:T(8,128)(2,1)S(1)}, bf16[256,512]{1,0:T(8,128)(2,1)S(1)}, bf16[2,4096,1024]{2,1,0:T(8,128)(2,1)S(1)}, f32[8,512,256]{2,1,0:T(8,128)S(1)}, f32[4,256]{1,0:T(4,128)S(1)}) custom-call(f32[1024]{0:T(1024)} %skip_hbm, bf16[512,256]{1,0:T(8,128)(2,1)} %constant.4.clone.fwd_hbm, bf16[256,512]{1,0:T(8,128)(2,1)} %constant.5.clone.inv_hbm, ...), custom_call_target="tpu_custom_call" | custom-call | flops 536870912 | bytes 30408704 | tf_op jit(solution)/shard_map/prologue/pallas_call | solution.py:123
  23.4 4.6 %collective-permute-done.3.refs_2_.refs_0_ = bf16[256,1024]{1,0:T(8,128)(2,1)S(1)} collective-permute-done((bf16[256,1024]{1,0:T(8,128)(2,1)S(1)}, bf16[256,1024]{1,0:T(8,128)(2,1)S(1)}, u32[]{:S(2)}, u32[]{:S(2)}) %collective-permute-start.3) | collective-permute-done | bytes 524320 | tf_op jit(solution)/shard_map/ppermute | solution.py:432
  28.0 2.4 %shard_map.76 = (f32[256,1024]{1,0:T(8,128)S(1)}, f32[256,1024]{1,0:T(8,128)S(1)}) custom-call(bf16[2,4096,1024]{2,1,0:T(8,128)(2,1)S(1)} %get-tuple-element.47.w_ref, bf16[512,1024]{1,0:T(8,128)(2,1)S(1)} %copy-done, bf16[512,1024]{1,0:T(8,128)(2,1)S(1)} %collective-permute-done.refs_1_), custom_call_target="tpu_custom_call" | custom-call | flops 2147483648 | bytes 9437184 | tf_op jit(solution)/shard_map/pallas_call | solution.py:42
  33.1 1.9 %collective-permute-start.5 = (bf16[256,256]{1,0:T(8,128)(2,1)S(1)}, bf16[256,256]{1,0:T(8,128)(2,1)S(1)}, u32[]{:S(2)}, u32[]{:S(2)}) collective-permute-start(bf16[256,256]{1,0:T(8,128)(2,1)S(1)} %get-tuple-element.64.refs_1_), channel_id=1, source_target_pairs={{0,1},{1,0},{2,3},{3,2},{4,5},{5,4},{6,7},{7,6},{8,9},{9,8},{10,11... | collective-permute-start | bytes 393224 | tf_op jit(solution)/shard_map/ppermute | solution.py:451
  35.0 2.6 %collective-permute-start.6 = (bf16[256,256]{1,0:T(8,128)(2,1)S(1)}, bf16[256,256]{1,0:T(8,128)(2,1)S(1)}, u32[]{:S(2)}, u32[]{:S(2)}) collective-permute-start(bf16[256,256]{1,0:T(8,128)(2,1)S(1)} %get-tuple-element.65.refs_2_), channel_id=1, source_target_pairs={{0,2},{1,3},{2,0},{3,1},{4,6},{5,7},{6,4},{7,5},{8,10},{9,11},{10,... | collective-permute-start | bytes 393224 | tf_op jit(solution)/shard_map/ppermute | solution.py:451
  37.6 2.4 %shard_map.73 = (f32[256,1024]{1,0:T(8,128)S(1)}, f32[256,1024]{1,0:T(8,128)S(1)}) custom-call(bf16[2,4096,1024]{2,1,0:T(8,128)(2,1)S(1)} %get-tuple-element.47.w_ref, bf16[512,1024]{1,0:T(8,128)(2,1)S(1)} %copy-done, bf16[512,1024]{1,0:T(8,128)(2,1)S(1)} %collective-permute-done.refs_1_), custom_call_target="tpu_custom_call" | custom-call | flops 2147483648 | bytes 9437184 | tf_op jit(solution)/shard_map/pallas_call | solution.py:42
  43.7 3.5 %collective-permute-start.9 = (bf16[256,256]{1,0:T(8,128)(2,1)S(1)}, bf16[256,256]{1,0:T(8,128)(2,1)S(1)}, u32[]{:S(2)}, u32[]{:S(2)}) collective-permute-start(bf16[256,256]{1,0:T(8,128)(2,1)S(1)} %get-tuple-element.54.refs_2_), channel_id=1, source_target_pairs={{0,2},{1,3},{2,0},{3,1},{4,6},{5,7},{6,4},{7,5},{8,10},{9,11},{10,... | collective-permute-start | bytes 393224 | tf_op jit(solution)/shard_map/ppermute | solution.py:451
  47.9 2.1 %shard_map.79.sum_ref = f32[8,512,256]{2,1,0:T(8,128)S(1)} custom-call(bf16[512,256]{1,0:T(8,128)(2,1)S(1)} %get-tuple-element.58.fwd_ref, f32[8,512,256]{2,1,0:T(8,128)S(1)} %get-tuple-element.57.g_ref, bf16[256,256]{1,0:T(8,128)(2,1)S(1)} %get-tuple-element.63.refs_0_, bf16[256,256]{1,0:T(8,128)(2,1)S(1)} %collective-permute-done.5.refs_1_, ...), custom_call_target="tpu_custom_call" | custom-call | flops 268435456 | bytes 8388608 | tf_op jit(solution)/shard_map/pallas_call | solution.py:42
  50.5 8.6 %collective-permute-done.9.refs_2_ = bf16[256,256]{1,0:T(8,128)(2,1)S(1)} collective-permute-done((bf16[256,256]{1,0:T(8,128)(2,1)S(1)}, bf16[256,256]{1,0:T(8,128)(2,1)S(1)}, u32[]{:S(2)}, u32[]{:S(2)}) %collective-permute-start.9) | collective-permute-done | bytes 131104 | tf_op jit(solution)/shard_map/ppermute | solution.py:451
  60.8 2.7 %collective-permute-start.23 = (bf16[256,256]{1,0:T(8,128)(2,1)S(1)}, bf16[256,256]{1,0:T(8,128)(2,1)S(1)}, u32[]{:S(2)}, u32[]{:S(2)}) collective-permute-start(bf16[256,256]{1,0:T(8,128)(2,1)S(1)} %get-tuple-element.78), channel_id=1, source_target_pairs={{0,1},{1,0},{2,3},{3,2},{4,5},{5,4},{6,7},{7,6},{8,9},{9,8},{10,11... | collective-permute-start | bytes 393224 | tf_op jit(solution)/shard_map/ppermute | solution.py:451
  66.0 4.3 %q_projection.2 = (bf16[256,1024]{1,0:T(8,128)(2,1)S(1)}, bf16[4096,1024]{1,0:T(8,128)(2,1)S(1)}) custom-call(bf16[3,4096,1024]{2,1,0:T(8,128)(2,1)} %bitcast.4, bf16[512,1024]{1,0:T(8,128)(2,1)S(1)} %copy-done, bf16[512,1024]{1,0:T(8,128)(2,1)S(1)} %collective-permute-done.refs_1_, bf16[256,1024]{1,0:T(8,128)(2,1)S(1)} %collective-permute-done.1.refs_2_.refs_0_, ...), custom_call_target="tpu_custom_call" | custom-call | flops 2147483648 | bytes 10485760 | tf_op jit(solution)/shard_map/q_projection/pallas_call | solution.py:228
  70.2 5.7 %collective-permute-done.24.refs_6_ = bf16[256,256]{1,0:T(8,128)(2,1)S(1)} collective-permute-done((bf16[256,256]{1,0:T(8,128)(2,1)S(1)}, bf16[256,256]{1,0:T(8,128)(2,1)S(1)}, u32[]{:S(2)}, u32[]{:S(2)}) %collective-permute-start.24) | collective-permute-done | bytes 131104 | tf_op jit(solution)/shard_map/ppermute | solution.py:451
  79.4 2.0 %collective-permute-start.16 = (bf16[128,256]{1,0:T(8,128)(2,1)S(1)}, bf16[128,256]{1,0:T(8,128)(2,1)S(1)}, u32[]{:S(2)}, u32[]{:S(2)}) collective-permute-start(bf16[128,256]{1,0:T(8,128)(2,1)S(1)} %get-tuple-element.73), channel_id=1, source_target_pairs={{0,1},{1,0},{2,3},{3,2},{4,5},{5,4},{6,7},{7,6},{8,9},{9,8},{10,11... | collective-permute-start | bytes 196616 | tf_op jit(solution)/shard_map/ppermute | solution.py:451
  83.8 2.4 %q_projection.3.q_ref = bf16[256,1024]{1,0:T(8,128)(2,1)S(1)} custom-call(bf16[4096,1024]{1,0:T(8,128)(2,1)S(1)} %get-tuple-element.45.w_ref, bf16[512,1024]{1,0:T(8,128)(2,1)S(1)} %copy-done, bf16[512,1024]{1,0:T(8,128)(2,1)S(1)} %collective-permute-done.refs_1_, bf16[256,1024]{1,0:T(8,128)(2,1)S(1)} %collective-permute-done.3.refs_2_.refs_0_, ...), custom_call_target="tpu_custom_call" | custom-call | flops 2147483648 | bytes 10485760 | tf_op jit(solution)/shard_map/q_projection/pallas_call | solution.py:228
  90.5 1.7 %collective-permute-start.12 = (bf16[128,256]{1,0:T(8,128)(2,1)S(1)}, bf16[128,256]{1,0:T(8,128)(2,1)S(1)}, u32[]{:S(2)}, u32[]{:S(2)}) collective-permute-start(bf16[128,256]{1,0:T(8,128)(2,1)S(1)} %get-tuple-element.70), channel_id=1, source_target_pairs={{0,2},{1,3},{2,0},{3,1},{4,6},{5,7},{6,4},{7,5},{8,10},{9,11},{10,... | collective-permute-start | bytes 196616 | tf_op jit(solution)/shard_map/ppermute | solution.py:451
  93.2 2.2 %collective-permute-start.13 = (bf16[128,256]{1,0:T(8,128)(2,1)S(1)}, bf16[128,256]{1,0:T(8,128)(2,1)S(1)}, u32[]{:S(2)}, u32[]{:S(2)}) collective-permute-start(bf16[128,256]{1,0:T(8,128)(2,1)S(1)} %get-tuple-element.71), channel_id=1, source_target_pairs={{0,3},{1,2},{2,1},{3,0},{4,7},{5,6},{6,5},{7,4},{8,11},{9,10},{10,... | collective-permute-start | bytes 196616 | tf_op jit(solution)/shard_map/ppermute | solution.py:451
  95.3 2.8 %collective-permute-done.12.refs_6_ = bf16[128,256]{1,0:T(8,128)(2,1)S(1)} collective-permute-done((bf16[128,256]{1,0:T(8,128)(2,1)S(1)}, bf16[128,256]{1,0:T(8,128)(2,1)S(1)}, u32[]{:S(2)}, u32[]{:S(2)}) %collective-permute-start.12) | collective-permute-done | bytes 65568 | tf_op jit(solution)/shard_map/ppermute | solution.py:451
  100.4 6.9 %collective-permute-done.19.refs_1_ = bf16[128,1024]{1,0:T(8,128)(2,1)S(1)} collective-permute-done((bf16[128,1024]{1,0:T(8,128)(2,1)S(1)}, bf16[128,1024]{1,0:T(8,128)(2,1)S(1)}, u32[]{:S(2)}, u32[]{:S(2)}) %collective-permute-start.19) | collective-permute-done | bytes 262176 | tf_op jit(solution)/shard_map/ppermute | solution.py:432
  107.3 3.1 %collective-permute-done.14.refs_0_ = bf16[128,1024]{1,0:T(8,128)(2,1)S(1)} collective-permute-done((bf16[128,1024]{1,0:T(8,128)(2,1)S(1)}, bf16[128,1024]{1,0:T(8,128)(2,1)S(1)}, u32[]{:S(2)}, u32[]{:S(2)}) %collective-permute-start.14) | collective-permute-done | bytes 262176 | tf_op jit(solution)/shard_map/ppermute | solution.py:432
  110.4 2.0 %out_projection.4.refs_2_ = f32[256,1024]{1,0:T(8,128)S(1)} custom-call(bf16[4096,1024]{1,0:T(8,128)(2,1)S(1)} %bitcast.2, bf16[128,1024]{1,0:T(8,128)(2,1)S(1)} %shard_map.82.refs_0_, bf16[128,1024]{1,0:T(8,128)(2,1)S(1)} %shard_map.83.refs_1_, bf16[128,1024]{1,0:T(8,128)(2,1)S(1)} %collective-permute-done.21.refs_2_, ...), custom_call_target="tpu_custom_call" | custom-call | flops 1073741824 | bytes 5767168 | tf_op jit(solution)/shard_map/out_projection/pallas_call | solution.py:413
  113.8 3.8 %out_projection.6.refs_3_ = bf16[512,1024]{1,0:T(8,128)(2,1)} custom-call(bf16[4096,1024]{1,0:T(8,128)(2,1)S(1)} %bitcast.2, bf16[256,1024]{1,0:T(8,128)(2,1)S(1)} %shard_map.84.refs_0_, bf16[256,1024]{1,0:T(8,128)(2,1)S(1)} %collective-permute-done.26.refs_1_, bf16[256,1024]{1,0:T(8,128)(2,1)S(1)} %collective-permute-done.27.refs_2_, ...), custom_call_target="tpu_custom_call" | custom-call | flops 2147483648 | bytes 11010048 | tf_op jit(solution)/shard_map/out_projection/pallas_call | solution.py:413
  117.6 2.3 %out_projection.7 = bf16[512,1024]{1,0:T(8,128)(2,1)} custom-call(bf16[4096,1024]{1,0:T(8,128)(2,1)S(1)} %bitcast.2, bf16[128,1024]{1,0:T(8,128)(2,1)S(1)} %collective-permute-done.15.refs_0_, bf16[128,1024]{1,0:T(8,128)(2,1)S(1)} %collective-permute-done.20.refs_1_, f32[256,1024]{1,0:T(8,128)S(1)} %out_projection.5.refs_2_, ...), custom_call_target="tpu_custom_call", output_to_operand_aliasing={{}: (4, {})} | custom-call | flops 536870912 | bytes 3145728 | tf_op jit(solution)/shard_map/out_projection/pallas_call | solution.py:413
  (62 shorter events, 29.1 us)
Async XLA Ops:
  0.0 28.0 %collective-permute-start = (bf16[512,1024]{1,0:T(8,128)(2,1)}, bf16[512,1024]{1,0:T(8,128)(2,1)S(1)}, u32[]{:S(2)}, u32[]{:S(2)}) collective-permute-start(bf16[512,1024]{1,0:T(8,128)(2,1)} %refs_0_.7), channel_id=1, source_target_pairs={{0,4},{4,0},{8,12},{12,8},{1,5},{5,1},{9,13},{13,9},{2,6},{6,2},{1... | collective-permute-start | bytes 3145736 | tf_op jit(solution)/shard_map/ppermute | solution.py:437
  1.6 15.3 %collective-permute-start.1 = (bf16[256,1024]{1,0:T(8,128)(2,1)S(1)}, bf16[256,1024]{1,0:T(8,128)(2,1)S(1)}, u32[]{:S(2)}, u32[]{:S(2)}) collective-permute-start(bf16[256,1024]{1,0:T(8,128)(2,1)S(1)} %slice.6), channel_id=1, source_target_pairs={{0,8},{4,12},{8,0},{12,4},{1,9},{5,13},{9,1},{13,5},{2,10},{6,14},... | collective-permute-start | bytes 1572872 | tf_op jit(solution)/shard_map/ppermute | solution.py:432
  5.2 22.8 %collective-permute-start.3 = (bf16[256,1024]{1,0:T(8,128)(2,1)S(1)}, bf16[256,1024]{1,0:T(8,128)(2,1)S(1)}, u32[]{:S(2)}, u32[]{:S(2)}) collective-permute-start(bf16[256,1024]{1,0:T(8,128)(2,1)S(1)} %slice.7), channel_id=1, source_target_pairs={{0,8},{4,12},{8,0},{12,4},{1,9},{5,13},{9,1},{13,5},{2,10},{6,14},... | collective-permute-start | bytes 1572872 | tf_op jit(solution)/shard_map/ppermute | solution.py:432
  16.9 14.9 %collective-permute-start.2 = (bf16[256,1024]{1,0:T(8,128)(2,1)S(1)}, bf16[256,1024]{1,0:T(8,128)(2,1)S(1)}, u32[]{:S(2)}, u32[]{:S(2)}) collective-permute-start(bf16[256,1024]{1,0:T(8,128)(2,1)S(1)} %collective-permute-done.1.refs_2_.refs_0_), channel_id=1, source_target_pairs={{0,4},{4,0},{8,12},{12,8},{1,5},{5,1},{9,13},{13,9},{2,6},{6,2},{1... | collective-permute-start | bytes 1572872 | tf_op jit(solution)/shard_map/ppermute | solution.py:437
  28.0 13.4 %collective-permute-start.4 = (bf16[256,1024]{1,0:T(8,128)(2,1)S(1)}, bf16[256,1024]{1,0:T(8,128)(2,1)S(1)}, u32[]{:S(2)}, u32[]{:S(2)}) collective-permute-start(bf16[256,1024]{1,0:T(8,128)(2,1)S(1)} %collective-permute-done.3.refs_2_.refs_0_), channel_id=1, source_target_pairs={{0,4},{4,0},{8,12},{12,8},{1,5},{5,1},{9,13},{13,9},{2,6},{6,2},{1... | collective-permute-start | bytes 1572872 | tf_op jit(solution)/shard_map/ppermute | solution.py:437
  33.1 14.1 %collective-permute-start.5 = (bf16[256,256]{1,0:T(8,128)(2,1)S(1)}, bf16[256,256]{1,0:T(8,128)(2,1)S(1)}, u32[]{:S(2)}, u32[]{:S(2)}) collective-permute-start(bf16[256,256]{1,0:T(8,128)(2,1)S(1)} %get-tuple-element.64.refs_1_), channel_id=1, source_target_pairs={{0,1},{1,0},{2,3},{3,2},{4,5},{5,4},{6,7},{7,6},{8,9},{9,8},{10,11... | collective-permute-start | bytes 393224 | tf_op jit(solution)/shard_map/ppermute | solution.py:451
  35.0 12.9 %collective-permute-start.6 = (bf16[256,256]{1,0:T(8,128)(2,1)S(1)}, bf16[256,256]{1,0:T(8,128)(2,1)S(1)}, u32[]{:S(2)}, u32[]{:S(2)}) collective-permute-start(bf16[256,256]{1,0:T(8,128)(2,1)S(1)} %get-tuple-element.65.refs_2_), channel_id=1, source_target_pairs={{0,2},{1,3},{2,0},{3,1},{4,6},{5,7},{6,4},{7,5},{8,10},{9,11},{10,... | collective-permute-start | bytes 393224 | tf_op jit(solution)/shard_map/ppermute | solution.py:451
  37.6 10.4 %collective-permute-start.7 = (bf16[256,256]{1,0:T(8,128)(2,1)S(1)}, bf16[256,256]{1,0:T(8,128)(2,1)S(1)}, u32[]{:S(2)}, u32[]{:S(2)}) collective-permute-start(bf16[256,256]{1,0:T(8,128)(2,1)S(1)} %get-tuple-element.66.refs_3_), channel_id=1, source_target_pairs={{0,3},{1,2},{2,1},{3,0},{4,7},{5,6},{6,5},{7,4},{8,11},{9,10},{10,... | collective-permute-start | bytes 393224 | tf_op jit(solution)/shard_map/ppermute | solution.py:451
  42.7 7.8 %collective-permute-start.8 = (bf16[256,256]{1,0:T(8,128)(2,1)S(1)}, bf16[256,256]{1,0:T(8,128)(2,1)S(1)}, u32[]{:S(2)}, u32[]{:S(2)}) collective-permute-start(bf16[256,256]{1,0:T(8,128)(2,1)S(1)} %get-tuple-element.53.refs_1_), channel_id=1, source_target_pairs={{0,1},{1,0},{2,3},{3,2},{4,5},{5,4},{6,7},{7,6},{8,9},{9,8},{10,11... | collective-permute-start | bytes 393224 | tf_op jit(solution)/shard_map/ppermute | solution.py:451
  43.7 15.5 %collective-permute-start.9 = (bf16[256,256]{1,0:T(8,128)(2,1)S(1)}, bf16[256,256]{1,0:T(8,128)(2,1)S(1)}, u32[]{:S(2)}, u32[]{:S(2)}) collective-permute-start(bf16[256,256]{1,0:T(8,128)(2,1)S(1)} %get-tuple-element.54.refs_2_), channel_id=1, source_target_pairs={{0,2},{1,3},{2,0},{3,1},{4,6},{5,7},{6,4},{7,5},{8,10},{9,11},{10,... | collective-permute-start | bytes 393224 | tf_op jit(solution)/shard_map/ppermute | solution.py:451
  47.2 12.0 %collective-permute-start.10 = (bf16[256,256]{1,0:T(8,128)(2,1)S(1)}, bf16[256,256]{1,0:T(8,128)(2,1)S(1)}, u32[]{:S(2)}, u32[]{:S(2)}) collective-permute-start(bf16[256,256]{1,0:T(8,128)(2,1)S(1)} %get-tuple-element.55.refs_3_), channel_id=1, source_target_pairs={{0,3},{1,2},{2,1},{3,0},{4,7},{5,6},{6,5},{7,4},{8,11},{9,10},{10,... | collective-permute-start | bytes 393224 | tf_op jit(solution)/shard_map/ppermute | solution.py:451
  60.8 9.4 %collective-permute-start.23 = (bf16[256,256]{1,0:T(8,128)(2,1)S(1)}, bf16[256,256]{1,0:T(8,128)(2,1)S(1)}, u32[]{:S(2)}, u32[]{:S(2)}) collective-permute-start(bf16[256,256]{1,0:T(8,128)(2,1)S(1)} %get-tuple-element.78), channel_id=1, source_target_pairs={{0,1},{1,0},{2,3},{3,2},{4,5},{5,4},{6,7},{7,6},{8,9},{9,8},{10,11... | collective-permute-start | bytes 393224 | tf_op jit(solution)/shard_map/ppermute | solution.py:451
  63.5 12.4 %collective-permute-start.24 = (bf16[256,256]{1,0:T(8,128)(2,1)S(1)}, bf16[256,256]{1,0:T(8,128)(2,1)S(1)}, u32[]{:S(2)}, u32[]{:S(2)}) collective-permute-start(bf16[256,256]{1,0:T(8,128)(2,1)S(1)} %get-tuple-element.79), channel_id=1, source_target_pairs={{0,2},{1,3},{2,0},{3,1},{4,6},{5,7},{6,4},{7,5},{8,10},{9,11},{10,... | collective-permute-start | bytes 393224 | tf_op jit(solution)/shard_map/ppermute | solution.py:451
  64.6 11.4 %collective-permute-start.25 = (bf16[256,256]{1,0:T(8,128)(2,1)S(1)}, bf16[256,256]{1,0:T(8,128)(2,1)S(1)}, u32[]{:S(2)}, u32[]{:S(2)}) collective-permute-start(bf16[256,256]{1,0:T(8,128)(2,1)S(1)} %get-tuple-element.80), channel_id=1, source_target_pairs={{0,3},{1,2},{2,1},{3,0},{4,7},{5,6},{6,5},{7,4},{8,11},{9,10},{10,... | collective-permute-start | bytes 393224 | tf_op jit(solution)/shard_map/ppermute | solution.py:451
  76.2 14.0 %collective-permute-start.27 = (bf16[256,1024]{1,0:T(8,128)(2,1)S(1)}, bf16[256,1024]{1,0:T(8,128)(2,1)S(1)}, u32[]{:S(2)}, u32[]{:S(2)}) collective-permute-start(bf16[256,1024]{1,0:T(8,128)(2,1)S(1)} %shard_map.84.refs_0_), channel_id=1, source_target_pairs={{0,8},{4,12},{8,0},{12,4},{1,9},{5,13},{9,1},{13,5},{2,10},{6,14},... | collective-permute-start | bytes 1572872 | tf_op jit(solution)/shard_map/ppermute | solution.py:432
  88.6 11.8 %collective-permute-start.22 = (bf16[128,1024]{1,0:T(8,128)(2,1)S(1)}, bf16[128,1024]{1,0:T(8,128)(2,1)S(1)}, u32[]{:S(2)}, u32[]{:S(2)}) collective-permute-start(bf16[128,1024]{1,0:T(8,128)(2,1)S(1)} %shard_map.83.refs_1_), channel_id=1, source_target_pairs={{0,4},{4,0},{8,12},{12,8},{1,5},{5,1},{9,13},{13,9},{2,6},{6,2},{1... | collective-permute-start | bytes 786440 | tf_op jit(solution)/shard_map/ppermute | solution.py:437
  90.0 23.8 %collective-permute-start.26 = (bf16[256,1024]{1,0:T(8,128)(2,1)S(1)}, bf16[256,1024]{1,0:T(8,128)(2,1)S(1)}, u32[]{:S(2)}, u32[]{:S(2)}) collective-permute-start(bf16[256,1024]{1,0:T(8,128)(2,1)S(1)} %shard_map.84.refs_0_), channel_id=1, source_target_pairs={{0,4},{4,0},{8,12},{12,8},{1,5},{5,1},{9,13},{13,9},{2,6},{6,2},{1... | collective-permute-start | bytes 1572872 | tf_op jit(solution)/shard_map/ppermute | solution.py:437
  90.1 23.7 %collective-permute-start.28 = (bf16[256,1024]{1,0:T(8,128)(2,1)S(1)}, bf16[256,1024]{1,0:T(8,128)(2,1)S(1)}, u32[]{:S(2)}, u32[]{:S(2)}) collective-permute-start(bf16[256,1024]{1,0:T(8,128)(2,1)S(1)} %collective-permute-done.27.refs_2_), channel_id=1, source_target_pairs={{0,4},{4,0},{8,12},{12,8},{1,5},{5,1},{9,13},{13,9},{2,6},{6,2},{1... | collective-permute-start | bytes 1572872 | tf_op jit(solution)/shard_map/ppermute | solution.py:437
  90.5 7.7 %collective-permute-start.12 = (bf16[128,256]{1,0:T(8,128)(2,1)S(1)}, bf16[128,256]{1,0:T(8,128)(2,1)S(1)}, u32[]{:S(2)}, u32[]{:S(2)}) collective-permute-start(bf16[128,256]{1,0:T(8,128)(2,1)S(1)} %get-tuple-element.70), channel_id=1, source_target_pairs={{0,2},{1,3},{2,0},{3,1},{4,6},{5,7},{6,4},{7,5},{8,10},{9,11},{10,... | collective-permute-start | bytes 196616 | tf_op jit(solution)/shard_map/ppermute | solution.py:451
  98.2 9.2 %collective-permute-start.19 = (bf16[128,1024]{1,0:T(8,128)(2,1)S(1)}, bf16[128,1024]{1,0:T(8,128)(2,1)S(1)}, u32[]{:S(2)}, u32[]{:S(2)}) collective-permute-start(bf16[128,1024]{1,0:T(8,128)(2,1)S(1)} %shard_map.83.refs_1_), channel_id=1, source_target_pairs={{0,8},{4,12},{8,0},{12,4},{1,9},{5,13},{9,1},{13,5},{2,10},{6,14},... | collective-permute-start | bytes 786440 | tf_op jit(solution)/shard_map/ppermute | solution.py:432
  99.4 10.9 %collective-permute-start.14 = (bf16[128,1024]{1,0:T(8,128)(2,1)S(1)}, bf16[128,1024]{1,0:T(8,128)(2,1)S(1)}, u32[]{:S(2)}, u32[]{:S(2)}) collective-permute-start(bf16[128,1024]{1,0:T(8,128)(2,1)S(1)} %shard_map.82.refs_0_), channel_id=1, source_target_pairs={{0,8},{4,12},{8,0},{12,4},{1,9},{5,13},{9,1},{13,5},{2,10},{6,14},... | collective-permute-start | bytes 786440 | tf_op jit(solution)/shard_map/ppermute | solution.py:432
  100.4 10.0 %collective-permute-start.21 = (bf16[128,1024]{1,0:T(8,128)(2,1)S(1)}, bf16[128,1024]{1,0:T(8,128)(2,1)S(1)}, u32[]{:S(2)}, u32[]{:S(2)}) collective-permute-start(bf16[128,1024]{1,0:T(8,128)(2,1)S(1)} %shard_map.82.refs_0_), channel_id=1, source_target_pairs={{0,4},{4,0},{8,12},{12,8},{1,5},{5,1},{9,13},{13,9},{2,6},{6,2},{1... | collective-permute-start | bytes 786440 | tf_op jit(solution)/shard_map/ppermute | solution.py:437
  107.3 10.3 %collective-permute-start.20 = (bf16[128,1024]{1,0:T(8,128)(2,1)S(1)}, bf16[128,1024]{1,0:T(8,128)(2,1)S(1)}, u32[]{:S(2)}, u32[]{:S(2)}) collective-permute-start(bf16[128,1024]{1,0:T(8,128)(2,1)S(1)} %collective-permute-done.19.refs_1_), channel_id=1, source_target_pairs={{0,4},{4,0},{8,12},{12,8},{1,5},{5,1},{9,13},{13,9},{2,6},{6,2},{1... | collective-permute-start | bytes 786440 | tf_op jit(solution)/shard_map/ppermute | solution.py:437
  110.4 7.2 %collective-permute-start.15 = (bf16[128,1024]{1,0:T(8,128)(2,1)S(1)}, bf16[128,1024]{1,0:T(8,128)(2,1)S(1)}, u32[]{:S(2)}, u32[]{:S(2)}) collective-permute-start(bf16[128,1024]{1,0:T(8,128)(2,1)S(1)} %collective-permute-done.14.refs_0_), channel_id=1, source_target_pairs={{0,4},{4,0},{8,12},{12,8},{1,5},{5,1},{9,13},{13,9},{2,6},{6,2},{1... | collective-permute-start | bytes 786440 | tf_op jit(solution)/shard_map/ppermute | solution.py:437
  (8 other events, 98.7 us)

commit v6 on v5

--- a/solution.py
+++ b/solution.py
@@ -300,7 +300,7 @@
 
 
 def middle_kernel(n_ctx, fwd_ref, inv_ref, g_ref, sum_ref, *refs):
-    ins, x_ref, outs, y_ref = refs[:n_ctx], refs[n_ctx], refs[n_ctx + 1 : 2 * n_ctx + 1], refs[-1]
+    ins, x_ref, outs, y_ref = refs[:n_ctx], refs[n_ctx], refs[n_ctx + 1 : -1], refs[-1]
     blocks, rows, width = g_ref.shape
     forward_dft(n_ctx, fwd_ref, ins, x_ref)
     plan = [(b, b // 2, [(b - a, a // 2) for a in range(1, b, 2)]) for b in range(0, blocks, 2)]
@@ -319,7 +319,7 @@
 def convolve(forward, inverse, spectra, arrived, n_ctx):
     blocks, rows, width = spectra.shape
     half = (n_ctx, rows, width)
-    piece = jax.ShapeDtypeStruct((rows // 2, width), BF16)
+    piece = jax.ShapeDtypeStruct((rows // 4, width), BF16)
     flops, moved = blocks * rows * rows * width // 2, blocks * rows * width * 8
     sums = call(
         functools.partial(early_kernel, n_ctx),
@@ -332,7 +332,7 @@
     )
     x, *even = call(
         functools.partial(middle_kernel, n_ctx),
-        [jax.ShapeDtypeStruct(half, F32)] + [piece] * n_ctx,
+        [jax.ShapeDtypeStruct(half, F32)] + [piece] * (2 * n_ctx),
         [forward, inverse, spectra, sums, *arrived[1]],
         6,
         flops,
@@ -341,14 +341,14 @@
     )
     odd = call(
         functools.partial(late_kernel, n_ctx),
-        [jax.ShapeDtypeStruct((rows // 4, width), BF16)] * (2 * n_ctx),
+        [piece] * (2 * n_ctx),
         [inverse, spectra, sums, x],
         6,
         flops,
         moved,
         [pltpu.VMEM(half, F32)],
     )
-    return even, odd[:n_ctx], odd[n_ctx:]
+    return even[:n_ctx], even[n_ctx:], odd[:n_ctx], odd[n_ctx:]
 
 
 def gate_kernel(n_ctx, start, skip_ref, q_ref, *refs):
@@ -485,16 +485,17 @@
     conv = convolve(forward, inverse, spectra, arrived, n_ctx)
 
     gathered = []
-    for r, (c, start) in enumerate(((0, 0), (1, 0), (1, tokens // 2))):
+    for r in range(2 * CHUNKS):
+        c, start = r // 2, r % 2 * (tokens // 2)
         back = exchange(conv[r])
         gated = gate(skip, query[c], mixed[c], back, start, n_ctx)
         beside = swap_cores(gated)
         gathered.append([gated, beside, *gather_far(gated)])
     every = range(len(gathered[0]))
-    out = project_out(gathered[:1], every, out_weight, None, n_ctx, (0, rows, None))
-    part = project_out(gathered[1:], every[:2], out_weight, None, n_ctx)
-    part = project_out(gathered[1:], every[2:-1], out_weight, part, n_ctx)
-    return project_out(gathered[1:], every[-1:], out_weight, part, n_ctx, (1, rows, out))
+    out = project_out(gathered[:2], every, out_weight, None, n_ctx, (0, rows, None))
+    part = project_out(gathered[2:], every[:2], out_weight, None, n_ctx)
+    part = project_out(gathered[2:], every[2:-1], out_weight, part, n_ctx)
+    return project_out(gathered[2:], every[-1:], out_weight, part, n_ctx, (1, rows, out))
 
 
 P_SIZE = 128

time: 120 us -> 123 us (1.025)
  starting transfers between devices: 30.1 us -> 39 us
  waiting for transfers between devices: 48.9 us -> 42.3 us
    ppermute x15 -> x18, waiting for transfers between devices: 22.6 us -> 10.7 us  [exchange(): lax.ppermute(parts[k], 'ctx', [(i, target(i, k, n)) for i in range(n)])]
    ppermute x15 -> x18, starting transfers between devices: 23.7 us -> 29.8 us  [exchange(): lax.ppermute(parts[k], 'ctx', [(i, target(i, k, n)) for i in range(n)])]
    ppermute x5 -> x6, waiting for transfers between devices: 26.2 us -> 31.6 us  [shift(): return lax.ppermute(x, axis, [(i, (i + by) % n) for i in range(n)])]
    ppermute x5 -> x6, starting transfers between devices: 5.29 us -> 7.36 us  [shift(): return lax.ppermute(x, axis, [(i, (i + by) % n) for i in range(n)])]
    pallas_call x12 -> x13, Pallas kernels: 16 us -> 16.1 us  [call(): pl.pallas_call(kernel, out_shape=out, in_specs=[VMEM] * len(operands), ou...]
  transfers between devices with their start and end apart: 29 -> 35, of which waited for: 13 -> 9; matrix products, arithmetic and copies ran while one was open for 2% -> 2% of each run, Pallas kernels for 29% -> 27%
where the time goes in v6:
time: 123 us; the launch traced here: 122 us
  waiting for transfers between devices  42.3 us (34%)
  starting transfers between devices  39 us (32%)
  Pallas kernels  38.6 us (31%)
  local copies, waits for them, and re-layouts  2.16 us (2%)
    ppermute x6, waiting for transfers between devices, shift(): return lax.ppermute(x, axis, [(i, (i + by) % n) for i in range(n)])  31.6 us
    ppermute x18, starting transfers between devices, exchange(): lax.ppermute(parts[k], 'ctx', [(i, target(i, k, n)) for i in range(n)])  29.8 us
    pallas_call x13, Pallas kernels, call(): pl.pallas_call(kernel, out_shape=out, in_specs=[VMEM] * len(operands), ou...  16.1 us
    ppermute x18, waiting for transfers between devices, exchange(): lax.ppermute(parts[k], 'ctx', [(i, target(i, k, n)) for i in range(n)])  10.7 us
    pallas_call x4, Pallas kernels, project_out(): pl.pallas_call(functools.partial(out_kernel, tuple(which), parts, before...  9.47 us
    ppermute x6, starting transfers between devices, shift(): return lax.ppermute(x, axis, [(i, (i + by) % n) for i in range(n)])  7.36 us
    pallas_call x2, Pallas kernels, queries(): pl.pallas_call(functools.partial(query_kernel, tuple(starts), n_ctx, load...  6.7 us
    pallas_call x1, Pallas kernels, prologue(): pl.pallas_call(functools.partial(prologue_kernel, width), out_shape=out,...  6.42 us
  transfers between devices with their start and end apart: 35, of which 9 were waited for; matrix products, arithmetic and copies ran while one was open for 2% of the time, Pallas kernels for 27%

profile of v6, /device:TPU:0, one launch (start us, length us, event | category | flops | bytes accessed | tf_op | source)
XLA Modules:
  0.0 122.3 jit_solution(1543538477447948440)
XLA Ops:
  1.6 2.6 %collective-permute-start.1 = (bf16[256,1024]{1,0:T(8,128)(2,1)S(1)}, bf16[256,1024]{1,0:T(8,128)(2,1)S(1)}, u32[]{:S(2)}, u32[]{:S(2)}) collective-permute-start(bf16[256,1024]{1,0:T(8,128)(2,1)S(1)} %slice.6), channel_id=1, source_target_pairs={{0,8},{4,12},{8,0},{12,4},{1,9},{5,13},{9,1},{13,5},{2,10},{6,14},... | collective-permute-start | bytes 1572872 | tf_op jit(solution)/shard_map/ppermute | solution.py:432
  5.3 11.6 %collective-permute-done.1.refs_2_.refs_0_ = bf16[256,1024]{1,0:T(8,128)(2,1)S(1)} collective-permute-done((bf16[256,1024]{1,0:T(8,128)(2,1)S(1)}, bf16[256,1024]{1,0:T(8,128)(2,1)S(1)}, u32[]{:S(2)}, u32[]{:S(2)}) %collective-permute-start.1) | collective-permute-done | bytes 524320 | tf_op jit(solution)/shard_map/ppermute | solution.py:432
  16.9 6.4 %prologue.1 = (bf16[512,256]{1,0:T(8,128)(2,1)S(1)}, bf16[256,512]{1,0:T(8,128)(2,1)S(1)}, bf16[2,4096,1024]{2,1,0:T(8,128)(2,1)S(1)}, f32[8,512,256]{2,1,0:T(8,128)S(1)}, f32[4,256]{1,0:T(4,128)S(1)}) custom-call(f32[1024]{0:T(1024)} %skip_hbm, bf16[512,256]{1,0:T(8,128)(2,1)} %constant.4.clone.fwd_hbm, bf16[256,512]{1,0:T(8,128)(2,1)} %constant.5.clone.inv_hbm, ...), custom_call_target="tpu_custom_call" | custom-call | flops 536870912 | bytes 30408704 | tf_op jit(solution)/shard_map/prologue/pallas_call | solution.py:123
  23.4 4.6 %collective-permute-done.3.refs_2_.refs_0_ = bf16[256,1024]{1,0:T(8,128)(2,1)S(1)} collective-permute-done((bf16[256,1024]{1,0:T(8,128)(2,1)S(1)}, bf16[256,1024]{1,0:T(8,128)(2,1)S(1)}, u32[]{:S(2)}, u32[]{:S(2)}) %collective-permute-start.3) | collective-permute-done | bytes 524320 | tf_op jit(solution)/shard_map/ppermute | solution.py:432
  28.0 2.4 %shard_map.76 = (f32[256,1024]{1,0:T(8,128)S(1)}, f32[256,1024]{1,0:T(8,128)S(1)}) custom-call(bf16[2,4096,1024]{2,1,0:T(8,128)(2,1)S(1)} %get-tuple-element.51.w_ref, bf16[512,1024]{1,0:T(8,128)(2,1)S(1)} %copy-done, bf16[512,1024]{1,0:T(8,128)(2,1)S(1)} %collective-permute-done.refs_1_), custom_call_target="tpu_custom_call" | custom-call | flops 2147483648 | bytes 9437184 | tf_op jit(solution)/shard_map/pallas_call | solution.py:42
  35.0 2.6 %collective-permute-start.6 = (bf16[256,256]{1,0:T(8,128)(2,1)S(1)}, bf16[256,256]{1,0:T(8,128)(2,1)S(1)}, u32[]{:S(2)}, u32[]{:S(2)}) collective-permute-start(bf16[256,256]{1,0:T(8,128)(2,1)S(1)} %get-tuple-element.69.refs_2_), channel_id=1, source_target_pairs={{0,2},{1,3},{2,0},{3,1},{4,6},{5,7},{6,4},{7,5},{8,10},{9,11},{10,... | collective-permute-start | bytes 393224 | tf_op jit(solution)/shard_map/ppermute | solution.py:451
  37.6 2.4 %shard_map.73 = (f32[256,1024]{1,0:T(8,128)S(1)}, f32[256,1024]{1,0:T(8,128)S(1)}) custom-call(bf16[2,4096,1024]{2,1,0:T(8,128)(2,1)S(1)} %get-tuple-element.51.w_ref, bf16[512,1024]{1,0:T(8,128)(2,1)S(1)} %copy-done, bf16[512,1024]{1,0:T(8,128)(2,1)S(1)} %collective-permute-done.refs_1_), custom_call_target="tpu_custom_call" | custom-call | flops 2147483648 | bytes 9437184 | tf_op jit(solution)/shard_map/pallas_call | solution.py:42
  43.7 3.5 %collective-permute-start.9 = (bf16[256,256]{1,0:T(8,128)(2,1)S(1)}, bf16[256,256]{1,0:T(8,128)(2,1)S(1)}, u32[]{:S(2)}, u32[]{:S(2)}) collective-permute-start(bf16[256,256]{1,0:T(8,128)(2,1)S(1)} %get-tuple-element.58.refs_2_), channel_id=1, source_target_pairs={{0,2},{1,3},{2,0},{3,1},{4,6},{5,7},{6,4},{7,5},{8,10},{9,11},{10,... | collective-permute-start | bytes 393224 | tf_op jit(solution)/shard_map/ppermute | solution.py:451
  47.9 2.1 %shard_map.79.sum_ref = f32[8,512,256]{2,1,0:T(8,128)S(1)} custom-call(bf16[512,256]{1,0:T(8,128)(2,1)S(1)} %get-tuple-element.62.fwd_ref, f32[8,512,256]{2,1,0:T(8,128)S(1)} %get-tuple-element.61.g_ref, bf16[256,256]{1,0:T(8,128)(2,1)S(1)} %get-tuple-element.67.refs_0_, bf16[256,256]{1,0:T(8,128)(2,1)S(1)} %collective-permute-done.5.refs_1_, ...), custom_call_target="tpu_custom_call" | custom-call | flops 268435456 | bytes 8388608 | tf_op jit(solution)/shard_map/pallas_call | solution.py:42
  50.5 8.6 %collective-permute-done.9.refs_2_ = bf16[256,256]{1,0:T(8,128)(2,1)S(1)} collective-permute-done((bf16[256,256]{1,0:T(8,128)(2,1)S(1)}, bf16[256,256]{1,0:T(8,128)(2,1)S(1)}, u32[]{:S(2)}, u32[]{:S(2)}) %collective-permute-start.9) | collective-permute-done | bytes 131104 | tf_op jit(solution)/shard_map/ppermute | solution.py:451
  62.4 2.7 %collective-permute-start.16 = (bf16[128,256]{1,0:T(8,128)(2,1)S(1)}, bf16[128,256]{1,0:T(8,128)(2,1)S(1)}, u32[]{:S(2)}, u32[]{:S(2)}) collective-permute-start(bf16[128,256]{1,0:T(8,128)(2,1)S(1)} %get-tuple-element.77), channel_id=1, source_target_pairs={{0,1},{1,0},{2,3},{3,2},{4,5},{5,4},{6,7},{7,6},{8,9},{9,8},{10,11... | collective-permute-start | bytes 196616 | tf_op jit(solution)/shard_map/ppermute | solution.py:451
  65.2 2.9 %collective-permute-start.27 = (bf16[128,256]{1,0:T(8,128)(2,1)S(1)}, bf16[128,256]{1,0:T(8,128)(2,1)S(1)}, u32[]{:S(2)}, u32[]{:S(2)}) collective-permute-start(bf16[128,256]{1,0:T(8,128)(2,1)S(1)} %get-tuple-element.87), channel_id=1, source_target_pairs={{0,2},{1,3},{2,0},{3,1},{4,6},{5,7},{6,4},{7,5},{8,10},{9,11},{10,... | collective-permute-start | bytes 196616 | tf_op jit(solution)/shard_map/ppermute | solution.py:451
  69.6 2.3 %collective-permute-start.18 = (bf16[128,256]{1,0:T(8,128)(2,1)S(1)}, bf16[128,256]{1,0:T(8,128)(2,1)S(1)}, u32[]{:S(2)}, u32[]{:S(2)}) collective-permute-start(bf16[128,256]{1,0:T(8,128)(2,1)S(1)} %get-tuple-element.79), channel_id=1, source_target_pairs={{0,3},{1,2},{2,1},{3,0},{4,7},{5,6},{6,5},{7,4},{8,11},{9,10},{10,... | collective-permute-start | bytes 196616 | tf_op jit(solution)/shard_map/ppermute | solution.py:451
  74.9 4.6 %collective-permute-start.25 = (bf16[128,256]{1,0:T(8,128)(2,1)S(1)}, bf16[128,256]{1,0:T(8,128)(2,1)S(1)}, u32[]{:S(2)}, u32[]{:S(2)}) collective-permute-start(bf16[128,256]{1,0:T(8,128)(2,1)S(1)} %get-tuple-element.84), channel_id=1, source_target_pairs={{0,3},{1,2},{2,1},{3,0},{4,7},{5,6},{6,5},{7,4},{8,11},{9,10},{10,... | collective-permute-start | bytes 196616 | tf_op jit(solution)/shard_map/ppermute | solution.py:451
  79.5 4.3 %q_projection.2 = (bf16[256,1024]{1,0:T(8,128)(2,1)S(1)}, bf16[4096,1024]{1,0:T(8,128)(2,1)S(1)}) custom-call(bf16[3,4096,1024]{2,1,0:T(8,128)(2,1)} %bitcast.4, bf16[512,1024]{1,0:T(8,128)(2,1)S(1)} %copy-done, bf16[512,1024]{1,0:T(8,128)(2,1)S(1)} %collective-permute-done.refs_1_, bf16[256,1024]{1,0:T(8,128)(2,1)S(1)} %collective-permute-done.1.refs_2_.refs_0_, ...), custom_call_target="tpu_custom_call" | custom-call | flops 2147483648 | bytes 10485760 | tf_op jit(solution)/shard_map/q_projection/pallas_call | solution.py:228
  83.9 2.2 %collective-permute-start.11 = (bf16[128,256]{1,0:T(8,128)(2,1)S(1)}, bf16[128,256]{1,0:T(8,128)(2,1)S(1)}, u32[]{:S(2)}, u32[]{:S(2)}) collective-permute-start(bf16[128,256]{1,0:T(8,128)(2,1)S(1)} %get-tuple-element.73), channel_id=1, source_target_pairs={{0,1},{1,0},{2,3},{3,2},{4,5},{5,4},{6,7},{7,6},{8,9},{9,8},{10,11... | collective-permute-start | bytes 196616 | tf_op jit(solution)/shard_map/ppermute | solution.py:451
  86.1 2.4 %collective-permute-start.13 = (bf16[128,256]{1,0:T(8,128)(2,1)S(1)}, bf16[128,256]{1,0:T(8,128)(2,1)S(1)}, u32[]{:S(2)}, u32[]{:S(2)}) collective-permute-start(bf16[128,256]{1,0:T(8,128)(2,1)S(1)} %get-tuple-element.75), channel_id=1, source_target_pairs={{0,3},{1,2},{2,1},{3,0},{4,7},{5,6},{6,5},{7,4},{8,11},{9,10},{10,... | collective-permute-start | bytes 196616 | tf_op jit(solution)/shard_map/ppermute | solution.py:451
  90.1 2.4 %q_projection.3.q_ref = bf16[256,1024]{1,0:T(8,128)(2,1)S(1)} custom-call(bf16[4096,1024]{1,0:T(8,128)(2,1)S(1)} %get-tuple-element.49.w_ref, bf16[512,1024]{1,0:T(8,128)(2,1)S(1)} %copy-done, bf16[512,1024]{1,0:T(8,128)(2,1)S(1)} %collective-permute-done.refs_1_, bf16[256,1024]{1,0:T(8,128)(2,1)S(1)} %collective-permute-done.3.refs_2_.refs_0_, ...), custom_call_target="tpu_custom_call" | custom-call | flops 2147483648 | bytes 10485760 | tf_op jit(solution)/shard_map/q_projection/pallas_call | solution.py:228
  96.4 5.6 %collective-permute-done.31.refs_4_ = bf16[128,1024]{1,0:T(8,128)(2,1)S(1)} collective-permute-done((bf16[128,1024]{1,0:T(8,128)(2,1)S(1)}, bf16[128,1024]{1,0:T(8,128)(2,1)S(1)}, u32[]{:S(2)}, u32[]{:S(2)}) %collective-permute-start.31) | collective-permute-done | bytes 262176 | tf_op jit(solution)/shard_map/ppermute | solution.py:432
  102.5 5.1 %collective-permute-done.19.refs_1_ = bf16[128,1024]{1,0:T(8,128)(2,1)S(1)} collective-permute-done((bf16[128,1024]{1,0:T(8,128)(2,1)S(1)}, bf16[128,1024]{1,0:T(8,128)(2,1)S(1)}, u32[]{:S(2)}, u32[]{:S(2)}) %collective-permute-start.19) | collective-permute-done | bytes 262176 | tf_op jit(solution)/shard_map/ppermute | solution.py:432
  108.1 4.6 %collective-permute-done.14.refs_0_ = bf16[128,1024]{1,0:T(8,128)(2,1)S(1)} collective-permute-done((bf16[128,1024]{1,0:T(8,128)(2,1)S(1)}, bf16[128,1024]{1,0:T(8,128)(2,1)S(1)}, u32[]{:S(2)}, u32[]{:S(2)}) %collective-permute-start.14) | collective-permute-done | bytes 262176 | tf_op jit(solution)/shard_map/ppermute | solution.py:432
  112.8 2.0 %out_projection.4.refs_2_ = f32[256,1024]{1,0:T(8,128)S(1)} custom-call(bf16[4096,1024]{1,0:T(8,128)(2,1)S(1)} %bitcast.2, bf16[128,1024]{1,0:T(8,128)(2,1)S(1)} %shard_map.82.refs_0_, bf16[128,1024]{1,0:T(8,128)(2,1)S(1)} %shard_map.83.refs_1_, bf16[128,1024]{1,0:T(8,128)(2,1)S(1)} %collective-permute-done.21.refs_2_, ...), custom_call_target="tpu_custom_call" | custom-call | flops 1073741824 | bytes 5767168 | tf_op jit(solution)/shard_map/out_projection/pallas_call | solution.py:413
  116.2 3.8 %out_projection.6.refs_3_ = bf16[512,1024]{1,0:T(8,128)(2,1)} custom-call(bf16[4096,1024]{1,0:T(8,128)(2,1)S(1)} %bitcast.2, bf16[128,1024]{1,0:T(8,128)(2,1)S(1)} %shard_map.84.refs_0_, bf16[128,1024]{1,0:T(8,128)(2,1)S(1)} %shard_map.85.refs_1_, bf16[128,1024]{1,0:T(8,128)(2,1)S(1)} %collective-permute-done.29.refs_2_, ...), custom_call_target="tpu_custom_call" | custom-call | flops 2147483648 | bytes 11010048 | tf_op jit(solution)/shard_map/out_projection/pallas_call | solution.py:413
  120.0 2.3 %out_projection.7 = bf16[512,1024]{1,0:T(8,128)(2,1)} custom-call(bf16[4096,1024]{1,0:T(8,128)(2,1)S(1)} %bitcast.2, bf16[128,1024]{1,0:T(8,128)(2,1)S(1)} %collective-permute-done.15.refs_0_, bf16[128,1024]{1,0:T(8,128)(2,1)S(1)} %collective-permute-done.20.refs_1_, f32[256,1024]{1,0:T(8,128)S(1)} %out_projection.5.refs_2_, ...), custom_call_target="tpu_custom_call", output_to_operand_aliasing={{}: (4, {})} | custom-call | flops 536870912 | bytes 3145728 | tf_op jit(solution)/shard_map/out_projection/pallas_call | solution.py:413
  (75 shorter events, 27.9 us)
Async XLA Ops:
  0.0 28.0 %collective-permute-start = (bf16[512,1024]{1,0:T(8,128)(2,1)}, bf16[512,1024]{1,0:T(8,128)(2,1)S(1)}, u32[]{:S(2)}, u32[]{:S(2)}) collective-permute-start(bf16[512,1024]{1,0:T(8,128)(2,1)} %refs_0_.7), channel_id=1, source_target_pairs={{0,4},{4,0},{8,12},{12,8},{1,5},{5,1},{9,13},{13,9},{2,6},{6,2},{1... | collective-permute-start | bytes 3145736 | tf_op jit(solution)/shard_map/ppermute | solution.py:437
  1.6 15.3 %collective-permute-start.1 = (bf16[256,1024]{1,0:T(8,128)(2,1)S(1)}, bf16[256,1024]{1,0:T(8,128)(2,1)S(1)}, u32[]{:S(2)}, u32[]{:S(2)}) collective-permute-start(bf16[256,1024]{1,0:T(8,128)(2,1)S(1)} %slice.6), channel_id=1, source_target_pairs={{0,8},{4,12},{8,0},{12,4},{1,9},{5,13},{9,1},{13,5},{2,10},{6,14},... | collective-permute-start | bytes 1572872 | tf_op jit(solution)/shard_map/ppermute | solution.py:432
  5.2 22.8 %collective-permute-start.3 = (bf16[256,1024]{1,0:T(8,128)(2,1)S(1)}, bf16[256,1024]{1,0:T(8,128)(2,1)S(1)}, u32[]{:S(2)}, u32[]{:S(2)}) collective-permute-start(bf16[256,1024]{1,0:T(8,128)(2,1)S(1)} %slice.7), channel_id=1, source_target_pairs={{0,8},{4,12},{8,0},{12,4},{1,9},{5,13},{9,1},{13,5},{2,10},{6,14},... | collective-permute-start | bytes 1572872 | tf_op jit(solution)/shard_map/ppermute | solution.py:432
  16.9 14.9 %collective-permute-start.2 = (bf16[256,1024]{1,0:T(8,128)(2,1)S(1)}, bf16[256,1024]{1,0:T(8,128)(2,1)S(1)}, u32[]{:S(2)}, u32[]{:S(2)}) collective-permute-start(bf16[256,1024]{1,0:T(8,128)(2,1)S(1)} %collective-permute-done.1.refs_2_.refs_0_), channel_id=1, source_target_pairs={{0,4},{4,0},{8,12},{12,8},{1,5},{5,1},{9,13},{13,9},{2,6},{6,2},{1... | collective-permute-start | bytes 1572872 | tf_op jit(solution)/shard_map/ppermute | solution.py:437
  28.0 13.4 %collective-permute-start.4 = (bf16[256,1024]{1,0:T(8,128)(2,1)S(1)}, bf16[256,1024]{1,0:T(8,128)(2,1)S(1)}, u32[]{:S(2)}, u32[]{:S(2)}) collective-permute-start(bf16[256,1024]{1,0:T(8,128)(2,1)S(1)} %collective-permute-done.3.refs_2_.refs_0_), channel_id=1, source_target_pairs={{0,4},{4,0},{8,12},{12,8},{1,5},{5,1},{9,13},{13,9},{2,6},{6,2},{1... | collective-permute-start | bytes 1572872 | tf_op jit(solution)/shard_map/ppermute | solution.py:437
  33.1 14.1 %collective-permute-start.5 = (bf16[256,256]{1,0:T(8,128)(2,1)S(1)}, bf16[256,256]{1,0:T(8,128)(2,1)S(1)}, u32[]{:S(2)}, u32[]{:S(2)}) collective-permute-start(bf16[256,256]{1,0:T(8,128)(2,1)S(1)} %get-tuple-element.68.refs_1_), channel_id=1, source_target_pairs={{0,1},{1,0},{2,3},{3,2},{4,5},{5,4},{6,7},{7,6},{8,9},{9,8},{10,11... | collective-permute-start | bytes 393224 | tf_op jit(solution)/shard_map/ppermute | solution.py:451
  35.0 12.9 %collective-permute-start.6 = (bf16[256,256]{1,0:T(8,128)(2,1)S(1)}, bf16[256,256]{1,0:T(8,128)(2,1)S(1)}, u32[]{:S(2)}, u32[]{:S(2)}) collective-permute-start(bf16[256,256]{1,0:T(8,128)(2,1)S(1)} %get-tuple-element.69.refs_2_), channel_id=1, source_target_pairs={{0,2},{1,3},{2,0},{3,1},{4,6},{5,7},{6,4},{7,5},{8,10},{9,11},{10,... | collective-permute-start | bytes 393224 | tf_op jit(solution)/shard_map/ppermute | solution.py:451
  37.6 10.4 %collective-permute-start.7 = (bf16[256,256]{1,0:T(8,128)(2,1)S(1)}, bf16[256,256]{1,0:T(8,128)(2,1)S(1)}, u32[]{:S(2)}, u32[]{:S(2)}) collective-permute-start(bf16[256,256]{1,0:T(8,128)(2,1)S(1)} %get-tuple-element.70.refs_3_), channel_id=1, source_target_pairs={{0,3},{1,2},{2,1},{3,0},{4,7},{5,6},{6,5},{7,4},{8,11},{9,10},{10,... | collective-permute-start | bytes 393224 | tf_op jit(solution)/shard_map/ppermute | solution.py:451
  43.7 15.5 %collective-permute-start.9 = (bf16[256,256]{1,0:T(8,128)(2,1)S(1)}, bf16[256,256]{1,0:T(8,128)(2,1)S(1)}, u32[]{:S(2)}, u32[]{:S(2)}) collective-permute-start(bf16[256,256]{1,0:T(8,128)(2,1)S(1)} %get-tuple-element.58.refs_2_), channel_id=1, source_target_pairs={{0,2},{1,3},{2,0},{3,1},{4,6},{5,7},{6,4},{7,5},{8,10},{9,11},{10,... | collective-permute-start | bytes 393224 | tf_op jit(solution)/shard_map/ppermute | solution.py:451
  47.2 12.0 %collective-permute-start.10 = (bf16[256,256]{1,0:T(8,128)(2,1)S(1)}, bf16[256,256]{1,0:T(8,128)(2,1)S(1)}, u32[]{:S(2)}, u32[]{:S(2)}) collective-permute-start(bf16[256,256]{1,0:T(8,128)(2,1)S(1)} %get-tuple-element.59.refs_3_), channel_id=1, source_target_pairs={{0,3},{1,2},{2,1},{3,0},{4,7},{5,6},{6,5},{7,4},{8,11},{9,10},{10,... | collective-permute-start | bytes 393224 | tf_op jit(solution)/shard_map/ppermute | solution.py:451
  69.5 14.4 %collective-permute-start.17 = (bf16[128,256]{1,0:T(8,128)(2,1)S(1)}, bf16[128,256]{1,0:T(8,128)(2,1)S(1)}, u32[]{:S(2)}, u32[]{:S(2)}) collective-permute-start(bf16[128,256]{1,0:T(8,128)(2,1)S(1)} %get-tuple-element.78), channel_id=1, source_target_pairs={{0,2},{1,3},{2,0},{3,1},{4,6},{5,7},{6,4},{7,5},{8,10},{9,11},{10,... | collective-permute-start | bytes 196616 | tf_op jit(solution)/shard_map/ppermute | solution.py:451
  69.6 16.5 %collective-permute-start.18 = (bf16[128,256]{1,0:T(8,128)(2,1)S(1)}, bf16[128,256]{1,0:T(8,128)(2,1)S(1)}, u32[]{:S(2)}, u32[]{:S(2)}) collective-permute-start(bf16[128,256]{1,0:T(8,128)(2,1)S(1)} %get-tuple-element.79), channel_id=1, source_target_pairs={{0,3},{1,2},{2,1},{3,0},{4,7},{5,6},{6,5},{7,4},{8,11},{9,10},{10,... | collective-permute-start | bytes 196616 | tf_op jit(solution)/shard_map/ppermute | solution.py:451
  71.9 14.2 %collective-permute-start.23 = (bf16[128,256]{1,0:T(8,128)(2,1)S(1)}, bf16[128,256]{1,0:T(8,128)(2,1)S(1)}, u32[]{:S(2)}, u32[]{:S(2)}) collective-permute-start(bf16[128,256]{1,0:T(8,128)(2,1)S(1)} %get-tuple-element.82), channel_id=1, source_target_pairs={{0,1},{1,0},{2,3},{3,2},{4,5},{5,4},{6,7},{7,6},{8,9},{9,8},{10,11... | collective-permute-start | bytes 196616 | tf_op jit(solution)/shard_map/ppermute | solution.py:451
  73.0 15.6 %collective-permute-start.24 = (bf16[128,256]{1,0:T(8,128)(2,1)S(1)}, bf16[128,256]{1,0:T(8,128)(2,1)S(1)}, u32[]{:S(2)}, u32[]{:S(2)}) collective-permute-start(bf16[128,256]{1,0:T(8,128)(2,1)S(1)} %get-tuple-element.83), channel_id=1, source_target_pairs={{0,2},{1,3},{2,0},{3,1},{4,6},{5,7},{6,4},{7,5},{8,10},{9,11},{10,... | collective-permute-start | bytes 196616 | tf_op jit(solution)/shard_map/ppermute | solution.py:451
  74.9 15.2 %collective-permute-start.25 = (bf16[128,256]{1,0:T(8,128)(2,1)S(1)}, bf16[128,256]{1,0:T(8,128)(2,1)S(1)}, u32[]{:S(2)}, u32[]{:S(2)}) collective-permute-start(bf16[128,256]{1,0:T(8,128)(2,1)S(1)} %get-tuple-element.84), channel_id=1, source_target_pairs={{0,3},{1,2},{2,1},{3,0},{4,7},{5,6},{6,5},{7,4},{8,11},{9,10},{10,... | collective-permute-start | bytes 196616 | tf_op jit(solution)/shard_map/ppermute | solution.py:451
  83.9 8.9 %collective-permute-start.11 = (bf16[128,256]{1,0:T(8,128)(2,1)S(1)}, bf16[128,256]{1,0:T(8,128)(2,1)S(1)}, u32[]{:S(2)}, u32[]{:S(2)}) collective-permute-start(bf16[128,256]{1,0:T(8,128)(2,1)S(1)} %get-tuple-element.73), channel_id=1, source_target_pairs={{0,1},{1,0},{2,3},{3,2},{4,5},{5,4},{6,7},{7,6},{8,9},{9,8},{10,11... | collective-permute-start | bytes 196616 | tf_op jit(solution)/shard_map/ppermute | solution.py:451
  92.8 9.2 %collective-permute-start.31 = (bf16[128,1024]{1,0:T(8,128)(2,1)S(1)}, bf16[128,1024]{1,0:T(8,128)(2,1)S(1)}, u32[]{:S(2)}, u32[]{:S(2)}) collective-permute-start(bf16[128,1024]{1,0:T(8,128)(2,1)S(1)} %shard_map.84.refs_0_), channel_id=1, source_target_pairs={{0,8},{4,12},{8,0},{12,4},{1,9},{5,13},{9,1},{13,5},{2,10},{6,14},... | collective-permute-start | bytes 786440 | tf_op jit(solution)/shard_map/ppermute | solution.py:432
  93.4 8.6 %collective-permute-start.22 = (bf16[128,1024]{1,0:T(8,128)(2,1)S(1)}, bf16[128,1024]{1,0:T(8,128)(2,1)S(1)}, u32[]{:S(2)}, u32[]{:S(2)}) collective-permute-start(bf16[128,1024]{1,0:T(8,128)(2,1)S(1)} %shard_map.83.refs_1_), channel_id=1, source_target_pairs={{0,4},{4,0},{8,12},{12,8},{1,5},{5,1},{9,13},{13,9},{2,6},{6,2},{1... | collective-permute-start | bytes 786440 | tf_op jit(solution)/shard_map/ppermute | solution.py:437
  93.6 14.1 %collective-permute-start.19 = (bf16[128,1024]{1,0:T(8,128)(2,1)S(1)}, bf16[128,1024]{1,0:T(8,128)(2,1)S(1)}, u32[]{:S(2)}, u32[]{:S(2)}) collective-permute-start(bf16[128,1024]{1,0:T(8,128)(2,1)S(1)} %shard_map.83.refs_1_), channel_id=1, source_target_pairs={{0,8},{4,12},{8,0},{12,4},{1,9},{5,13},{9,1},{13,5},{2,10},{6,14},... | collective-permute-start | bytes 786440 | tf_op jit(solution)/shard_map/ppermute | solution.py:432
  95.2 12.4 %collective-permute-start.21 = (bf16[128,1024]{1,0:T(8,128)(2,1)S(1)}, bf16[128,1024]{1,0:T(8,128)(2,1)S(1)}, u32[]{:S(2)}, u32[]{:S(2)}) collective-permute-start(bf16[128,1024]{1,0:T(8,128)(2,1)S(1)} %shard_map.82.refs_0_), channel_id=1, source_target_pairs={{0,4},{4,0},{8,12},{12,8},{1,5},{5,1},{9,13},{13,9},{2,6},{6,2},{1... | collective-permute-start | bytes 786440 | tf_op jit(solution)/shard_map/ppermute | solution.py:437
  95.3 17.5 %collective-permute-start.14 = (bf16[128,1024]{1,0:T(8,128)(2,1)S(1)}, bf16[128,1024]{1,0:T(8,128)(2,1)S(1)}, u32[]{:S(2)}, u32[]{:S(2)}) collective-permute-start(bf16[128,1024]{1,0:T(8,128)(2,1)S(1)} %shard_map.82.refs_0_), channel_id=1, source_target_pairs={{0,8},{4,12},{8,0},{12,4},{1,9},{5,13},{9,1},{13,5},{2,10},{6,14},... | collective-permute-start | bytes 786440 | tf_op jit(solution)/shard_map/ppermute | solution.py:432
  102.0 14.2 %collective-permute-start.29 = (bf16[128,1024]{1,0:T(8,128)(2,1)S(1)}, bf16[128,1024]{1,0:T(8,128)(2,1)S(1)}, u32[]{:S(2)}, u32[]{:S(2)}) collective-permute-start(bf16[128,1024]{1,0:T(8,128)(2,1)S(1)} %shard_map.84.refs_0_), channel_id=1, source_target_pairs={{0,4},{4,0},{8,12},{12,8},{1,5},{5,1},{9,13},{13,9},{2,6},{6,2},{1... | collective-permute-start | bytes 786440 | tf_op jit(solution)/shard_map/ppermute | solution.py:437
  102.0 14.2 %collective-permute-start.34 = (bf16[128,1024]{1,0:T(8,128)(2,1)S(1)}, bf16[128,1024]{1,0:T(8,128)(2,1)S(1)}, u32[]{:S(2)}, u32[]{:S(2)}) collective-permute-start(bf16[128,1024]{1,0:T(8,128)(2,1)S(1)} %collective-permute-done.32.refs_5_), channel_id=1, source_target_pairs={{0,4},{4,0},{8,12},{12,8},{1,5},{5,1},{9,13},{13,9},{2,6},{6,2},{1... | collective-permute-start | bytes 786440 | tf_op jit(solution)/shard_map/ppermute | solution.py:437
  107.6 12.3 %collective-permute-start.20 = (bf16[128,1024]{1,0:T(8,128)(2,1)S(1)}, bf16[128,1024]{1,0:T(8,128)(2,1)S(1)}, u32[]{:S(2)}, u32[]{:S(2)}) collective-permute-start(bf16[128,1024]{1,0:T(8,128)(2,1)S(1)} %collective-permute-done.19.refs_1_), channel_id=1, source_target_pairs={{0,4},{4,0},{8,12},{12,8},{1,5},{5,1},{9,13},{13,9},{2,6},{6,2},{1... | collective-permute-start | bytes 786440 | tf_op jit(solution)/shard_map/ppermute | solution.py:437
  (14 other events, 135.4 us)

commit v7 on v6

--- a/solution.py
+++ b/solution.py
@@ -77,6 +77,32 @@
 
 def rows_at(first, count):
     return pl.ds(pl.multiple_of(first * count, count), count)
+
+
+def halves_kernel(x_ref, *refs):
+    outs, sems = refs[:-1], refs[-1]
+    rows = outs[0].shape[0]
+    copies = [
+        pltpu.make_async_copy(x_ref.at[c * rows : (c + 1) * rows], out, sems.at[c]) for c, out in enumerate(outs)
+    ]
+    for copy in copies:
+        copy.start()
+    for copy in copies:
+        copy.wait()
+
+
+def halves(x):
+    out = [jax.ShapeDtypeStruct((x.shape[0] // CHUNKS, x.shape[1]), x.dtype)] * CHUNKS
+    return pl.pallas_call(
+        halves_kernel,
+        out_shape=out,
+        in_specs=[HBM],
+        out_specs=[VMEM] * CHUNKS,
+        scratch_shapes=[pltpu.SemaphoreType.DMA((CHUNKS,))],
+        compiler_params=pltpu.CompilerParams(vmem_limit_bytes=2 * MIB),
+        cost_estimate=pl.CostEstimate(flops=0, bytes_accessed=4 * x.size, transcendentals=0),
+        name="halves",
+    )(pltpu.with_memory_space_constraint(x, pltpu.HBM))
 
 
 def prologue_kernel(
@@ -141,7 +167,7 @@
     )(*(pltpu.with_memory_space_constraint(x, pltpu.HBM) for x in (skip, *tables, taps, w)))
 
 
-def kv_kernel(which, starts, n_ctx, has_before, last, w_ref, *refs):
+def kv_kernel(which, starts, n_ctx, has_before, slices, w_ref, *refs):
     pieces, refs = refs[: len(which)], refs[len(which) :]
     before, outs = (refs[:2], refs[2:]) if has_before else ((), refs)
     tokens = outs[0].shape[0]
@@ -149,7 +175,7 @@
     depth = pieces[0].shape[1]
     me = lax.axis_index("ctx")
     sources = chan_sources()
-    for k in range(n_ctx):
+    for k in slices or range(n_ctx):
         cols = rows_at(target(me, k, n_ctx), width)
         mine = slice(k * width, (k + 1) * width)
         key, value = (ref[:, mine] for ref in before) if has_before else (None, None)
@@ -160,26 +186,26 @@
             b = jnp.dot(x, w_ref[1, rows, cols], preferred_element_type=F32)
             key = a if key is None else key + a
             value = b if value is None else value + b
-        if last:
-            outs[k][...] = (key * value).astype(BF16)
+        if slices:
+            outs[slices.index(k)][...] = (key * value).astype(BF16)
         else:
             outs[0][:, mine] = key
             outs[1][:, mine] = value
 
 
-def keys_values(pieces, which, starts, tokens, w, before, n_ctx, last):
+def keys_values(pieces, which, starts, tokens, w, before, n_ctx, slices=()):
     channels = w.shape[2]
     share = len(which) * pieces[0].shape[1]
-    if last:
-        out = [jax.ShapeDtypeStruct((tokens, channels // n_ctx), BF16)] * n_ctx
+    if slices:
+        out = [jax.ShapeDtypeStruct((tokens, channels // n_ctx), BF16)] * len(slices)
     else:
         out = [jax.ShapeDtypeStruct((tokens, channels), F32)] * 2
     return call(
-        functools.partial(kv_kernel, tuple(which), tuple(starts), n_ctx, bool(before), last),
+        functools.partial(kv_kernel, tuple(which), tuple(starts), n_ctx, bool(before), slices),
         out,
         [w, *(pieces[j] for j in which), *before],
         6,
-        4 * tokens * share * channels,
+        4 * tokens * share * channels * (len(slices) or n_ctx) // n_ctx,
         4 * share * channels + 2 * tokens * share,
     )
 
@@ -376,22 +402,33 @@
     )
 
 
-def out_kernel(which, parts, has_before, n_ctx, w_ref, *refs):
-    pieces, out_ref = refs[: len(which) * parts], refs[-1]
-    columns = out_ref.shape[1]
+def out_kernel(which, parts, has_before, n_ctx, columns, row, w_ref, *refs):
+    pieces, out_ref = refs[: len(which) * parts], refs[-1 if row is None else -3]
     width = pieces[0].shape[1] // n_ctx
-    cols = rows_at(pl.program_id(0), columns)
     me = lax.axis_index("ctx")
     sources = chan_sources()
-    acc = refs[len(pieces)][:, cols] if has_before else None
-    for i, j in enumerate(which):
-        for m in range(n_ctx):
-            w = w_ref[rows_at(sources[j] * n_ctx + target(me, m, n_ctx), width), cols]
-            mine = slice(m * width, (m + 1) * width)
-            x = jnp.concatenate([p[:, mine] for p in pieces[i * parts : (i + 1) * parts]], axis=0)
-            a = jnp.dot(x, w, preferred_element_type=F32)
-            acc = a if acc is None else acc + a
-    out_ref[...] = acc.astype(out_ref.dtype)
+    copies = []
+    for i in range(w_ref.shape[1] // columns):
+        cols = slice(i * columns, (i + 1) * columns)
+        acc = refs[len(pieces)][:, cols] if has_before else None
+        for i_piece, j in enumerate(which):
+            for m in range(n_ctx):
+                w = w_ref[rows_at(sources[j] * n_ctx + target(me, m, n_ctx), width), cols]
+                mine = slice(m * width, (m + 1) * width)
+                group = pieces[i_piece * parts : (i_piece + 1) * parts]
+                x = jnp.concatenate([p[:, mine] for p in group], axis=0)
+                a = jnp.dot(x, w, preferred_element_type=F32)
+                acc = a if acc is None else acc + a
+        if row is None:
+            out_ref[:, cols] = acc
+            continue
+        made_ref, sems = refs[-2:]
+        made_ref[:, cols] = acc.astype(BF16)
+        there = out_ref.at[row : row + made_ref.shape[0], cols]
+        copies.append(pltpu.make_async_copy(made_ref.at[:, cols], there, sems.at[i]))
+        copies[-1].start()
+    for copy in copies:
+        copy.wait()
 
 
 def project_out(gathered, which, w, before, n_ctx, final=None, columns=256):
@@ -400,22 +437,23 @@
     _, out_width = w.shape
     operands = [w, *(pieces[j] for j in which for pieces in gathered)] + ([] if before is None else [before])
     specs = [VMEM] * len(operands)
-    aliases = {}
-    out_spec, shape = pl.BlockSpec((tokens, columns), lambda i: (0, i)), (tokens, out_width)
+    aliases, scratch, row = {}, [], None
+    out_spec, shape = VMEM, (tokens, out_width)
     if final is not None:
-        chunk, rows, so_far = final
-        out_spec, shape = pl.BlockSpec((tokens, columns), lambda i: (chunk, i)), (rows, out_width)
+        row, rows, so_far = final
+        out_spec, shape = HBM, (rows, out_width)
+        scratch = [pltpu.VMEM((tokens, out_width), BF16), pltpu.SemaphoreType.DMA((out_width // columns,))]
         if so_far is not None:
-            specs.append(pl.BlockSpec(memory_space=pl.ANY))
+            specs.append(HBM)
             aliases = {len(operands): 0}
             operands.append(so_far)
     share = len(which) * gathered[0][0].shape[1]
     return pl.pallas_call(
-        functools.partial(out_kernel, tuple(which), parts, before is not None, n_ctx),
+        functools.partial(out_kernel, tuple(which), parts, before is not None, n_ctx, columns, row),
         out_shape=jax.ShapeDtypeStruct(shape, F32 if final is None else BF16),
-        grid=(out_width // columns,),
         in_specs=specs,
         out_specs=out_spec,
+        scratch_shapes=scratch,
         input_output_aliases=aliases,
         compiler_params=pltpu.CompilerParams(vmem_limit_bytes=6 * MIB),
         cost_estimate=pl.CostEstimate(
@@ -463,21 +501,23 @@
     tables = [jnp.asarray(t) for t in real_dft_tables(tokens)]
     w = in_weight.transpose(1, 0, 2)
 
-    far = [gather_far(features[:tokens])]
+    own = halves(features)
+    far = [gather_far(own[c]) for c in range(CHUNKS)]
     near = swap_cores(features)
-    later, skip = lax.optimization_barrier((features, skip_gain))
-    far.append(gather_far(later[tokens:]))
-    forward, inverse, w_kv, spectra, skip = prologue(tables, skip, filter_taps, w, n_ctx)
+    forward, inverse, w_kv, spectra, skip = prologue(tables, skip_gain, filter_taps, w, n_ctx)
 
     mixed, arrived, query, w_q = [], [], [], None
     for c in range(CHUNKS):
-        pieces = [features, near, *far[c]]
-        starts = [c * tokens] * 2 + [0] * len(far[c])
+        pieces = [own[c], near, *far[c]]
+        starts = [0, c * tokens] + [0] * len(far[c])
         total = ()
-        for part, which in ("a", (0, 1)), ("b", range(2, len(pieces) - 1)), ("c", (len(pieces) - 1,)):
-            chosen = [starts[j] for j in which]
-            total = keys_values(pieces, which, chosen, tokens, w_kv, total, n_ctx, part == "c")
-        mixed.append(total)
+        for part, which in ("a", (0, 1)), ("b", range(2, len(pieces) - 1)):
+            total = keys_values(pieces, which, [starts[j] for j in which], tokens, w_kv, total, n_ctx)
+        last, made = len(pieces) - 1, {}
+        for part, slices in ("c", tuple(range(2, n_ctx))), ("d", (1, 0)):
+            some = keys_values(pieces, (last,), (starts[last],), tokens, w_kv, total, n_ctx, slices)
+            made.update(zip(slices, some))
+        mixed.append([made[k] for k in range(n_ctx)])
         arrived.append(exchange(mixed[c]))
         made, *kept = queries(pieces, starts, tokens, w if c == 0 else w_q, n_ctx, c == 0)
         query.append(made)
@@ -495,7 +535,7 @@
     out = project_out(gathered[:2], every, out_weight, None, n_ctx, (0, rows, None))
     part = project_out(gathered[2:], every[:2], out_weight, None, n_ctx)
     part = project_out(gathered[2:], every[2:-1], out_weight, part, n_ctx)
-    return project_out(gathered[2:], every[-1:], out_weight, part, n_ctx, (1, rows, out))
+    return project_out(gathered[2:], every[-1:], out_weight, part, n_ctx, (tokens, rows, out))
 
 
 P_SIZE = 128

time: 123 us -> 121 us (0.984)
  starting transfers between devices: 39 us -> 41.2 us
  local copies, waits for them, and re-layouts: 2.16 us -> 0.01 us
  Pallas kernels: 38.6 us -> 37.2 us
    pallas_call x4, Pallas kernels: 9.47 us -> 6.55 us  [project_out(): pl.pallas_call(functools.partial(out_kernel, tuple(which), parts, before...]
    ppermute x18, starting transfers between devices: 29.8 us -> 32 us  [exchange(): lax.ppermute(parts[k], 'ctx', [(i, target(i, k, n)) for i in range(n)])]
    slice x2 -> x0, local copies, waits for them, and re-layouts: 2.15 us -> none  [the longest x1 1.08 us: layer_body(): far = [gather_far(features[:tokens])]]
    ppermute x18, waiting for transfers between devices: 10.7 us -> 8.87 us  [exchange(): lax.ppermute(parts[k], 'ctx', [(i, target(i, k, n)) for i in range(n)])]
    pallas_call x13 -> x15, Pallas kernels: 16.1 us -> 16.4 us  [call(): pl.pallas_call(kernel, out_shape=out, in_specs=[VMEM] * len(operands), ou...]
  transfers between devices with their start and end apart: 35 -> 35, of which waited for: 9 -> 8; matrix products, arithmetic and copies ran while one was open for 2% -> 0% of each run, Pallas kernels for 27% -> 27%
where the time goes in v7:
time: 121 us; the launch traced here: 120 us
  waiting for transfers between devices  41.6 us (34%)
  starting transfers between devices  41.2 us (34%)
  Pallas kernels  37.2 us (31%)
    ppermute x6, waiting for transfers between devices, shift(): return lax.ppermute(x, axis, [(i, (i + by) % n) for i in range(n)])  32.7 us
    ppermute x18, starting transfers between devices, exchange(): lax.ppermute(parts[k], 'ctx', [(i, target(i, k, n)) for i in range(n)])  32 us
    pallas_call x15, Pallas kernels, call(): pl.pallas_call(kernel, out_shape=out, in_specs=[VMEM] * len(operands), ou...  16.4 us
    ppermute x18, waiting for transfers between devices, exchange(): lax.ppermute(parts[k], 'ctx', [(i, target(i, k, n)) for i in range(n)])  8.87 us
    ppermute x6, starting transfers between devices, shift(): return lax.ppermute(x, axis, [(i, (i + by) % n) for i in range(n)])  7.39 us
    pallas_call x2, Pallas kernels, queries(): pl.pallas_call(functools.partial(query_kernel, tuple(starts), n_ctx, load...  6.7 us
    pallas_call x4, Pallas kernels, project_out(): pl.pallas_call(functools.partial(out_kernel, tuple(which), parts, before...  6.55 us
    pallas_call x1, Pallas kernels, prologue(): pl.pallas_call(functools.partial(prologue_kernel, width), out_shape=out,...  6.34 us
  transfers between devices with their start and end apart: 35, of which 8 were waited for; matrix products, arithmetic and copies ran while one was open for 0% of the time, Pallas kernels for 27%

profile of v7, /device:TPU:0, one launch (start us, length us, event | category | flops | bytes accessed | tf_op | source)
XLA Modules:
  0.0 120.5 jit_solution(7142540075904755367)
XLA Ops:
  1.7 2.6 %collective-permute-start.1 = (bf16[256,1024]{1,0:T(8,128)(2,1)S(1)}, bf16[256,1024]{1,0:T(8,128)(2,1)S(1)}, u32[]{:S(2)}, u32[]{:S(2)}) collective-permute-start(bf16[256,1024]{1,0:T(8,128)(2,1)S(1)} %get-tuple-element.48.refs_0_), channel_id=1, source_target_pairs={{0,8},{4,12},{8,0},{12,4},{1,9},{5,13},{9,1},{13,5},{2,10},{6,14},... | collective-permute-start | bytes 1572872 | tf_op jit(solution)/shard_map/ppermute | solution.py:470
  4.4 12.7 %collective-permute-done.1.refs_2_.refs_0_ = bf16[256,1024]{1,0:T(8,128)(2,1)S(1)} collective-permute-done((bf16[256,1024]{1,0:T(8,128)(2,1)S(1)}, bf16[256,1024]{1,0:T(8,128)(2,1)S(1)}, u32[]{:S(2)}, u32[]{:S(2)}) %collective-permute-start.1) | collective-permute-done | bytes 524320 | tf_op jit(solution)/shard_map/ppermute | solution.py:470
  17.1 6.3 %prologue.1 = (bf16[512,256]{1,0:T(8,128)(2,1)S(1)}, bf16[256,512]{1,0:T(8,128)(2,1)S(1)}, bf16[2,4096,1024]{2,1,0:T(8,128)(2,1)S(1)}, f32[8,512,256]{2,1,0:T(8,128)S(1)}, f32[4,256]{1,0:T(4,128)S(1)}) custom-call(f32[1024]{0:T(1024)} %skip_hbm.1, bf16[512,256]{1,0:T(8,128)(2,1)} %constant.4.clone.fwd_hbm, bf16[256,512]{1,0:T(8,128)(2,1)} %constant.5.clone.inv_hbm, ...), custom_call_target="tpu_custom_call" | custom-call | flops 536870912 | bytes 30408704 | tf_op jit(solution)/shard_map/prologue/pallas_call | solution.py:149
  23.4 4.7 %collective-permute-done.3.refs_2_.refs_0_ = bf16[256,1024]{1,0:T(8,128)(2,1)S(1)} collective-permute-done((bf16[256,1024]{1,0:T(8,128)(2,1)S(1)}, bf16[256,1024]{1,0:T(8,128)(2,1)S(1)}, u32[]{:S(2)}, u32[]{:S(2)}) %collective-permute-start.3) | collective-permute-done | bytes 524320 | tf_op jit(solution)/shard_map/ppermute | solution.py:470
  28.1 2.4 %shard_map.77 = (f32[256,1024]{1,0:T(8,128)S(1)}, f32[256,1024]{1,0:T(8,128)S(1)}) custom-call(bf16[2,4096,1024]{2,1,0:T(8,128)(2,1)S(1)} %get-tuple-element.51.w_ref, bf16[256,1024]{1,0:T(8,128)(2,1)S(1)} %get-tuple-element.48.refs_0_, bf16[512,1024]{1,0:T(8,128)(2,1)S(1)} %collective-permute-done.refs_1_), custom_call_target="tpu_custom_call" | custom-call | flops 2147483648 | bytes 9437184 | tf_op jit(solution)/shard_map/pallas_call | solution.py:42
  32.7 2.9 %collective-permute-start.6 = (bf16[256,256]{1,0:T(8,128)(2,1)S(1)}, bf16[256,256]{1,0:T(8,128)(2,1)S(1)}, u32[]{:S(2)}, u32[]{:S(2)}) collective-permute-start(bf16[256,256]{1,0:T(8,128)(2,1)S(1)} %get-tuple-element.69.refs_2_), channel_id=1, source_target_pairs={{0,2},{1,3},{2,0},{3,1},{4,6},{5,7},{6,4},{7,5},{8,10},{9,11},{10,... | collective-permute-start | bytes 393224 | tf_op jit(solution)/shard_map/ppermute | solution.py:489
  38.0 2.4 %shard_map.73 = (f32[256,1024]{1,0:T(8,128)S(1)}, f32[256,1024]{1,0:T(8,128)S(1)}) custom-call(bf16[2,4096,1024]{2,1,0:T(8,128)(2,1)S(1)} %get-tuple-element.51.w_ref, bf16[256,1024]{1,0:T(8,128)(2,1)S(1)} %get-tuple-element.50.refs_0_, bf16[512,1024]{1,0:T(8,128)(2,1)S(1)} %collective-permute-done.refs_1_), custom_call_target="tpu_custom_call" | custom-call | flops 2147483648 | bytes 9437184 | tf_op jit(solution)/shard_map/pallas_call | solution.py:42
  42.6 2.8 %collective-permute-start.9 = (bf16[256,256]{1,0:T(8,128)(2,1)S(1)}, bf16[256,256]{1,0:T(8,128)(2,1)S(1)}, u32[]{:S(2)}, u32[]{:S(2)}) collective-permute-start(bf16[256,256]{1,0:T(8,128)(2,1)S(1)} %get-tuple-element.58.refs_2_), channel_id=1, source_target_pairs={{0,2},{1,3},{2,0},{3,1},{4,6},{5,7},{6,4},{7,5},{8,10},{9,11},{10,... | collective-permute-start | bytes 393224 | tf_op jit(solution)/shard_map/ppermute | solution.py:489
  47.6 2.1 %shard_map.81.sum_ref = f32[8,512,256]{2,1,0:T(8,128)S(1)} custom-call(bf16[512,256]{1,0:T(8,128)(2,1)S(1)} %get-tuple-element.62.fwd_ref, f32[8,512,256]{2,1,0:T(8,128)S(1)} %get-tuple-element.61.g_ref, bf16[256,256]{1,0:T(8,128)(2,1)S(1)} %get-tuple-element.67.refs_0_, bf16[256,256]{1,0:T(8,128)(2,1)S(1)} %collective-permute-done.5.refs_1_, ...), custom_call_target="tpu_custom_call" | custom-call | flops 268435456 | bytes 8388608 | tf_op jit(solution)/shard_map/pallas_call | solution.py:42
  49.7 7.2 %collective-permute-done.9.refs_2_ = bf16[256,256]{1,0:T(8,128)(2,1)S(1)} collective-permute-done((bf16[256,256]{1,0:T(8,128)(2,1)S(1)}, bf16[256,256]{1,0:T(8,128)(2,1)S(1)}, u32[]{:S(2)}, u32[]{:S(2)}) %collective-permute-start.9) | collective-permute-done | bytes 131104 | tf_op jit(solution)/shard_map/ppermute | solution.py:489
  57.7 1.6 %shard_map.82 = (f32[4,512,256]{2,1,0:T(8,128)S(1)}, bf16[128,256]{1,0:T(8,128)(2,1)S(1)}, bf16[128,256]{1,0:T(8,128)(2,1)S(1)}, bf16[128,256]{1,0:T(8,128)(2,1)...) custom-call(bf16[512,256]{1,0:T(8,128)(2,1)S(1)} %get-tuple-element., ...), custom_call_target="tpu_custom_call" | custom-call | flops 268435456 | bytes 8388608 | tf_op jit(solution)/shard_map/pallas_call | solution.py:42
  59.3 1.6 %shard_map.83 = (bf16[128,256]{1,0:T(8,128)(2,1)S(1)}, bf16[128,256]{1,0:T(8,128)(2,1)S(1)}, bf16[128,256]{1,0:T(8,128)(2,1)S(1)}, bf16[128,256]{1,0:T(8,128)(2,...) custom-call(bf16[256,512]{1,0:T(8,128)(2,1)S(1)} %get-tuple-element., ...), custom_call_target="tpu_custom_call" | custom-call | flops 268435456 | bytes 8388608 | tf_op jit(solution)/shard_map/pallas_call | solution.py:42
  60.9 2.6 %collective-permute-start.16 = (bf16[128,256]{1,0:T(8,128)(2,1)S(1)}, bf16[128,256]{1,0:T(8,128)(2,1)S(1)}, u32[]{:S(2)}, u32[]{:S(2)}) collective-permute-start(bf16[128,256]{1,0:T(8,128)(2,1)S(1)} %get-tuple-element.77), channel_id=1, source_target_pairs={{0,1},{1,0},{2,3},{3,2},{4,5},{5,4},{6,7},{7,6},{8,9},{9,8},{10,11... | collective-permute-start | bytes 196616 | tf_op jit(solution)/shard_map/ppermute | solution.py:489
  63.6 3.8 %collective-permute-start.27 = (bf16[128,256]{1,0:T(8,128)(2,1)S(1)}, bf16[128,256]{1,0:T(8,128)(2,1)S(1)}, u32[]{:S(2)}, u32[]{:S(2)}) collective-permute-start(bf16[128,256]{1,0:T(8,128)(2,1)S(1)} %get-tuple-element.87), channel_id=1, source_target_pairs={{0,2},{1,3},{2,0},{3,1},{4,6},{5,7},{6,4},{7,5},{8,10},{9,11},{10,... | collective-permute-start | bytes 196616 | tf_op jit(solution)/shard_map/ppermute | solution.py:489
  68.9 2.3 %collective-permute-start.18 = (bf16[128,256]{1,0:T(8,128)(2,1)S(1)}, bf16[128,256]{1,0:T(8,128)(2,1)S(1)}, u32[]{:S(2)}, u32[]{:S(2)}) collective-permute-start(bf16[128,256]{1,0:T(8,128)(2,1)S(1)} %get-tuple-element.79), channel_id=1, source_target_pairs={{0,3},{1,2},{2,1},{3,0},{4,7},{5,6},{6,5},{7,4},{8,11},{9,10},{10,... | collective-permute-start | bytes 196616 | tf_op jit(solution)/shard_map/ppermute | solution.py:489
  74.2 6.3 %collective-permute-start.25 = (bf16[128,256]{1,0:T(8,128)(2,1)S(1)}, bf16[128,256]{1,0:T(8,128)(2,1)S(1)}, u32[]{:S(2)}, u32[]{:S(2)}) collective-permute-start(bf16[128,256]{1,0:T(8,128)(2,1)S(1)} %get-tuple-element.84), channel_id=1, source_target_pairs={{0,3},{1,2},{2,1},{3,0},{4,7},{5,6},{6,5},{7,4},{8,11},{9,10},{10,... | collective-permute-start | bytes 196616 | tf_op jit(solution)/shard_map/ppermute | solution.py:489
  80.5 4.3 %q_projection.2 = (bf16[256,1024]{1,0:T(8,128)(2,1)S(1)}, bf16[4096,1024]{1,0:T(8,128)(2,1)S(1)}) custom-call(bf16[3,4096,1024]{2,1,0:T(8,128)(2,1)} %bitcast.4, bf16[256,1024]{1,0:T(8,128)(2,1)S(1)} %get-tuple-element.48.refs_0_, bf16[512,1024]{1,0:T(8,128)(2,1)S(1)} %collective-permute-done.refs_1_, ...), custom_call_target="tpu_custom_call" | custom-call | flops 2147483648 | bytes 10485760 | tf_op jit(solution)/shard_map/q_projection/pallas_call | solution.py:254
  87.2 2.3 %collective-permute-start.13 = (bf16[128,256]{1,0:T(8,128)(2,1)S(1)}, bf16[128,256]{1,0:T(8,128)(2,1)S(1)}, u32[]{:S(2)}, u32[]{:S(2)}) collective-permute-start(bf16[128,256]{1,0:T(8,128)(2,1)S(1)} %get-tuple-element.75), channel_id=1, source_target_pairs={{0,3},{1,2},{2,1},{3,0},{4,7},{5,6},{6,5},{7,4},{8,11},{9,10},{10,... | collective-permute-start | bytes 196616 | tf_op jit(solution)/shard_map/ppermute | solution.py:489
  91.0 2.4 %q_projection.3.q_ref = bf16[256,1024]{1,0:T(8,128)(2,1)S(1)} custom-call(bf16[4096,1024]{1,0:T(8,128)(2,1)S(1)} %get-tuple-element.49.w_ref, bf16[256,1024]{1,0:T(8,128)(2,1)S(1)} %get-tuple-element.50.refs_0_, bf16[512,1024]{1,0:T(8,128)(2,1)S(1)} %collective-permute-done.refs_1_, bf16[256,1024]{1,0:T(8,128)(2,1)S(1)} %collective-permute-done.3.refs_2_.refs_0_, ...), custom_call_target="tpu_custom_call" | custom-call | flops 2147483648 | bytes 10485760 | tf_op jit(solution)/shard_map/q_projection/pallas_call | solution.py:254
  94.5 1.5 %collective-permute-start.19 = (bf16[128,1024]{1,0:T(8,128)(2,1)S(1)}, bf16[128,1024]{1,0:T(8,128)(2,1)S(1)}, u32[]{:S(2)}, u32[]{:S(2)}) collective-permute-start(bf16[128,1024]{1,0:T(8,128)(2,1)S(1)} %shard_map.85.refs_1_), channel_id=1, source_target_pairs={{0,8},{4,12},{8,0},{12,4},{1,9},{5,13},{9,1},{13,5},{2,10},{6,14},... | collective-permute-start | bytes 786440 | tf_op jit(solution)/shard_map/ppermute | solution.py:470
  97.3 5.6 %collective-permute-done.31.refs_4_ = bf16[128,1024]{1,0:T(8,128)(2,1)S(1)} collective-permute-done((bf16[128,1024]{1,0:T(8,128)(2,1)S(1)}, bf16[128,1024]{1,0:T(8,128)(2,1)S(1)}, u32[]{:S(2)}, u32[]{:S(2)}) %collective-permute-start.31) | collective-permute-done | bytes 262176 | tf_op jit(solution)/shard_map/ppermute | solution.py:470
  103.4 5.1 %collective-permute-done.19.refs_1_ = bf16[128,1024]{1,0:T(8,128)(2,1)S(1)} collective-permute-done((bf16[128,1024]{1,0:T(8,128)(2,1)S(1)}, bf16[128,1024]{1,0:T(8,128)(2,1)S(1)}, u32[]{:S(2)}, u32[]{:S(2)}) %collective-permute-start.19) | collective-permute-done | bytes 262176 | tf_op jit(solution)/shard_map/ppermute | solution.py:470
  109.1 4.6 %collective-permute-done.14.refs_0_ = bf16[128,1024]{1,0:T(8,128)(2,1)S(1)} collective-permute-done((bf16[128,1024]{1,0:T(8,128)(2,1)S(1)}, bf16[128,1024]{1,0:T(8,128)(2,1)S(1)}, u32[]{:S(2)}, u32[]{:S(2)}) %collective-permute-start.14) | collective-permute-done | bytes 262176 | tf_op jit(solution)/shard_map/ppermute | solution.py:470
  115.7 3.1 %out_projection.6.refs_3_ = bf16[512,1024]{1,0:T(8,128)(2,1)} custom-call(bf16[4096,1024]{1,0:T(8,128)(2,1)S(1)} %bitcast.2, bf16[128,1024]{1,0:T(8,128)(2,1)S(1)} %shard_map.86.refs_0_, bf16[128,1024]{1,0:T(8,128)(2,1)S(1)} %shard_map.87.refs_1_, bf16[128,1024]{1,0:T(8,128)(2,1)S(1)} %collective-permute-done.29.refs_2_, ...), custom_call_target="tpu_custom_call" | custom-call | flops 2147483648 | bytes 11010048 | tf_op jit(solution)/shard_map/out_projection/pallas_call | solution.py:451
  (74 shorter events, 26.8 us)
Async XLA Ops:
  0.0 28.1 %collective-permute-start = (bf16[512,1024]{1,0:T(8,128)(2,1)}, bf16[512,1024]{1,0:T(8,128)(2,1)S(1)}, u32[]{:S(2)}, u32[]{:S(2)}) collective-permute-start(bf16[512,1024]{1,0:T(8,128)(2,1)} %x_ref.1), channel_id=1, source_target_pairs={{0,4},{4,0},{8,12},{12,8},{1,5},{5,1},{9,13},{13,9},{2,6},{6,2},{1... | collective-permute-start | bytes 3145736 | tf_op jit(solution)/shard_map/ppermute | solution.py:475
  1.7 15.3 %collective-permute-start.1 = (bf16[256,1024]{1,0:T(8,128)(2,1)S(1)}, bf16[256,1024]{1,0:T(8,128)(2,1)S(1)}, u32[]{:S(2)}, u32[]{:S(2)}) collective-permute-start(bf16[256,1024]{1,0:T(8,128)(2,1)S(1)} %get-tuple-element.48.refs_0_), channel_id=1, source_target_pairs={{0,8},{4,12},{8,0},{12,4},{1,9},{5,13},{9,1},{13,5},{2,10},{6,14},... | collective-permute-start | bytes 1572872 | tf_op jit(solution)/shard_map/ppermute | solution.py:470
  4.3 23.8 %collective-permute-start.3 = (bf16[256,1024]{1,0:T(8,128)(2,1)S(1)}, bf16[256,1024]{1,0:T(8,128)(2,1)S(1)}, u32[]{:S(2)}, u32[]{:S(2)}) collective-permute-start(bf16[256,1024]{1,0:T(8,128)(2,1)S(1)} %get-tuple-element.50.refs_0_), channel_id=1, source_target_pairs={{0,8},{4,12},{8,0},{12,4},{1,9},{5,13},{9,1},{13,5},{2,10},{6,14},... | collective-permute-start | bytes 1572872 | tf_op jit(solution)/shard_map/ppermute | solution.py:470
  17.1 14.8 %collective-permute-start.2 = (bf16[256,1024]{1,0:T(8,128)(2,1)S(1)}, bf16[256,1024]{1,0:T(8,128)(2,1)S(1)}, u32[]{:S(2)}, u32[]{:S(2)}) collective-permute-start(bf16[256,1024]{1,0:T(8,128)(2,1)S(1)} %collective-permute-done.1.refs_2_.refs_0_), channel_id=1, source_target_pairs={{0,4},{4,0},{8,12},{12,8},{1,5},{5,1},{9,13},{13,9},{2,6},{6,2},{1... | collective-permute-start | bytes 1572872 | tf_op jit(solution)/shard_map/ppermute | solution.py:475
  28.1 13.7 %collective-permute-start.4 = (bf16[256,1024]{1,0:T(8,128)(2,1)S(1)}, bf16[256,1024]{1,0:T(8,128)(2,1)S(1)}, u32[]{:S(2)}, u32[]{:S(2)}) collective-permute-start(bf16[256,1024]{1,0:T(8,128)(2,1)S(1)} %collective-permute-done.3.refs_2_.refs_0_), channel_id=1, source_target_pairs={{0,4},{4,0},{8,12},{12,8},{1,5},{5,1},{9,13},{13,9},{2,6},{6,2},{1... | collective-permute-start | bytes 1572872 | tf_op jit(solution)/shard_map/ppermute | solution.py:475
  32.7 14.8 %collective-permute-start.6 = (bf16[256,256]{1,0:T(8,128)(2,1)S(1)}, bf16[256,256]{1,0:T(8,128)(2,1)S(1)}, u32[]{:S(2)}, u32[]{:S(2)}) collective-permute-start(bf16[256,256]{1,0:T(8,128)(2,1)S(1)} %get-tuple-element.69.refs_2_), channel_id=1, source_target_pairs={{0,2},{1,3},{2,0},{3,1},{4,6},{5,7},{6,4},{7,5},{8,10},{9,11},{10,... | collective-permute-start | bytes 393224 | tf_op jit(solution)/shard_map/ppermute | solution.py:489
  35.6 12.0 %collective-permute-start.7 = (bf16[256,256]{1,0:T(8,128)(2,1)S(1)}, bf16[256,256]{1,0:T(8,128)(2,1)S(1)}, u32[]{:S(2)}, u32[]{:S(2)}) collective-permute-start(bf16[256,256]{1,0:T(8,128)(2,1)S(1)} %get-tuple-element.70.refs_3_), channel_id=1, source_target_pairs={{0,3},{1,2},{2,1},{3,0},{4,7},{5,6},{6,5},{7,4},{8,11},{9,10},{10,... | collective-permute-start | bytes 393224 | tf_op jit(solution)/shard_map/ppermute | solution.py:489
  37.7 9.9 %collective-permute-start.5 = (bf16[256,256]{1,0:T(8,128)(2,1)S(1)}, bf16[256,256]{1,0:T(8,128)(2,1)S(1)}, u32[]{:S(2)}, u32[]{:S(2)}) collective-permute-start(bf16[256,256]{1,0:T(8,128)(2,1)S(1)} %get-tuple-element.68.refs_1_), channel_id=1, source_target_pairs={{0,1},{1,0},{2,3},{3,2},{4,5},{5,4},{6,7},{7,6},{8,9},{9,8},{10,11... | collective-permute-start | bytes 393224 | tf_op jit(solution)/shard_map/ppermute | solution.py:489
  42.6 14.3 %collective-permute-start.9 = (bf16[256,256]{1,0:T(8,128)(2,1)S(1)}, bf16[256,256]{1,0:T(8,128)(2,1)S(1)}, u32[]{:S(2)}, u32[]{:S(2)}) collective-permute-start(bf16[256,256]{1,0:T(8,128)(2,1)S(1)} %get-tuple-element.58.refs_2_), channel_id=1, source_target_pairs={{0,2},{1,3},{2,0},{3,1},{4,6},{5,7},{6,4},{7,5},{8,10},{9,11},{10,... | collective-permute-start | bytes 393224 | tf_op jit(solution)/shard_map/ppermute | solution.py:489
  45.4 11.6 %collective-permute-start.10 = (bf16[256,256]{1,0:T(8,128)(2,1)S(1)}, bf16[256,256]{1,0:T(8,128)(2,1)S(1)}, u32[]{:S(2)}, u32[]{:S(2)}) collective-permute-start(bf16[256,256]{1,0:T(8,128)(2,1)S(1)} %get-tuple-element.59.refs_3_), channel_id=1, source_target_pairs={{0,3},{1,2},{2,1},{3,0},{4,7},{5,6},{6,5},{7,4},{8,11},{9,10},{10,... | collective-permute-start | bytes 393224 | tf_op jit(solution)/shard_map/ppermute | solution.py:489
  47.5 10.2 %collective-permute-start.8 = (bf16[256,256]{1,0:T(8,128)(2,1)S(1)}, bf16[256,256]{1,0:T(8,128)(2,1)S(1)}, u32[]{:S(2)}, u32[]{:S(2)}) collective-permute-start(bf16[256,256]{1,0:T(8,128)(2,1)S(1)} %get-tuple-element.57.refs_1_), channel_id=1, source_target_pairs={{0,1},{1,0},{2,3},{3,2},{4,5},{5,4},{6,7},{7,6},{8,9},{9,8},{10,11... | collective-permute-start | bytes 393224 | tf_op jit(solution)/shard_map/ppermute | solution.py:489
  67.9 17.1 %collective-permute-start.17 = (bf16[128,256]{1,0:T(8,128)(2,1)S(1)}, bf16[128,256]{1,0:T(8,128)(2,1)S(1)}, u32[]{:S(2)}, u32[]{:S(2)}) collective-permute-start(bf16[128,256]{1,0:T(8,128)(2,1)S(1)} %get-tuple-element.78), channel_id=1, source_target_pairs={{0,2},{1,3},{2,0},{3,1},{4,6},{5,7},{6,4},{7,5},{8,10},{9,11},{10,... | collective-permute-start | bytes 196616 | tf_op jit(solution)/shard_map/ppermute | solution.py:489
  68.9 17.2 %collective-permute-start.18 = (bf16[128,256]{1,0:T(8,128)(2,1)S(1)}, bf16[128,256]{1,0:T(8,128)(2,1)S(1)}, u32[]{:S(2)}, u32[]{:S(2)}) collective-permute-start(bf16[128,256]{1,0:T(8,128)(2,1)S(1)} %get-tuple-element.79), channel_id=1, source_target_pairs={{0,3},{1,2},{2,1},{3,0},{4,7},{5,6},{6,5},{7,4},{8,11},{9,10},{10,... | collective-permute-start | bytes 196616 | tf_op jit(solution)/shard_map/ppermute | solution.py:489
  71.2 15.9 %collective-permute-start.23 = (bf16[128,256]{1,0:T(8,128)(2,1)S(1)}, bf16[128,256]{1,0:T(8,128)(2,1)S(1)}, u32[]{:S(2)}, u32[]{:S(2)}) collective-permute-start(bf16[128,256]{1,0:T(8,128)(2,1)S(1)} %get-tuple-element.82), channel_id=1, source_target_pairs={{0,1},{1,0},{2,3},{3,2},{4,5},{5,4},{6,7},{7,6},{8,9},{9,8},{10,11... | collective-permute-start | bytes 196616 | tf_op jit(solution)/shard_map/ppermute | solution.py:489
  71.9 17.6 %collective-permute-start.24 = (bf16[128,256]{1,0:T(8,128)(2,1)S(1)}, bf16[128,256]{1,0:T(8,128)(2,1)S(1)}, u32[]{:S(2)}, u32[]{:S(2)}) collective-permute-start(bf16[128,256]{1,0:T(8,128)(2,1)S(1)} %get-tuple-element.83), channel_id=1, source_target_pairs={{0,2},{1,3},{2,0},{3,1},{4,6},{5,7},{6,4},{7,5},{8,10},{9,11},{10,... | collective-permute-start | bytes 196616 | tf_op jit(solution)/shard_map/ppermute | solution.py:489
  74.2 16.7 %collective-permute-start.25 = (bf16[128,256]{1,0:T(8,128)(2,1)S(1)}, bf16[128,256]{1,0:T(8,128)(2,1)S(1)}, u32[]{:S(2)}, u32[]{:S(2)}) collective-permute-start(bf16[128,256]{1,0:T(8,128)(2,1)S(1)} %get-tuple-element.84), channel_id=1, source_target_pairs={{0,3},{1,2},{2,1},{3,0},{4,7},{5,6},{6,5},{7,4},{8,11},{9,10},{10,... | collective-permute-start | bytes 196616 | tf_op jit(solution)/shard_map/ppermute | solution.py:489
  85.0 8.7 %collective-permute-start.11 = (bf16[128,256]{1,0:T(8,128)(2,1)S(1)}, bf16[128,256]{1,0:T(8,128)(2,1)S(1)}, u32[]{:S(2)}, u32[]{:S(2)}) collective-permute-start(bf16[128,256]{1,0:T(8,128)(2,1)S(1)} %get-tuple-element.73), channel_id=1, source_target_pairs={{0,1},{1,0},{2,3},{3,2},{4,5},{5,4},{6,7},{7,6},{8,9},{9,8},{10,11... | collective-permute-start | bytes 196616 | tf_op jit(solution)/shard_map/ppermute | solution.py:489
  93.7 9.2 %collective-permute-start.31 = (bf16[128,1024]{1,0:T(8,128)(2,1)S(1)}, bf16[128,1024]{1,0:T(8,128)(2,1)S(1)}, u32[]{:S(2)}, u32[]{:S(2)}) collective-permute-start(bf16[128,1024]{1,0:T(8,128)(2,1)S(1)} %shard_map.86.refs_0_), channel_id=1, source_target_pairs={{0,8},{4,12},{8,0},{12,4},{1,9},{5,13},{9,1},{13,5},{2,10},{6,14},... | collective-permute-start | bytes 786440 | tf_op jit(solution)/shard_map/ppermute | solution.py:470
  94.5 14.1 %collective-permute-start.19 = (bf16[128,1024]{1,0:T(8,128)(2,1)S(1)}, bf16[128,1024]{1,0:T(8,128)(2,1)S(1)}, u32[]{:S(2)}, u32[]{:S(2)}) collective-permute-start(bf16[128,1024]{1,0:T(8,128)(2,1)S(1)} %shard_map.85.refs_1_), channel_id=1, source_target_pairs={{0,8},{4,12},{8,0},{12,4},{1,9},{5,13},{9,1},{13,5},{2,10},{6,14},... | collective-permute-start | bytes 786440 | tf_op jit(solution)/shard_map/ppermute | solution.py:470
  96.1 12.4 %collective-permute-start.21 = (bf16[128,1024]{1,0:T(8,128)(2,1)S(1)}, bf16[128,1024]{1,0:T(8,128)(2,1)S(1)}, u32[]{:S(2)}, u32[]{:S(2)}) collective-permute-start(bf16[128,1024]{1,0:T(8,128)(2,1)S(1)} %shard_map.84.refs_0_), channel_id=1, source_target_pairs={{0,4},{4,0},{8,12},{12,8},{1,5},{5,1},{9,13},{13,9},{2,6},{6,2},{1... | collective-permute-start | bytes 786440 | tf_op jit(solution)/shard_map/ppermute | solution.py:475
  96.2 17.5 %collective-permute-start.14 = (bf16[128,1024]{1,0:T(8,128)(2,1)S(1)}, bf16[128,1024]{1,0:T(8,128)(2,1)S(1)}, u32[]{:S(2)}, u32[]{:S(2)}) collective-permute-start(bf16[128,1024]{1,0:T(8,128)(2,1)S(1)} %shard_map.84.refs_0_), channel_id=1, source_target_pairs={{0,8},{4,12},{8,0},{12,4},{1,9},{5,13},{9,1},{13,5},{2,10},{6,14},... | collective-permute-start | bytes 786440 | tf_op jit(solution)/shard_map/ppermute | solution.py:470
  102.9 12.8 %collective-permute-start.29 = (bf16[128,1024]{1,0:T(8,128)(2,1)S(1)}, bf16[128,1024]{1,0:T(8,128)(2,1)S(1)}, u32[]{:S(2)}, u32[]{:S(2)}) collective-permute-start(bf16[128,1024]{1,0:T(8,128)(2,1)S(1)} %shard_map.86.refs_0_), channel_id=1, source_target_pairs={{0,4},{4,0},{8,12},{12,8},{1,5},{5,1},{9,13},{13,9},{2,6},{6,2},{1... | collective-permute-start | bytes 786440 | tf_op jit(solution)/shard_map/ppermute | solution.py:475
  102.9 12.8 %collective-permute-start.34 = (bf16[128,1024]{1,0:T(8,128)(2,1)S(1)}, bf16[128,1024]{1,0:T(8,128)(2,1)S(1)}, u32[]{:S(2)}, u32[]{:S(2)}) collective-permute-start(bf16[128,1024]{1,0:T(8,128)(2,1)S(1)} %collective-permute-done.32.refs_5_), channel_id=1, source_target_pairs={{0,4},{4,0},{8,12},{12,8},{1,5},{5,1},{9,13},{13,9},{2,6},{6,2},{1... | collective-permute-start | bytes 786440 | tf_op jit(solution)/shard_map/ppermute | solution.py:475
  108.5 10.3 %collective-permute-start.20 = (bf16[128,1024]{1,0:T(8,128)(2,1)S(1)}, bf16[128,1024]{1,0:T(8,128)(2,1)S(1)}, u32[]{:S(2)}, u32[]{:S(2)}) collective-permute-start(bf16[128,1024]{1,0:T(8,128)(2,1)S(1)} %collective-permute-done.19.refs_1_), channel_id=1, source_target_pairs={{0,4},{4,0},{8,12},{12,8},{1,5},{5,1},{9,13},{13,9},{2,6},{6,2},{1... | collective-permute-start | bytes 786440 | tf_op jit(solution)/shard_map/ppermute | solution.py:475
  (13 other events, 130.7 us)

commit v8 on v7

--- a/solution.py
+++ b/solution.py
@@ -16,6 +16,7 @@
 LANES = 128
 MIB = 1 << 20
 CHUNKS = 2
+PARTS = 2
 VMEM = pl.BlockSpec(memory_space=pltpu.VMEM)
 HBM = pl.BlockSpec(memory_space=pltpu.HBM)
 
@@ -106,7 +107,7 @@
 
 
 def prologue_kernel(
-    width, skip_hbm, fwd_hbm, inv_hbm, taps_ref, w_ref, fwd_ref, inv_ref, kv_ref, out_ref, skip_out, skip_ref, taps_in, prev_ref, sems
+    width, skip_hbm, fwd_hbm, inv_hbm, taps_ref, w_ref, fwd_ref, inv_ref, kv_ref, query_ref, out_ref, skip_out, skip_ref, taps_in, prev_ref, sems
 ):
     block = inv_ref.shape[0]
     cols = rows_at(lax.axis_index("ctx"), width)
@@ -116,6 +117,7 @@
         pltpu.make_async_copy(taps_ref.at[:, cols], taps_in, sems.at[1]),
         pltpu.make_async_copy(inv_hbm, inv_ref, sems.at[2]),
         pltpu.make_async_copy(w_ref.at[1:3], kv_ref, sems.at[3]),
+        pltpu.make_async_copy(w_ref.at[0], query_ref, sems.at[5]),
     ]
     for copy in copies:
         copy.start()
@@ -143,6 +145,7 @@
     out = [
         *(jax.ShapeDtypeStruct(t.shape, BF16) for t in tables),
         jax.ShapeDtypeStruct((2, *w.shape[1:]), BF16),
+        jax.ShapeDtypeStruct(w.shape[1:], BF16),
         jax.ShapeDtypeStruct((count, rows, width), F32),
         jax.ShapeDtypeStruct((n_ctx, width), F32),
     ]
@@ -155,7 +158,7 @@
             pltpu.VMEM(skip.shape, F32),
             pltpu.VMEM((taps.shape[0], width), BF16),
             pltpu.VMEM((rows, width), F32),
-            pltpu.SemaphoreType.DMA((5,)),
+            pltpu.SemaphoreType.DMA((6,)),
         ],
         compiler_params=pltpu.CompilerParams(vmem_limit_bytes=6 * MIB),
         cost_estimate=pl.CostEstimate(
@@ -167,7 +170,7 @@
     )(*(pltpu.with_memory_space_constraint(x, pltpu.HBM) for x in (skip, *tables, taps, w)))
 
 
-def kv_kernel(which, starts, n_ctx, has_before, slices, w_ref, *refs):
+def kv_kernel(which, starts, n_ctx, has_before, slices, parts, w_ref, *refs):
     pieces, refs = refs[: len(which)], refs[len(which) :]
     before, outs = (refs[:2], refs[2:]) if has_before else ((), refs)
     tokens = outs[0].shape[0]
@@ -187,21 +190,24 @@
             key = a if key is None else key + a
             value = b if value is None else value + b
         if slices:
-            outs[slices.index(k)][...] = (key * value).astype(BF16)
+            made = (key * value).astype(BF16)
+            for p in range(parts):
+                cut = slice(p * width // parts, (p + 1) * width // parts)
+                outs[slices.index(k) * parts + p][...] = made[:, cut]
         else:
             outs[0][:, mine] = key
             outs[1][:, mine] = value
 
 
-def keys_values(pieces, which, starts, tokens, w, before, n_ctx, slices=()):
+def keys_values(pieces, which, starts, tokens, w, before, n_ctx, slices=(), parts=1):
     channels = w.shape[2]
     share = len(which) * pieces[0].shape[1]
     if slices:
-        out = [jax.ShapeDtypeStruct((tokens, channels // n_ctx), BF16)] * len(slices)
+        out = [jax.ShapeDtypeStruct((tokens, channels // n_ctx // parts), BF16)] * (len(slices) * parts)
     else:
         out = [jax.ShapeDtypeStruct((tokens, channels), F32)] * 2
     return call(
-        functools.partial(kv_kernel, tuple(which), tuple(starts), n_ctx, bool(before), slices),
+        functools.partial(kv_kernel, tuple(which), tuple(starts), n_ctx, bool(before), slices, parts),
         out,
         [w, *(pieces[j] for j in which), *before],
         6,
@@ -210,201 +216,182 @@
     )
 
 
-def query_kernel(starts, n_ctx, load, w_ref, *refs):
-    pieces, refs = refs[: len(starts)], refs[len(starts) :]
-    out_ref, acc_ref = refs[0], refs[-1]
+def query_kernel(starts, n_ctx, w_ref, *refs):
+    pieces, out_ref = refs[:-1], refs[-1]
     tokens = out_ref.shape[0]
     depth = pieces[0].shape[1]
     width = out_ref.shape[1] // n_ctx
     me = lax.axis_index("ctx")
     rows = [rows_at(source, depth) for source in chan_sources()]
-    copies = []
-    if load:
-        kept_ref, sems = refs[1:3]
-        copies = [
-            pltpu.make_async_copy(w_ref.at[0, r], kept_ref.at[r], sems.at[j]) for j, r in enumerate(rows)
-        ]
-        w_ref = kept_ref
-    for copy in copies:
-        copy.start()
-    for j, piece in enumerate(pieces):
-        if load:
-            copies[j].wait()
-        for k in range(n_ctx):
-            mine = slice(k * width, (k + 1) * width)
+    for k in range(n_ctx):
+        cols = rows_at(target(me, k, n_ctx), width)
+        acc = None
+        for j, piece in enumerate(pieces):
             x = piece[starts[j] : starts[j] + tokens, :]
-            cols = rows_at(target(me, k, n_ctx), width)
             a = jnp.dot(x, w_ref[rows[j], cols], preferred_element_type=F32)
-            if j > 0:
-                a = acc_ref[:, mine] + a
-            if j < len(pieces) - 1:
-                acc_ref[:, mine] = a
-            else:
-                out_ref[:, mine] = a.astype(BF16)
-
-
-def queries(pieces, starts, tokens, w, n_ctx, load):
-    total, channels = w.shape[-2:]
-    out = [jax.ShapeDtypeStruct((tokens, channels), BF16)]
-    scratch = [pltpu.VMEM((tokens, channels), F32)]
-    if load:
-        w = pltpu.with_memory_space_constraint(w, pltpu.HBM)
-        out.append(jax.ShapeDtypeStruct((total, channels), BF16))
-        scratch.insert(0, pltpu.SemaphoreType.DMA((len(pieces),)))
-    return pl.pallas_call(
-        functools.partial(query_kernel, tuple(starts), n_ctx, load),
-        out_shape=out,
-        in_specs=[HBM if load else VMEM] + [VMEM] * len(pieces),
-        out_specs=[VMEM] * len(out),
-        scratch_shapes=scratch,
-        compiler_params=pltpu.CompilerParams(vmem_limit_bytes=6 * MIB),
-        cost_estimate=pl.CostEstimate(
-            flops=2 * tokens * total * channels,
-            bytes_accessed=2 * total * channels + 2 * tokens * total,
-            transcendentals=0,
-        ),
-        name="q_projection",
-    )(w, *pieces)
-
-
-def block_products(g_ref, x_ref, before_ref, after_ref, plan, width, block):
+            acc = a if acc is None else acc + a
+        out_ref[:, k * width : (k + 1) * width] = acc.astype(BF16)
+
+
+def queries(pieces, starts, tokens, w, n_ctx):
+    total, channels = w.shape
+    return call(
+        functools.partial(query_kernel, tuple(starts), n_ctx),
+        jax.ShapeDtypeStruct((tokens, channels), BF16),
+        [w, *pieces],
+        6,
+        2 * tokens * total * channels,
+        2 * total * channels + 2 * tokens * total,
+    )
+
+
+def block_products(g_ref, x_ref, before_ref, after_ref, plan, start, block):
     lags = sorted({lag for _, _, terms in plan for lag, _ in terms})
     slots = sorted({slot for _, _, terms in plan for _, slot in terms})
 
     def tile(i, first):
         upper = pl.ds(i * 8, 8) if first else rows_at(i, 8)
         lower = pl.ds(block + i * 8, 8) if first else rows_at(block // 8 + i, 8)
-        for lane in range(width // LANES):
-            cols = pl.ds(lane * LANES, LANES)
+        for lane in range(x_ref.shape[2] // LANES):
+            cols, own = pl.ds(start + lane * LANES, LANES), pl.ds(lane * LANES, LANES)
             g_re = {b: g_ref[b, upper, cols] for b in lags}
             g_im = {b: g_ref[b, lower, cols] for b in lags}
-            x_re = {b: x_ref[b, upper, cols] for b in slots}
-            x_im = {b: x_ref[b, lower, cols] for b in slots}
+            x_re = {b: x_ref[b, upper, own] for b in slots}
+            x_im = {b: x_ref[b, lower, own] for b in slots}
             g_di = g_re
             if first:
                 edge = lax.broadcasted_iota(jnp.int32, (8, LANES), 0) == 0
                 g_di = {b: jnp.where(edge, g_im[b], g_re[b]) for b in lags}
                 g_im = {b: jnp.where(edge, 0.0, g_im[b]) for b in lags}
-            for start, end, terms in plan:
+            for here, end, terms in plan:
                 re = im = None
-                if start is not None:
-                    re, im = before_ref[start, upper, cols], before_ref[start, lower, cols]
+                if here is not None:
+                    re, im = before_ref[here, upper, cols], before_ref[here, lower, cols]
                 for lag, slot in terms:
                     up = g_re[lag] * x_re[slot] - g_im[lag] * x_im[slot]
                     down = g_di[lag] * x_im[slot] + g_im[lag] * x_re[slot]
                     re = up if re is None else re + up
                     im = down if im is None else im + down
-                after_ref[end, upper, cols] = re
-                after_ref[end, lower, cols] = im
+                after_ref[end, upper, own] = re
+                after_ref[end, lower, own] = im
 
     tile(0, True)
     pl.loop(1, block // 8)(lambda i: tile(i, False))
 
 
-def forward_dft(n_ctx, fwd_ref, ins, x_ref):
+def part_of(ref, start, width):
+    return ref[...] if ref.shape[1] == width else ref[:, start : start + width]
+
+
+def forward_dft(n_ctx, fwd_ref, ins, x_ref, start):
     me = lax.axis_index("ctx")
     for k in range(n_ctx):
-        x_ref[origin(me, k, n_ctx)] = jnp.dot(fwd_ref[...], ins[k][...], preferred_element_type=F32)
+        piece = part_of(ins[k], start, x_ref.shape[2])
+        x_ref[origin(me, k, n_ctx)] = jnp.dot(fwd_ref[...], piece, preferred_element_type=F32)
 
 
 def inverse_dft(n_ctx, inv_ref, y_ref, outs):
     me = lax.axis_index("ctx")
-    tokens = outs[0].shape[0]
-    for p in range(len(outs) // n_ctx):
-        for k in range(n_ctx):
-            spectrum = y_ref[target(me, k, n_ctx)].astype(BF16)
-            part = inv_ref[p * tokens : (p + 1) * tokens, :]
-            outs[p * n_ctx + k][...] = jnp.dot(part, spectrum, preferred_element_type=F32).astype(BF16)
+    for k in range(n_ctx):
+        spectrum = y_ref[target(me, k, n_ctx)].astype(BF16)
+        outs[k][...] = jnp.dot(inv_ref[...], spectrum, preferred_element_type=F32).astype(BF16)
 
 
 def early_kernel(n_ctx, fwd_ref, g_ref, *refs):
     ins, sum_ref, x_ref = refs[:n_ctx], refs[n_ctx], refs[n_ctx + 1]
-    blocks, rows, width = g_ref.shape
-    forward_dft(n_ctx, fwd_ref, ins, x_ref)
+    blocks, rows, _ = g_ref.shape
+    forward_dft(n_ctx, fwd_ref, ins, x_ref, 0)
     plan = [(None, b, [(b - a, a // 2) for a in range(0, b + 1, 2)]) for b in range(blocks)]
-    block_products(g_ref, x_ref, None, sum_ref, plan, width, rows // 2)
-
-
-def middle_kernel(n_ctx, fwd_ref, inv_ref, g_ref, sum_ref, *refs):
+    block_products(g_ref, x_ref, None, sum_ref, plan, 0, rows // 2)
+
+
+def middle_kernel(n_ctx, start, fwd_ref, inv_ref, g_ref, sum_ref, *refs):
     ins, x_ref, outs, y_ref = refs[:n_ctx], refs[n_ctx], refs[n_ctx + 1 : -1], refs[-1]
-    blocks, rows, width = g_ref.shape
-    forward_dft(n_ctx, fwd_ref, ins, x_ref)
+    blocks, rows, _ = g_ref.shape
+    forward_dft(n_ctx, fwd_ref, ins, x_ref, start)
     plan = [(b, b // 2, [(b - a, a // 2) for a in range(1, b, 2)]) for b in range(0, blocks, 2)]
-    block_products(g_ref, x_ref, sum_ref, y_ref, plan, width, rows // 2)
+    block_products(g_ref, x_ref, sum_ref, y_ref, plan, start, rows // 2)
     inverse_dft(n_ctx, inv_ref, y_ref, outs)
 
 
-def late_kernel(n_ctx, inv_ref, g_ref, sum_ref, x_ref, *refs):
+def late_kernel(n_ctx, start, inv_ref, g_ref, sum_ref, x_ref, *refs):
     outs, y_ref = refs[:-1], refs[-1]
-    blocks, rows, width = g_ref.shape
+    blocks, rows, _ = g_ref.shape
     plan = [(b, b // 2, [(b - a, a // 2) for a in range(1, b + 1, 2)]) for b in range(1, blocks, 2)]
-    block_products(g_ref, x_ref, sum_ref, y_ref, plan, width, rows // 2)
+    block_products(g_ref, x_ref, sum_ref, y_ref, plan, start, rows // 2)
     inverse_dft(n_ctx, inv_ref, y_ref, outs)
 
 
-def convolve(forward, inverse, spectra, arrived, n_ctx):
+def convolve(forward, inverse, spectra, even, odd, n_ctx):
     blocks, rows, width = spectra.shape
-    half = (n_ctx, rows, width)
-    piece = jax.ShapeDtypeStruct((rows // 4, width), BF16)
+    parts = len(odd)
+    share = width // parts
+    some = (n_ctx, rows, share)
+    piece = jax.ShapeDtypeStruct((rows // 2, share), BF16)
     flops, moved = blocks * rows * rows * width // 2, blocks * rows * width * 8
     sums = call(
         functools.partial(early_kernel, n_ctx),
         jax.ShapeDtypeStruct(spectra.shape, F32),
-        [forward, spectra, *arrived[0]],
+        [forward, spectra, *even],
         6,
         flops,
         moved,
-        [pltpu.VMEM(half, F32)],
+        [pltpu.VMEM((n_ctx, rows, width), F32)],
     )
-    x, *even = call(
-        functools.partial(middle_kernel, n_ctx),
-        [jax.ShapeDtypeStruct(half, F32)] + [piece] * (2 * n_ctx),
-        [forward, inverse, spectra, sums, *arrived[1]],
-        6,
-        flops,
-        moved,
-        [pltpu.VMEM(half, F32)],
-    )
-    odd = call(
-        functools.partial(late_kernel, n_ctx),
-        [piece] * (2 * n_ctx),
-        [inverse, spectra, sums, x],
-        6,
-        flops,
-        moved,
-        [pltpu.VMEM(half, F32)],
-    )
-    return even[:n_ctx], even[n_ctx:], odd[:n_ctx], odd[n_ctx:]
+    first, second = [], []
+    for h in range(parts):
+        x, *made = call(
+            functools.partial(middle_kernel, n_ctx, h * share),
+            [jax.ShapeDtypeStruct(some, F32)] + [piece] * n_ctx,
+            [forward, inverse, spectra, sums, *odd[h]],
+            6,
+            flops // parts,
+            moved // parts,
+            [pltpu.VMEM(some, F32)],
+        )
+        first.append(made)
+        second.append(
+            call(
+                functools.partial(late_kernel, n_ctx, h * share),
+                [piece] * n_ctx,
+                [inverse, spectra, sums, x],
+                6,
+                flops // parts,
+                moved // parts,
+                [pltpu.VMEM(some, F32)],
+            )
+        )
+    return [*first, *second]
 
 
 def gate_kernel(n_ctx, start, skip_ref, q_ref, *refs):
     mixed, conv, out_ref = refs[:n_ctx], refs[n_ctx : 2 * n_ctx], refs[-1]
-    tokens, width = conv[0].shape
-    rows = slice(start, start + tokens)
+    share, width = conv[0].shape[1], q_ref.shape[1] // n_ctx
     me = lax.axis_index("ctx")
     for m in range(n_ctx):
-        cols = slice(m * width, (m + 1) * width)
-        skip = skip_ref[pl.ds(target(me, m, n_ctx), 1), :]
-        query = q_ref[rows, cols].astype(F32)
-        total = conv[mirror(m, n_ctx)][...].astype(F32) + skip * mixed[m][rows, :].astype(F32)
-        out_ref[:, cols] = (query * total).astype(BF16)
+        skip = skip_ref[pl.ds(target(me, m, n_ctx), 1), :][:, start : start + share]
+        query = q_ref[:, m * width + start : m * width + start + share].astype(F32)
+        source = part_of(mixed[m], start, share).astype(F32)
+        total = conv[mirror(m, n_ctx)][...].astype(F32) + skip * source
+        out_ref[:, m * share : (m + 1) * share] = (query * total).astype(BF16)
 
 
 def gate(skip, query, mixed, conv, start, n_ctx):
-    shape = (conv[0].shape[0], query.shape[1])
+    tokens, share = conv[0].shape
     return call(
         functools.partial(gate_kernel, n_ctx, start),
-        jax.ShapeDtypeStruct(shape, BF16),
+        jax.ShapeDtypeStruct((tokens, share * n_ctx), BF16),
         [skip, query, *mixed, *conv],
         4,
-        3 * shape[0] * shape[1],
-        8 * shape[0] * shape[1],
+        3 * tokens * share * n_ctx,
+        8 * tokens * share * n_ctx,
     )
 
 
 def out_kernel(which, parts, has_before, n_ctx, columns, row, w_ref, *refs):
     pieces, out_ref = refs[: len(which) * parts], refs[-1 if row is None else -3]
-    width = pieces[0].shape[1] // n_ctx
+    share = pieces[0].shape[1] // n_ctx
+    width = share * parts
     me = lax.axis_index("ctx")
     sources = chan_sources()
     copies = []
@@ -414,9 +401,9 @@
         for i_piece, j in enumerate(which):
             for m in range(n_ctx):
                 w = w_ref[rows_at(sources[j] * n_ctx + target(me, m, n_ctx), width), cols]
-                mine = slice(m * width, (m + 1) * width)
+                mine = slice(m * share, (m + 1) * share)
                 group = pieces[i_piece * parts : (i_piece + 1) * parts]
-                x = jnp.concatenate([p[:, mine] for p in group], axis=0)
+                x = jnp.concatenate([p[:, mine] for p in group], axis=1)
                 a = jnp.dot(x, w, preferred_element_type=F32)
                 acc = a if acc is None else acc + a
         if row is None:
@@ -433,7 +420,7 @@
 
 def project_out(gathered, which, w, before, n_ctx, final=None, columns=256):
     parts = len(gathered)
-    tokens = sum(pieces[0].shape[0] for pieces in gathered)
+    tokens = gathered[0][0].shape[0]
     _, out_width = w.shape
     operands = [w, *(pieces[j] for j in which for pieces in gathered)] + ([] if before is None else [before])
     specs = [VMEM] * len(operands)
@@ -447,7 +434,7 @@
             specs.append(HBM)
             aliases = {len(operands): 0}
             operands.append(so_far)
-    share = len(which) * gathered[0][0].shape[1]
+    share = len(which) * parts * gathered[0][0].shape[1]
     return pl.pallas_call(
         functools.partial(out_kernel, tuple(which), parts, before is not None, n_ctx, columns, row),
         out_shape=jax.ShapeDtypeStruct(shape, F32 if final is None else BF16),
@@ -483,9 +470,9 @@
     return pieces
 
 
-def exchange(parts):
-    out, n = [parts[0]], len(parts)
-    for k in range(1, n):
+def exchange(parts, first=1):
+    out, n = list(parts[:first]), len(parts)
+    for k in range(first, n):
         out.append(lax.ppermute(parts[k], "ctx", [(i, target(i, k, n)) for i in range(n)]))
     return out
 
@@ -504,9 +491,9 @@
     own = halves(features)
     far = [gather_far(own[c]) for c in range(CHUNKS)]
     near = swap_cores(features)
-    forward, inverse, w_kv, spectra, skip = prologue(tables, skip_gain, filter_taps, w, n_ctx)
-
-    mixed, arrived, query, w_q = [], [], [], None
+    forward, inverse, w_kv, w_q, spectra, skip = prologue(tables, skip_gain, filter_taps, w, n_ctx)
+
+    mixed, query = [], []
     for c in range(CHUNKS):
         pieces = [own[c], near, *far[c]]
         starts = [0, c * tokens] + [0] * len(far[c])
@@ -514,21 +501,21 @@
         for part, which in ("a", (0, 1)), ("b", range(2, len(pieces) - 1)):
             total = keys_values(pieces, which, [starts[j] for j in which], tokens, w_kv, total, n_ctx)
         last, made = len(pieces) - 1, {}
-        for part, slices in ("c", tuple(range(2, n_ctx))), ("d", (1, 0)):
-            some = keys_values(pieces, (last,), (starts[last],), tokens, w_kv, total, n_ctx, slices)
-            made.update(zip(slices, some))
-        mixed.append([made[k] for k in range(n_ctx)])
-        arrived.append(exchange(mixed[c]))
-        made, *kept = queries(pieces, starts, tokens, w if c == 0 else w_q, n_ctx, c == 0)
-        query.append(made)
-        w_q = kept[0] if kept else w_q
-    conv = convolve(forward, inverse, spectra, arrived, n_ctx)
+        for part, slices, cuts in ("c", tuple(range(2, n_ctx)), c + 1), ("d", (1, 0), 1):
+            some = keys_values(pieces, (last,), (starts[last],), tokens, w_kv, total, n_ctx, slices, cuts)
+            made.update({k: some[i * cuts : (i + 1) * cuts] for i, k in enumerate(slices)})
+        mixed.append([[made[k][h % len(made[k])] for k in range(n_ctx)] for h in range(PARTS)])
+        query.append(queries(pieces, starts, tokens, w_q, n_ctx))
+    even = exchange(mixed[0][0])
+    odd = [exchange(mixed[1][0])]
+    odd += [odd[0][:2] + exchange(mixed[1][h], 2)[2:] for h in range(1, PARTS)]
+    conv = convolve(forward, inverse, spectra, even, odd, n_ctx)
 
     gathered = []
-    for r in range(2 * CHUNKS):
-        c, start = r // 2, r % 2 * (tokens // 2)
+    for r in range(CHUNKS * PARTS):
+        c, h = r // PARTS, r % PARTS
         back = exchange(conv[r])
-        gated = gate(skip, query[c], mixed[c], back, start, n_ctx)
+        gated = gate(skip, query[c], mixed[c][h], back, h * back[0].shape[1], n_ctx)
         beside = swap_cores(gated)
         gathered.append([gated, beside, *gather_far(gated)])
     every = range(len(gathered[0]))
@@ -592,7 +579,7 @@
 
 
 def shards(features, filter_taps, skip_gain, in_weight, out_weight):
-    slices = in_weight.shape[2] % (lax.axis_size("ctx") * LANES) == 0
+    slices = lax.axis_size("ctx") > 2 and in_weight.shape[2] % (lax.axis_size("ctx") * PARTS * LANES) == 0
     cores = lax.axis_size("chan") % 2 == 0 and lax.axis_size("chan") > 2
     blocks = features.shape[0] % (CHUNKS * LANES) == 0
     chosen = layer if slices and cores and blocks else plain_layer

time: 121 us -> 116 us (0.959)
  waiting for transfers between devices: 41.6 us -> 31.5 us
  starting transfers between devices: 41.2 us -> 43.8 us
  Pallas kernels: 37.2 us -> 39.6 us
    ppermute x18 -> x20, waiting for transfers between devices: 8.87 us -> 0.79 us  [exchange(): lax.ppermute(parts[k], 'ctx', [(i, target(i, k, n)) for i in range(n)])]
    pallas_call x2 -> x0, Pallas kernels: 6.7 us -> none  [queries(): pl.pallas_call(functools.partial(query_kernel, tuple(starts), n_ctx, load...]
    pallas_call x15 -> x19, Pallas kernels: 16.4 us -> 23.1 us  [call(): pl.pallas_call(kernel, out_shape=out, in_specs=[VMEM] * len(operands), ou...]
    ppermute x18 -> x20, starting transfers between devices: 32 us -> 34.9 us  [exchange(): lax.ppermute(parts[k], 'ctx', [(i, target(i, k, n)) for i in range(n)])]
    pallas_call x1, Pallas kernels: 6.34 us -> 8.73 us  [prologue(): pl.pallas_call(functools.partial(prologue_kernel, width), out_shape=out,...]
    ppermute x6, waiting for transfers between devices: 32.7 us -> 30.7 us  [shift(): return lax.ppermute(x, axis, [(i, (i + by) % n) for i in range(n)])]
  transfers between devices with their start and end apart: 35 -> 37, of which waited for: 8 -> 7; matrix products, arithmetic and copies ran while one was open for 0% -> 0% of each run, Pallas kernels for 27% -> 33%
where the time goes in v8:
time: 116 us; the launch traced here: 115 us
  starting transfers between devices  43.8 us (38%)
  Pallas kernels  39.6 us (34%)
  waiting for transfers between devices  31.5 us (27%)
    ppermute x20, starting transfers between devices, exchange(): lax.ppermute(parts[k], 'ctx', [(i, target(i, k, n)) for i in range(n)])  34.9 us
    ppermute x6, waiting for transfers between devices, shift(): return lax.ppermute(x, axis, [(i, (i + by) % n) for i in range(n)])  30.7 us
    pallas_call x19, Pallas kernels, call(): pl.pallas_call(kernel, out_shape=out, in_specs=[VMEM] * len(operands), ou...  23.1 us
    pallas_call x1, Pallas kernels, prologue(): pl.pallas_call(functools.partial(prologue_kernel, width), out_shape=out,...  8.73 us
    ppermute x6, starting transfers between devices, shift(): return lax.ppermute(x, axis, [(i, (i + by) % n) for i in range(n)])  7.01 us
    pallas_call x4, Pallas kernels, project_out(): pl.pallas_call(functools.partial(out_kernel, tuple(which), parts, before...  6.55 us
  transfers between devices with their start and end apart: 37, of which 7 were waited for; matrix products, arithmetic and copies ran while one was open for 0% of the time, Pallas kernels for 33%

profile of v8, /device:TPU:0, one launch (start us, length us, event | category | flops | bytes accessed | tf_op | source)
XLA Modules:
  0.0 115.4 jit_solution(11694264009164428777)
XLA Ops:
  1.7 2.6 %collective-permute-start.3 = (bf16[256,1024]{1,0:T(8,128)(2,1)S(1)}, bf16[256,1024]{1,0:T(8,128)(2,1)S(1)}, u32[]{:S(2)}, u32[]{:S(2)}) collective-permute-start(bf16[256,1024]{1,0:T(8,128)(2,1)S(1)} %get-tuple-element.64.refs_0_), channel_id=1, source_target_pairs={{0,8},{4,12},{8,0},{12,4},{1,9},{5,13},{9,1},{13,5},{2,10},{6,14},... | collective-permute-start | bytes 1572872 | tf_op jit(solution)/shard_map/ppermute | solution.py:457
  4.4 12.7 %collective-permute-done.3.refs_0_.refs_2_ = bf16[256,1024]{1,0:T(8,128)(2,1)S(1)} collective-permute-done((bf16[256,1024]{1,0:T(8,128)(2,1)S(1)}, bf16[256,1024]{1,0:T(8,128)(2,1)S(1)}, u32[]{:S(2)}, u32[]{:S(2)}) %collective-permute-start.3) | collective-permute-done | bytes 524320 | tf_op jit(solution)/shard_map/ppermute | solution.py:457
  17.1 8.7 %prologue.1 = (bf16[512,256]{1,0:T(8,128)(2,1)S(1)}, bf16[256,512]{1,0:T(8,128)(2,1)S(1)}, bf16[2,4096,1024]{2,1,0:T(8,128)(2,1)S(1)}, bf16[4096,1024]{1,0:T(8,1...) custom-call(f32[1024]{0:T(1024)} %skip_hbm.1, bf16[512,256]{1,0:T(8,128)(2,1)} %constant.4.clone.fwd_hbm, ...), custom_call_target="tpu_custom_call" | custom-call | flops 536870912 | bytes 30408704 | tf_op jit(solution)/shard_map/prologue/pallas_call | solution.py:152
  25.8 2.3 %collective-permute-done.1.refs_2_.refs_0_ = bf16[256,1024]{1,0:T(8,128)(2,1)S(1)} collective-permute-done((bf16[256,1024]{1,0:T(8,128)(2,1)S(1)}, bf16[256,1024]{1,0:T(8,128)(2,1)S(1)}, u32[]{:S(2)}, u32[]{:S(2)}) %collective-permute-start.1) | collective-permute-done | bytes 524320 | tf_op jit(solution)/shard_map/ppermute | solution.py:457
  28.1 2.4 %shard_map.78 = (f32[256,1024]{1,0:T(8,128)S(1)}, f32[256,1024]{1,0:T(8,128)S(1)}) custom-call(bf16[2,4096,1024]{2,1,0:T(8,128)(2,1)S(1)} %get-tuple-element.52.w_ref, bf16[256,1024]{1,0:T(8,128)(2,1)S(1)} %get-tuple-element.64.refs_0_, bf16[512,1024]{1,0:T(8,128)(2,1)S(1)} %collective-permute-done.refs_1_), custom_call_target="tpu_custom_call" | custom-call | flops 2147483648 | bytes 9437184 | tf_op jit(solution)/shard_map/pallas_call | solution.py:43
  32.7 2.9 %collective-permute-start.6 = (bf16[256,256]{1,0:T(8,128)(2,1)S(1)}, bf16[256,256]{1,0:T(8,128)(2,1)S(1)}, u32[]{:S(2)}, u32[]{:S(2)}) collective-permute-start(bf16[256,256]{1,0:T(8,128)(2,1)S(1)} %get-tuple-element.71.refs_2_), channel_id=1, source_target_pairs={{0,2},{1,3},{2,0},{3,1},{4,6},{5,7},{6,4},{7,5},{8,10},{9,11},{10,... | collective-permute-start | bytes 393224 | tf_op jit(solution)/shard_map/ppermute | solution.py:476
  38.0 2.4 %shard_map.74 = (f32[256,1024]{1,0:T(8,128)S(1)}, f32[256,1024]{1,0:T(8,128)S(1)}) custom-call(bf16[2,4096,1024]{2,1,0:T(8,128)(2,1)S(1)} %get-tuple-element.52.w_ref, bf16[256,1024]{1,0:T(8,128)(2,1)S(1)} %get-tuple-element.51.refs_0_, bf16[512,1024]{1,0:T(8,128)(2,1)S(1)} %collective-permute-done.refs_1_), custom_call_target="tpu_custom_call" | custom-call | flops 2147483648 | bytes 9437184 | tf_op jit(solution)/shard_map/pallas_call | solution.py:43
  42.6 1.8 %collective-permute-start.8 = (bf16[256,256]{1,0:T(8,128)(2,1)S(1)}, bf16[256,256]{1,0:T(8,128)(2,1)S(1)}, u32[]{:S(2)}, u32[]{:S(2)}) collective-permute-start(bf16[256,256]{1,0:T(8,128)(2,1)S(1)} %get-tuple-element.58.refs_1_), channel_id=1, source_target_pairs={{0,1},{1,0},{2,3},{3,2},{4,5},{5,4},{6,7},{7,6},{8,9},{9,8},{10,11... | collective-permute-start | bytes 393224 | tf_op jit(solution)/shard_map/ppermute | solution.py:476
  45.1 1.8 %collective-permute-start.16 = (bf16[256,128]{1,0:T(8,128)(2,1)S(1)}, bf16[256,128]{1,0:T(8,128)(2,1)S(1)}, u32[]{:S(2)}, u32[]{:S(2)}) collective-permute-start(bf16[256,128]{1,0:T(8,128)(2,1)S(1)} %get-tuple-element.78.refs_2_), channel_id=1, source_target_pairs={{0,2},{1,3},{2,0},{3,1},{4,6},{5,7},{6,4},{7,5},{8,10},{9,11},{10,... | collective-permute-start | bytes 196616 | tf_op jit(solution)/shard_map/ppermute | solution.py:476
  46.9 2.0 %collective-permute-start.17 = (bf16[256,128]{1,0:T(8,128)(2,1)S(1)}, bf16[256,128]{1,0:T(8,128)(2,1)S(1)}, u32[]{:S(2)}, u32[]{:S(2)}) collective-permute-start(bf16[256,128]{1,0:T(8,128)(2,1)S(1)} %get-tuple-element.79.refs_3_), channel_id=1, source_target_pairs={{0,3},{1,2},{2,1},{3,0},{4,7},{5,6},{6,5},{7,4},{8,11},{9,10},{10,... | collective-permute-start | bytes 196616 | tf_op jit(solution)/shard_map/ppermute | solution.py:476
  49.0 2.6 %collective-permute-start.9 = (bf16[256,128]{1,0:T(8,128)(2,1)S(1)}, bf16[256,128]{1,0:T(8,128)(2,1)S(1)}, u32[]{:S(2)}, u32[]{:S(2)}) collective-permute-start(bf16[256,128]{1,0:T(8,128)(2,1)S(1)} %get-tuple-element.59.refs_2_), channel_id=1, source_target_pairs={{0,2},{1,3},{2,0},{3,1},{4,6},{5,7},{6,4},{7,5},{8,10},{9,11},{10,... | collective-permute-start | bytes 196616 | tf_op jit(solution)/shard_map/ppermute | solution.py:476
  52.0 2.1 %shard_map.82.sum_ref = f32[8,512,256]{2,1,0:T(8,128)S(1)} custom-call(bf16[512,256]{1,0:T(8,128)(2,1)S(1)} %get-tuple-element.63.fwd_ref, f32[8,512,256]{2,1,0:T(8,128)S(1)} %get-tuple-element.62.g_ref, bf16[256,256]{1,0:T(8,128)(2,1)S(1)} %get-tuple-element.69.refs_0_, bf16[256,256]{1,0:T(8,128)(2,1)S(1)} %collective-permute-done.5.refs_1_, ...), custom_call_target="tpu_custom_call" | custom-call | flops 268435456 | bytes 8388608 | tf_op jit(solution)/shard_map/pallas_call | solution.py:43
  57.2 2.8 %collective-permute-start.18 = (bf16[256,128]{1,0:T(8,128)(2,1)S(1)}, bf16[256,128]{1,0:T(8,128)(2,1)S(1)}, u32[]{:S(2)}, u32[]{:S(2)}) collective-permute-start(bf16[256,128]{1,0:T(8,128)(2,1)S(1)} %get-tuple-element.82), channel_id=1, source_target_pairs={{0,1},{1,0},{2,3},{3,2},{4,5},{5,4},{6,7},{7,6},{8,9},{9,8},{10,11... | collective-permute-start | bytes 196616 | tf_op jit(solution)/shard_map/ppermute | solution.py:476
  60.0 3.9 %collective-permute-start.29 = (bf16[256,128]{1,0:T(8,128)(2,1)S(1)}, bf16[256,128]{1,0:T(8,128)(2,1)S(1)}, u32[]{:S(2)}, u32[]{:S(2)}) collective-permute-start(bf16[256,128]{1,0:T(8,128)(2,1)S(1)} %get-tuple-element.91), channel_id=1, source_target_pairs={{0,2},{1,3},{2,0},{3,1},{4,6},{5,7},{6,4},{7,5},{8,10},{9,11},{10,... | collective-permute-start | bytes 196616 | tf_op jit(solution)/shard_map/ppermute | solution.py:476
  67.0 2.4 %collective-permute-start.20 = (bf16[256,128]{1,0:T(8,128)(2,1)S(1)}, bf16[256,128]{1,0:T(8,128)(2,1)S(1)}, u32[]{:S(2)}, u32[]{:S(2)}) collective-permute-start(bf16[256,128]{1,0:T(8,128)(2,1)S(1)} %get-tuple-element.84), channel_id=1, source_target_pairs={{0,3},{1,2},{2,1},{3,0},{4,7},{5,6},{6,5},{7,4},{8,11},{9,10},{10,... | collective-permute-start | bytes 196616 | tf_op jit(solution)/shard_map/ppermute | solution.py:476
  71.4 2.9 %collective-permute-start.27 = (bf16[256,128]{1,0:T(8,128)(2,1)S(1)}, bf16[256,128]{1,0:T(8,128)(2,1)S(1)}, u32[]{:S(2)}, u32[]{:S(2)}) collective-permute-start(bf16[256,128]{1,0:T(8,128)(2,1)S(1)} %get-tuple-element.88), channel_id=1, source_target_pairs={{0,3},{1,2},{2,1},{3,0},{4,7},{5,6},{6,5},{7,4},{8,11},{9,10},{10,... | collective-permute-start | bytes 196616 | tf_op jit(solution)/shard_map/ppermute | solution.py:476
  74.3 2.4 %shard_map.89.q_ref = bf16[256,1024]{1,0:T(8,128)(2,1)S(1)} custom-call(bf16[4096,1024]{1,0:T(8,128)(2,1)S(1)} %get-tuple-element.50.w_ref, bf16[256,1024]{1,0:T(8,128)(2,1)S(1)} %get-tuple-element.64.refs_0_, bf16[512,1024]{1,0:T(8,128)(2,1)S(1)} %collective-permute-done.refs_1_, bf16[256,1024]{1,0:T(8,128)(2,1)S(1)} %collective-permute-done.3.refs_0_.refs_2_, ...), custom_call_target="tpu_custom_call" | custom-call | flops 2147483648 | bytes 10485760 | tf_op jit(solution)/shard_map/pallas_call | solution.py:43
  78.0 3.7 %collective-permute-start.11 = (bf16[256,128]{1,0:T(8,128)(2,1)S(1)}, bf16[256,128]{1,0:T(8,128)(2,1)S(1)}, u32[]{:S(2)}, u32[]{:S(2)}) collective-permute-start(bf16[256,128]{1,0:T(8,128)(2,1)S(1)} %get-tuple-element.75), channel_id=1, source_target_pairs={{0,1},{1,0},{2,3},{3,2},{4,5},{5,4},{6,7},{7,6},{8,9},{9,8},{10,11... | collective-permute-start | bytes 196616 | tf_op jit(solution)/shard_map/ppermute | solution.py:476
  81.8 2.4 %collective-permute-start.13 = (bf16[256,128]{1,0:T(8,128)(2,1)S(1)}, bf16[256,128]{1,0:T(8,128)(2,1)S(1)}, u32[]{:S(2)}, u32[]{:S(2)}) collective-permute-start(bf16[256,128]{1,0:T(8,128)(2,1)S(1)} %get-tuple-element.77), channel_id=1, source_target_pairs={{0,3},{1,2},{2,1},{3,0},{4,7},{5,6},{6,5},{7,4},{8,11},{9,10},{10,... | collective-permute-start | bytes 196616 | tf_op jit(solution)/shard_map/ppermute | solution.py:476
  85.8 2.4 %shard_map.73.q_ref = bf16[256,1024]{1,0:T(8,128)(2,1)S(1)} custom-call(bf16[4096,1024]{1,0:T(8,128)(2,1)S(1)} %get-tuple-element.50.w_ref, bf16[256,1024]{1,0:T(8,128)(2,1)S(1)} %get-tuple-element.51.refs_0_, bf16[512,1024]{1,0:T(8,128)(2,1)S(1)} %collective-permute-done.refs_1_, bf16[256,1024]{1,0:T(8,128)(2,1)S(1)} %collective-permute-done.1.refs_2_.refs_0_, ...), custom_call_target="tpu_custom_call" | custom-call | flops 2147483648 | bytes 10485760 | tf_op jit(solution)/shard_map/pallas_call | solution.py:43
  92.4 5.9 %collective-permute-done.21.refs_1_ = bf16[256,512]{1,0:T(8,128)(2,1)S(1)} collective-permute-done((bf16[256,512]{1,0:T(8,128)(2,1)S(1)}, bf16[256,512]{1,0:T(8,128)(2,1)S(1)}, u32[]{:S(2)}, u32[]{:S(2)}) %collective-permute-start.21) | collective-permute-done | bytes 262176 | tf_op jit(solution)/shard_map/ppermute | solution.py:457
  98.3 5.6 %collective-permute-done.33.refs_4_ = bf16[256,512]{1,0:T(8,128)(2,1)S(1)} collective-permute-done((bf16[256,512]{1,0:T(8,128)(2,1)S(1)}, bf16[256,512]{1,0:T(8,128)(2,1)S(1)}, u32[]{:S(2)}, u32[]{:S(2)}) %collective-permute-start.33) | collective-permute-done | bytes 262176 | tf_op jit(solution)/shard_map/ppermute | solution.py:457
  104.4 4.2 %collective-permute-done.14.refs_0_ = bf16[256,512]{1,0:T(8,128)(2,1)S(1)} collective-permute-done((bf16[256,512]{1,0:T(8,128)(2,1)S(1)}, bf16[256,512]{1,0:T(8,128)(2,1)S(1)}, u32[]{:S(2)}, u32[]{:S(2)}) %collective-permute-start.14) | collective-permute-done | bytes 262176 | tf_op jit(solution)/shard_map/ppermute | solution.py:457
  110.7 3.1 %out_projection.6.refs_3_ = bf16[512,1024]{1,0:T(8,128)(2,1)} custom-call(bf16[4096,1024]{1,0:T(8,128)(2,1)S(1)} %bitcast.2, bf16[256,512]{1,0:T(8,128)(2,1)S(1)} %shard_map.90.refs_0_, bf16[256,512]{1,0:T(8,128)(2,1)S(1)} %shard_map.91.refs_1_, bf16[256,512]{1,0:T(8,128)(2,1)S(1)} %collective-permute-done.31.refs_2_, ...), custom_call_target="tpu_custom_call" | custom-call | flops 2147483648 | bytes 11010048 | tf_op jit(solution)/shard_map/out_projection/pallas_call | solution.py:438
  (80 shorter events, 29.0 us)
Async XLA Ops:
  0.0 28.1 %collective-permute-start = (bf16[512,1024]{1,0:T(8,128)(2,1)}, bf16[512,1024]{1,0:T(8,128)(2,1)S(1)}, u32[]{:S(2)}, u32[]{:S(2)}) collective-permute-start(bf16[512,1024]{1,0:T(8,128)(2,1)} %x_ref.1), channel_id=1, source_target_pairs={{0,4},{4,0},{8,12},{12,8},{1,5},{5,1},{9,13},{13,9},{2,6},{6,2},{1... | collective-permute-start | bytes 3145736 | tf_op jit(solution)/shard_map/ppermute | solution.py:462
  1.7 15.3 %collective-permute-start.3 = (bf16[256,1024]{1,0:T(8,128)(2,1)S(1)}, bf16[256,1024]{1,0:T(8,128)(2,1)S(1)}, u32[]{:S(2)}, u32[]{:S(2)}) collective-permute-start(bf16[256,1024]{1,0:T(8,128)(2,1)S(1)} %get-tuple-element.64.refs_0_), channel_id=1, source_target_pairs={{0,8},{4,12},{8,0},{12,4},{1,9},{5,13},{9,1},{13,5},{2,10},{6,14},... | collective-permute-start | bytes 1572872 | tf_op jit(solution)/shard_map/ppermute | solution.py:457
  4.3 23.8 %collective-permute-start.1 = (bf16[256,1024]{1,0:T(8,128)(2,1)S(1)}, bf16[256,1024]{1,0:T(8,128)(2,1)S(1)}, u32[]{:S(2)}, u32[]{:S(2)}) collective-permute-start(bf16[256,1024]{1,0:T(8,128)(2,1)S(1)} %get-tuple-element.51.refs_0_), channel_id=1, source_target_pairs={{0,8},{4,12},{8,0},{12,4},{1,9},{5,13},{9,1},{13,5},{2,10},{6,14},... | collective-permute-start | bytes 1572872 | tf_op jit(solution)/shard_map/ppermute | solution.py:457
  17.1 14.8 %collective-permute-start.4 = (bf16[256,1024]{1,0:T(8,128)(2,1)S(1)}, bf16[256,1024]{1,0:T(8,128)(2,1)S(1)}, u32[]{:S(2)}, u32[]{:S(2)}) collective-permute-start(bf16[256,1024]{1,0:T(8,128)(2,1)S(1)} %collective-permute-done.3.refs_0_.refs_2_), channel_id=1, source_target_pairs={{0,4},{4,0},{8,12},{12,8},{1,5},{5,1},{9,13},{13,9},{2,6},{6,2},{1... | collective-permute-start | bytes 1572872 | tf_op jit(solution)/shard_map/ppermute | solution.py:462
  28.1 13.7 %collective-permute-start.2 = (bf16[256,1024]{1,0:T(8,128)(2,1)S(1)}, bf16[256,1024]{1,0:T(8,128)(2,1)S(1)}, u32[]{:S(2)}, u32[]{:S(2)}) collective-permute-start(bf16[256,1024]{1,0:T(8,128)(2,1)S(1)} %collective-permute-done.1.refs_2_.refs_0_), channel_id=1, source_target_pairs={{0,4},{4,0},{8,12},{12,8},{1,5},{5,1},{9,13},{13,9},{2,6},{6,2},{1... | collective-permute-start | bytes 1572872 | tf_op jit(solution)/shard_map/ppermute | solution.py:462
  32.7 14.3 %collective-permute-start.6 = (bf16[256,256]{1,0:T(8,128)(2,1)S(1)}, bf16[256,256]{1,0:T(8,128)(2,1)S(1)}, u32[]{:S(2)}, u32[]{:S(2)}) collective-permute-start(bf16[256,256]{1,0:T(8,128)(2,1)S(1)} %get-tuple-element.71.refs_2_), channel_id=1, source_target_pairs={{0,2},{1,3},{2,0},{3,1},{4,6},{5,7},{6,4},{7,5},{8,10},{9,11},{10,... | collective-permute-start | bytes 393224 | tf_op jit(solution)/shard_map/ppermute | solution.py:476
  35.5 13.4 %collective-permute-start.7 = (bf16[256,256]{1,0:T(8,128)(2,1)S(1)}, bf16[256,256]{1,0:T(8,128)(2,1)S(1)}, u32[]{:S(2)}, u32[]{:S(2)}) collective-permute-start(bf16[256,256]{1,0:T(8,128)(2,1)S(1)} %get-tuple-element.72.refs_3_), channel_id=1, source_target_pairs={{0,3},{1,2},{2,1},{3,0},{4,7},{5,6},{6,5},{7,4},{8,11},{9,10},{10,... | collective-permute-start | bytes 393224 | tf_op jit(solution)/shard_map/ppermute | solution.py:476
  37.7 13.9 %collective-permute-start.5 = (bf16[256,256]{1,0:T(8,128)(2,1)S(1)}, bf16[256,256]{1,0:T(8,128)(2,1)S(1)}, u32[]{:S(2)}, u32[]{:S(2)}) collective-permute-start(bf16[256,256]{1,0:T(8,128)(2,1)S(1)} %get-tuple-element.70.refs_1_), channel_id=1, source_target_pairs={{0,1},{1,0},{2,3},{3,2},{4,5},{5,4},{6,7},{7,6},{8,9},{9,8},{10,11... | collective-permute-start | bytes 393224 | tf_op jit(solution)/shard_map/ppermute | solution.py:476
  42.6 12.1 %collective-permute-start.8 = (bf16[256,256]{1,0:T(8,128)(2,1)S(1)}, bf16[256,256]{1,0:T(8,128)(2,1)S(1)}, u32[]{:S(2)}, u32[]{:S(2)}) collective-permute-start(bf16[256,256]{1,0:T(8,128)(2,1)S(1)} %get-tuple-element.58.refs_1_), channel_id=1, source_target_pairs={{0,1},{1,0},{2,3},{3,2},{4,5},{5,4},{6,7},{7,6},{8,9},{9,8},{10,11... | collective-permute-start | bytes 393224 | tf_op jit(solution)/shard_map/ppermute | solution.py:476
  49.0 14.9 %collective-permute-start.9 = (bf16[256,128]{1,0:T(8,128)(2,1)S(1)}, bf16[256,128]{1,0:T(8,128)(2,1)S(1)}, u32[]{:S(2)}, u32[]{:S(2)}) collective-permute-start(bf16[256,128]{1,0:T(8,128)(2,1)S(1)} %get-tuple-element.59.refs_2_), channel_id=1, source_target_pairs={{0,2},{1,3},{2,0},{3,1},{4,6},{5,7},{6,4},{7,5},{8,10},{9,11},{10,... | collective-permute-start | bytes 196616 | tf_op jit(solution)/shard_map/ppermute | solution.py:476
  51.6 12.8 %collective-permute-start.10 = (bf16[256,128]{1,0:T(8,128)(2,1)S(1)}, bf16[256,128]{1,0:T(8,128)(2,1)S(1)}, u32[]{:S(2)}, u32[]{:S(2)}) collective-permute-start(bf16[256,128]{1,0:T(8,128)(2,1)S(1)} %get-tuple-element.60.refs_3_), channel_id=1, source_target_pairs={{0,3},{1,2},{2,1},{3,0},{4,7},{5,6},{6,5},{7,4},{8,11},{9,10},{10,... | collective-permute-start | bytes 196616 | tf_op jit(solution)/shard_map/ppermute | solution.py:476
  60.0 9.9 %collective-permute-start.29 = (bf16[256,128]{1,0:T(8,128)(2,1)S(1)}, bf16[256,128]{1,0:T(8,128)(2,1)S(1)}, u32[]{:S(2)}, u32[]{:S(2)}) collective-permute-start(bf16[256,128]{1,0:T(8,128)(2,1)S(1)} %get-tuple-element.91), channel_id=1, source_target_pairs={{0,2},{1,3},{2,0},{3,1},{4,6},{5,7},{6,4},{7,5},{8,10},{9,11},{10,... | collective-permute-start | bytes 196616 | tf_op jit(solution)/shard_map/ppermute | solution.py:476
  64.3 13.7 %collective-permute-start.19 = (bf16[256,128]{1,0:T(8,128)(2,1)S(1)}, bf16[256,128]{1,0:T(8,128)(2,1)S(1)}, u32[]{:S(2)}, u32[]{:S(2)}) collective-permute-start(bf16[256,128]{1,0:T(8,128)(2,1)S(1)} %get-tuple-element.83), channel_id=1, source_target_pairs={{0,2},{1,3},{2,0},{3,1},{4,6},{5,7},{6,4},{7,5},{8,10},{9,11},{10,... | collective-permute-start | bytes 196616 | tf_op jit(solution)/shard_map/ppermute | solution.py:476
  67.0 14.8 %collective-permute-start.20 = (bf16[256,128]{1,0:T(8,128)(2,1)S(1)}, bf16[256,128]{1,0:T(8,128)(2,1)S(1)}, u32[]{:S(2)}, u32[]{:S(2)}) collective-permute-start(bf16[256,128]{1,0:T(8,128)(2,1)S(1)} %get-tuple-element.84), channel_id=1, source_target_pairs={{0,3},{1,2},{2,1},{3,0},{4,7},{5,6},{6,5},{7,4},{8,11},{9,10},{10,... | collective-permute-start | bytes 196616 | tf_op jit(solution)/shard_map/ppermute | solution.py:476
  69.3 12.5 %collective-permute-start.25 = (bf16[256,128]{1,0:T(8,128)(2,1)S(1)}, bf16[256,128]{1,0:T(8,128)(2,1)S(1)}, u32[]{:S(2)}, u32[]{:S(2)}) collective-permute-start(bf16[256,128]{1,0:T(8,128)(2,1)S(1)} %get-tuple-element.86), channel_id=1, source_target_pairs={{0,1},{1,0},{2,3},{3,2},{4,5},{5,4},{6,7},{7,6},{8,9},{9,8},{10,11... | collective-permute-start | bytes 196616 | tf_op jit(solution)/shard_map/ppermute | solution.py:476
  70.0 14.3 %collective-permute-start.26 = (bf16[256,128]{1,0:T(8,128)(2,1)S(1)}, bf16[256,128]{1,0:T(8,128)(2,1)S(1)}, u32[]{:S(2)}, u32[]{:S(2)}) collective-permute-start(bf16[256,128]{1,0:T(8,128)(2,1)S(1)} %get-tuple-element.87), channel_id=1, source_target_pairs={{0,2},{1,3},{2,0},{3,1},{4,6},{5,7},{6,4},{7,5},{8,10},{9,11},{10,... | collective-permute-start | bytes 196616 | tf_op jit(solution)/shard_map/ppermute | solution.py:476
  71.4 14.3 %collective-permute-start.27 = (bf16[256,128]{1,0:T(8,128)(2,1)S(1)}, bf16[256,128]{1,0:T(8,128)(2,1)S(1)}, u32[]{:S(2)}, u32[]{:S(2)}) collective-permute-start(bf16[256,128]{1,0:T(8,128)(2,1)S(1)} %get-tuple-element.88), channel_id=1, source_target_pairs={{0,3},{1,2},{2,1},{3,0},{4,7},{5,6},{6,5},{7,4},{8,11},{9,10},{10,... | collective-permute-start | bytes 196616 | tf_op jit(solution)/shard_map/ppermute | solution.py:476
  78.0 10.5 %collective-permute-start.11 = (bf16[256,128]{1,0:T(8,128)(2,1)S(1)}, bf16[256,128]{1,0:T(8,128)(2,1)S(1)}, u32[]{:S(2)}, u32[]{:S(2)}) collective-permute-start(bf16[256,128]{1,0:T(8,128)(2,1)S(1)} %get-tuple-element.75), channel_id=1, source_target_pairs={{0,1},{1,0},{2,3},{3,2},{4,5},{5,4},{6,7},{7,6},{8,9},{9,8},{10,11... | collective-permute-start | bytes 196616 | tf_op jit(solution)/shard_map/ppermute | solution.py:476
  89.6 14.3 %collective-permute-start.33 = (bf16[256,512]{1,0:T(8,128)(2,1)S(1)}, bf16[256,512]{1,0:T(8,128)(2,1)S(1)}, u32[]{:S(2)}, u32[]{:S(2)}) collective-permute-start(bf16[256,512]{1,0:T(8,128)(2,1)S(1)} %shard_map.90.refs_0_), channel_id=1, source_target_pairs={{0,8},{4,12},{8,0},{12,4},{1,9},{5,13},{9,1},{13,5},{2,10},{6,14},... | collective-permute-start | bytes 786440 | tf_op jit(solution)/shard_map/ppermute | solution.py:457
  91.3 12.6 %collective-permute-start.23 = (bf16[256,512]{1,0:T(8,128)(2,1)S(1)}, bf16[256,512]{1,0:T(8,128)(2,1)S(1)}, u32[]{:S(2)}, u32[]{:S(2)}) collective-permute-start(bf16[256,512]{1,0:T(8,128)(2,1)S(1)} %shard_map.85.refs_0_), channel_id=1, source_target_pairs={{0,4},{4,0},{8,12},{12,8},{1,5},{5,1},{9,13},{13,9},{2,6},{6,2},{1... | collective-permute-start | bytes 786440 | tf_op jit(solution)/shard_map/ppermute | solution.py:462
  91.3 17.3 %collective-permute-start.14 = (bf16[256,512]{1,0:T(8,128)(2,1)S(1)}, bf16[256,512]{1,0:T(8,128)(2,1)S(1)}, u32[]{:S(2)}, u32[]{:S(2)}) collective-permute-start(bf16[256,512]{1,0:T(8,128)(2,1)S(1)} %shard_map.85.refs_0_), channel_id=1, source_target_pairs={{0,8},{4,12},{8,0},{12,4},{1,9},{5,13},{9,1},{13,5},{2,10},{6,14},... | collective-permute-start | bytes 786440 | tf_op jit(solution)/shard_map/ppermute | solution.py:457
  92.2 18.5 %collective-permute-start.31 = (bf16[256,512]{1,0:T(8,128)(2,1)S(1)}, bf16[256,512]{1,0:T(8,128)(2,1)S(1)}, u32[]{:S(2)}, u32[]{:S(2)}) collective-permute-start(bf16[256,512]{1,0:T(8,128)(2,1)S(1)} %shard_map.90.refs_0_), channel_id=1, source_target_pairs={{0,4},{4,0},{8,12},{12,8},{1,5},{5,1},{9,13},{13,9},{2,6},{6,2},{1... | collective-permute-start | bytes 786440 | tf_op jit(solution)/shard_map/ppermute | solution.py:462
  98.3 12.4 %collective-permute-start.36 = (bf16[256,512]{1,0:T(8,128)(2,1)S(1)}, bf16[256,512]{1,0:T(8,128)(2,1)S(1)}, u32[]{:S(2)}, u32[]{:S(2)}) collective-permute-start(bf16[256,512]{1,0:T(8,128)(2,1)S(1)} %collective-permute-done.34.refs_5_), channel_id=1, source_target_pairs={{0,4},{4,0},{8,12},{12,8},{1,5},{5,1},{9,13},{13,9},{2,6},{6,2},{1... | collective-permute-start | bytes 786440 | tf_op jit(solution)/shard_map/ppermute | solution.py:462
  103.9 9.9 %collective-permute-start.22 = (bf16[256,512]{1,0:T(8,128)(2,1)S(1)}, bf16[256,512]{1,0:T(8,128)(2,1)S(1)}, u32[]{:S(2)}, u32[]{:S(2)}) collective-permute-start(bf16[256,512]{1,0:T(8,128)(2,1)S(1)} %collective-permute-done.21.refs_1_), channel_id=1, source_target_pairs={{0,4},{4,0},{8,12},{12,8},{1,5},{5,1},{9,13},{13,9},{2,6},{6,2},{1... | collective-permute-start | bytes 786440 | tf_op jit(solution)/shard_map/ppermute | solution.py:462
  (15 other events, 153.9 us)

commit v9 on v8

--- a/solution.py
+++ b/solution.py
@@ -216,32 +216,34 @@
     )
 
 
-def query_kernel(starts, n_ctx, w_ref, *refs):
-    pieces, out_ref = refs[:-1], refs[-1]
+def query_kernel(which, starts, n_ctx, has_before, w_ref, *refs):
+    pieces, out_ref = refs[: len(which)], refs[-1]
     tokens = out_ref.shape[0]
     depth = pieces[0].shape[1]
     width = out_ref.shape[1] // n_ctx
     me = lax.axis_index("ctx")
-    rows = [rows_at(source, depth) for source in chan_sources()]
+    sources = chan_sources()
     for k in range(n_ctx):
         cols = rows_at(target(me, k, n_ctx), width)
-        acc = None
-        for j, piece in enumerate(pieces):
-            x = piece[starts[j] : starts[j] + tokens, :]
-            a = jnp.dot(x, w_ref[rows[j], cols], preferred_element_type=F32)
+        mine = slice(k * width, (k + 1) * width)
+        acc = refs[len(which)][:, mine] if has_before else None
+        for piece, j, start in zip(pieces, which, starts):
+            x = piece[start : start + tokens, :]
+            a = jnp.dot(x, w_ref[rows_at(sources[j], depth), cols], preferred_element_type=F32)
             acc = a if acc is None else acc + a
-        out_ref[:, k * width : (k + 1) * width] = acc.astype(BF16)
-
-
-def queries(pieces, starts, tokens, w, n_ctx):
-    total, channels = w.shape
+        out_ref[:, mine] = acc.astype(out_ref.dtype)
+
+
+def queries(pieces, which, starts, tokens, w, before, n_ctx, last):
+    channels = w.shape[1]
+    share = len(which) * pieces[0].shape[1]
     return call(
-        functools.partial(query_kernel, tuple(starts), n_ctx),
-        jax.ShapeDtypeStruct((tokens, channels), BF16),
-        [w, *pieces],
+        functools.partial(query_kernel, tuple(which), tuple(starts), n_ctx, before is not None),
+        jax.ShapeDtypeStruct((tokens, channels), BF16 if last else F32),
+        [w, *(pieces[j] for j in which)] + ([] if before is None else [before]),
         6,
-        2 * tokens * total * channels,
-        2 * total * channels + 2 * tokens * total,
+        2 * tokens * share * channels,
+        2 * share * channels + 2 * tokens * share,
     )
 
 
@@ -505,7 +507,12 @@
             some = keys_values(pieces, (last,), (starts[last],), tokens, w_kv, total, n_ctx, slices, cuts)
             made.update({k: some[i * cuts : (i + 1) * cuts] for i, k in enumerate(slices)})
         mixed.append([[made[k][h % len(made[k])] for k in range(n_ctx)] for h in range(PARTS)])
-        query.append(queries(pieces, starts, tokens, w_q, n_ctx))
+        every, before = range(len(pieces)), None
+        if c == 0:
+            before = queries(pieces, every[:2], starts[:2], tokens, w_q, None, n_ctx, False)
+            every = every[2:]
+        left = [starts[j] for j in every]
+        query.append(queries(pieces, every, left, tokens, w_q, before, n_ctx, True))
     even = exchange(mixed[0][0])
     odd = [exchange(mixed[1][0])]
     odd += [odd[0][:2] + exchange(mixed[1][h], 2)[2:] for h in range(1, PARTS)]

time: 116 us -> 114 us (0.983)
  starting transfers between devices: 43.8 us -> 41.8 us
    ppermute x20, starting transfers between devices: 34.9 us -> 33 us  [exchange(): lax.ppermute(parts[k], 'ctx', [(i, target(i, k, n)) for i in range(n)])]
    pallas_call x19 -> x20, Pallas kernels: 23.1 us -> 23.2 us  [call(): pl.pallas_call(kernel, out_shape=out, in_specs=[VMEM] * len(operands), ou...]
  transfers between devices with their start and end apart: 37 -> 37, of which waited for: 7 -> 7; matrix products, arithmetic and copies ran while one was open for 0% -> 0% of each run, Pallas kernels for 33% -> 34%
where the time goes in v9:
time: 114 us
  starting transfers between devices  41.8 us (37%)
  Pallas kernels  39.7 us (35%)
  waiting for transfers between devices  31.5 us (28%)
    ppermute x20, starting transfers between devices, exchange(): lax.ppermute(parts[k], 'ctx', [(i, target(i, k, n)) for i in range(n)])  33 us
    ppermute x6, waiting for transfers between devices, shift(): return lax.ppermute(x, axis, [(i, (i + by) % n) for i in range(n)])  30.7 us
    pallas_call x20, Pallas kernels, call(): pl.pallas_call(kernel, out_shape=out, in_specs=[VMEM] * len(operands), ou...  23.2 us
    pallas_call x1, Pallas kernels, prologue(): pl.pallas_call(functools.partial(prologue_kernel, width), out_shape=out,...  8.73 us
    ppermute x6, starting transfers between devices, shift(): return lax.ppermute(x, axis, [(i, (i + by) % n) for i in range(n)])  6.94 us
    pallas_call x4, Pallas kernels, project_out(): pl.pallas_call(functools.partial(out_kernel, tuple(which), parts, before...  6.55 us
  transfers between devices with their start and end apart: 37, of which 7 were waited for; matrix products, arithmetic and copies ran while one was open for 0% of the time, Pallas kernels for 34%

profile of v9, /device:TPU:0, one launch (start us, length us, event | category | flops | bytes accessed | tf_op | source)
XLA Modules:
  0.0 113.5 jit_solution(14625798601169446727)
XLA Ops:
  1.7 2.6 %collective-permute-start.3 = (bf16[256,1024]{1,0:T(8,128)(2,1)S(1)}, bf16[256,1024]{1,0:T(8,128)(2,1)S(1)}, u32[]{:S(2)}, u32[]{:S(2)}) collective-permute-start(bf16[256,1024]{1,0:T(8,128)(2,1)S(1)} %get-tuple-element.64.refs_0_), channel_id=1, source_target_pairs={{0,8},{4,12},{8,0},{12,4},{1,9},{5,13},{9,1},{13,5},{2,10},{6,14},... | collective-permute-start | bytes 1572872 | tf_op jit(solution)/shard_map/ppermute | solution.py:459
  4.4 12.7 %collective-permute-done.3.refs_0_ = bf16[256,1024]{1,0:T(8,128)(2,1)S(1)} collective-permute-done((bf16[256,1024]{1,0:T(8,128)(2,1)S(1)}, bf16[256,1024]{1,0:T(8,128)(2,1)S(1)}, u32[]{:S(2)}, u32[]{:S(2)}) %collective-permute-start.3) | collective-permute-done | bytes 524320 | tf_op jit(solution)/shard_map/ppermute | solution.py:459
  17.1 8.7 %prologue.1 = (bf16[512,256]{1,0:T(8,128)(2,1)S(1)}, bf16[256,512]{1,0:T(8,128)(2,1)S(1)}, bf16[2,4096,1024]{2,1,0:T(8,128)(2,1)S(1)}, bf16[4096,1024]{1,0:T(8,1...) custom-call(f32[1024]{0:T(1024)} %skip_hbm.1, bf16[512,256]{1,0:T(8,128)(2,1)} %constant.4.clone.fwd_hbm, ...), custom_call_target="tpu_custom_call" | custom-call | flops 536870912 | bytes 30408704 | tf_op jit(solution)/shard_map/prologue/pallas_call | solution.py:152
  25.8 2.3 %collective-permute-done.1.refs_2_.refs_0_ = bf16[256,1024]{1,0:T(8,128)(2,1)S(1)} collective-permute-done((bf16[256,1024]{1,0:T(8,128)(2,1)S(1)}, bf16[256,1024]{1,0:T(8,128)(2,1)S(1)}, u32[]{:S(2)}, u32[]{:S(2)}) %collective-permute-start.1) | collective-permute-done | bytes 524320 | tf_op jit(solution)/shard_map/ppermute | solution.py:459
  28.1 2.4 %shard_map.78 = (f32[256,1024]{1,0:T(8,128)S(1)}, f32[256,1024]{1,0:T(8,128)S(1)}) custom-call(bf16[2,4096,1024]{2,1,0:T(8,128)(2,1)S(1)} %get-tuple-element.52.w_ref, bf16[256,1024]{1,0:T(8,128)(2,1)S(1)} %get-tuple-element.64.refs_0_, bf16[512,1024]{1,0:T(8,128)(2,1)S(1)} %collective-permute-done.refs_1_), custom_call_target="tpu_custom_call" | custom-call | flops 2147483648 | bytes 9437184 | tf_op jit(solution)/shard_map/pallas_call | solution.py:43
  32.7 2.9 %collective-permute-start.6 = (bf16[256,256]{1,0:T(8,128)(2,1)S(1)}, bf16[256,256]{1,0:T(8,128)(2,1)S(1)}, u32[]{:S(2)}, u32[]{:S(2)}) collective-permute-start(bf16[256,256]{1,0:T(8,128)(2,1)S(1)} %get-tuple-element.71.refs_2_), channel_id=1, source_target_pairs={{0,2},{1,3},{2,0},{3,1},{4,6},{5,7},{6,4},{7,5},{8,10},{9,11},{10,... | collective-permute-start | bytes 393224 | tf_op jit(solution)/shard_map/ppermute | solution.py:478
  38.0 2.4 %shard_map.74 = (f32[256,1024]{1,0:T(8,128)S(1)}, f32[256,1024]{1,0:T(8,128)S(1)}) custom-call(bf16[2,4096,1024]{2,1,0:T(8,128)(2,1)S(1)} %get-tuple-element.52.w_ref, bf16[256,1024]{1,0:T(8,128)(2,1)S(1)} %get-tuple-element.51.refs_0_, bf16[512,1024]{1,0:T(8,128)(2,1)S(1)} %collective-permute-done.refs_1_), custom_call_target="tpu_custom_call" | custom-call | flops 2147483648 | bytes 9437184 | tf_op jit(solution)/shard_map/pallas_call | solution.py:43
  42.6 1.8 %collective-permute-start.8 = (bf16[256,256]{1,0:T(8,128)(2,1)S(1)}, bf16[256,256]{1,0:T(8,128)(2,1)S(1)}, u32[]{:S(2)}, u32[]{:S(2)}) collective-permute-start(bf16[256,256]{1,0:T(8,128)(2,1)S(1)} %get-tuple-element.58.refs_1_), channel_id=1, source_target_pairs={{0,1},{1,0},{2,3},{3,2},{4,5},{5,4},{6,7},{7,6},{8,9},{9,8},{10,11... | collective-permute-start | bytes 393224 | tf_op jit(solution)/shard_map/ppermute | solution.py:478
  45.1 1.8 %collective-permute-start.16 = (bf16[256,128]{1,0:T(8,128)(2,1)S(1)}, bf16[256,128]{1,0:T(8,128)(2,1)S(1)}, u32[]{:S(2)}, u32[]{:S(2)}) collective-permute-start(bf16[256,128]{1,0:T(8,128)(2,1)S(1)} %get-tuple-element.78.refs_2_), channel_id=1, source_target_pairs={{0,2},{1,3},{2,0},{3,1},{4,6},{5,7},{6,4},{7,5},{8,10},{9,11},{10,... | collective-permute-start | bytes 196616 | tf_op jit(solution)/shard_map/ppermute | solution.py:478
  46.9 2.0 %collective-permute-start.17 = (bf16[256,128]{1,0:T(8,128)(2,1)S(1)}, bf16[256,128]{1,0:T(8,128)(2,1)S(1)}, u32[]{:S(2)}, u32[]{:S(2)}) collective-permute-start(bf16[256,128]{1,0:T(8,128)(2,1)S(1)} %get-tuple-element.79.refs_3_), channel_id=1, source_target_pairs={{0,3},{1,2},{2,1},{3,0},{4,7},{5,6},{6,5},{7,4},{8,11},{9,10},{10,... | collective-permute-start | bytes 196616 | tf_op jit(solution)/shard_map/ppermute | solution.py:478
  49.0 2.6 %collective-permute-start.9 = (bf16[256,128]{1,0:T(8,128)(2,1)S(1)}, bf16[256,128]{1,0:T(8,128)(2,1)S(1)}, u32[]{:S(2)}, u32[]{:S(2)}) collective-permute-start(bf16[256,128]{1,0:T(8,128)(2,1)S(1)} %get-tuple-element.59.refs_2_), channel_id=1, source_target_pairs={{0,2},{1,3},{2,0},{3,1},{4,6},{5,7},{6,4},{7,5},{8,10},{9,11},{10,... | collective-permute-start | bytes 196616 | tf_op jit(solution)/shard_map/ppermute | solution.py:478
  52.0 2.1 %shard_map.82.sum_ref = f32[8,512,256]{2,1,0:T(8,128)S(1)} custom-call(bf16[512,256]{1,0:T(8,128)(2,1)S(1)} %get-tuple-element.63.fwd_ref, f32[8,512,256]{2,1,0:T(8,128)S(1)} %get-tuple-element.62.g_ref, bf16[256,256]{1,0:T(8,128)(2,1)S(1)} %get-tuple-element.69.refs_0_, bf16[256,256]{1,0:T(8,128)(2,1)S(1)} %collective-permute-done.5.refs_1_, ...), custom_call_target="tpu_custom_call" | custom-call | flops 268435456 | bytes 8388608 | tf_op jit(solution)/shard_map/pallas_call | solution.py:43
  57.2 2.8 %collective-permute-start.18 = (bf16[256,128]{1,0:T(8,128)(2,1)S(1)}, bf16[256,128]{1,0:T(8,128)(2,1)S(1)}, u32[]{:S(2)}, u32[]{:S(2)}) collective-permute-start(bf16[256,128]{1,0:T(8,128)(2,1)S(1)} %get-tuple-element.82), channel_id=1, source_target_pairs={{0,1},{1,0},{2,3},{3,2},{4,5},{5,4},{6,7},{7,6},{8,9},{9,8},{10,11... | collective-permute-start | bytes 196616 | tf_op jit(solution)/shard_map/ppermute | solution.py:478
  60.0 3.9 %collective-permute-start.29 = (bf16[256,128]{1,0:T(8,128)(2,1)S(1)}, bf16[256,128]{1,0:T(8,128)(2,1)S(1)}, u32[]{:S(2)}, u32[]{:S(2)}) collective-permute-start(bf16[256,128]{1,0:T(8,128)(2,1)S(1)} %get-tuple-element.91), channel_id=1, source_target_pairs={{0,2},{1,3},{2,0},{3,1},{4,6},{5,7},{6,4},{7,5},{8,10},{9,11},{10,... | collective-permute-start | bytes 196616 | tf_op jit(solution)/shard_map/ppermute | solution.py:478
  68.3 2.4 %collective-permute-start.20 = (bf16[256,128]{1,0:T(8,128)(2,1)S(1)}, bf16[256,128]{1,0:T(8,128)(2,1)S(1)}, u32[]{:S(2)}, u32[]{:S(2)}) collective-permute-start(bf16[256,128]{1,0:T(8,128)(2,1)S(1)} %get-tuple-element.84), channel_id=1, source_target_pairs={{0,3},{1,2},{2,1},{3,0},{4,7},{5,6},{6,5},{7,4},{8,11},{9,10},{10,... | collective-permute-start | bytes 196616 | tf_op jit(solution)/shard_map/ppermute | solution.py:478
  72.8 2.3 %collective-permute-start.27 = (bf16[256,128]{1,0:T(8,128)(2,1)S(1)}, bf16[256,128]{1,0:T(8,128)(2,1)S(1)}, u32[]{:S(2)}, u32[]{:S(2)}) collective-permute-start(bf16[256,128]{1,0:T(8,128)(2,1)S(1)} %get-tuple-element.88), channel_id=1, source_target_pairs={{0,3},{1,2},{2,1},{3,0},{4,7},{5,6},{6,5},{7,4},{8,11},{9,10},{10,... | collective-permute-start | bytes 196616 | tf_op jit(solution)/shard_map/ppermute | solution.py:478
  77.9 3.8 %collective-permute-start.12 = (bf16[256,128]{1,0:T(8,128)(2,1)S(1)}, bf16[256,128]{1,0:T(8,128)(2,1)S(1)}, u32[]{:S(2)}, u32[]{:S(2)}) collective-permute-start(bf16[256,128]{1,0:T(8,128)(2,1)S(1)} %get-tuple-element.76), channel_id=1, source_target_pairs={{0,2},{1,3},{2,0},{3,1},{4,6},{5,7},{6,4},{7,5},{8,10},{9,11},{10,... | collective-permute-start | bytes 196616 | tf_op jit(solution)/shard_map/ppermute | solution.py:478
  82.4 1.5 %collective-permute-start.34 = (bf16[256,512]{1,0:T(8,128)(2,1)S(1)}, bf16[256,512]{1,0:T(8,128)(2,1)S(1)}, u32[]{:S(2)}, u32[]{:S(2)}) collective-permute-start(bf16[256,512]{1,0:T(8,128)(2,1)S(1)} %shard_map.92.refs_1_), channel_id=1, source_target_pairs={{0,8},{4,12},{8,0},{12,4},{1,9},{5,13},{9,1},{13,5},{2,10},{6,14},... | collective-permute-start | bytes 786440 | tf_op jit(solution)/shard_map/ppermute | solution.py:459
  83.9 2.4 %shard_map.73.q_ref = bf16[256,1024]{1,0:T(8,128)(2,1)S(1)} custom-call(bf16[4096,1024]{1,0:T(8,128)(2,1)S(1)} %get-tuple-element.50.w_ref, bf16[256,1024]{1,0:T(8,128)(2,1)S(1)} %get-tuple-element.51.refs_0_, bf16[512,1024]{1,0:T(8,128)(2,1)S(1)} %collective-permute-done.refs_1_, bf16[256,1024]{1,0:T(8,128)(2,1)S(1)} %collective-permute-done.1.refs_2_.refs_0_, ...), custom_call_target="tpu_custom_call" | custom-call | flops 2147483648 | bytes 10485760 | tf_op jit(solution)/shard_map/pallas_call | solution.py:43
  87.8 1.5 %collective-permute-start.33 = (bf16[256,512]{1,0:T(8,128)(2,1)S(1)}, bf16[256,512]{1,0:T(8,128)(2,1)S(1)}, u32[]{:S(2)}, u32[]{:S(2)}) collective-permute-start(bf16[256,512]{1,0:T(8,128)(2,1)S(1)} %shard_map.91.refs_0_), channel_id=1, source_target_pairs={{0,8},{4,12},{8,0},{12,4},{1,9},{5,13},{9,1},{13,5},{2,10},{6,14},... | collective-permute-start | bytes 786440 | tf_op jit(solution)/shard_map/ppermute | solution.py:459
  90.5 5.9 %collective-permute-done.21.refs_1_ = bf16[256,512]{1,0:T(8,128)(2,1)S(1)} collective-permute-done((bf16[256,512]{1,0:T(8,128)(2,1)S(1)}, bf16[256,512]{1,0:T(8,128)(2,1)S(1)}, u32[]{:S(2)}, u32[]{:S(2)}) %collective-permute-start.21) | collective-permute-done | bytes 262176 | tf_op jit(solution)/shard_map/ppermute | solution.py:459
  96.4 5.6 %collective-permute-done.33.refs_4_ = bf16[256,512]{1,0:T(8,128)(2,1)S(1)} collective-permute-done((bf16[256,512]{1,0:T(8,128)(2,1)S(1)}, bf16[256,512]{1,0:T(8,128)(2,1)S(1)}, u32[]{:S(2)}, u32[]{:S(2)}) %collective-permute-start.33) | collective-permute-done | bytes 262176 | tf_op jit(solution)/shard_map/ppermute | solution.py:459
  102.5 4.2 %collective-permute-done.14.refs_0_ = bf16[256,512]{1,0:T(8,128)(2,1)S(1)} collective-permute-done((bf16[256,512]{1,0:T(8,128)(2,1)S(1)}, bf16[256,512]{1,0:T(8,128)(2,1)S(1)}, u32[]{:S(2)}, u32[]{:S(2)}) %collective-permute-start.14) | collective-permute-done | bytes 262176 | tf_op jit(solution)/shard_map/ppermute | solution.py:459
  108.8 3.1 %out_projection.6.refs_3_ = bf16[512,1024]{1,0:T(8,128)(2,1)} custom-call(bf16[4096,1024]{1,0:T(8,128)(2,1)S(1)} %bitcast.2, bf16[256,512]{1,0:T(8,128)(2,1)S(1)} %shard_map.91.refs_0_, bf16[256,512]{1,0:T(8,128)(2,1)S(1)} %shard_map.92.refs_1_, bf16[256,512]{1,0:T(8,128)(2,1)S(1)} %collective-permute-done.31.refs_2_, ...), custom_call_target="tpu_custom_call" | custom-call | flops 2147483648 | bytes 11010048 | tf_op jit(solution)/shard_map/out_projection/pallas_call | solution.py:440
  (81 shorter events, 29.3 us)
Async XLA Ops:
  0.0 28.1 %collective-permute-start = (bf16[512,1024]{1,0:T(8,128)(2,1)}, bf16[512,1024]{1,0:T(8,128)(2,1)S(1)}, u32[]{:S(2)}, u32[]{:S(2)}) collective-permute-start(bf16[512,1024]{1,0:T(8,128)(2,1)} %x_ref.1), channel_id=1, source_target_pairs={{0,4},{4,0},{8,12},{12,8},{1,5},{5,1},{9,13},{13,9},{2,6},{6,2},{1... | collective-permute-start | bytes 3145736 | tf_op jit(solution)/shard_map/ppermute | solution.py:464
  1.7 15.3 %collective-permute-start.3 = (bf16[256,1024]{1,0:T(8,128)(2,1)S(1)}, bf16[256,1024]{1,0:T(8,128)(2,1)S(1)}, u32[]{:S(2)}, u32[]{:S(2)}) collective-permute-start(bf16[256,1024]{1,0:T(8,128)(2,1)S(1)} %get-tuple-element.64.refs_0_), channel_id=1, source_target_pairs={{0,8},{4,12},{8,0},{12,4},{1,9},{5,13},{9,1},{13,5},{2,10},{6,14},... | collective-permute-start | bytes 1572872 | tf_op jit(solution)/shard_map/ppermute | solution.py:459
  4.3 23.8 %collective-permute-start.1 = (bf16[256,1024]{1,0:T(8,128)(2,1)S(1)}, bf16[256,1024]{1,0:T(8,128)(2,1)S(1)}, u32[]{:S(2)}, u32[]{:S(2)}) collective-permute-start(bf16[256,1024]{1,0:T(8,128)(2,1)S(1)} %get-tuple-element.51.refs_0_), channel_id=1, source_target_pairs={{0,8},{4,12},{8,0},{12,4},{1,9},{5,13},{9,1},{13,5},{2,10},{6,14},... | collective-permute-start | bytes 1572872 | tf_op jit(solution)/shard_map/ppermute | solution.py:459
  17.1 14.8 %collective-permute-start.4 = (bf16[256,1024]{1,0:T(8,128)(2,1)S(1)}, bf16[256,1024]{1,0:T(8,128)(2,1)S(1)}, u32[]{:S(2)}, u32[]{:S(2)}) collective-permute-start(bf16[256,1024]{1,0:T(8,128)(2,1)S(1)} %collective-permute-done.3.refs_0_), channel_id=1, source_target_pairs={{0,4},{4,0},{8,12},{12,8},{1,5},{5,1},{9,13},{13,9},{2,6},{6,2},{1... | collective-permute-start | bytes 1572872 | tf_op jit(solution)/shard_map/ppermute | solution.py:464
  28.1 13.7 %collective-permute-start.2 = (bf16[256,1024]{1,0:T(8,128)(2,1)S(1)}, bf16[256,1024]{1,0:T(8,128)(2,1)S(1)}, u32[]{:S(2)}, u32[]{:S(2)}) collective-permute-start(bf16[256,1024]{1,0:T(8,128)(2,1)S(1)} %collective-permute-done.1.refs_2_.refs_0_), channel_id=1, source_target_pairs={{0,4},{4,0},{8,12},{12,8},{1,5},{5,1},{9,13},{13,9},{2,6},{6,2},{1... | collective-permute-start | bytes 1572872 | tf_op jit(solution)/shard_map/ppermute | solution.py:464
  32.7 14.3 %collective-permute-start.6 = (bf16[256,256]{1,0:T(8,128)(2,1)S(1)}, bf16[256,256]{1,0:T(8,128)(2,1)S(1)}, u32[]{:S(2)}, u32[]{:S(2)}) collective-permute-start(bf16[256,256]{1,0:T(8,128)(2,1)S(1)} %get-tuple-element.71.refs_2_), channel_id=1, source_target_pairs={{0,2},{1,3},{2,0},{3,1},{4,6},{5,7},{6,4},{7,5},{8,10},{9,11},{10,... | collective-permute-start | bytes 393224 | tf_op jit(solution)/shard_map/ppermute | solution.py:478
  35.5 13.4 %collective-permute-start.7 = (bf16[256,256]{1,0:T(8,128)(2,1)S(1)}, bf16[256,256]{1,0:T(8,128)(2,1)S(1)}, u32[]{:S(2)}, u32[]{:S(2)}) collective-permute-start(bf16[256,256]{1,0:T(8,128)(2,1)S(1)} %get-tuple-element.72.refs_3_), channel_id=1, source_target_pairs={{0,3},{1,2},{2,1},{3,0},{4,7},{5,6},{6,5},{7,4},{8,11},{9,10},{10,... | collective-permute-start | bytes 393224 | tf_op jit(solution)/shard_map/ppermute | solution.py:478
  37.7 13.9 %collective-permute-start.5 = (bf16[256,256]{1,0:T(8,128)(2,1)S(1)}, bf16[256,256]{1,0:T(8,128)(2,1)S(1)}, u32[]{:S(2)}, u32[]{:S(2)}) collective-permute-start(bf16[256,256]{1,0:T(8,128)(2,1)S(1)} %get-tuple-element.70.refs_1_), channel_id=1, source_target_pairs={{0,1},{1,0},{2,3},{3,2},{4,5},{5,4},{6,7},{7,6},{8,9},{9,8},{10,11... | collective-permute-start | bytes 393224 | tf_op jit(solution)/shard_map/ppermute | solution.py:478
  42.6 12.1 %collective-permute-start.8 = (bf16[256,256]{1,0:T(8,128)(2,1)S(1)}, bf16[256,256]{1,0:T(8,128)(2,1)S(1)}, u32[]{:S(2)}, u32[]{:S(2)}) collective-permute-start(bf16[256,256]{1,0:T(8,128)(2,1)S(1)} %get-tuple-element.58.refs_1_), channel_id=1, source_target_pairs={{0,1},{1,0},{2,3},{3,2},{4,5},{5,4},{6,7},{7,6},{8,9},{9,8},{10,11... | collective-permute-start | bytes 393224 | tf_op jit(solution)/shard_map/ppermute | solution.py:478
  49.0 14.9 %collective-permute-start.9 = (bf16[256,128]{1,0:T(8,128)(2,1)S(1)}, bf16[256,128]{1,0:T(8,128)(2,1)S(1)}, u32[]{:S(2)}, u32[]{:S(2)}) collective-permute-start(bf16[256,128]{1,0:T(8,128)(2,1)S(1)} %get-tuple-element.59.refs_2_), channel_id=1, source_target_pairs={{0,2},{1,3},{2,0},{3,1},{4,6},{5,7},{6,4},{7,5},{8,10},{9,11},{10,... | collective-permute-start | bytes 196616 | tf_op jit(solution)/shard_map/ppermute | solution.py:478
  51.6 14.1 %collective-permute-start.10 = (bf16[256,128]{1,0:T(8,128)(2,1)S(1)}, bf16[256,128]{1,0:T(8,128)(2,1)S(1)}, u32[]{:S(2)}, u32[]{:S(2)}) collective-permute-start(bf16[256,128]{1,0:T(8,128)(2,1)S(1)} %get-tuple-element.60.refs_3_), channel_id=1, source_target_pairs={{0,3},{1,2},{2,1},{3,0},{4,7},{5,6},{6,5},{7,4},{8,11},{9,10},{10,... | collective-permute-start | bytes 196616 | tf_op jit(solution)/shard_map/ppermute | solution.py:478
  57.2 11.1 %collective-permute-start.18 = (bf16[256,128]{1,0:T(8,128)(2,1)S(1)}, bf16[256,128]{1,0:T(8,128)(2,1)S(1)}, u32[]{:S(2)}, u32[]{:S(2)}) collective-permute-start(bf16[256,128]{1,0:T(8,128)(2,1)S(1)} %get-tuple-element.82), channel_id=1, source_target_pairs={{0,1},{1,0},{2,3},{3,2},{4,5},{5,4},{6,7},{7,6},{8,9},{9,8},{10,11... | collective-permute-start | bytes 196616 | tf_op jit(solution)/shard_map/ppermute | solution.py:478
  60.0 10.8 %collective-permute-start.28 = (bf16[256,128]{1,0:T(8,128)(2,1)S(1)}, bf16[256,128]{1,0:T(8,128)(2,1)S(1)}, u32[]{:S(2)}, u32[]{:S(2)}) collective-permute-start(bf16[256,128]{1,0:T(8,128)(2,1)S(1)} %get-tuple-element.90), channel_id=1, source_target_pairs={{0,1},{1,0},{2,3},{3,2},{4,5},{5,4},{6,7},{7,6},{8,9},{9,8},{10,11... | collective-permute-start | bytes 196616 | tf_op jit(solution)/shard_map/ppermute | solution.py:478
  60.0 11.3 %collective-permute-start.29 = (bf16[256,128]{1,0:T(8,128)(2,1)S(1)}, bf16[256,128]{1,0:T(8,128)(2,1)S(1)}, u32[]{:S(2)}, u32[]{:S(2)}) collective-permute-start(bf16[256,128]{1,0:T(8,128)(2,1)S(1)} %get-tuple-element.91), channel_id=1, source_target_pairs={{0,2},{1,3},{2,0},{3,1},{4,6},{5,7},{6,4},{7,5},{8,10},{9,11},{10,... | collective-permute-start | bytes 196616 | tf_op jit(solution)/shard_map/ppermute | solution.py:478
  65.7 12.0 %collective-permute-start.19 = (bf16[256,128]{1,0:T(8,128)(2,1)S(1)}, bf16[256,128]{1,0:T(8,128)(2,1)S(1)}, u32[]{:S(2)}, u32[]{:S(2)}) collective-permute-start(bf16[256,128]{1,0:T(8,128)(2,1)S(1)} %get-tuple-element.83), channel_id=1, source_target_pairs={{0,2},{1,3},{2,0},{3,1},{4,6},{5,7},{6,4},{7,5},{8,10},{9,11},{10,... | collective-permute-start | bytes 196616 | tf_op jit(solution)/shard_map/ppermute | solution.py:478
  70.7 11.0 %collective-permute-start.25 = (bf16[256,128]{1,0:T(8,128)(2,1)S(1)}, bf16[256,128]{1,0:T(8,128)(2,1)S(1)}, u32[]{:S(2)}, u32[]{:S(2)}) collective-permute-start(bf16[256,128]{1,0:T(8,128)(2,1)S(1)} %get-tuple-element.86), channel_id=1, source_target_pairs={{0,1},{1,0},{2,3},{3,2},{4,5},{5,4},{6,7},{7,6},{8,9},{9,8},{10,11... | collective-permute-start | bytes 196616 | tf_op jit(solution)/shard_map/ppermute | solution.py:478
  71.3 11.0 %collective-permute-start.26 = (bf16[256,128]{1,0:T(8,128)(2,1)S(1)}, bf16[256,128]{1,0:T(8,128)(2,1)S(1)}, u32[]{:S(2)}, u32[]{:S(2)}) collective-permute-start(bf16[256,128]{1,0:T(8,128)(2,1)S(1)} %get-tuple-element.87), channel_id=1, source_target_pairs={{0,2},{1,3},{2,0},{3,1},{4,6},{5,7},{6,4},{7,5},{8,10},{9,11},{10,... | collective-permute-start | bytes 196616 | tf_op jit(solution)/shard_map/ppermute | solution.py:478
  72.8 11.1 %collective-permute-start.27 = (bf16[256,128]{1,0:T(8,128)(2,1)S(1)}, bf16[256,128]{1,0:T(8,128)(2,1)S(1)}, u32[]{:S(2)}, u32[]{:S(2)}) collective-permute-start(bf16[256,128]{1,0:T(8,128)(2,1)S(1)} %get-tuple-element.88), channel_id=1, source_target_pairs={{0,3},{1,2},{2,1},{3,0},{4,7},{5,6},{6,5},{7,4},{8,11},{9,10},{10,... | collective-permute-start | bytes 196616 | tf_op jit(solution)/shard_map/ppermute | solution.py:478
  87.8 14.2 %collective-permute-start.33 = (bf16[256,512]{1,0:T(8,128)(2,1)S(1)}, bf16[256,512]{1,0:T(8,128)(2,1)S(1)}, u32[]{:S(2)}, u32[]{:S(2)}) collective-permute-start(bf16[256,512]{1,0:T(8,128)(2,1)S(1)} %shard_map.91.refs_0_), channel_id=1, source_target_pairs={{0,8},{4,12},{8,0},{12,4},{1,9},{5,13},{9,1},{13,5},{2,10},{6,14},... | collective-permute-start | bytes 786440 | tf_op jit(solution)/shard_map/ppermute | solution.py:459
  89.5 12.6 %collective-permute-start.23 = (bf16[256,512]{1,0:T(8,128)(2,1)S(1)}, bf16[256,512]{1,0:T(8,128)(2,1)S(1)}, u32[]{:S(2)}, u32[]{:S(2)}) collective-permute-start(bf16[256,512]{1,0:T(8,128)(2,1)S(1)} %shard_map.85.refs_0_), channel_id=1, source_target_pairs={{0,4},{4,0},{8,12},{12,8},{1,5},{5,1},{9,13},{13,9},{2,6},{6,2},{1... | collective-permute-start | bytes 786440 | tf_op jit(solution)/shard_map/ppermute | solution.py:464
  89.5 17.2 %collective-permute-start.14 = (bf16[256,512]{1,0:T(8,128)(2,1)S(1)}, bf16[256,512]{1,0:T(8,128)(2,1)S(1)}, u32[]{:S(2)}, u32[]{:S(2)}) collective-permute-start(bf16[256,512]{1,0:T(8,128)(2,1)S(1)} %shard_map.85.refs_0_), channel_id=1, source_target_pairs={{0,8},{4,12},{8,0},{12,4},{1,9},{5,13},{9,1},{13,5},{2,10},{6,14},... | collective-permute-start | bytes 786440 | tf_op jit(solution)/shard_map/ppermute | solution.py:459
  90.3 18.5 %collective-permute-start.31 = (bf16[256,512]{1,0:T(8,128)(2,1)S(1)}, bf16[256,512]{1,0:T(8,128)(2,1)S(1)}, u32[]{:S(2)}, u32[]{:S(2)}) collective-permute-start(bf16[256,512]{1,0:T(8,128)(2,1)S(1)} %shard_map.91.refs_0_), channel_id=1, source_target_pairs={{0,4},{4,0},{8,12},{12,8},{1,5},{5,1},{9,13},{13,9},{2,6},{6,2},{1... | collective-permute-start | bytes 786440 | tf_op jit(solution)/shard_map/ppermute | solution.py:464
  96.4 12.4 %collective-permute-start.36 = (bf16[256,512]{1,0:T(8,128)(2,1)S(1)}, bf16[256,512]{1,0:T(8,128)(2,1)S(1)}, u32[]{:S(2)}, u32[]{:S(2)}) collective-permute-start(bf16[256,512]{1,0:T(8,128)(2,1)S(1)} %collective-permute-done.34.refs_5_), channel_id=1, source_target_pairs={{0,4},{4,0},{8,12},{12,8},{1,5},{5,1},{9,13},{13,9},{2,6},{6,2},{1... | collective-permute-start | bytes 786440 | tf_op jit(solution)/shard_map/ppermute | solution.py:464
  102.0 9.9 %collective-permute-start.22 = (bf16[256,512]{1,0:T(8,128)(2,1)S(1)}, bf16[256,512]{1,0:T(8,128)(2,1)S(1)}, u32[]{:S(2)}, u32[]{:S(2)}) collective-permute-start(bf16[256,512]{1,0:T(8,128)(2,1)S(1)} %collective-permute-done.21.refs_1_), channel_id=1, source_target_pairs={{0,4},{4,0},{8,12},{12,8},{1,5},{5,1},{9,13},{13,9},{2,6},{6,2},{1... | collective-permute-start | bytes 786440 | tf_op jit(solution)/shard_map/ppermute | solution.py:464
  (15 other events, 151.8 us)

commit v10 on v9

--- a/solution.py
+++ b/solution.py
@@ -317,7 +317,12 @@
 
 
 def late_kernel(n_ctx, start, inv_ref, g_ref, sum_ref, x_ref, *refs):
-    outs, y_ref = refs[:-1], refs[-1]
+    others, outs, y_ref = refs[: -n_ctx - 1], list(refs[-n_ctx - 1 : -1]), refs[-1]
+    share = x_ref.shape[2]
+    for h, other in enumerate(others):
+        outs[1][:, h * share : (h + 1) * share] = other[...]
+    if others:
+        outs[1] = outs[1].at[:, len(others) * share :]
     blocks, rows, _ = g_ref.shape
     plan = [(b, b // 2, [(b - a, a // 2) for a in range(1, b + 1, 2)]) for b in range(1, blocks, 2)]
     block_products(g_ref, x_ref, sum_ref, y_ref, plan, start, rows // 2)
@@ -352,11 +357,13 @@
             [pltpu.VMEM(some, F32)],
         )
         first.append(made)
+        others = [made[1] for made in second] if h == parts - 1 else []
+        together = jax.ShapeDtypeStruct((rows // 2, share * (1 + len(others))), BF16)
         second.append(
             call(
                 functools.partial(late_kernel, n_ctx, h * share),
-                [piece] * n_ctx,
-                [inverse, spectra, sums, x],
+                [piece, together] + [piece] * (n_ctx - 2),
+                [inverse, spectra, sums, x, *others],
                 6,
                 flops // parts,
                 moved // parts,
@@ -374,7 +381,7 @@
         skip = skip_ref[pl.ds(target(me, m, n_ctx), 1), :][:, start : start + share]
         query = q_ref[:, m * width + start : m * width + start + share].astype(F32)
         source = part_of(mixed[m], start, share).astype(F32)
-        total = conv[mirror(m, n_ctx)][...].astype(F32) + skip * source
+        total = part_of(conv[mirror(m, n_ctx)], start, share).astype(F32) + skip * source
         out_ref[:, m * share : (m + 1) * share] = (query * total).astype(BF16)
 
 
@@ -518,10 +525,13 @@
     odd += [odd[0][:2] + exchange(mixed[1][h], 2)[2:] for h in range(1, PARTS)]
     conv = convolve(forward, inverse, spectra, even, odd, n_ctx)
 
+    joint = lax.ppermute(conv[-1][1], "ctx", [(i, target(i, 1, n_ctx)) for i in range(n_ctx)])
     gathered = []
     for r in range(CHUNKS * PARTS):
         c, h = r // PARTS, r % PARTS
-        back = exchange(conv[r])
+        back = exchange(conv[r], 1 if c == 0 else 2)
+        if c > 0:
+            back[1] = joint
         gated = gate(skip, query[c], mixed[c][h], back, h * back[0].shape[1], n_ctx)
         beside = swap_cores(gated)
         gathered.append([gated, beside, *gather_far(gated)])

time: 114 us -> 113 us (level)
    ppermute x20 -> x18, starting transfers between devices: 33 us -> 29.8 us  [exchange(): lax.ppermute(parts[k], 'ctx', [(i, target(i, k, n)) for i in range(n)])]
    ppermute x0 -> x1, starting transfers between devices: none -> 1.61 us  [layer_body(): lax.ppermute(conv[-1][1], 'ctx', [(i, target(i, 1, n_ctx)) for i in range...]
  transfers between devices with their start and end apart: 37 -> 36, of which waited for: 7 -> 7; matrix products, arithmetic and copies ran while one was open for 0% -> 0% of each run, Pallas kernels for 34% -> 34%
where the time goes in v10:
time: 113 us
  starting transfers between devices  40.7 us (36%)
  Pallas kernels  39.8 us (35%)
  waiting for transfers between devices  31.9 us (28%)
    ppermute x6, waiting for transfers between devices, shift(): return lax.ppermute(x, axis, [(i, (i + by) % n) for i in range(n)])  30 us
    ppermute x18, starting transfers between devices, exchange(): lax.ppermute(parts[k], 'ctx', [(i, target(i, k, n)) for i in range(n)])  29.8 us
    pallas_call x20, Pallas kernels, call(): pl.pallas_call(kernel, out_shape=out, in_specs=[VMEM] * len(operands), ou...  23.3 us
    pallas_call x1, Pallas kernels, prologue(): pl.pallas_call(functools.partial(prologue_kernel, width), out_shape=out,...  8.73 us
    ppermute x6, starting transfers between devices, shift(): return lax.ppermute(x, axis, [(i, (i + by) % n) for i in range(n)])  7.67 us
    pallas_call x4, Pallas kernels, project_out(): pl.pallas_call(functools.partial(out_kernel, tuple(which), parts, before...  6.55 us
  transfers between devices with their start and end apart: 36, of which 7 were waited for; matrix products, arithmetic and copies ran while one was open for 0% of the time, Pallas kernels for 34%

profile of v10, /device:TPU:0, one launch (start us, length us, event | category | flops | bytes accessed | tf_op | source)
XLA Modules:
  0.0 112.9 jit_solution(7502683002868683288)
XLA Ops:
  1.7 2.6 %collective-permute-start.3 = (bf16[256,1024]{1,0:T(8,128)(2,1)S(1)}, bf16[256,1024]{1,0:T(8,128)(2,1)S(1)}, u32[]{:S(2)}, u32[]{:S(2)}) collective-permute-start(bf16[256,1024]{1,0:T(8,128)(2,1)S(1)} %get-tuple-element.64.refs_0_), channel_id=1, source_target_pairs={{0,8},{4,12},{8,0},{12,4},{1,9},{5,13},{9,1},{13,5},{2,10},{6,14},... | collective-permute-start | bytes 1572872 | tf_op jit(solution)/shard_map/ppermute | solution.py:466
  4.4 12.7 %collective-permute-done.3.refs_0_ = bf16[256,1024]{1,0:T(8,128)(2,1)S(1)} collective-permute-done((bf16[256,1024]{1,0:T(8,128)(2,1)S(1)}, bf16[256,1024]{1,0:T(8,128)(2,1)S(1)}, u32[]{:S(2)}, u32[]{:S(2)}) %collective-permute-start.3) | collective-permute-done | bytes 524320 | tf_op jit(solution)/shard_map/ppermute | solution.py:466
  17.1 8.7 %prologue.1 = (bf16[512,256]{1,0:T(8,128)(2,1)S(1)}, bf16[256,512]{1,0:T(8,128)(2,1)S(1)}, bf16[2,4096,1024]{2,1,0:T(8,128)(2,1)S(1)}, bf16[4096,1024]{1,0:T(8,1...) custom-call(f32[1024]{0:T(1024)} %skip_hbm.1, bf16[512,256]{1,0:T(8,128)(2,1)} %constant.4.clone.fwd_hbm, ...), custom_call_target="tpu_custom_call" | custom-call | flops 536870912 | bytes 30408704 | tf_op jit(solution)/shard_map/prologue/pallas_call | solution.py:152
  25.8 2.3 %collective-permute-done.1.refs_2_.refs_0_ = bf16[256,1024]{1,0:T(8,128)(2,1)S(1)} collective-permute-done((bf16[256,1024]{1,0:T(8,128)(2,1)S(1)}, bf16[256,1024]{1,0:T(8,128)(2,1)S(1)}, u32[]{:S(2)}, u32[]{:S(2)}) %collective-permute-start.1) | collective-permute-done | bytes 524320 | tf_op jit(solution)/shard_map/ppermute | solution.py:466
  28.1 2.4 %shard_map.78 = (f32[256,1024]{1,0:T(8,128)S(1)}, f32[256,1024]{1,0:T(8,128)S(1)}) custom-call(bf16[2,4096,1024]{2,1,0:T(8,128)(2,1)S(1)} %get-tuple-element.52.w_ref, bf16[256,1024]{1,0:T(8,128)(2,1)S(1)} %get-tuple-element.64.refs_0_, bf16[512,1024]{1,0:T(8,128)(2,1)S(1)} %collective-permute-done.refs_1_), custom_call_target="tpu_custom_call" | custom-call | flops 2147483648 | bytes 9437184 | tf_op jit(solution)/shard_map/pallas_call | solution.py:43
  32.7 2.9 %collective-permute-start.6 = (bf16[256,256]{1,0:T(8,128)(2,1)S(1)}, bf16[256,256]{1,0:T(8,128)(2,1)S(1)}, u32[]{:S(2)}, u32[]{:S(2)}) collective-permute-start(bf16[256,256]{1,0:T(8,128)(2,1)S(1)} %get-tuple-element.71.refs_2_), channel_id=1, source_target_pairs={{0,2},{1,3},{2,0},{3,1},{4,6},{5,7},{6,4},{7,5},{8,10},{9,11},{10,... | collective-permute-start | bytes 393224 | tf_op jit(solution)/shard_map/ppermute | solution.py:485
  38.0 2.4 %shard_map.74 = (f32[256,1024]{1,0:T(8,128)S(1)}, f32[256,1024]{1,0:T(8,128)S(1)}) custom-call(bf16[2,4096,1024]{2,1,0:T(8,128)(2,1)S(1)} %get-tuple-element.52.w_ref, bf16[256,1024]{1,0:T(8,128)(2,1)S(1)} %get-tuple-element.51.refs_0_, bf16[512,1024]{1,0:T(8,128)(2,1)S(1)} %collective-permute-done.refs_1_), custom_call_target="tpu_custom_call" | custom-call | flops 2147483648 | bytes 9437184 | tf_op jit(solution)/shard_map/pallas_call | solution.py:43
  42.6 1.8 %collective-permute-start.8 = (bf16[256,256]{1,0:T(8,128)(2,1)S(1)}, bf16[256,256]{1,0:T(8,128)(2,1)S(1)}, u32[]{:S(2)}, u32[]{:S(2)}) collective-permute-start(bf16[256,256]{1,0:T(8,128)(2,1)S(1)} %get-tuple-element.58.refs_1_), channel_id=1, source_target_pairs={{0,1},{1,0},{2,3},{3,2},{4,5},{5,4},{6,7},{7,6},{8,9},{9,8},{10,11... | collective-permute-start | bytes 393224 | tf_op jit(solution)/shard_map/ppermute | solution.py:485
  45.1 1.8 %collective-permute-start.11 = (bf16[256,128]{1,0:T(8,128)(2,1)S(1)}, bf16[256,128]{1,0:T(8,128)(2,1)S(1)}, u32[]{:S(2)}, u32[]{:S(2)}) collective-permute-start(bf16[256,128]{1,0:T(8,128)(2,1)S(1)} %get-tuple-element.75.refs_2_), channel_id=1, source_target_pairs={{0,2},{1,3},{2,0},{3,1},{4,6},{5,7},{6,4},{7,5},{8,10},{9,11},{10,... | collective-permute-start | bytes 196616 | tf_op jit(solution)/shard_map/ppermute | solution.py:485
  46.9 2.0 %collective-permute-start.12 = (bf16[256,128]{1,0:T(8,128)(2,1)S(1)}, bf16[256,128]{1,0:T(8,128)(2,1)S(1)}, u32[]{:S(2)}, u32[]{:S(2)}) collective-permute-start(bf16[256,128]{1,0:T(8,128)(2,1)S(1)} %get-tuple-element.76.refs_3_), channel_id=1, source_target_pairs={{0,3},{1,2},{2,1},{3,0},{4,7},{5,6},{6,5},{7,4},{8,11},{9,10},{10,... | collective-permute-start | bytes 196616 | tf_op jit(solution)/shard_map/ppermute | solution.py:485
  49.0 2.6 %collective-permute-start.9 = (bf16[256,128]{1,0:T(8,128)(2,1)S(1)}, bf16[256,128]{1,0:T(8,128)(2,1)S(1)}, u32[]{:S(2)}, u32[]{:S(2)}) collective-permute-start(bf16[256,128]{1,0:T(8,128)(2,1)S(1)} %get-tuple-element.59.refs_2_), channel_id=1, source_target_pairs={{0,2},{1,3},{2,0},{3,1},{4,6},{5,7},{6,4},{7,5},{8,10},{9,11},{10,... | collective-permute-start | bytes 196616 | tf_op jit(solution)/shard_map/ppermute | solution.py:485
  52.0 2.1 %shard_map.82.sum_ref = f32[8,512,256]{2,1,0:T(8,128)S(1)} custom-call(bf16[512,256]{1,0:T(8,128)(2,1)S(1)} %get-tuple-element.63.fwd_ref, f32[8,512,256]{2,1,0:T(8,128)S(1)} %get-tuple-element.62.g_ref, bf16[256,256]{1,0:T(8,128)(2,1)S(1)} %get-tuple-element.69.refs_0_, bf16[256,256]{1,0:T(8,128)(2,1)S(1)} %collective-permute-done.5.refs_1_, ...), custom_call_target="tpu_custom_call" | custom-call | flops 268435456 | bytes 8388608 | tf_op jit(solution)/shard_map/pallas_call | solution.py:43
  56.1 2.8 %collective-permute-start.27 = (bf16[256,128]{1,0:T(8,128)(2,1)S(1)}, bf16[256,128]{1,0:T(8,128)(2,1)S(1)}, u32[]{:S(2)}, u32[]{:S(2)}) collective-permute-start(bf16[256,128]{1,0:T(8,128)(2,1)S(1)} %get-tuple-element.90), channel_id=1, source_target_pairs={{0,1},{1,0},{2,3},{3,2},{4,5},{5,4},{6,7},{7,6},{8,9},{9,8},{10,11... | collective-permute-start | bytes 196616 | tf_op jit(solution)/shard_map/ppermute | solution.py:485
  58.9 2.0 %collective-permute-start.28 = (bf16[256,128]{1,0:T(8,128)(2,1)S(1)}, bf16[256,128]{1,0:T(8,128)(2,1)S(1)}, u32[]{:S(2)}, u32[]{:S(2)}) collective-permute-start(bf16[256,128]{1,0:T(8,128)(2,1)S(1)} %get-tuple-element.91), channel_id=1, source_target_pairs={{0,2},{1,3},{2,0},{3,1},{4,6},{5,7},{6,4},{7,5},{8,10},{9,11},{10,... | collective-permute-start | bytes 196616 | tf_op jit(solution)/shard_map/ppermute | solution.py:485
  66.1 2.1 %collective-permute-start.14 = (bf16[256,128]{1,0:T(8,128)(2,1)S(1)}, bf16[256,128]{1,0:T(8,128)(2,1)S(1)}, u32[]{:S(2)}, u32[]{:S(2)}) collective-permute-start(bf16[256,128]{1,0:T(8,128)(2,1)S(1)} %get-tuple-element.80), channel_id=1, source_target_pairs={{0,2},{1,3},{2,0},{3,1},{4,6},{5,7},{6,4},{7,5},{8,10},{9,11},{10,... | collective-permute-start | bytes 196616 | tf_op jit(solution)/shard_map/ppermute | solution.py:485
  69.7 2.9 %collective-permute-start.25 = (bf16[256,128]{1,0:T(8,128)(2,1)S(1)}, bf16[256,128]{1,0:T(8,128)(2,1)S(1)}, u32[]{:S(2)}, u32[]{:S(2)}) collective-permute-start(bf16[256,128]{1,0:T(8,128)(2,1)S(1)} %get-tuple-element.87), channel_id=1, source_target_pairs={{0,2},{1,3},{2,0},{3,1},{4,6},{5,7},{6,4},{7,5},{8,10},{9,11},{10,... | collective-permute-start | bytes 196616 | tf_op jit(solution)/shard_map/ppermute | solution.py:485
  76.8 2.4 %collective-permute-start.19 = (bf16[256,128]{1,0:T(8,128)(2,1)S(1)}, bf16[256,128]{1,0:T(8,128)(2,1)S(1)}, u32[]{:S(2)}, u32[]{:S(2)}) collective-permute-start(bf16[256,128]{1,0:T(8,128)(2,1)S(1)} %get-tuple-element.84), channel_id=1, source_target_pairs={{0,3},{1,2},{2,1},{3,0},{4,7},{5,6},{6,5},{7,4},{8,11},{9,10},{10,... | collective-permute-start | bytes 196616 | tf_op jit(solution)/shard_map/ppermute | solution.py:485
  79.2 1.6 %collective-permute-start.13 = (bf16[256,256]{1,0:T(8,128)(2,1)S(1)}, bf16[256,256]{1,0:T(8,128)(2,1)S(1)}, u32[]{:S(2)}, u32[]{:S(2)}) collective-permute-start(bf16[256,256]{1,0:T(8,128)(2,1)S(1)} %get-tuple-element.79), channel_id=1, source_target_pairs={{0,1},{1,0},{2,3},{3,2},{4,5},{5,4},{6,7},{7,6},{8,9},{9,8},{10,11... | collective-permute-start | bytes 393224 | tf_op jit(solution)/shard_map/ppermute | solution.py:528
  82.0 1.5 %collective-permute-start.33 = (bf16[256,512]{1,0:T(8,128)(2,1)S(1)}, bf16[256,512]{1,0:T(8,128)(2,1)S(1)}, u32[]{:S(2)}, u32[]{:S(2)}) collective-permute-start(bf16[256,512]{1,0:T(8,128)(2,1)S(1)} %shard_map.92.refs_1_), channel_id=1, source_target_pairs={{0,8},{4,12},{8,0},{12,4},{1,9},{5,13},{9,1},{13,5},{2,10},{6,14},... | collective-permute-start | bytes 786440 | tf_op jit(solution)/shard_map/ppermute | solution.py:466
  83.5 2.4 %shard_map.73.q_ref = bf16[256,1024]{1,0:T(8,128)(2,1)S(1)} custom-call(bf16[4096,1024]{1,0:T(8,128)(2,1)S(1)} %get-tuple-element.50.w_ref, bf16[256,1024]{1,0:T(8,128)(2,1)S(1)} %get-tuple-element.51.refs_0_, bf16[512,1024]{1,0:T(8,128)(2,1)S(1)} %collective-permute-done.refs_1_, bf16[256,1024]{1,0:T(8,128)(2,1)S(1)} %collective-permute-done.1.refs_2_.refs_0_, ...), custom_call_target="tpu_custom_call" | custom-call | flops 2147483648 | bytes 10485760 | tf_op jit(solution)/shard_map/pallas_call | solution.py:43
  90.1 5.3 %collective-permute-done.32.refs_4_ = bf16[256,512]{1,0:T(8,128)(2,1)S(1)} collective-permute-done((bf16[256,512]{1,0:T(8,128)(2,1)S(1)}, bf16[256,512]{1,0:T(8,128)(2,1)S(1)}, u32[]{:S(2)}, u32[]{:S(2)}) %collective-permute-start.32) | collective-permute-done | bytes 262176 | tf_op jit(solution)/shard_map/ppermute | solution.py:466
  95.8 5.1 %collective-permute-done.16.refs_0_ = bf16[256,512]{1,0:T(8,128)(2,1)S(1)} collective-permute-done((bf16[256,512]{1,0:T(8,128)(2,1)S(1)}, bf16[256,512]{1,0:T(8,128)(2,1)S(1)}, u32[]{:S(2)}, u32[]{:S(2)}) %collective-permute-start.16) | collective-permute-done | bytes 262176 | tf_op jit(solution)/shard_map/ppermute | solution.py:466
  101.5 4.6 %collective-permute-done.20.refs_1_ = bf16[256,512]{1,0:T(8,128)(2,1)S(1)} collective-permute-done((bf16[256,512]{1,0:T(8,128)(2,1)S(1)}, bf16[256,512]{1,0:T(8,128)(2,1)S(1)}, u32[]{:S(2)}, u32[]{:S(2)}) %collective-permute-start.20) | collective-permute-done | bytes 262176 | tf_op jit(solution)/shard_map/ppermute | solution.py:466
  108.1 3.1 %out_projection.6.refs_3_ = bf16[512,1024]{1,0:T(8,128)(2,1)} custom-call(bf16[4096,1024]{1,0:T(8,128)(2,1)S(1)} %bitcast.2, bf16[256,512]{1,0:T(8,128)(2,1)S(1)} %shard_map.91.refs_0_, bf16[256,512]{1,0:T(8,128)(2,1)S(1)} %shard_map.92.refs_1_, bf16[256,512]{1,0:T(8,128)(2,1)S(1)} %collective-permute-done.30.refs_2_, ...), custom_call_target="tpu_custom_call" | custom-call | flops 2147483648 | bytes 11010048 | tf_op jit(solution)/shard_map/out_projection/pallas_call | solution.py:447
  (79 shorter events, 32.3 us)
Async XLA Ops:
  0.0 28.1 %collective-permute-start = (bf16[512,1024]{1,0:T(8,128)(2,1)}, bf16[512,1024]{1,0:T(8,128)(2,1)S(1)}, u32[]{:S(2)}, u32[]{:S(2)}) collective-permute-start(bf16[512,1024]{1,0:T(8,128)(2,1)} %x_ref.1), channel_id=1, source_target_pairs={{0,4},{4,0},{8,12},{12,8},{1,5},{5,1},{9,13},{13,9},{2,6},{6,2},{1... | collective-permute-start | bytes 3145736 | tf_op jit(solution)/shard_map/ppermute | solution.py:471
  1.7 15.3 %collective-permute-start.3 = (bf16[256,1024]{1,0:T(8,128)(2,1)S(1)}, bf16[256,1024]{1,0:T(8,128)(2,1)S(1)}, u32[]{:S(2)}, u32[]{:S(2)}) collective-permute-start(bf16[256,1024]{1,0:T(8,128)(2,1)S(1)} %get-tuple-element.64.refs_0_), channel_id=1, source_target_pairs={{0,8},{4,12},{8,0},{12,4},{1,9},{5,13},{9,1},{13,5},{2,10},{6,14},... | collective-permute-start | bytes 1572872 | tf_op jit(solution)/shard_map/ppermute | solution.py:466
  4.3 23.8 %collective-permute-start.1 = (bf16[256,1024]{1,0:T(8,128)(2,1)S(1)}, bf16[256,1024]{1,0:T(8,128)(2,1)S(1)}, u32[]{:S(2)}, u32[]{:S(2)}) collective-permute-start(bf16[256,1024]{1,0:T(8,128)(2,1)S(1)} %get-tuple-element.51.refs_0_), channel_id=1, source_target_pairs={{0,8},{4,12},{8,0},{12,4},{1,9},{5,13},{9,1},{13,5},{2,10},{6,14},... | collective-permute-start | bytes 1572872 | tf_op jit(solution)/shard_map/ppermute | solution.py:466
  17.1 14.8 %collective-permute-start.4 = (bf16[256,1024]{1,0:T(8,128)(2,1)S(1)}, bf16[256,1024]{1,0:T(8,128)(2,1)S(1)}, u32[]{:S(2)}, u32[]{:S(2)}) collective-permute-start(bf16[256,1024]{1,0:T(8,128)(2,1)S(1)} %collective-permute-done.3.refs_0_), channel_id=1, source_target_pairs={{0,4},{4,0},{8,12},{12,8},{1,5},{5,1},{9,13},{13,9},{2,6},{6,2},{1... | collective-permute-start | bytes 1572872 | tf_op jit(solution)/shard_map/ppermute | solution.py:471
  28.1 13.7 %collective-permute-start.2 = (bf16[256,1024]{1,0:T(8,128)(2,1)S(1)}, bf16[256,1024]{1,0:T(8,128)(2,1)S(1)}, u32[]{:S(2)}, u32[]{:S(2)}) collective-permute-start(bf16[256,1024]{1,0:T(8,128)(2,1)S(1)} %collective-permute-done.1.refs_2_.refs_0_), channel_id=1, source_target_pairs={{0,4},{4,0},{8,12},{12,8},{1,5},{5,1},{9,13},{13,9},{2,6},{6,2},{1... | collective-permute-start | bytes 1572872 | tf_op jit(solution)/shard_map/ppermute | solution.py:471
  32.7 14.3 %collective-permute-start.6 = (bf16[256,256]{1,0:T(8,128)(2,1)S(1)}, bf16[256,256]{1,0:T(8,128)(2,1)S(1)}, u32[]{:S(2)}, u32[]{:S(2)}) collective-permute-start(bf16[256,256]{1,0:T(8,128)(2,1)S(1)} %get-tuple-element.71.refs_2_), channel_id=1, source_target_pairs={{0,2},{1,3},{2,0},{3,1},{4,6},{5,7},{6,4},{7,5},{8,10},{9,11},{10,... | collective-permute-start | bytes 393224 | tf_op jit(solution)/shard_map/ppermute | solution.py:485
  35.5 13.4 %collective-permute-start.7 = (bf16[256,256]{1,0:T(8,128)(2,1)S(1)}, bf16[256,256]{1,0:T(8,128)(2,1)S(1)}, u32[]{:S(2)}, u32[]{:S(2)}) collective-permute-start(bf16[256,256]{1,0:T(8,128)(2,1)S(1)} %get-tuple-element.72.refs_3_), channel_id=1, source_target_pairs={{0,3},{1,2},{2,1},{3,0},{4,7},{5,6},{6,5},{7,4},{8,11},{9,10},{10,... | collective-permute-start | bytes 393224 | tf_op jit(solution)/shard_map/ppermute | solution.py:485
  37.7 13.9 %collective-permute-start.5 = (bf16[256,256]{1,0:T(8,128)(2,1)S(1)}, bf16[256,256]{1,0:T(8,128)(2,1)S(1)}, u32[]{:S(2)}, u32[]{:S(2)}) collective-permute-start(bf16[256,256]{1,0:T(8,128)(2,1)S(1)} %get-tuple-element.70.refs_1_), channel_id=1, source_target_pairs={{0,1},{1,0},{2,3},{3,2},{4,5},{5,4},{6,7},{7,6},{8,9},{9,8},{10,11... | collective-permute-start | bytes 393224 | tf_op jit(solution)/shard_map/ppermute | solution.py:485
  42.6 12.1 %collective-permute-start.8 = (bf16[256,256]{1,0:T(8,128)(2,1)S(1)}, bf16[256,256]{1,0:T(8,128)(2,1)S(1)}, u32[]{:S(2)}, u32[]{:S(2)}) collective-permute-start(bf16[256,256]{1,0:T(8,128)(2,1)S(1)} %get-tuple-element.58.refs_1_), channel_id=1, source_target_pairs={{0,1},{1,0},{2,3},{3,2},{4,5},{5,4},{6,7},{7,6},{8,9},{9,8},{10,11... | collective-permute-start | bytes 393224 | tf_op jit(solution)/shard_map/ppermute | solution.py:485
  49.0 14.6 %collective-permute-start.9 = (bf16[256,128]{1,0:T(8,128)(2,1)S(1)}, bf16[256,128]{1,0:T(8,128)(2,1)S(1)}, u32[]{:S(2)}, u32[]{:S(2)}) collective-permute-start(bf16[256,128]{1,0:T(8,128)(2,1)S(1)} %get-tuple-element.59.refs_2_), channel_id=1, source_target_pairs={{0,2},{1,3},{2,0},{3,1},{4,6},{5,7},{6,4},{7,5},{8,10},{9,11},{10,... | collective-permute-start | bytes 196616 | tf_op jit(solution)/shard_map/ppermute | solution.py:485
  51.6 12.0 %collective-permute-start.10 = (bf16[256,128]{1,0:T(8,128)(2,1)S(1)}, bf16[256,128]{1,0:T(8,128)(2,1)S(1)}, u32[]{:S(2)}, u32[]{:S(2)}) collective-permute-start(bf16[256,128]{1,0:T(8,128)(2,1)S(1)} %get-tuple-element.60.refs_3_), channel_id=1, source_target_pairs={{0,3},{1,2},{2,1},{3,0},{4,7},{5,6},{6,5},{7,4},{8,11},{9,10},{10,... | collective-permute-start | bytes 196616 | tf_op jit(solution)/shard_map/ppermute | solution.py:485
  56.1 13.0 %collective-permute-start.27 = (bf16[256,128]{1,0:T(8,128)(2,1)S(1)}, bf16[256,128]{1,0:T(8,128)(2,1)S(1)}, u32[]{:S(2)}, u32[]{:S(2)}) collective-permute-start(bf16[256,128]{1,0:T(8,128)(2,1)S(1)} %get-tuple-element.90), channel_id=1, source_target_pairs={{0,1},{1,0},{2,3},{3,2},{4,5},{5,4},{6,7},{7,6},{8,9},{9,8},{10,11... | collective-permute-start | bytes 196616 | tf_op jit(solution)/shard_map/ppermute | solution.py:485
  58.9 10.8 %collective-permute-start.28 = (bf16[256,128]{1,0:T(8,128)(2,1)S(1)}, bf16[256,128]{1,0:T(8,128)(2,1)S(1)}, u32[]{:S(2)}, u32[]{:S(2)}) collective-permute-start(bf16[256,128]{1,0:T(8,128)(2,1)S(1)} %get-tuple-element.91), channel_id=1, source_target_pairs={{0,2},{1,3},{2,0},{3,1},{4,6},{5,7},{6,4},{7,5},{8,10},{9,11},{10,... | collective-permute-start | bytes 196616 | tf_op jit(solution)/shard_map/ppermute | solution.py:485
  60.8 11.8 %collective-permute-start.29 = (bf16[256,128]{1,0:T(8,128)(2,1)S(1)}, bf16[256,128]{1,0:T(8,128)(2,1)S(1)}, u32[]{:S(2)}, u32[]{:S(2)}) collective-permute-start(bf16[256,128]{1,0:T(8,128)(2,1)S(1)} %get-tuple-element.92), channel_id=1, source_target_pairs={{0,3},{1,2},{2,1},{3,0},{4,7},{5,6},{6,5},{7,4},{8,11},{9,10},{10,... | collective-permute-start | bytes 196616 | tf_op jit(solution)/shard_map/ppermute | solution.py:485
  69.7 12.3 %collective-permute-start.25 = (bf16[256,128]{1,0:T(8,128)(2,1)S(1)}, bf16[256,128]{1,0:T(8,128)(2,1)S(1)}, u32[]{:S(2)}, u32[]{:S(2)}) collective-permute-start(bf16[256,128]{1,0:T(8,128)(2,1)S(1)} %get-tuple-element.87), channel_id=1, source_target_pairs={{0,2},{1,3},{2,0},{3,1},{4,6},{5,7},{6,4},{7,5},{8,10},{9,11},{10,... | collective-permute-start | bytes 196616 | tf_op jit(solution)/shard_map/ppermute | solution.py:485
  72.6 10.9 %collective-permute-start.26 = (bf16[256,128]{1,0:T(8,128)(2,1)S(1)}, bf16[256,128]{1,0:T(8,128)(2,1)S(1)}, u32[]{:S(2)}, u32[]{:S(2)}) collective-permute-start(bf16[256,128]{1,0:T(8,128)(2,1)S(1)} %get-tuple-element.88), channel_id=1, source_target_pairs={{0,3},{1,2},{2,1},{3,0},{4,7},{5,6},{6,5},{7,4},{8,11},{9,10},{10,... | collective-permute-start | bytes 196616 | tf_op jit(solution)/shard_map/ppermute | solution.py:485
  76.1 11.4 %collective-permute-start.18 = (bf16[256,128]{1,0:T(8,128)(2,1)S(1)}, bf16[256,128]{1,0:T(8,128)(2,1)S(1)}, u32[]{:S(2)}, u32[]{:S(2)}) collective-permute-start(bf16[256,128]{1,0:T(8,128)(2,1)S(1)} %get-tuple-element.83), channel_id=1, source_target_pairs={{0,2},{1,3},{2,0},{3,1},{4,6},{5,7},{6,4},{7,5},{8,10},{9,11},{10,... | collective-permute-start | bytes 196616 | tf_op jit(solution)/shard_map/ppermute | solution.py:485
  76.8 10.8 %collective-permute-start.19 = (bf16[256,128]{1,0:T(8,128)(2,1)S(1)}, bf16[256,128]{1,0:T(8,128)(2,1)S(1)}, u32[]{:S(2)}, u32[]{:S(2)}) collective-permute-start(bf16[256,128]{1,0:T(8,128)(2,1)S(1)} %get-tuple-element.84), channel_id=1, source_target_pairs={{0,3},{1,2},{2,1},{3,0},{4,7},{5,6},{6,5},{7,4},{8,11},{9,10},{10,... | collective-permute-start | bytes 196616 | tf_op jit(solution)/shard_map/ppermute | solution.py:485
  87.6 13.3 %collective-permute-start.16 = (bf16[256,512]{1,0:T(8,128)(2,1)S(1)}, bf16[256,512]{1,0:T(8,128)(2,1)S(1)}, u32[]{:S(2)}, u32[]{:S(2)}) collective-permute-start(bf16[256,512]{1,0:T(8,128)(2,1)S(1)} %shard_map.87.refs_0_), channel_id=1, source_target_pairs={{0,8},{4,12},{8,0},{12,4},{1,9},{5,13},{9,1},{13,5},{2,10},{6,14},... | collective-permute-start | bytes 786440 | tf_op jit(solution)/shard_map/ppermute | solution.py:466
  88.8 12.2 %collective-permute-start.23 = (bf16[256,512]{1,0:T(8,128)(2,1)S(1)}, bf16[256,512]{1,0:T(8,128)(2,1)S(1)}, u32[]{:S(2)}, u32[]{:S(2)}) collective-permute-start(bf16[256,512]{1,0:T(8,128)(2,1)S(1)} %shard_map.88.refs_1_), channel_id=1, source_target_pairs={{0,4},{4,0},{8,12},{12,8},{1,5},{5,1},{9,13},{13,9},{2,6},{6,2},{1... | collective-permute-start | bytes 786440 | tf_op jit(solution)/shard_map/ppermute | solution.py:471
  88.9 17.2 %collective-permute-start.20 = (bf16[256,512]{1,0:T(8,128)(2,1)S(1)}, bf16[256,512]{1,0:T(8,128)(2,1)S(1)}, u32[]{:S(2)}, u32[]{:S(2)}) collective-permute-start(bf16[256,512]{1,0:T(8,128)(2,1)S(1)} %shard_map.88.refs_1_), channel_id=1, source_target_pairs={{0,8},{4,12},{8,0},{12,4},{1,9},{5,13},{9,1},{13,5},{2,10},{6,14},... | collective-permute-start | bytes 786440 | tf_op jit(solution)/shard_map/ppermute | solution.py:466
  95.3 12.8 %collective-permute-start.30 = (bf16[256,512]{1,0:T(8,128)(2,1)S(1)}, bf16[256,512]{1,0:T(8,128)(2,1)S(1)}, u32[]{:S(2)}, u32[]{:S(2)}) collective-permute-start(bf16[256,512]{1,0:T(8,128)(2,1)S(1)} %shard_map.91.refs_0_), channel_id=1, source_target_pairs={{0,4},{4,0},{8,12},{12,8},{1,5},{5,1},{9,13},{13,9},{2,6},{6,2},{1... | collective-permute-start | bytes 786440 | tf_op jit(solution)/shard_map/ppermute | solution.py:471
  95.3 12.8 %collective-permute-start.35 = (bf16[256,512]{1,0:T(8,128)(2,1)S(1)}, bf16[256,512]{1,0:T(8,128)(2,1)S(1)}, u32[]{:S(2)}, u32[]{:S(2)}) collective-permute-start(bf16[256,512]{1,0:T(8,128)(2,1)S(1)} %collective-permute-done.33.refs_5_), channel_id=1, source_target_pairs={{0,4},{4,0},{8,12},{12,8},{1,5},{5,1},{9,13},{13,9},{2,6},{6,2},{1... | collective-permute-start | bytes 786440 | tf_op jit(solution)/shard_map/ppermute | solution.py:471
  101.0 10.3 %collective-permute-start.17 = (bf16[256,512]{1,0:T(8,128)(2,1)S(1)}, bf16[256,512]{1,0:T(8,128)(2,1)S(1)}, u32[]{:S(2)}, u32[]{:S(2)}) collective-permute-start(bf16[256,512]{1,0:T(8,128)(2,1)S(1)} %collective-permute-done.16.refs_0_), channel_id=1, source_target_pairs={{0,4},{4,0},{8,12},{12,8},{1,5},{5,1},{9,13},{13,9},{2,6},{6,2},{1... | collective-permute-start | bytes 786440 | tf_op jit(solution)/shard_map/ppermute | solution.py:471
  (14 other events, 151.4 us)

commit v11 on v10

--- a/solution.py
+++ b/solution.py
@@ -296,7 +296,10 @@
     me = lax.axis_index("ctx")
     for k in range(n_ctx):
         spectrum = y_ref[target(me, k, n_ctx)].astype(BF16)
-        outs[k][...] = jnp.dot(inv_ref[...], spectrum, preferred_element_type=F32).astype(BF16)
+        made = jnp.dot(inv_ref[...], spectrum, preferred_element_type=F32).astype(BF16)
+        share = outs[k][0].shape[1]
+        for h, out in enumerate(outs[k]):
+            out[...] = made[:, h * share : (h + 1) * share]
 
 
 def early_kernel(n_ctx, fwd_ref, g_ref, *refs):
@@ -313,20 +316,19 @@
     forward_dft(n_ctx, fwd_ref, ins, x_ref, start)
     plan = [(b, b // 2, [(b - a, a // 2) for a in range(1, b, 2)]) for b in range(0, blocks, 2)]
     block_products(g_ref, x_ref, sum_ref, y_ref, plan, start, rows // 2)
-    inverse_dft(n_ctx, inv_ref, y_ref, outs)
-
-
-def late_kernel(n_ctx, start, inv_ref, g_ref, sum_ref, x_ref, *refs):
-    others, outs, y_ref = refs[: -n_ctx - 1], list(refs[-n_ctx - 1 : -1]), refs[-1]
-    share = x_ref.shape[2]
-    for h, other in enumerate(others):
-        outs[1][:, h * share : (h + 1) * share] = other[...]
-    if others:
-        outs[1] = outs[1].at[:, len(others) * share :]
-    blocks, rows, _ = g_ref.shape
+    inverse_dft(n_ctx, inv_ref, y_ref, [[out] for out in outs])
+
+
+def late_kernel(n_ctx, parts, inv_ref, g_ref, sum_ref, *refs):
+    xs, outs, y_ref = refs[:parts], refs[parts:-1], refs[-1]
+    blocks, rows, width = g_ref.shape
+    share = width // parts
     plan = [(b, b // 2, [(b - a, a // 2) for a in range(1, b + 1, 2)]) for b in range(1, blocks, 2)]
-    block_products(g_ref, x_ref, sum_ref, y_ref, plan, start, rows // 2)
-    inverse_dft(n_ctx, inv_ref, y_ref, outs)
+    for h, x_ref in enumerate(xs):
+        mine = y_ref.at[:, :, h * share : (h + 1) * share]
+        block_products(g_ref, x_ref, sum_ref, mine, plan, h * share, rows // 2)
+    cut = [outs[2 + i * parts : 2 + (i + 1) * parts] for i in range(n_ctx - 2)]
+    inverse_dft(n_ctx, inv_ref, y_ref, [outs[:1], outs[1:2], *cut])
 
 
 def convolve(forward, inverse, spectra, even, odd, n_ctx):
@@ -345,7 +347,7 @@
         moved,
         [pltpu.VMEM((n_ctx, rows, width), F32)],
     )
-    first, second = [], []
+    first, xs = [], []
     for h in range(parts):
         x, *made = call(
             functools.partial(middle_kernel, n_ctx, h * share),
@@ -357,25 +359,23 @@
             [pltpu.VMEM(some, F32)],
         )
         first.append(made)
-        others = [made[1] for made in second] if h == parts - 1 else []
-        together = jax.ShapeDtypeStruct((rows // 2, share * (1 + len(others))), BF16)
-        second.append(
-            call(
-                functools.partial(late_kernel, n_ctx, h * share),
-                [piece, together] + [piece] * (n_ctx - 2),
-                [inverse, spectra, sums, x, *others],
-                6,
-                flops // parts,
-                moved // parts,
-                [pltpu.VMEM(some, F32)],
-            )
-        )
-    return [*first, *second]
-
-
-def gate_kernel(n_ctx, start, skip_ref, q_ref, *refs):
+        xs.append(x)
+    whole = jax.ShapeDtypeStruct((rows // 2, width), BF16)
+    made = call(
+        functools.partial(late_kernel, n_ctx, parts),
+        [whole] * 2 + [piece] * ((n_ctx - 2) * parts),
+        [inverse, spectra, sums, *xs],
+        6,
+        flops,
+        moved,
+        [pltpu.VMEM((n_ctx, rows, width), F32)],
+    )
+    return [*first, *(made[:2] + made[2 + h :: parts] for h in range(parts))]
+
+
+def gate_kernel(n_ctx, start, share, skip_ref, q_ref, *refs):
     mixed, conv, out_ref = refs[:n_ctx], refs[n_ctx : 2 * n_ctx], refs[-1]
-    share, width = conv[0].shape[1], q_ref.shape[1] // n_ctx
+    width = q_ref.shape[1] // n_ctx
     me = lax.axis_index("ctx")
     for m in range(n_ctx):
         skip = skip_ref[pl.ds(target(me, m, n_ctx), 1), :][:, start : start + share]
@@ -385,10 +385,10 @@
         out_ref[:, m * share : (m + 1) * share] = (query * total).astype(BF16)
 
 
-def gate(skip, query, mixed, conv, start, n_ctx):
-    tokens, share = conv[0].shape
+def gate(skip, query, mixed, conv, start, share, n_ctx):
+    tokens = conv[0].shape[0]
     return call(
-        functools.partial(gate_kernel, n_ctx, start),
+        functools.partial(gate_kernel, n_ctx, start, share),
         jax.ShapeDtypeStruct((tokens, share * n_ctx), BF16),
         [skip, query, *mixed, *conv],
         4,
@@ -398,7 +398,7 @@
 
 
 def out_kernel(which, parts, has_before, n_ctx, columns, row, w_ref, *refs):
-    pieces, out_ref = refs[: len(which) * parts], refs[-1 if row is None else -3]
+    pieces, out_ref = refs[: sum(len(some) for _, some in which)], refs[-1 if row is None else -3]
     share = pieces[0].shape[1] // n_ctx
     width = share * parts
     me = lax.axis_index("ctx")
@@ -407,11 +407,14 @@
     for i in range(w_ref.shape[1] // columns):
         cols = slice(i * columns, (i + 1) * columns)
         acc = refs[len(pieces)][:, cols] if has_before else None
-        for i_piece, j in enumerate(which):
+        used = 0
+        for j, some in which:
+            group = pieces[used : used + len(some)]
+            used += len(some)
             for m in range(n_ctx):
-                w = w_ref[rows_at(sources[j] * n_ctx + target(me, m, n_ctx), width), cols]
+                first = (sources[j] * n_ctx + target(me, m, n_ctx)) * width + some[0] * share
+                w = w_ref[pl.ds(pl.multiple_of(first, share), len(some) * share), cols]
                 mine = slice(m * share, (m + 1) * share)
-                group = pieces[i_piece * parts : (i_piece + 1) * parts]
                 x = jnp.concatenate([p[:, mine] for p in group], axis=1)
                 a = jnp.dot(x, w, preferred_element_type=F32)
                 acc = a if acc is None else acc + a
@@ -431,7 +434,7 @@
     parts = len(gathered)
     tokens = gathered[0][0].shape[0]
     _, out_width = w.shape
-    operands = [w, *(pieces[j] for j in which for pieces in gathered)] + ([] if before is None else [before])
+    operands = [w, *(gathered[h][j] for j, some in which for h in some)] + ([] if before is None else [before])
     specs = [VMEM] * len(operands)
     aliases, scratch, row = {}, [], None
     out_spec, shape = VMEM, (tokens, out_width)
@@ -443,7 +446,7 @@
             specs.append(HBM)
             aliases = {len(operands): 0}
             operands.append(so_far)
-    share = len(which) * parts * gathered[0][0].shape[1]
+    share = sum(len(some) for _, some in which) * gathered[0][0].shape[1]
     return pl.pallas_call(
         functools.partial(out_kernel, tuple(which), parts, before is not None, n_ctx, columns, row),
         out_shape=jax.ShapeDtypeStruct(shape, F32 if final is None else BF16),
@@ -532,14 +535,18 @@
         back = exchange(conv[r], 1 if c == 0 else 2)
         if c > 0:
             back[1] = joint
-        gated = gate(skip, query[c], mixed[c][h], back, h * back[0].shape[1], n_ctx)
+        share = back[2].shape[1]
+        gated = gate(skip, query[c], mixed[c][h], back, h * share, share, n_ctx)
         beside = swap_cores(gated)
         gathered.append([gated, beside, *gather_far(gated)])
-    every = range(len(gathered[0]))
-    out = project_out(gathered[:2], every, out_weight, None, n_ctx, (0, rows, None))
-    part = project_out(gathered[2:], every[:2], out_weight, None, n_ctx)
-    part = project_out(gathered[2:], every[2:-1], out_weight, part, n_ctx)
-    return project_out(gathered[2:], every[-1:], out_weight, part, n_ctx, (tokens, rows, out))
+    both = tuple(range(PARTS))
+    every = [(j, both) for j in range(len(gathered[0]))]
+    last = every[-1][0]
+    even, odd = gathered[:PARTS], gathered[PARTS:]
+    out = project_out(even, every, out_weight, None, n_ctx, (0, rows, None))
+    part = project_out(odd, every[:2], out_weight, None, n_ctx)
+    part = project_out(odd, [*every[2:-1], (last, both[:-1])], out_weight, part, n_ctx)
+    return project_out(odd, [(last, both[-1:])], out_weight, part, n_ctx, (tokens, rows, out))
 
 
 P_SIZE = 128

time: 113 us -> 112 us (level); the launches traced: 113 us -> 111 us
  waiting for transfers between devices: 31.9 us -> 30 us
    ppermute x6, waiting for transfers between devices: 30 us -> 26.8 us  [shift(): return lax.ppermute(x, axis, [(i, (i + by) % n) for i in range(n)])]
    ppermute x1, waiting for transfers between devices: 0.01 us -> 1.83 us  [layer_body(): lax.ppermute(conv[-1][1], 'ctx', [(i, target(i, 1, n_ctx)) for i in range...]
    pallas_call x20 -> x19, Pallas kernels: 23.3 us -> 22.8 us  [call(): pl.pallas_call(kernel, out_shape=out, in_specs=[VMEM] * len(operands), ou...]
  transfers between devices with their start and end apart: 36 -> 36, of which waited for: 7 -> 8; matrix products, arithmetic and copies ran while one was open for 0% -> 0% of each run, Pallas kernels for 34% -> 35%
where the time goes in v11:
time: 112 us; the launch traced here: 111 us
  starting transfers between devices  40.2 us (36%)
  Pallas kernels  39.8 us (36%)
  waiting for transfers between devices  30 us (27%)
    ppermute x18, starting transfers between devices, exchange(): lax.ppermute(parts[k], 'ctx', [(i, target(i, k, n)) for i in range(n)])  29.9 us
    ppermute x6, waiting for transfers between devices, shift(): return lax.ppermute(x, axis, [(i, (i + by) % n) for i in range(n)])  26.8 us
    pallas_call x19, Pallas kernels, call(): pl.pallas_call(kernel, out_shape=out, in_specs=[VMEM] * len(operands), ou...  22.8 us
    pallas_call x1, Pallas kernels, prologue(): pl.pallas_call(functools.partial(prologue_kernel, width), out_shape=out,...  8.73 us
    ppermute x6, starting transfers between devices, shift(): return lax.ppermute(x, axis, [(i, (i + by) % n) for i in range(n)])  7.75 us
    pallas_call x4, Pallas kernels, project_out(): pl.pallas_call(functools.partial(out_kernel, tuple(which), parts, before...  7.07 us
  transfers between devices with their start and end apart: 36, of which 8 were waited for; matrix products, arithmetic and copies ran while one was open for 0% of the time, Pallas kernels for 35%

profile of v11, /device:TPU:0, one launch (start us, length us, event | category | flops | bytes accessed | tf_op | source)
XLA Modules:
  0.0 110.5 jit_solution(3516359299073020368)
XLA Ops:
  1.7 2.6 %collective-permute-start.3 = (bf16[256,1024]{1,0:T(8,128)(2,1)S(1)}, bf16[256,1024]{1,0:T(8,128)(2,1)S(1)}, u32[]{:S(2)}, u32[]{:S(2)}) collective-permute-start(bf16[256,1024]{1,0:T(8,128)(2,1)S(1)} %get-tuple-element.62.refs_0_), channel_id=1, source_target_pairs={{0,8},{4,12},{8,0},{12,4},{1,9},{5,13},{9,1},{13,5},{2,10},{6,14},... | collective-permute-start | bytes 1572872 | tf_op jit(solution)/shard_map/ppermute | solution.py:469
  4.4 12.7 %collective-permute-done.3.refs_0_ = bf16[256,1024]{1,0:T(8,128)(2,1)S(1)} collective-permute-done((bf16[256,1024]{1,0:T(8,128)(2,1)S(1)}, bf16[256,1024]{1,0:T(8,128)(2,1)S(1)}, u32[]{:S(2)}, u32[]{:S(2)}) %collective-permute-start.3) | collective-permute-done | bytes 524320 | tf_op jit(solution)/shard_map/ppermute | solution.py:469
  17.1 8.7 %prologue.1 = (bf16[512,256]{1,0:T(8,128)(2,1)S(1)}, bf16[256,512]{1,0:T(8,128)(2,1)S(1)}, bf16[2,4096,1024]{2,1,0:T(8,128)(2,1)S(1)}, bf16[4096,1024]{1,0:T(8,1...) custom-call(f32[1024]{0:T(1024)} %skip_hbm.1, bf16[512,256]{1,0:T(8,128)(2,1)} %constant.4.clone.fwd_hbm, ...), custom_call_target="tpu_custom_call" | custom-call | flops 536870912 | bytes 30408704 | tf_op jit(solution)/shard_map/prologue/pallas_call | solution.py:152
  25.8 2.3 %collective-permute-done.1.refs_2_.refs_0_ = bf16[256,1024]{1,0:T(8,128)(2,1)S(1)} collective-permute-done((bf16[256,1024]{1,0:T(8,128)(2,1)S(1)}, bf16[256,1024]{1,0:T(8,128)(2,1)S(1)}, u32[]{:S(2)}, u32[]{:S(2)}) %collective-permute-start.1) | collective-permute-done | bytes 524320 | tf_op jit(solution)/shard_map/ppermute | solution.py:469
  28.1 2.4 %shard_map.78 = (f32[256,1024]{1,0:T(8,128)S(1)}, f32[256,1024]{1,0:T(8,128)S(1)}) custom-call(bf16[2,4096,1024]{2,1,0:T(8,128)(2,1)S(1)} %get-tuple-element.50.w_ref, bf16[256,1024]{1,0:T(8,128)(2,1)S(1)} %get-tuple-element.62.refs_0_, bf16[512,1024]{1,0:T(8,128)(2,1)S(1)} %collective-permute-done.refs_1_), custom_call_target="tpu_custom_call" | custom-call | flops 2147483648 | bytes 9437184 | tf_op jit(solution)/shard_map/pallas_call | solution.py:43
  32.7 2.9 %collective-permute-start.6 = (bf16[256,256]{1,0:T(8,128)(2,1)S(1)}, bf16[256,256]{1,0:T(8,128)(2,1)S(1)}, u32[]{:S(2)}, u32[]{:S(2)}) collective-permute-start(bf16[256,256]{1,0:T(8,128)(2,1)S(1)} %get-tuple-element.69.refs_2_), channel_id=1, source_target_pairs={{0,2},{1,3},{2,0},{3,1},{4,6},{5,7},{6,4},{7,5},{8,10},{9,11},{10,... | collective-permute-start | bytes 393224 | tf_op jit(solution)/shard_map/ppermute | solution.py:488
  38.0 2.4 %shard_map.74 = (f32[256,1024]{1,0:T(8,128)S(1)}, f32[256,1024]{1,0:T(8,128)S(1)}) custom-call(bf16[2,4096,1024]{2,1,0:T(8,128)(2,1)S(1)} %get-tuple-element.50.w_ref, bf16[256,1024]{1,0:T(8,128)(2,1)S(1)} %get-tuple-element.49.refs_0_, bf16[512,1024]{1,0:T(8,128)(2,1)S(1)} %collective-permute-done.refs_1_), custom_call_target="tpu_custom_call" | custom-call | flops 2147483648 | bytes 9437184 | tf_op jit(solution)/shard_map/pallas_call | solution.py:43
  42.6 1.8 %collective-permute-start.8 = (bf16[256,256]{1,0:T(8,128)(2,1)S(1)}, bf16[256,256]{1,0:T(8,128)(2,1)S(1)}, u32[]{:S(2)}, u32[]{:S(2)}) collective-permute-start(bf16[256,256]{1,0:T(8,128)(2,1)S(1)} %get-tuple-element.56.refs_1_), channel_id=1, source_target_pairs={{0,1},{1,0},{2,3},{3,2},{4,5},{5,4},{6,7},{7,6},{8,9},{9,8},{10,11... | collective-permute-start | bytes 393224 | tf_op jit(solution)/shard_map/ppermute | solution.py:488
  45.1 1.8 %collective-permute-start.11 = (bf16[256,128]{1,0:T(8,128)(2,1)S(1)}, bf16[256,128]{1,0:T(8,128)(2,1)S(1)}, u32[]{:S(2)}, u32[]{:S(2)}) collective-permute-start(bf16[256,128]{1,0:T(8,128)(2,1)S(1)} %get-tuple-element.57.refs_2_), channel_id=1, source_target_pairs={{0,2},{1,3},{2,0},{3,1},{4,6},{5,7},{6,4},{7,5},{8,10},{9,11},{10,... | collective-permute-start | bytes 196616 | tf_op jit(solution)/shard_map/ppermute | solution.py:488
  46.9 2.0 %collective-permute-start.12 = (bf16[256,128]{1,0:T(8,128)(2,1)S(1)}, bf16[256,128]{1,0:T(8,128)(2,1)S(1)}, u32[]{:S(2)}, u32[]{:S(2)}) collective-permute-start(bf16[256,128]{1,0:T(8,128)(2,1)S(1)} %get-tuple-element.58.refs_3_), channel_id=1, source_target_pairs={{0,3},{1,2},{2,1},{3,0},{4,7},{5,6},{6,5},{7,4},{8,11},{9,10},{10,... | collective-permute-start | bytes 196616 | tf_op jit(solution)/shard_map/ppermute | solution.py:488
  49.0 2.6 %collective-permute-start.9 = (bf16[256,128]{1,0:T(8,128)(2,1)S(1)}, bf16[256,128]{1,0:T(8,128)(2,1)S(1)}, u32[]{:S(2)}, u32[]{:S(2)}) collective-permute-start(bf16[256,128]{1,0:T(8,128)(2,1)S(1)} %get-tuple-element.71.refs_2_), channel_id=1, source_target_pairs={{0,2},{1,3},{2,0},{3,1},{4,6},{5,7},{6,4},{7,5},{8,10},{9,11},{10,... | collective-permute-start | bytes 196616 | tf_op jit(solution)/shard_map/ppermute | solution.py:488
  52.0 2.1 %shard_map.82.sum_ref = f32[8,512,256]{2,1,0:T(8,128)S(1)} custom-call(bf16[512,256]{1,0:T(8,128)(2,1)S(1)} %get-tuple-element.61.fwd_ref, f32[8,512,256]{2,1,0:T(8,128)S(1)} %get-tuple-element.60.g_ref, bf16[256,256]{1,0:T(8,128)(2,1)S(1)} %get-tuple-element.67.refs_0_, bf16[256,256]{1,0:T(8,128)(2,1)S(1)} %collective-permute-done.5.refs_1_, ...), custom_call_target="tpu_custom_call" | custom-call | flops 268435456 | bytes 8388608 | tf_op jit(solution)/shard_map/pallas_call | solution.py:43
  56.1 2.8 %collective-permute-start.27 = (bf16[256,128]{1,0:T(8,128)(2,1)S(1)}, bf16[256,128]{1,0:T(8,128)(2,1)S(1)}, u32[]{:S(2)}, u32[]{:S(2)}) collective-permute-start(bf16[256,128]{1,0:T(8,128)(2,1)S(1)} %get-tuple-element.86), channel_id=1, source_target_pairs={{0,1},{1,0},{2,3},{3,2},{4,5},{5,4},{6,7},{7,6},{8,9},{9,8},{10,11... | collective-permute-start | bytes 196616 | tf_op jit(solution)/shard_map/ppermute | solution.py:488
  58.9 2.0 %collective-permute-start.28 = (bf16[256,128]{1,0:T(8,128)(2,1)S(1)}, bf16[256,128]{1,0:T(8,128)(2,1)S(1)}, u32[]{:S(2)}, u32[]{:S(2)}) collective-permute-start(bf16[256,128]{1,0:T(8,128)(2,1)S(1)} %get-tuple-element.87), channel_id=1, source_target_pairs={{0,2},{1,3},{2,0},{3,1},{4,6},{5,7},{6,4},{7,5},{8,10},{9,11},{10,... | collective-permute-start | bytes 196616 | tf_op jit(solution)/shard_map/ppermute | solution.py:488
  64.9 1.8 %shard_map.85 = (bf16[256,256]{1,0:T(8,128)(2,1)S(1)}, bf16[256,256]{1,0:T(8,128)(2,1)S(1)}, bf16[256,128]{1,0:T(8,128)(2,1)S(1)}, bf16[256,128]{1,0:T(8,128)(2,...) custom-call(bf16[256,512]{1,0:T(8,128)(2,1)S(1)} %get-tuple-element.59.inv_ref, ...), custom_call_target="tpu_custom_call" | custom-call | flops 268435456 | bytes 8388608 | tf_op jit(solution)/shard_map/pallas_call | solution.py:43
  66.8 2.1 %collective-permute-start.14 = (bf16[256,128]{1,0:T(8,128)(2,1)S(1)}, bf16[256,128]{1,0:T(8,128)(2,1)S(1)}, u32[]{:S(2)}, u32[]{:S(2)}) collective-permute-start(bf16[256,128]{1,0:T(8,128)(2,1)S(1)} %get-tuple-element.77), channel_id=1, source_target_pairs={{0,2},{1,3},{2,0},{3,1},{4,6},{5,7},{6,4},{7,5},{8,10},{9,11},{10,... | collective-permute-start | bytes 196616 | tf_op jit(solution)/shard_map/ppermute | solution.py:488
  70.4 2.9 %collective-permute-start.26 = (bf16[256,128]{1,0:T(8,128)(2,1)S(1)}, bf16[256,128]{1,0:T(8,128)(2,1)S(1)}, u32[]{:S(2)}, u32[]{:S(2)}) collective-permute-start(bf16[256,128]{1,0:T(8,128)(2,1)S(1)} %get-tuple-element.84), channel_id=1, source_target_pairs={{0,3},{1,2},{2,1},{3,0},{4,7},{5,6},{6,5},{7,4},{8,11},{9,10},{10,... | collective-permute-start | bytes 196616 | tf_op jit(solution)/shard_map/ppermute | solution.py:488
  76.4 2.4 %collective-permute-start.19 = (bf16[256,128]{1,0:T(8,128)(2,1)S(1)}, bf16[256,128]{1,0:T(8,128)(2,1)S(1)}, u32[]{:S(2)}, u32[]{:S(2)}) collective-permute-start(bf16[256,128]{1,0:T(8,128)(2,1)S(1)} %get-tuple-element.80), channel_id=1, source_target_pairs={{0,3},{1,2},{2,1},{3,0},{4,7},{5,6},{6,5},{7,4},{8,11},{9,10},{10,... | collective-permute-start | bytes 196616 | tf_op jit(solution)/shard_map/ppermute | solution.py:488
  81.9 2.4 %shard_map.73.q_ref = bf16[256,1024]{1,0:T(8,128)(2,1)S(1)} custom-call(bf16[4096,1024]{1,0:T(8,128)(2,1)S(1)} %get-tuple-element.48.w_ref, bf16[256,1024]{1,0:T(8,128)(2,1)S(1)} %get-tuple-element.49.refs_0_, bf16[512,1024]{1,0:T(8,128)(2,1)S(1)} %collective-permute-done.refs_1_, bf16[256,1024]{1,0:T(8,128)(2,1)S(1)} %collective-permute-done.1.refs_2_.refs_0_, ...), custom_call_target="tpu_custom_call" | custom-call | flops 2147483648 | bytes 10485760 | tf_op jit(solution)/shard_map/pallas_call | solution.py:43
  84.5 1.8 %collective-permute-done.13.refs_5_ = bf16[256,256]{1,0:T(8,128)(2,1)S(1)} collective-permute-done((bf16[256,256]{1,0:T(8,128)(2,1)S(1)}, bf16[256,256]{1,0:T(8,128)(2,1)S(1)}, u32[]{:S(2)}, u32[]{:S(2)}) %collective-permute-start.13) | collective-permute-done | bytes 131104 | tf_op jit(solution)/shard_map/ppermute | solution.py:531
  89.3 5.6 %collective-permute-done.32.refs_4_ = bf16[256,512]{1,0:T(8,128)(2,1)S(1)} collective-permute-done((bf16[256,512]{1,0:T(8,128)(2,1)S(1)}, bf16[256,512]{1,0:T(8,128)(2,1)S(1)}, u32[]{:S(2)}, u32[]{:S(2)}) %collective-permute-start.32) | collective-permute-done | bytes 262176 | tf_op jit(solution)/shard_map/ppermute | solution.py:469
  97.0 3.6 %collective-permute-done.20.refs_0_ = bf16[256,512]{1,0:T(8,128)(2,1)S(1)} collective-permute-done((bf16[256,512]{1,0:T(8,128)(2,1)S(1)}, bf16[256,512]{1,0:T(8,128)(2,1)S(1)}, u32[]{:S(2)}, u32[]{:S(2)}) %collective-permute-start.20) | collective-permute-done | bytes 262176 | tf_op jit(solution)/shard_map/ppermute | solution.py:469
  101.9 2.6 %collective-permute-done.16.refs_1_ = bf16[256,512]{1,0:T(8,128)(2,1)S(1)} collective-permute-done((bf16[256,512]{1,0:T(8,128)(2,1)S(1)}, bf16[256,512]{1,0:T(8,128)(2,1)S(1)}, u32[]{:S(2)}, u32[]{:S(2)}) %collective-permute-start.16) | collective-permute-done | bytes 262176 | tf_op jit(solution)/shard_map/ppermute | solution.py:469
  104.5 3.1 %out_projection.6.refs_2_ = bf16[512,1024]{1,0:T(8,128)(2,1)} custom-call(bf16[4096,1024]{1,0:T(8,128)(2,1)S(1)} %bitcast.2, bf16[256,512]{1,0:T(8,128)(2,1)S(1)} %shard_map.90.refs_0_, bf16[256,512]{1,0:T(8,128)(2,1)S(1)} %shard_map.91.refs_1_, bf16[256,512]{1,0:T(8,128)(2,1)S(1)} %collective-permute-done.30.refs_2_, ...), custom_call_target="tpu_custom_call" | custom-call | flops 2147483648 | bytes 11010048 | tf_op jit(solution)/shard_map/out_projection/pallas_call | solution.py:450
  (78 shorter events, 32.7 us)
Async XLA Ops:
  0.0 28.1 %collective-permute-start = (bf16[512,1024]{1,0:T(8,128)(2,1)}, bf16[512,1024]{1,0:T(8,128)(2,1)S(1)}, u32[]{:S(2)}, u32[]{:S(2)}) collective-permute-start(bf16[512,1024]{1,0:T(8,128)(2,1)} %x_ref.1), channel_id=1, source_target_pairs={{0,4},{4,0},{8,12},{12,8},{1,5},{5,1},{9,13},{13,9},{2,6},{6,2},{1... | collective-permute-start | bytes 3145736 | tf_op jit(solution)/shard_map/ppermute | solution.py:474
  1.7 15.3 %collective-permute-start.3 = (bf16[256,1024]{1,0:T(8,128)(2,1)S(1)}, bf16[256,1024]{1,0:T(8,128)(2,1)S(1)}, u32[]{:S(2)}, u32[]{:S(2)}) collective-permute-start(bf16[256,1024]{1,0:T(8,128)(2,1)S(1)} %get-tuple-element.62.refs_0_), channel_id=1, source_target_pairs={{0,8},{4,12},{8,0},{12,4},{1,9},{5,13},{9,1},{13,5},{2,10},{6,14},... | collective-permute-start | bytes 1572872 | tf_op jit(solution)/shard_map/ppermute | solution.py:469
  4.3 23.8 %collective-permute-start.1 = (bf16[256,1024]{1,0:T(8,128)(2,1)S(1)}, bf16[256,1024]{1,0:T(8,128)(2,1)S(1)}, u32[]{:S(2)}, u32[]{:S(2)}) collective-permute-start(bf16[256,1024]{1,0:T(8,128)(2,1)S(1)} %get-tuple-element.49.refs_0_), channel_id=1, source_target_pairs={{0,8},{4,12},{8,0},{12,4},{1,9},{5,13},{9,1},{13,5},{2,10},{6,14},... | collective-permute-start | bytes 1572872 | tf_op jit(solution)/shard_map/ppermute | solution.py:469
  17.1 14.8 %collective-permute-start.4 = (bf16[256,1024]{1,0:T(8,128)(2,1)S(1)}, bf16[256,1024]{1,0:T(8,128)(2,1)S(1)}, u32[]{:S(2)}, u32[]{:S(2)}) collective-permute-start(bf16[256,1024]{1,0:T(8,128)(2,1)S(1)} %collective-permute-done.3.refs_0_), channel_id=1, source_target_pairs={{0,4},{4,0},{8,12},{12,8},{1,5},{5,1},{9,13},{13,9},{2,6},{6,2},{1... | collective-permute-start | bytes 1572872 | tf_op jit(solution)/shard_map/ppermute | solution.py:474
  28.1 13.7 %collective-permute-start.2 = (bf16[256,1024]{1,0:T(8,128)(2,1)S(1)}, bf16[256,1024]{1,0:T(8,128)(2,1)S(1)}, u32[]{:S(2)}, u32[]{:S(2)}) collective-permute-start(bf16[256,1024]{1,0:T(8,128)(2,1)S(1)} %collective-permute-done.1.refs_2_.refs_0_), channel_id=1, source_target_pairs={{0,4},{4,0},{8,12},{12,8},{1,5},{5,1},{9,13},{13,9},{2,6},{6,2},{1... | collective-permute-start | bytes 1572872 | tf_op jit(solution)/shard_map/ppermute | solution.py:474
  32.7 14.3 %collective-permute-start.6 = (bf16[256,256]{1,0:T(8,128)(2,1)S(1)}, bf16[256,256]{1,0:T(8,128)(2,1)S(1)}, u32[]{:S(2)}, u32[]{:S(2)}) collective-permute-start(bf16[256,256]{1,0:T(8,128)(2,1)S(1)} %get-tuple-element.69.refs_2_), channel_id=1, source_target_pairs={{0,2},{1,3},{2,0},{3,1},{4,6},{5,7},{6,4},{7,5},{8,10},{9,11},{10,... | collective-permute-start | bytes 393224 | tf_op jit(solution)/shard_map/ppermute | solution.py:488
  35.5 13.4 %collective-permute-start.7 = (bf16[256,256]{1,0:T(8,128)(2,1)S(1)}, bf16[256,256]{1,0:T(8,128)(2,1)S(1)}, u32[]{:S(2)}, u32[]{:S(2)}) collective-permute-start(bf16[256,256]{1,0:T(8,128)(2,1)S(1)} %get-tuple-element.70.refs_3_), channel_id=1, source_target_pairs={{0,3},{1,2},{2,1},{3,0},{4,7},{5,6},{6,5},{7,4},{8,11},{9,10},{10,... | collective-permute-start | bytes 393224 | tf_op jit(solution)/shard_map/ppermute | solution.py:488
  37.7 13.9 %collective-permute-start.5 = (bf16[256,256]{1,0:T(8,128)(2,1)S(1)}, bf16[256,256]{1,0:T(8,128)(2,1)S(1)}, u32[]{:S(2)}, u32[]{:S(2)}) collective-permute-start(bf16[256,256]{1,0:T(8,128)(2,1)S(1)} %get-tuple-element.68.refs_1_), channel_id=1, source_target_pairs={{0,1},{1,0},{2,3},{3,2},{4,5},{5,4},{6,7},{7,6},{8,9},{9,8},{10,11... | collective-permute-start | bytes 393224 | tf_op jit(solution)/shard_map/ppermute | solution.py:488
  42.6 12.1 %collective-permute-start.8 = (bf16[256,256]{1,0:T(8,128)(2,1)S(1)}, bf16[256,256]{1,0:T(8,128)(2,1)S(1)}, u32[]{:S(2)}, u32[]{:S(2)}) collective-permute-start(bf16[256,256]{1,0:T(8,128)(2,1)S(1)} %get-tuple-element.56.refs_1_), channel_id=1, source_target_pairs={{0,1},{1,0},{2,3},{3,2},{4,5},{5,4},{6,7},{7,6},{8,9},{9,8},{10,11... | collective-permute-start | bytes 393224 | tf_op jit(solution)/shard_map/ppermute | solution.py:488
  45.1 9.6 %collective-permute-start.11 = (bf16[256,128]{1,0:T(8,128)(2,1)S(1)}, bf16[256,128]{1,0:T(8,128)(2,1)S(1)}, u32[]{:S(2)}, u32[]{:S(2)}) collective-permute-start(bf16[256,128]{1,0:T(8,128)(2,1)S(1)} %get-tuple-element.57.refs_2_), channel_id=1, source_target_pairs={{0,2},{1,3},{2,0},{3,1},{4,6},{5,7},{6,4},{7,5},{8,10},{9,11},{10,... | collective-permute-start | bytes 196616 | tf_op jit(solution)/shard_map/ppermute | solution.py:488
  49.0 14.6 %collective-permute-start.9 = (bf16[256,128]{1,0:T(8,128)(2,1)S(1)}, bf16[256,128]{1,0:T(8,128)(2,1)S(1)}, u32[]{:S(2)}, u32[]{:S(2)}) collective-permute-start(bf16[256,128]{1,0:T(8,128)(2,1)S(1)} %get-tuple-element.71.refs_2_), channel_id=1, source_target_pairs={{0,2},{1,3},{2,0},{3,1},{4,6},{5,7},{6,4},{7,5},{8,10},{9,11},{10,... | collective-permute-start | bytes 196616 | tf_op jit(solution)/shard_map/ppermute | solution.py:488
  51.6 12.0 %collective-permute-start.10 = (bf16[256,128]{1,0:T(8,128)(2,1)S(1)}, bf16[256,128]{1,0:T(8,128)(2,1)S(1)}, u32[]{:S(2)}, u32[]{:S(2)}) collective-permute-start(bf16[256,128]{1,0:T(8,128)(2,1)S(1)} %get-tuple-element.72.refs_3_), channel_id=1, source_target_pairs={{0,3},{1,2},{2,1},{3,0},{4,7},{5,6},{6,5},{7,4},{8,11},{9,10},{10,... | collective-permute-start | bytes 196616 | tf_op jit(solution)/shard_map/ppermute | solution.py:488
  56.1 13.7 %collective-permute-start.27 = (bf16[256,128]{1,0:T(8,128)(2,1)S(1)}, bf16[256,128]{1,0:T(8,128)(2,1)S(1)}, u32[]{:S(2)}, u32[]{:S(2)}) collective-permute-start(bf16[256,128]{1,0:T(8,128)(2,1)S(1)} %get-tuple-element.86), channel_id=1, source_target_pairs={{0,1},{1,0},{2,3},{3,2},{4,5},{5,4},{6,7},{7,6},{8,9},{9,8},{10,11... | collective-permute-start | bytes 196616 | tf_op jit(solution)/shard_map/ppermute | solution.py:488
  58.9 11.5 %collective-permute-start.28 = (bf16[256,128]{1,0:T(8,128)(2,1)S(1)}, bf16[256,128]{1,0:T(8,128)(2,1)S(1)}, u32[]{:S(2)}, u32[]{:S(2)}) collective-permute-start(bf16[256,128]{1,0:T(8,128)(2,1)S(1)} %get-tuple-element.87), channel_id=1, source_target_pairs={{0,2},{1,3},{2,0},{3,1},{4,6},{5,7},{6,4},{7,5},{8,10},{9,11},{10,... | collective-permute-start | bytes 196616 | tf_op jit(solution)/shard_map/ppermute | solution.py:488
  62.1 12.4 %collective-permute-start.29 = (bf16[256,128]{1,0:T(8,128)(2,1)S(1)}, bf16[256,128]{1,0:T(8,128)(2,1)S(1)}, u32[]{:S(2)}, u32[]{:S(2)}) collective-permute-start(bf16[256,128]{1,0:T(8,128)(2,1)S(1)} %get-tuple-element.88), channel_id=1, source_target_pairs={{0,3},{1,2},{2,1},{3,0},{4,7},{5,6},{6,5},{7,4},{8,11},{9,10},{10,... | collective-permute-start | bytes 196616 | tf_op jit(solution)/shard_map/ppermute | solution.py:488
  66.8 9.0 %collective-permute-start.14 = (bf16[256,128]{1,0:T(8,128)(2,1)S(1)}, bf16[256,128]{1,0:T(8,128)(2,1)S(1)}, u32[]{:S(2)}, u32[]{:S(2)}) collective-permute-start(bf16[256,128]{1,0:T(8,128)(2,1)S(1)} %get-tuple-element.77), channel_id=1, source_target_pairs={{0,2},{1,3},{2,0},{3,1},{4,6},{5,7},{6,4},{7,5},{8,10},{9,11},{10,... | collective-permute-start | bytes 196616 | tf_op jit(solution)/shard_map/ppermute | solution.py:488
  69.8 9.6 %collective-permute-start.25 = (bf16[256,128]{1,0:T(8,128)(2,1)S(1)}, bf16[256,128]{1,0:T(8,128)(2,1)S(1)}, u32[]{:S(2)}, u32[]{:S(2)}) collective-permute-start(bf16[256,128]{1,0:T(8,128)(2,1)S(1)} %get-tuple-element.83), channel_id=1, source_target_pairs={{0,2},{1,3},{2,0},{3,1},{4,6},{5,7},{6,4},{7,5},{8,10},{9,11},{10,... | collective-permute-start | bytes 196616 | tf_op jit(solution)/shard_map/ppermute | solution.py:488
  70.4 10.0 %collective-permute-start.26 = (bf16[256,128]{1,0:T(8,128)(2,1)S(1)}, bf16[256,128]{1,0:T(8,128)(2,1)S(1)}, u32[]{:S(2)}, u32[]{:S(2)}) collective-permute-start(bf16[256,128]{1,0:T(8,128)(2,1)S(1)} %get-tuple-element.84), channel_id=1, source_target_pairs={{0,3},{1,2},{2,1},{3,0},{4,7},{5,6},{6,5},{7,4},{8,11},{9,10},{10,... | collective-permute-start | bytes 196616 | tf_op jit(solution)/shard_map/ppermute | solution.py:488
  74.6 9.9 %collective-permute-start.15 = (bf16[256,128]{1,0:T(8,128)(2,1)S(1)}, bf16[256,128]{1,0:T(8,128)(2,1)S(1)}, u32[]{:S(2)}, u32[]{:S(2)}) collective-permute-start(bf16[256,128]{1,0:T(8,128)(2,1)S(1)} %get-tuple-element.78), channel_id=1, source_target_pairs={{0,3},{1,2},{2,1},{3,0},{4,7},{5,6},{6,5},{7,4},{8,11},{9,10},{10,... | collective-permute-start | bytes 196616 | tf_op jit(solution)/shard_map/ppermute | solution.py:488
  75.7 12.3 %collective-permute-start.18 = (bf16[256,128]{1,0:T(8,128)(2,1)S(1)}, bf16[256,128]{1,0:T(8,128)(2,1)S(1)}, u32[]{:S(2)}, u32[]{:S(2)}) collective-permute-start(bf16[256,128]{1,0:T(8,128)(2,1)S(1)} %get-tuple-element.79), channel_id=1, source_target_pairs={{0,2},{1,3},{2,0},{3,1},{4,6},{5,7},{6,4},{7,5},{8,10},{9,11},{10,... | collective-permute-start | bytes 196616 | tf_op jit(solution)/shard_map/ppermute | solution.py:488
  76.4 11.7 %collective-permute-start.19 = (bf16[256,128]{1,0:T(8,128)(2,1)S(1)}, bf16[256,128]{1,0:T(8,128)(2,1)S(1)}, u32[]{:S(2)}, u32[]{:S(2)}) collective-permute-start(bf16[256,128]{1,0:T(8,128)(2,1)S(1)} %get-tuple-element.80), channel_id=1, source_target_pairs={{0,3},{1,2},{2,1},{3,0},{4,7},{5,6},{6,5},{7,4},{8,11},{9,10},{10,... | collective-permute-start | bytes 196616 | tf_op jit(solution)/shard_map/ppermute | solution.py:488
  88.8 11.7 %collective-permute-start.20 = (bf16[256,512]{1,0:T(8,128)(2,1)S(1)}, bf16[256,512]{1,0:T(8,128)(2,1)S(1)}, u32[]{:S(2)}, u32[]{:S(2)}) collective-permute-start(bf16[256,512]{1,0:T(8,128)(2,1)S(1)} %shard_map.87.refs_0_), channel_id=1, source_target_pairs={{0,8},{4,12},{8,0},{12,4},{1,9},{5,13},{9,1},{13,5},{2,10},{6,14},... | collective-permute-start | bytes 786440 | tf_op jit(solution)/shard_map/ppermute | solution.py:469
  89.3 15.1 %collective-permute-start.30 = (bf16[256,512]{1,0:T(8,128)(2,1)S(1)}, bf16[256,512]{1,0:T(8,128)(2,1)S(1)}, u32[]{:S(2)}, u32[]{:S(2)}) collective-permute-start(bf16[256,512]{1,0:T(8,128)(2,1)S(1)} %shard_map.90.refs_0_), channel_id=1, source_target_pairs={{0,4},{4,0},{8,12},{12,8},{1,5},{5,1},{9,13},{13,9},{2,6},{6,2},{1... | collective-permute-start | bytes 786440 | tf_op jit(solution)/shard_map/ppermute | solution.py:474
  95.0 9.5 %collective-permute-start.16 = (bf16[256,512]{1,0:T(8,128)(2,1)S(1)}, bf16[256,512]{1,0:T(8,128)(2,1)S(1)}, u32[]{:S(2)}, u32[]{:S(2)}) collective-permute-start(bf16[256,512]{1,0:T(8,128)(2,1)S(1)} %shard_map.86.refs_1_), channel_id=1, source_target_pairs={{0,8},{4,12},{8,0},{12,4},{1,9},{5,13},{9,1},{13,5},{2,10},{6,14},... | collective-permute-start | bytes 786440 | tf_op jit(solution)/shard_map/ppermute | solution.py:469
  (14 other events, 134.2 us)

commit v12 on v11

--- a/solution.py
+++ b/solution.py
@@ -327,8 +327,7 @@
     for h, x_ref in enumerate(xs):
         mine = y_ref.at[:, :, h * share : (h + 1) * share]
         block_products(g_ref, x_ref, sum_ref, mine, plan, h * share, rows // 2)
-    cut = [outs[2 + i * parts : 2 + (i + 1) * parts] for i in range(n_ctx - 2)]
-    inverse_dft(n_ctx, inv_ref, y_ref, [outs[:1], outs[1:2], *cut])
+    inverse_dft(n_ctx, inv_ref, y_ref, [outs[k * parts : (k + 1) * parts] for k in range(n_ctx)])
 
 
 def convolve(forward, inverse, spectra, even, odd, n_ctx):
@@ -360,17 +359,16 @@
         )
         first.append(made)
         xs.append(x)
-    whole = jax.ShapeDtypeStruct((rows // 2, width), BF16)
     made = call(
         functools.partial(late_kernel, n_ctx, parts),
-        [whole] * 2 + [piece] * ((n_ctx - 2) * parts),
+        [piece] * (n_ctx * parts),
         [inverse, spectra, sums, *xs],
         6,
         flops,
         moved,
         [pltpu.VMEM((n_ctx, rows, width), F32)],
     )
-    return [*first, *(made[:2] + made[2 + h :: parts] for h in range(parts))]
+    return [*first, *(made[h::parts] for h in range(parts))]
 
 
 def gate_kernel(n_ctx, start, share, skip_ref, q_ref, *refs):
@@ -528,14 +526,11 @@
     odd += [odd[0][:2] + exchange(mixed[1][h], 2)[2:] for h in range(1, PARTS)]
     conv = convolve(forward, inverse, spectra, even, odd, n_ctx)
 
-    joint = lax.ppermute(conv[-1][1], "ctx", [(i, target(i, 1, n_ctx)) for i in range(n_ctx)])
     gathered = []
     for r in range(CHUNKS * PARTS):
         c, h = r // PARTS, r % PARTS
-        back = exchange(conv[r], 1 if c == 0 else 2)
-        if c > 0:
-            back[1] = joint
-        share = back[2].shape[1]
+        back = exchange(conv[r])
+        share = back[0].shape[1]
         gated = gate(skip, query[c], mixed[c][h], back, h * share, share, n_ctx)
         beside = swap_cores(gated)
         gathered.append([gated, beside, *gather_far(gated)])

time: 112 us -> 108 us (0.964)
  waiting for transfers between devices: 30 us -> 25.3 us
  starting transfers between devices: 40.2 us -> 41.8 us
    ppermute x6, waiting for transfers between devices: 26.8 us -> 22.3 us  [shift(): return lax.ppermute(x, axis, [(i, (i + by) % n) for i in range(n)])]
    ppermute x18 -> x20, starting transfers between devices: 29.9 us -> 32 us  [exchange(): lax.ppermute(parts[k], 'ctx', [(i, target(i, k, n)) for i in range(n)])]
    ppermute x1 -> x0, waiting for transfers between devices: 1.83 us -> none  [layer_body(): lax.ppermute(conv[-1][1], 'ctx', [(i, target(i, 1, n_ctx)) for i in range...]
    ppermute x18 -> x20, waiting for transfers between devices: 1.34 us -> 2.96 us  [exchange(): lax.ppermute(parts[k], 'ctx', [(i, target(i, k, n)) for i in range(n)])]
  transfers between devices with their start and end apart: 36 -> 37, of which waited for: 8 -> 6; matrix products, arithmetic and copies ran while one was open for 0% -> 0% of each run, Pallas kernels for 35% -> 36%
where the time goes in v12:
time: 108 us; the launch traced here: 107 us
  starting transfers between devices  41.8 us (39%)
  Pallas kernels  39.7 us (37%)
  waiting for transfers between devices  25.3 us (23%)
    ppermute x20, starting transfers between devices, exchange(): lax.ppermute(parts[k], 'ctx', [(i, target(i, k, n)) for i in range(n)])  32 us
    pallas_call x19, Pallas kernels, call(): pl.pallas_call(kernel, out_shape=out, in_specs=[VMEM] * len(operands), ou...  22.7 us
    ppermute x6, waiting for transfers between devices, shift(): return lax.ppermute(x, axis, [(i, (i + by) % n) for i in range(n)])  22.3 us
    pallas_call x1, Pallas kernels, prologue(): pl.pallas_call(functools.partial(prologue_kernel, width), out_shape=out,...  8.73 us
    ppermute x6, starting transfers between devices, shift(): return lax.ppermute(x, axis, [(i, (i + by) % n) for i in range(n)])  7.86 us
    pallas_call x4, Pallas kernels, project_out(): pl.pallas_call(functools.partial(out_kernel, tuple(which), parts, before...  7.06 us
    ppermute x20, waiting for transfers between devices, exchange(): lax.ppermute(parts[k], 'ctx', [(i, target(i, k, n)) for i in range(n)])  2.96 us
  transfers between devices with their start and end apart: 37, of which 6 were waited for; matrix products, arithmetic and copies ran while one was open for 0% of the time, Pallas kernels for 36%

profile of v12, /device:TPU:0, one launch (start us, length us, event | category | flops | bytes accessed | tf_op | source)
XLA Modules:
  0.0 107.4 jit_solution(12488961704399415223)
XLA Ops:
  1.7 2.6 %collective-permute-start.3 = (bf16[256,1024]{1,0:T(8,128)(2,1)S(1)}, bf16[256,1024]{1,0:T(8,128)(2,1)S(1)}, u32[]{:S(2)}, u32[]{:S(2)}) collective-permute-start(bf16[256,1024]{1,0:T(8,128)(2,1)S(1)} %get-tuple-element.64.refs_0_), channel_id=1, source_target_pairs={{0,8},{4,12},{8,0},{12,4},{1,9},{5,13},{9,1},{13,5},{2,10},{6,14},... | collective-permute-start | bytes 1572872 | tf_op jit(solution)/shard_map/ppermute | solution.py:467
  4.4 12.7 %collective-permute-done.3.refs_0_ = bf16[256,1024]{1,0:T(8,128)(2,1)S(1)} collective-permute-done((bf16[256,1024]{1,0:T(8,128)(2,1)S(1)}, bf16[256,1024]{1,0:T(8,128)(2,1)S(1)}, u32[]{:S(2)}, u32[]{:S(2)}) %collective-permute-start.3) | collective-permute-done | bytes 524320 | tf_op jit(solution)/shard_map/ppermute | solution.py:467
  17.1 8.7 %prologue.1 = (bf16[512,256]{1,0:T(8,128)(2,1)S(1)}, bf16[256,512]{1,0:T(8,128)(2,1)S(1)}, bf16[2,4096,1024]{2,1,0:T(8,128)(2,1)S(1)}, bf16[4096,1024]{1,0:T(8,1...) custom-call(f32[1024]{0:T(1024)} %skip_hbm.1, bf16[512,256]{1,0:T(8,128)(2,1)} %constant.4.clone.fwd_hbm, ...), custom_call_target="tpu_custom_call" | custom-call | flops 536870912 | bytes 30408704 | tf_op jit(solution)/shard_map/prologue/pallas_call | solution.py:152
  25.8 2.3 %collective-permute-done.1.refs_2_.refs_0_ = bf16[256,1024]{1,0:T(8,128)(2,1)S(1)} collective-permute-done((bf16[256,1024]{1,0:T(8,128)(2,1)S(1)}, bf16[256,1024]{1,0:T(8,128)(2,1)S(1)}, u32[]{:S(2)}, u32[]{:S(2)}) %collective-permute-start.1) | collective-permute-done | bytes 524320 | tf_op jit(solution)/shard_map/ppermute | solution.py:467
  28.1 2.4 %shard_map.78 = (f32[256,1024]{1,0:T(8,128)S(1)}, f32[256,1024]{1,0:T(8,128)S(1)}) custom-call(bf16[2,4096,1024]{2,1,0:T(8,128)(2,1)S(1)} %get-tuple-element.52.w_ref, bf16[256,1024]{1,0:T(8,128)(2,1)S(1)} %get-tuple-element.64.refs_0_, bf16[512,1024]{1,0:T(8,128)(2,1)S(1)} %collective-permute-done.refs_1_), custom_call_target="tpu_custom_call" | custom-call | flops 2147483648 | bytes 9437184 | tf_op jit(solution)/shard_map/pallas_call | solution.py:43
  32.7 2.9 %collective-permute-start.6 = (bf16[256,256]{1,0:T(8,128)(2,1)S(1)}, bf16[256,256]{1,0:T(8,128)(2,1)S(1)}, u32[]{:S(2)}, u32[]{:S(2)}) collective-permute-start(bf16[256,256]{1,0:T(8,128)(2,1)S(1)} %get-tuple-element.71.refs_2_), channel_id=1, source_target_pairs={{0,2},{1,3},{2,0},{3,1},{4,6},{5,7},{6,4},{7,5},{8,10},{9,11},{10,... | collective-permute-start | bytes 393224 | tf_op jit(solution)/shard_map/ppermute | solution.py:486
  38.0 2.4 %shard_map.74 = (f32[256,1024]{1,0:T(8,128)S(1)}, f32[256,1024]{1,0:T(8,128)S(1)}) custom-call(bf16[2,4096,1024]{2,1,0:T(8,128)(2,1)S(1)} %get-tuple-element.52.w_ref, bf16[256,1024]{1,0:T(8,128)(2,1)S(1)} %get-tuple-element.51.refs_0_, bf16[512,1024]{1,0:T(8,128)(2,1)S(1)} %collective-permute-done.refs_1_), custom_call_target="tpu_custom_call" | custom-call | flops 2147483648 | bytes 9437184 | tf_op jit(solution)/shard_map/pallas_call | solution.py:43
  42.6 1.8 %collective-permute-start.8 = (bf16[256,256]{1,0:T(8,128)(2,1)S(1)}, bf16[256,256]{1,0:T(8,128)(2,1)S(1)}, u32[]{:S(2)}, u32[]{:S(2)}) collective-permute-start(bf16[256,256]{1,0:T(8,128)(2,1)S(1)} %get-tuple-element.58.refs_1_), channel_id=1, source_target_pairs={{0,1},{1,0},{2,3},{3,2},{4,5},{5,4},{6,7},{7,6},{8,9},{9,8},{10,11... | collective-permute-start | bytes 393224 | tf_op jit(solution)/shard_map/ppermute | solution.py:486
  45.1 1.8 %collective-permute-start.11 = (bf16[256,128]{1,0:T(8,128)(2,1)S(1)}, bf16[256,128]{1,0:T(8,128)(2,1)S(1)}, u32[]{:S(2)}, u32[]{:S(2)}) collective-permute-start(bf16[256,128]{1,0:T(8,128)(2,1)S(1)} %get-tuple-element.59.refs_2_), channel_id=1, source_target_pairs={{0,2},{1,3},{2,0},{3,1},{4,6},{5,7},{6,4},{7,5},{8,10},{9,11},{10,... | collective-permute-start | bytes 196616 | tf_op jit(solution)/shard_map/ppermute | solution.py:486
  46.9 2.0 %collective-permute-start.12 = (bf16[256,128]{1,0:T(8,128)(2,1)S(1)}, bf16[256,128]{1,0:T(8,128)(2,1)S(1)}, u32[]{:S(2)}, u32[]{:S(2)}) collective-permute-start(bf16[256,128]{1,0:T(8,128)(2,1)S(1)} %get-tuple-element.60.refs_3_), channel_id=1, source_target_pairs={{0,3},{1,2},{2,1},{3,0},{4,7},{5,6},{6,5},{7,4},{8,11},{9,10},{10,... | collective-permute-start | bytes 196616 | tf_op jit(solution)/shard_map/ppermute | solution.py:486
  49.0 2.6 %collective-permute-start.9 = (bf16[256,128]{1,0:T(8,128)(2,1)S(1)}, bf16[256,128]{1,0:T(8,128)(2,1)S(1)}, u32[]{:S(2)}, u32[]{:S(2)}) collective-permute-start(bf16[256,128]{1,0:T(8,128)(2,1)S(1)} %get-tuple-element.73.refs_2_), channel_id=1, source_target_pairs={{0,2},{1,3},{2,0},{3,1},{4,6},{5,7},{6,4},{7,5},{8,10},{9,11},{10,... | collective-permute-start | bytes 196616 | tf_op jit(solution)/shard_map/ppermute | solution.py:486
  53.3 2.1 %shard_map.82.sum_ref = f32[8,512,256]{2,1,0:T(8,128)S(1)} custom-call(bf16[512,256]{1,0:T(8,128)(2,1)S(1)} %get-tuple-element.63.fwd_ref, f32[8,512,256]{2,1,0:T(8,128)S(1)} %get-tuple-element.62.g_ref, bf16[256,256]{1,0:T(8,128)(2,1)S(1)} %get-tuple-element.69.refs_0_, bf16[256,256]{1,0:T(8,128)(2,1)S(1)} %collective-permute-done.5.refs_1_, ...), custom_call_target="tpu_custom_call" | custom-call | flops 268435456 | bytes 8388608 | tf_op jit(solution)/shard_map/pallas_call | solution.py:43
  56.8 2.0 %collective-permute-start.28 = (bf16[256,128]{1,0:T(8,128)(2,1)S(1)}, bf16[256,128]{1,0:T(8,128)(2,1)S(1)}, u32[]{:S(2)}, u32[]{:S(2)}) collective-permute-start(bf16[256,128]{1,0:T(8,128)(2,1)S(1)} %get-tuple-element.90), channel_id=1, source_target_pairs={{0,1},{1,0},{2,3},{3,2},{4,5},{5,4},{6,7},{7,6},{8,9},{9,8},{10,11... | collective-permute-start | bytes 196616 | tf_op jit(solution)/shard_map/ppermute | solution.py:486
  58.9 2.0 %collective-permute-start.29 = (bf16[256,128]{1,0:T(8,128)(2,1)S(1)}, bf16[256,128]{1,0:T(8,128)(2,1)S(1)}, u32[]{:S(2)}, u32[]{:S(2)}) collective-permute-start(bf16[256,128]{1,0:T(8,128)(2,1)S(1)} %get-tuple-element.91), channel_id=1, source_target_pairs={{0,2},{1,3},{2,0},{3,1},{4,6},{5,7},{6,4},{7,5},{8,10},{9,11},{10,... | collective-permute-start | bytes 196616 | tf_op jit(solution)/shard_map/ppermute | solution.py:486
  63.6 1.8 %shard_map.85 = (bf16[256,128]{1,0:T(8,128)(2,1)S(1)}, bf16[256,128]{1,0:T(8,128)(2,1)S(1)}, bf16[256,128]{1,0:T(8,128)(2,1)S(1)}, bf16[256,128]{1,0:T(8,128)(2,...) custom-call(bf16[256,512]{1,0:T(8,128)(2,1)S(1)} %get-tuple-element., ...), custom_call_target="tpu_custom_call" | custom-call | flops 268435456 | bytes 8388608 | tf_op jit(solution)/shard_map/pallas_call | solution.py:43
  66.0 2.4 %collective-permute-start.19 = (bf16[256,128]{1,0:T(8,128)(2,1)S(1)}, bf16[256,128]{1,0:T(8,128)(2,1)S(1)}, u32[]{:S(2)}, u32[]{:S(2)}) collective-permute-start(bf16[256,128]{1,0:T(8,128)(2,1)S(1)} %get-tuple-element.83), channel_id=1, source_target_pairs={{0,2},{1,3},{2,0},{3,1},{4,6},{5,7},{6,4},{7,5},{8,10},{9,11},{10,... | collective-permute-start | bytes 196616 | tf_op jit(solution)/shard_map/ppermute | solution.py:486
  71.2 3.0 %collective-permute-start.26 = (bf16[256,128]{1,0:T(8,128)(2,1)S(1)}, bf16[256,128]{1,0:T(8,128)(2,1)S(1)}, u32[]{:S(2)}, u32[]{:S(2)}) collective-permute-start(bf16[256,128]{1,0:T(8,128)(2,1)S(1)} %get-tuple-element.87), channel_id=1, source_target_pairs={{0,2},{1,3},{2,0},{3,1},{4,6},{5,7},{6,4},{7,5},{8,10},{9,11},{10,... | collective-permute-start | bytes 196616 | tf_op jit(solution)/shard_map/ppermute | solution.py:486
  77.4 2.4 %shard_map.73.q_ref = bf16[256,1024]{1,0:T(8,128)(2,1)S(1)} custom-call(bf16[4096,1024]{1,0:T(8,128)(2,1)S(1)} %get-tuple-element.50.w_ref, bf16[256,1024]{1,0:T(8,128)(2,1)S(1)} %get-tuple-element.51.refs_0_, bf16[512,1024]{1,0:T(8,128)(2,1)S(1)} %collective-permute-done.refs_1_, bf16[256,1024]{1,0:T(8,128)(2,1)S(1)} %collective-permute-done.1.refs_2_.refs_0_, ...), custom_call_target="tpu_custom_call" | custom-call | flops 2147483648 | bytes 10485760 | tf_op jit(solution)/shard_map/pallas_call | solution.py:43
  80.5 3.0 %collective-permute-start.14 = (bf16[256,128]{1,0:T(8,128)(2,1)S(1)}, bf16[256,128]{1,0:T(8,128)(2,1)S(1)}, u32[]{:S(2)}, u32[]{:S(2)}) collective-permute-start(bf16[256,128]{1,0:T(8,128)(2,1)S(1)} %get-tuple-element.79), channel_id=1, source_target_pairs={{0,2},{1,3},{2,0},{3,1},{4,6},{5,7},{6,4},{7,5},{8,10},{9,11},{10,... | collective-permute-start | bytes 196616 | tf_op jit(solution)/shard_map/ppermute | solution.py:486
  87.8 1.8 %collective-permute-done.15.refs_7_ = bf16[256,128]{1,0:T(8,128)(2,1)S(1)} collective-permute-done((bf16[256,128]{1,0:T(8,128)(2,1)S(1)}, bf16[256,128]{1,0:T(8,128)(2,1)S(1)}, u32[]{:S(2)}, u32[]{:S(2)}) %collective-permute-start.15) | collective-permute-done | bytes 65568 | tf_op jit(solution)/shard_map/ppermute | solution.py:486
  89.8 1.6 %collective-permute-start.16 = (bf16[256,512]{1,0:T(8,128)(2,1)S(1)}, bf16[256,512]{1,0:T(8,128)(2,1)S(1)}, u32[]{:S(2)}, u32[]{:S(2)}) collective-permute-start(bf16[256,512]{1,0:T(8,128)(2,1)S(1)} %shard_map.86.refs_1_), channel_id=1, source_target_pairs={{0,8},{4,12},{8,0},{12,4},{1,9},{5,13},{9,1},{13,5},{2,10},{6,14},... | collective-permute-start | bytes 786440 | tf_op jit(solution)/shard_map/ppermute | solution.py:467
  91.6 3.3 %collective-permute-done.33.refs_4_ = bf16[256,512]{1,0:T(8,128)(2,1)S(1)} collective-permute-done((bf16[256,512]{1,0:T(8,128)(2,1)S(1)}, bf16[256,512]{1,0:T(8,128)(2,1)S(1)}, u32[]{:S(2)}, u32[]{:S(2)}) %collective-permute-start.33) | collective-permute-done | bytes 262176 | tf_op jit(solution)/shard_map/ppermute | solution.py:467
  95.4 4.1 %collective-permute-done.16.refs_1_ = bf16[256,512]{1,0:T(8,128)(2,1)S(1)} collective-permute-done((bf16[256,512]{1,0:T(8,128)(2,1)S(1)}, bf16[256,512]{1,0:T(8,128)(2,1)S(1)}, u32[]{:S(2)}, u32[]{:S(2)}) %collective-permute-start.16) | collective-permute-done | bytes 262176 | tf_op jit(solution)/shard_map/ppermute | solution.py:467
  102.6 3.1 %out_projection.6.refs_2_ = bf16[512,1024]{1,0:T(8,128)(2,1)} custom-call(bf16[4096,1024]{1,0:T(8,128)(2,1)S(1)} %bitcast.2, bf16[256,512]{1,0:T(8,128)(2,1)S(1)} %shard_map.90.refs_0_, bf16[256,512]{1,0:T(8,128)(2,1)S(1)} %shard_map.91.refs_1_, bf16[256,512]{1,0:T(8,128)(2,1)S(1)} %collective-permute-done.31.refs_2_, ...), custom_call_target="tpu_custom_call" | custom-call | flops 2147483648 | bytes 11010048 | tf_op jit(solution)/shard_map/out_projection/pallas_call | solution.py:448
  (80 shorter events, 32.0 us)
Async XLA Ops:
  0.0 28.1 %collective-permute-start = (bf16[512,1024]{1,0:T(8,128)(2,1)}, bf16[512,1024]{1,0:T(8,128)(2,1)S(1)}, u32[]{:S(2)}, u32[]{:S(2)}) collective-permute-start(bf16[512,1024]{1,0:T(8,128)(2,1)} %x_ref.1), channel_id=1, source_target_pairs={{0,4},{4,0},{8,12},{12,8},{1,5},{5,1},{9,13},{13,9},{2,6},{6,2},{1... | collective-permute-start | bytes 3145736 | tf_op jit(solution)/shard_map/ppermute | solution.py:472
  1.7 15.3 %collective-permute-start.3 = (bf16[256,1024]{1,0:T(8,128)(2,1)S(1)}, bf16[256,1024]{1,0:T(8,128)(2,1)S(1)}, u32[]{:S(2)}, u32[]{:S(2)}) collective-permute-start(bf16[256,1024]{1,0:T(8,128)(2,1)S(1)} %get-tuple-element.64.refs_0_), channel_id=1, source_target_pairs={{0,8},{4,12},{8,0},{12,4},{1,9},{5,13},{9,1},{13,5},{2,10},{6,14},... | collective-permute-start | bytes 1572872 | tf_op jit(solution)/shard_map/ppermute | solution.py:467
  4.3 23.8 %collective-permute-start.1 = (bf16[256,1024]{1,0:T(8,128)(2,1)S(1)}, bf16[256,1024]{1,0:T(8,128)(2,1)S(1)}, u32[]{:S(2)}, u32[]{:S(2)}) collective-permute-start(bf16[256,1024]{1,0:T(8,128)(2,1)S(1)} %get-tuple-element.51.refs_0_), channel_id=1, source_target_pairs={{0,8},{4,12},{8,0},{12,4},{1,9},{5,13},{9,1},{13,5},{2,10},{6,14},... | collective-permute-start | bytes 1572872 | tf_op jit(solution)/shard_map/ppermute | solution.py:467
  17.1 14.8 %collective-permute-start.4 = (bf16[256,1024]{1,0:T(8,128)(2,1)S(1)}, bf16[256,1024]{1,0:T(8,128)(2,1)S(1)}, u32[]{:S(2)}, u32[]{:S(2)}) collective-permute-start(bf16[256,1024]{1,0:T(8,128)(2,1)S(1)} %collective-permute-done.3.refs_0_), channel_id=1, source_target_pairs={{0,4},{4,0},{8,12},{12,8},{1,5},{5,1},{9,13},{13,9},{2,6},{6,2},{1... | collective-permute-start | bytes 1572872 | tf_op jit(solution)/shard_map/ppermute | solution.py:472
  28.1 13.7 %collective-permute-start.2 = (bf16[256,1024]{1,0:T(8,128)(2,1)S(1)}, bf16[256,1024]{1,0:T(8,128)(2,1)S(1)}, u32[]{:S(2)}, u32[]{:S(2)}) collective-permute-start(bf16[256,1024]{1,0:T(8,128)(2,1)S(1)} %collective-permute-done.1.refs_2_.refs_0_), channel_id=1, source_target_pairs={{0,4},{4,0},{8,12},{12,8},{1,5},{5,1},{9,13},{13,9},{2,6},{6,2},{1... | collective-permute-start | bytes 1572872 | tf_op jit(solution)/shard_map/ppermute | solution.py:472
  32.7 14.3 %collective-permute-start.6 = (bf16[256,256]{1,0:T(8,128)(2,1)S(1)}, bf16[256,256]{1,0:T(8,128)(2,1)S(1)}, u32[]{:S(2)}, u32[]{:S(2)}) collective-permute-start(bf16[256,256]{1,0:T(8,128)(2,1)S(1)} %get-tuple-element.71.refs_2_), channel_id=1, source_target_pairs={{0,2},{1,3},{2,0},{3,1},{4,6},{5,7},{6,4},{7,5},{8,10},{9,11},{10,... | collective-permute-start | bytes 393224 | tf_op jit(solution)/shard_map/ppermute | solution.py:486
  35.5 13.4 %collective-permute-start.7 = (bf16[256,256]{1,0:T(8,128)(2,1)S(1)}, bf16[256,256]{1,0:T(8,128)(2,1)S(1)}, u32[]{:S(2)}, u32[]{:S(2)}) collective-permute-start(bf16[256,256]{1,0:T(8,128)(2,1)S(1)} %get-tuple-element.72.refs_3_), channel_id=1, source_target_pairs={{0,3},{1,2},{2,1},{3,0},{4,7},{5,6},{6,5},{7,4},{8,11},{9,10},{10,... | collective-permute-start | bytes 393224 | tf_op jit(solution)/shard_map/ppermute | solution.py:486
  37.7 13.9 %collective-permute-start.5 = (bf16[256,256]{1,0:T(8,128)(2,1)S(1)}, bf16[256,256]{1,0:T(8,128)(2,1)S(1)}, u32[]{:S(2)}, u32[]{:S(2)}) collective-permute-start(bf16[256,256]{1,0:T(8,128)(2,1)S(1)} %get-tuple-element.70.refs_1_), channel_id=1, source_target_pairs={{0,1},{1,0},{2,3},{3,2},{4,5},{5,4},{6,7},{7,6},{8,9},{9,8},{10,11... | collective-permute-start | bytes 393224 | tf_op jit(solution)/shard_map/ppermute | solution.py:486
  42.6 12.8 %collective-permute-start.8 = (bf16[256,256]{1,0:T(8,128)(2,1)S(1)}, bf16[256,256]{1,0:T(8,128)(2,1)S(1)}, u32[]{:S(2)}, u32[]{:S(2)}) collective-permute-start(bf16[256,256]{1,0:T(8,128)(2,1)S(1)} %get-tuple-element.58.refs_1_), channel_id=1, source_target_pairs={{0,1},{1,0},{2,3},{3,2},{4,5},{5,4},{6,7},{7,6},{8,9},{9,8},{10,11... | collective-permute-start | bytes 393224 | tf_op jit(solution)/shard_map/ppermute | solution.py:486
  45.1 10.3 %collective-permute-start.11 = (bf16[256,128]{1,0:T(8,128)(2,1)S(1)}, bf16[256,128]{1,0:T(8,128)(2,1)S(1)}, u32[]{:S(2)}, u32[]{:S(2)}) collective-permute-start(bf16[256,128]{1,0:T(8,128)(2,1)S(1)} %get-tuple-element.59.refs_2_), channel_id=1, source_target_pairs={{0,2},{1,3},{2,0},{3,1},{4,6},{5,7},{6,4},{7,5},{8,10},{9,11},{10,... | collective-permute-start | bytes 196616 | tf_op jit(solution)/shard_map/ppermute | solution.py:486
  49.0 13.3 %collective-permute-start.9 = (bf16[256,128]{1,0:T(8,128)(2,1)S(1)}, bf16[256,128]{1,0:T(8,128)(2,1)S(1)}, u32[]{:S(2)}, u32[]{:S(2)}) collective-permute-start(bf16[256,128]{1,0:T(8,128)(2,1)S(1)} %get-tuple-element.73.refs_2_), channel_id=1, source_target_pairs={{0,2},{1,3},{2,0},{3,1},{4,6},{5,7},{6,4},{7,5},{8,10},{9,11},{10,... | collective-permute-start | bytes 196616 | tf_op jit(solution)/shard_map/ppermute | solution.py:486
  51.6 10.7 %collective-permute-start.10 = (bf16[256,128]{1,0:T(8,128)(2,1)S(1)}, bf16[256,128]{1,0:T(8,128)(2,1)S(1)}, u32[]{:S(2)}, u32[]{:S(2)}) collective-permute-start(bf16[256,128]{1,0:T(8,128)(2,1)S(1)} %get-tuple-element.74.refs_3_), channel_id=1, source_target_pairs={{0,3},{1,2},{2,1},{3,0},{4,7},{5,6},{6,5},{7,4},{8,11},{9,10},{10,... | collective-permute-start | bytes 196616 | tf_op jit(solution)/shard_map/ppermute | solution.py:486
  56.8 13.0 %collective-permute-start.28 = (bf16[256,128]{1,0:T(8,128)(2,1)S(1)}, bf16[256,128]{1,0:T(8,128)(2,1)S(1)}, u32[]{:S(2)}, u32[]{:S(2)}) collective-permute-start(bf16[256,128]{1,0:T(8,128)(2,1)S(1)} %get-tuple-element.90), channel_id=1, source_target_pairs={{0,1},{1,0},{2,3},{3,2},{4,5},{5,4},{6,7},{7,6},{8,9},{9,8},{10,11... | collective-permute-start | bytes 196616 | tf_op jit(solution)/shard_map/ppermute | solution.py:486
  58.9 12.4 %collective-permute-start.29 = (bf16[256,128]{1,0:T(8,128)(2,1)S(1)}, bf16[256,128]{1,0:T(8,128)(2,1)S(1)}, u32[]{:S(2)}, u32[]{:S(2)}) collective-permute-start(bf16[256,128]{1,0:T(8,128)(2,1)S(1)} %get-tuple-element.91), channel_id=1, source_target_pairs={{0,2},{1,3},{2,0},{3,1},{4,6},{5,7},{6,4},{7,5},{8,10},{9,11},{10,... | collective-permute-start | bytes 196616 | tf_op jit(solution)/shard_map/ppermute | solution.py:486
  60.9 10.4 %collective-permute-start.30 = (bf16[256,128]{1,0:T(8,128)(2,1)S(1)}, bf16[256,128]{1,0:T(8,128)(2,1)S(1)}, u32[]{:S(2)}, u32[]{:S(2)}) collective-permute-start(bf16[256,128]{1,0:T(8,128)(2,1)S(1)} %get-tuple-element.92), channel_id=1, source_target_pairs={{0,3},{1,2},{2,1},{3,0},{4,7},{5,6},{6,5},{7,4},{8,11},{9,10},{10,... | collective-permute-start | bytes 196616 | tf_op jit(solution)/shard_map/ppermute | solution.py:486
  66.0 9.8 %collective-permute-start.19 = (bf16[256,128]{1,0:T(8,128)(2,1)S(1)}, bf16[256,128]{1,0:T(8,128)(2,1)S(1)}, u32[]{:S(2)}, u32[]{:S(2)}) collective-permute-start(bf16[256,128]{1,0:T(8,128)(2,1)S(1)} %get-tuple-element.83), channel_id=1, source_target_pairs={{0,2},{1,3},{2,0},{3,1},{4,6},{5,7},{6,4},{7,5},{8,10},{9,11},{10,... | collective-permute-start | bytes 196616 | tf_op jit(solution)/shard_map/ppermute | solution.py:486
  69.8 10.0 %collective-permute-start.20 = (bf16[256,128]{1,0:T(8,128)(2,1)S(1)}, bf16[256,128]{1,0:T(8,128)(2,1)S(1)}, u32[]{:S(2)}, u32[]{:S(2)}) collective-permute-start(bf16[256,128]{1,0:T(8,128)(2,1)S(1)} %get-tuple-element.84), channel_id=1, source_target_pairs={{0,3},{1,2},{2,1},{3,0},{4,7},{5,6},{6,5},{7,4},{8,11},{9,10},{10,... | collective-permute-start | bytes 196616 | tf_op jit(solution)/shard_map/ppermute | solution.py:486
  71.2 9.3 %collective-permute-start.25 = (bf16[256,128]{1,0:T(8,128)(2,1)S(1)}, bf16[256,128]{1,0:T(8,128)(2,1)S(1)}, u32[]{:S(2)}, u32[]{:S(2)}) collective-permute-start(bf16[256,128]{1,0:T(8,128)(2,1)S(1)} %get-tuple-element.86), channel_id=1, source_target_pairs={{0,1},{1,0},{2,3},{3,2},{4,5},{5,4},{6,7},{7,6},{8,9},{9,8},{10,11... | collective-permute-start | bytes 196616 | tf_op jit(solution)/shard_map/ppermute | solution.py:486
  71.2 9.3 %collective-permute-start.26 = (bf16[256,128]{1,0:T(8,128)(2,1)S(1)}, bf16[256,128]{1,0:T(8,128)(2,1)S(1)}, u32[]{:S(2)}, u32[]{:S(2)}) collective-permute-start(bf16[256,128]{1,0:T(8,128)(2,1)S(1)} %get-tuple-element.87), channel_id=1, source_target_pairs={{0,2},{1,3},{2,0},{3,1},{4,6},{5,7},{6,4},{7,5},{8,10},{9,11},{10,... | collective-permute-start | bytes 196616 | tf_op jit(solution)/shard_map/ppermute | solution.py:486
  75.9 14.0 %collective-permute-start.34 = (bf16[256,512]{1,0:T(8,128)(2,1)S(1)}, bf16[256,512]{1,0:T(8,128)(2,1)S(1)}, u32[]{:S(2)}, u32[]{:S(2)}) collective-permute-start(bf16[256,512]{1,0:T(8,128)(2,1)S(1)} %shard_map.91.refs_1_), channel_id=1, source_target_pairs={{0,8},{4,12},{8,0},{12,4},{1,9},{5,13},{9,1},{13,5},{2,10},{6,14},... | collective-permute-start | bytes 786440 | tf_op jit(solution)/shard_map/ppermute | solution.py:467
  80.0 11.5 %collective-permute-start.21 = (bf16[256,512]{1,0:T(8,128)(2,1)S(1)}, bf16[256,512]{1,0:T(8,128)(2,1)S(1)}, u32[]{:S(2)}, u32[]{:S(2)}) collective-permute-start(bf16[256,512]{1,0:T(8,128)(2,1)S(1)} %shard_map.87.refs_0_), channel_id=1, source_target_pairs={{0,8},{4,12},{8,0},{12,4},{1,9},{5,13},{9,1},{13,5},{2,10},{6,14},... | collective-permute-start | bytes 786440 | tf_op jit(solution)/shard_map/ppermute | solution.py:467
  85.1 9.8 %collective-permute-start.23 = (bf16[256,512]{1,0:T(8,128)(2,1)S(1)}, bf16[256,512]{1,0:T(8,128)(2,1)S(1)}, u32[]{:S(2)}, u32[]{:S(2)}) collective-permute-start(bf16[256,512]{1,0:T(8,128)(2,1)S(1)} %shard_map.87.refs_0_), channel_id=1, source_target_pairs={{0,4},{4,0},{8,12},{12,8},{1,5},{5,1},{9,13},{13,9},{2,6},{6,2},{1... | collective-permute-start | bytes 786440 | tf_op jit(solution)/shard_map/ppermute | solution.py:472
  89.8 9.7 %collective-permute-start.16 = (bf16[256,512]{1,0:T(8,128)(2,1)S(1)}, bf16[256,512]{1,0:T(8,128)(2,1)S(1)}, u32[]{:S(2)}, u32[]{:S(2)}) collective-permute-start(bf16[256,512]{1,0:T(8,128)(2,1)S(1)} %shard_map.86.refs_1_), channel_id=1, source_target_pairs={{0,8},{4,12},{8,0},{12,4},{1,9},{5,13},{9,1},{13,5},{2,10},{6,14},... | collective-permute-start | bytes 786440 | tf_op jit(solution)/shard_map/ppermute | solution.py:467
  91.4 9.3 %collective-permute-start.22 = (bf16[256,512]{1,0:T(8,128)(2,1)S(1)}, bf16[256,512]{1,0:T(8,128)(2,1)S(1)}, u32[]{:S(2)}, u32[]{:S(2)}) collective-permute-start(bf16[256,512]{1,0:T(8,128)(2,1)S(1)} %collective-permute-done.21.refs_0_), channel_id=1, source_target_pairs={{0,4},{4,0},{8,12},{12,8},{1,5},{5,1},{9,13},{13,9},{2,6},{6,2},{1... | collective-permute-start | bytes 786440 | tf_op jit(solution)/shard_map/ppermute | solution.py:472
  (15 other events, 138.2 us)
